TPU v7x, 32 devices: a whole 2x2x4 slice. The times are simulated.
32 devices in a mesh: seq: 8 (over y, x, core), tp: 4 (over z).
Axes of the slice: x: 2, y: 2, z: 4, core: 2. Of those that a mesh axis runs over, the one named last changes fastest.
Arguments:
- x_prefix: bfloat16 [2048, 2048], P('seq', 'tp'), may hold values from -6 to 6
- x_action: bfloat16 [128, 1024], P('seq', 'tp'), may hold values from -6 to 6
- prefix_segment: int32 [2048], replicated, may hold values from 0 to 2, as said below
- prefix_attn_gain: bfloat16 [2048], P('seq'), may hold values from 0.5 to 1.5
- prefix_query: bfloat16 [2048, 2048], P('seq', 'tp'), may hold values from -0.125 to 0.125
- prefix_key: bfloat16 [2048, 256], P('seq'), may hold values from -0.125 to 0.125
- prefix_value: bfloat16 [2048, 256], P('seq'), may hold values from -0.125 to 0.125
- prefix_out: bfloat16 [2048, 2048], P('tp', 'seq'), may hold values from -2 to 2
- prefix_mlp_gain: bfloat16 [2048], P('seq'), may hold values from 0.5 to 1.5
- prefix_gate: bfloat16 [2048, 16384], P('seq', 'tp'), may hold values from -0.125 to 0.125
- prefix_up: bfloat16 [2048, 16384], P('seq', 'tp'), may hold values from -0.125 to 0.125
- prefix_down: bfloat16 [16384, 2048], P('tp', 'seq'), may hold values from -0.046875 to 0.046875
- action_attn_gain: bfloat16 [1024], P('seq'), may hold values from 0.5 to 1.5
- action_query: bfloat16 [1024, 2048], P('seq', 'tp'), may hold values from -0.1875 to 0.1875
- action_key: bfloat16 [1024, 256], P('seq'), may hold values from -0.1875 to 0.1875
- action_value: bfloat16 [1024, 256], P('seq'), may hold values from -0.1875 to 0.1875
- action_out: bfloat16 [2048, 1024], P('tp', 'seq'), may hold values from -2 to 2
- action_mlp_gain: bfloat16 [1024], P('seq'), may hold values from 0.5 to 1.5
- action_gate: bfloat16 [1024, 4096], P('seq', 'tp'), may hold values from -0.1875 to 0.1875
- action_up: bfloat16 [1024, 4096], P('seq', 'tp'), may hold values from -0.1875 to 0.1875
- action_down: bfloat16 [4096, 1024], P('tp', 'seq'), may hold values from -0.09375 to 0.09375
- cot_prefix: bfloat16 [2048, 2048], P('seq'), may hold values from -6 to 6
- cot_action: bfloat16 [128, 1024], P('seq'), may hold values from -6 to 6
Outputs:
- out_prefix: bfloat16 [2048, 2048], P('seq', 'tp')
- out_action: bfloat16 [128, 1024], P('seq', 'tp')
- grad_x_prefix: bfloat16 [2048, 2048], P('seq', 'tp')
- grad_x_action: bfloat16 [128, 1024], P('seq', 'tp')
- grad_prefix_attn_gain: float32 [2048], P('seq')
- grad_prefix_query: float32 [2048, 2048], P('seq', 'tp')
- grad_prefix_key: float32 [2048, 256], P(('seq', 'tp'))
- grad_prefix_value: float32 [2048, 256], P(('seq', 'tp'))
- grad_prefix_out: float32 [2048, 2048], P('tp', 'seq')
- grad_prefix_mlp_gain: float32 [2048], P('seq')
- grad_prefix_gate: float32 [2048, 16384], P('seq', 'tp')
- grad_prefix_up: float32 [2048, 16384], P('seq', 'tp')
- grad_prefix_down: float32 [16384, 2048], P('tp', 'seq')
- grad_action_attn_gain: float32 [1024], P('seq')
- grad_action_query: float32 [1024, 2048], P('seq', 'tp')
- grad_action_key: float32 [1024, 256], P(('seq', 'tp'))
- grad_action_value: float32 [1024, 256], P(('seq', 'tp'))
- grad_action_out: float32 [2048, 1024], P('tp', 'seq')
- grad_action_mlp_gain: float32 [1024], P('seq')
- grad_action_gate: float32 [1024, 4096], P('seq', 'tp')
- grad_action_up: float32 [1024, 4096], P('seq', 'tp')
- grad_action_down: float32 [4096, 1024], P('tp', 'seq')
Inputs may be any that keep to these rules, and one draw needn't show every extreme that they name: prefix_segment never falls along the rows; items 0 to 1 follow in order, each of 768 + t rows with t from 5 to 48; all later rows carry 2.
All inputs are finite; a program needn't handle non-finite values.
Results may differ from a plain program's by a relative error of at most 0.028.
Values may be sent and summed in bfloat16 or wider, within the bound.
No kernel may reach another device: no remote copies, remote signals or barrier semaphores. Data moves between devices by JAX's collectives and lax.ppermute only.
A program may use at most 256 MiB of HBM per device.

v0:
```python
import math

import jax
import jax.numpy as jnp
from jax import lax
from jax.sharding import PartitionSpec as P

HD = 256
IMG = 768
TXT = 48
ACT = 50


EPS = 1e-06
NEG = -1e30


def normalized_rows(values):
    inverse_norm = lax.rsqrt(jnp.mean(values * values, axis=1, keepdims=True) + EPS)
    return (values * inverse_norm, inverse_norm)


def norm_backward(output_gradient, centered_input, inverse_norm, norm_scale):
    inner_output = output_gradient * norm_scale
    moved_state = inverse_norm * (
        inner_output
        - centered_input * jnp.mean(inner_output * centered_input, axis=1, keepdims=True)
    )
    return (moved_state, jnp.sum(output_gradient * centered_input, axis=0))


def gated(gate_in, up_in):
    return jax.nn.gelu(gate_in, approximate=True) * up_in


def key_tables(prefix_segment, seq_count, pre_rows, suf_rows):
    items_all = prefix_segment.shape[0] // (IMG + TXT)
    places = jnp.arange(seq_count * suf_rows, dtype=jnp.int32)
    items_of = places // (ACT + 1)
    suffix_seg = jnp.where(items_of < items_all, items_of, items_all)
    suffix_lvl = jnp.where((items_of < items_all) & (places % (ACT + 1) == 0), 1, 2).astype(
        jnp.int32
    )
    segment = jnp.concatenate(
        [prefix_segment.reshape(seq_count, pre_rows), suffix_seg.reshape(seq_count, suf_rows)],
        axis=1,
    ).reshape(-1)
    levels = jnp.concatenate(
        [jnp.zeros((seq_count, pre_rows), jnp.int32), suffix_lvl.reshape(seq_count, suf_rows)],
        axis=1,
    ).reshape(-1)
    return (segment, levels)


def shards(
    x_prefix,
    x_action,
    prefix_segment,
    prefix_attn_gain,
    prefix_query,
    prefix_key,
    prefix_value,
    prefix_out,
    prefix_mlp_gain,
    prefix_gate,
    prefix_up,
    prefix_down,
    action_attn_gain,
    action_query,
    action_key,
    action_value,
    action_out,
    action_mlp_gain,
    action_gate,
    action_up,
    action_down,
    cot_prefix,
    cot_action,
):
    seq_count = lax.axis_size("seq")
    tp_count = lax.axis_size("tp")
    seq_rank = lax.axis_index("seq")
    tp_rank = lax.axis_index("tp")
    pre_rows = x_prefix.shape[0]
    suf_rows = x_action.shape[0]
    rows_all = pre_rows + suf_rows
    score_scale = HD ** (-0.5)
    gathered = (
        lax.all_gather(prefix_attn_gain, "seq", axis=0, tiled=True),
        lax.all_gather(prefix_query, "seq", axis=0, tiled=True),
        lax.all_gather(prefix_key, "seq", axis=0, tiled=True),
        lax.all_gather(prefix_value, "seq", axis=0, tiled=True),
        lax.all_gather(prefix_out, "seq", axis=1, tiled=True),
        lax.all_gather(prefix_mlp_gain, "seq", axis=0, tiled=True),
        lax.all_gather(prefix_gate, "seq", axis=0, tiled=True),
        lax.all_gather(prefix_up, "seq", axis=0, tiled=True),
        lax.all_gather(prefix_down, "seq", axis=1, tiled=True),
        lax.all_gather(action_attn_gain, "seq", axis=0, tiled=True),
        lax.all_gather(action_query, "seq", axis=0, tiled=True),
        lax.all_gather(action_key, "seq", axis=0, tiled=True),
        lax.all_gather(action_value, "seq", axis=0, tiled=True),
        lax.all_gather(action_out, "seq", axis=1, tiled=True),
        lax.all_gather(action_mlp_gain, "seq", axis=0, tiled=True),
        lax.all_gather(action_gate, "seq", axis=0, tiled=True),
        lax.all_gather(action_up, "seq", axis=0, tiled=True),
        lax.all_gather(action_down, "seq", axis=1, tiled=True),
    )
    stream_weights = (gathered[:9], gathered[9:])
    locals_in = (x_prefix, x_action)
    cots = (cot_prefix, cot_action)
    layer_inputs = (
        lax.all_gather(x_prefix, "tp", axis=1, tiled=True),
        lax.all_gather(x_action, "tp", axis=1, tiled=True),
    )
    front_outputs = []
    for residual_state in range(2):
        weights = stream_weights[residual_state]
        centered_input1, inverse_norm1 = normalized_rows(
            layer_inputs[residual_state].astype(jnp.float32)
        )
        attention_norm_scale = weights[0].astype(jnp.float32)
        normalized_first1 = (centered_input1 * attention_norm_scale).astype(jnp.bfloat16)
        query_matrix = jnp.dot(
            normalized_first1, weights[1], preferred_element_type=jnp.float32
        ).astype(jnp.bfloat16)
        key_matrix = jnp.dot(
            normalized_first1, weights[2], preferred_element_type=jnp.float32
        ).astype(jnp.bfloat16)
        value_matrix = jnp.dot(
            normalized_first1, weights[3], preferred_element_type=jnp.float32
        ).astype(jnp.bfloat16)
        front_outputs.append(
            (
                centered_input1,
                inverse_norm1,
                attention_norm_scale,
                normalized_first1,
                query_matrix,
                key_matrix,
                value_matrix,
            )
        )
    segment_all, levels_all = key_tables(prefix_segment, seq_count, pre_rows, suf_rows)
    query_seg = lax.dynamic_slice_in_dim(segment_all, seq_rank * rows_all, rows_all)
    query_lvl = lax.dynamic_slice_in_dim(levels_all, seq_rank * rows_all, rows_all)
    heads_here = front_outputs[0][4].shape[1] // HD
    queries = jnp.concatenate([front_outputs[0][4], front_outputs[1][4]], axis=0).reshape(
        rows_all, heads_here, HD
    )
    key_local = jnp.concatenate([front_outputs[0][5], front_outputs[1][5]], axis=0)
    value_local = jnp.concatenate([front_outputs[0][6], front_outputs[1][6]], axis=0)

    def allowed_at(offset, width):
        key_seg = lax.dynamic_slice_in_dim(segment_all, offset, width)
        key_lvl = lax.dynamic_slice_in_dim(levels_all, offset, width)
        return (query_seg[:, None] == key_seg[None, :]) & (key_lvl[None, :] <= query_lvl[:, None])

    def forward_block(running, key_block, value_block, offset):
        allowed = allowed_at(offset, key_block.shape[0])

        def forward_compute(running):
            row_max, row_sum, weighted = running
            scores = (
                jnp.einsum("qhd,kd->qhk", queries, key_block, preferred_element_type=jnp.float32)
                * score_scale
            )
            scores = jnp.where(allowed[:, None, :], scores, NEG)
            new_max = jnp.maximum(row_max, jnp.max(scores, axis=2))
            expo = jnp.where(allowed[:, None, :], jnp.exp(scores - new_max[:, :, None]), 0.0)
            shrink = jnp.exp(row_max - new_max)
            row_sum = row_sum * shrink + jnp.sum(expo, axis=2)
            weighted = weighted * shrink[:, :, None] + jnp.einsum(
                "qhk,kd->qhd",
                expo.astype(jnp.bfloat16),
                value_block,
                preferred_element_type=jnp.float32,
            )
            return (new_max, row_sum, weighted)

        def unchanged(running):
            return running

        return lax.cond(jnp.any(allowed), forward_compute, unchanged, running)

    def fold_keys(running, pieces):
        key_piece, value_piece = pieces
        width = math.gcd(key_piece.shape[0], rows_all)

        def step(running, number):
            begin = number * width
            key_block = lax.dynamic_slice_in_dim(key_piece, begin, width)
            value_block = lax.dynamic_slice_in_dim(value_piece, begin, width)
            return (forward_block(running, key_block, value_block, begin), None)

        running, _ = lax.scan(
            step, running, jnp.arange(key_piece.shape[0] // width, dtype=jnp.int32)
        )
        return running

    start_state = (
        jnp.full((rows_all, heads_here), NEG, jnp.float32),
        jnp.zeros((rows_all, heads_here), jnp.float32),
        jnp.zeros((rows_all, heads_here, HD), jnp.float32),
    )
    row_max, row_sum, weighted = fold_keys(
        start_state,
        (
            lax.all_gather(key_local, "seq", axis=0, tiled=True),
            lax.all_gather(value_local, "seq", axis=0, tiled=True),
        ),
    )
    attended = weighted / row_sum[:, :, None]
    log_sum = row_max + jnp.log(row_sum)
    mixed_heads = attended.astype(jnp.bfloat16).reshape(rows_all, heads_here * HD)
    mixed_parts = (mixed_heads[:pre_rows], mixed_heads[pre_rows:])
    branch_pre = jnp.dot(mixed_parts[0], stream_weights[0][4], preferred_element_type=jnp.float32)
    branch_act = jnp.dot(mixed_parts[1], stream_weights[1][4], preferred_element_type=jnp.float32)
    attn_sums = (
        lax.psum_scatter(
            branch_pre.astype(jnp.bfloat16), "tp", scatter_dimension=1, tiled=True
        ).astype(jnp.float32),
        lax.psum_scatter(
            branch_act.astype(jnp.bfloat16), "tp", scatter_dimension=1, tiled=True
        ).astype(jnp.float32),
    )
    residuals = (
        locals_in[0].astype(jnp.float32) + attn_sums[0],
        locals_in[1].astype(jnp.float32) + attn_sums[1],
    )
    middle_values = (
        lax.all_gather(residuals[0].astype(jnp.bfloat16), "tp", axis=1, tiled=True),
        lax.all_gather(residuals[1].astype(jnp.bfloat16), "tp", axis=1, tiled=True),
    )
    middle_outputs = []
    for residual_state in range(2):
        weights = stream_weights[residual_state]
        centered_input2, inverse_norm2 = normalized_rows(
            middle_values[residual_state].astype(jnp.float32)
        )
        feedforward_norm_scale = weights[5].astype(jnp.float32)
        normalized_second2 = (centered_input2 * feedforward_norm_scale).astype(jnp.bfloat16)
        gate_output = jnp.dot(normalized_second2, weights[6], preferred_element_type=jnp.float32)
        up_output = jnp.dot(normalized_second2, weights[7], preferred_element_type=jnp.float32)
        hidden_state = gated(gate_output, up_output).astype(jnp.bfloat16)
        lifted_output = jnp.dot(hidden_state, weights[8], preferred_element_type=jnp.float32)
        middle_outputs.append(
            (
                centered_input2,
                inverse_norm2,
                feedforward_norm_scale,
                normalized_second2,
                gate_output,
                up_output,
                hidden_state,
                lifted_output,
            )
        )
    mlp_sums = (
        lax.psum_scatter(
            middle_outputs[0][7].astype(jnp.bfloat16), "tp", scatter_dimension=1, tiled=True
        ).astype(jnp.float32),
        lax.psum_scatter(
            middle_outputs[1][7].astype(jnp.bfloat16), "tp", scatter_dimension=1, tiled=True
        ).astype(jnp.float32),
    )
    outputs = (
        (residuals[0] + mlp_sums[0]).astype(jnp.bfloat16),
        (residuals[1] + mlp_sums[1]).astype(jnp.bfloat16),
    )
    mlp_grads = []
    for residual_state in range(2):
        weights = stream_weights[residual_state]
        (
            centered_input2,
            inverse_norm2,
            feedforward_norm_scale,
            normalized_second2,
            gate_output,
            up_output,
            hidden_state,
            lifted_output,
        ) = middle_outputs[residual_state]
        cot_rows = cots[residual_state]
        dhidden = jnp.einsum("rd,fd->rf", cot_rows, weights[8], preferred_element_type=jnp.float32)
        grad_down = jnp.einsum(
            "rf,rd->fd", hidden_state, cot_rows, preferred_element_type=jnp.float32
        )
        _, pull = jax.vjp(gated, gate_output, up_output)
        dgate_full, dup_full = pull(dhidden)
        dgate = dgate_full.astype(jnp.bfloat16)
        dup = dup_full.astype(jnp.bfloat16)
        grad_gate = jnp.einsum(
            "rd,rf->df", normalized_second2, dgate, preferred_element_type=jnp.float32
        )
        grad_up = jnp.einsum(
            "rd,rf->df", normalized_second2, dup, preferred_element_type=jnp.float32
        )
        dnormed2 = jnp.einsum(
            "rf,df->rd", dgate, weights[6], preferred_element_type=jnp.float32
        ) + jnp.einsum("rf,df->rd", dup, weights[7], preferred_element_type=jnp.float32)
        mlp_grads.append((grad_gate, grad_up, grad_down, dnormed2))
    feedforward_backward = (
        lax.psum(mlp_grads[0][3].astype(jnp.bfloat16), "tp").astype(jnp.float32),
        lax.psum(mlp_grads[1][3].astype(jnp.bfloat16), "tp").astype(jnp.float32),
    )
    dresids = []
    mlp_gain_grads = []
    for residual_state in range(2):
        centered_input2, inverse_norm2, feedforward_norm_scale = (
            middle_outputs[residual_state][0],
            middle_outputs[residual_state][1],
            middle_outputs[residual_state][2],
        )
        middle_gradient, feedforward_scale_gradient = norm_backward(
            feedforward_backward[residual_state],
            centered_input2,
            inverse_norm2,
            feedforward_norm_scale,
        )
        cols = locals_in[residual_state].shape[1]
        dresid = lax.dynamic_slice_in_dim(cots[residual_state], tp_rank * cols, cols, 1).astype(
            jnp.float32
        ) + lax.dynamic_slice_in_dim(middle_gradient, tp_rank * cols, cols, 1)
        dresids.append(dresid)
        mlp_gain_grads.append(feedforward_scale_gradient)
    branch_cot = (
        lax.all_gather(dresids[0].astype(jnp.bfloat16), "tp", axis=1, tiled=True),
        lax.all_gather(dresids[1].astype(jnp.bfloat16), "tp", axis=1, tiled=True),
    )
    dmixed_parts = []
    out_grads = []
    for residual_state in range(2):
        dmixed = jnp.einsum(
            "rd,ed->re",
            branch_cot[residual_state],
            stream_weights[residual_state][4],
            preferred_element_type=jnp.float32,
        ).astype(jnp.bfloat16)
        out_grads.append(
            jnp.einsum(
                "re,rd->ed",
                mixed_parts[residual_state],
                branch_cot[residual_state],
                preferred_element_type=jnp.float32,
            )
        )
        dmixed_parts.append(dmixed)
    dmixed_all = jnp.concatenate(dmixed_parts, axis=0).reshape(rows_all, heads_here, HD)
    row_delta = jnp.sum(dmixed_all.astype(jnp.float32) * attended, axis=2)
    key_whole, value_whole = (
        lax.all_gather(key_local, "seq", axis=0, tiled=True),
        lax.all_gather(value_local, "seq", axis=0, tiled=True),
    )

    def back_block(dquery, number):
        begin = number * rows_all
        key_block = lax.dynamic_slice_in_dim(key_whole, begin, rows_all)
        value_block = lax.dynamic_slice_in_dim(value_whole, begin, rows_all)
        allowed = allowed_at(begin, rows_all)

        def back_compute(dquery):
            scores = (
                jnp.einsum("qhd,kd->qhk", queries, key_block, preferred_element_type=jnp.float32)
                * score_scale
            )
            attn_probs = jnp.where(allowed[:, None, :], jnp.exp(scores - log_sum[:, :, None]), 0.0)
            dprobs = jnp.einsum(
                "qhd,kd->qhk", dmixed_all, value_block, preferred_element_type=jnp.float32
            )
            dscores = (attn_probs * (dprobs - row_delta[:, :, None])).astype(jnp.bfloat16)
            dquery = (
                dquery
                + jnp.einsum("qhk,kd->qhd", dscores, key_block, preferred_element_type=jnp.float32)
                * score_scale
            )
            dkey = (
                jnp.einsum("qhk,qhd->kd", dscores, queries, preferred_element_type=jnp.float32)
                * score_scale
            )
            dvalue = jnp.einsum(
                "qhk,qhd->kd",
                attn_probs.astype(jnp.bfloat16),
                dmixed_all,
                preferred_element_type=jnp.float32,
            )
            return (dquery, (dkey, dvalue))

        def skipped(dquery):
            zero_rows = jnp.zeros((rows_all, HD), jnp.float32)
            return (dquery, (zero_rows, zero_rows))

        return lax.cond(jnp.any(allowed), back_compute, skipped, dquery)

    dquery, (dkey_blocks, dvalue_blocks) = lax.scan(
        back_block,
        jnp.zeros((rows_all, heads_here, HD), jnp.float32),
        jnp.arange(seq_count, dtype=jnp.int32),
    )
    quarter = rows_all // tp_count
    key_grads = (
        lax.psum_scatter(
            dkey_blocks.reshape(-1, HD), ("seq", "tp"), scatter_dimension=0, tiled=True
        ),
        lax.psum_scatter(
            dvalue_blocks.reshape(-1, HD), ("seq", "tp"), scatter_dimension=0, tiled=True
        ),
    )
    dkey_rows = lax.dynamic_update_slice_in_dim(
        jnp.zeros((rows_all, HD), jnp.bfloat16),
        key_grads[0].astype(jnp.bfloat16),
        tp_rank * quarter,
        0,
    )
    dvalue_rows = lax.dynamic_update_slice_in_dim(
        jnp.zeros((rows_all, HD), jnp.bfloat16),
        key_grads[1].astype(jnp.bfloat16),
        tp_rank * quarter,
        0,
    )
    dquery_rows = dquery.astype(jnp.bfloat16).reshape(rows_all, heads_here * HD)
    bounds = ((0, pre_rows), (pre_rows, rows_all))
    attn_grads = []
    for residual_state in range(2):
        weights = stream_weights[residual_state]
        normalized_first1 = front_outputs[residual_state][3]
        first, last = bounds[residual_state]
        dq_part = dquery_rows[first:last]
        dk_part = dkey_rows[first:last]
        dv_part = dvalue_rows[first:last]
        grad_query = jnp.einsum(
            "rd,re->de", normalized_first1, dq_part, preferred_element_type=jnp.float32
        )
        grad_key = jnp.einsum(
            "rd,rk->dk", normalized_first1, dk_part, preferred_element_type=jnp.float32
        )
        grad_value = jnp.einsum(
            "rd,rk->dk", normalized_first1, dv_part, preferred_element_type=jnp.float32
        )
        dnormed1 = (
            jnp.einsum("re,de->rd", dq_part, weights[1], preferred_element_type=jnp.float32)
            + jnp.einsum("rk,dk->rd", dk_part, weights[2], preferred_element_type=jnp.float32)
            + jnp.einsum("rk,dk->rd", dv_part, weights[3], preferred_element_type=jnp.float32)
        )
        attn_grads.append((grad_query, grad_key, grad_value, dnormed1))
    attention_backward = (
        lax.psum(attn_grads[0][3].astype(jnp.bfloat16), "tp").astype(jnp.float32),
        lax.psum(attn_grads[1][3].astype(jnp.bfloat16), "tp").astype(jnp.float32),
    )
    input_grads = []
    attn_gain_grads = []
    for residual_state in range(2):
        centered_input1, inverse_norm1, attention_norm_scale = (
            front_outputs[residual_state][0],
            front_outputs[residual_state][1],
            front_outputs[residual_state][2],
        )
        norm_input_gradient, attention_scale_gradient = norm_backward(
            attention_backward[residual_state], centered_input1, inverse_norm1, attention_norm_scale
        )
        cols = locals_in[residual_state].shape[1]
        grad_x = dresids[residual_state] + lax.dynamic_slice_in_dim(
            norm_input_gradient, tp_rank * cols, cols, 1
        )
        input_grads.append(grad_x.astype(jnp.bfloat16))
        attn_gain_grads.append(attention_scale_gradient)
    seq_grads = (
        lax.psum_scatter(
            attn_gain_grads[0].astype(jnp.bfloat16), "seq", scatter_dimension=0, tiled=True
        ).astype(jnp.float32),
        lax.psum_scatter(
            attn_grads[0][0].astype(jnp.bfloat16), "seq", scatter_dimension=0, tiled=True
        ).astype(jnp.float32),
        lax.psum_scatter(
            out_grads[0].astype(jnp.bfloat16), "seq", scatter_dimension=1, tiled=True
        ).astype(jnp.float32),
        lax.psum_scatter(
            mlp_gain_grads[0].astype(jnp.bfloat16), "seq", scatter_dimension=0, tiled=True
        ).astype(jnp.float32),
        lax.psum_scatter(
            mlp_grads[0][0].astype(jnp.bfloat16), "seq", scatter_dimension=0, tiled=True
        ).astype(jnp.float32),
        lax.psum_scatter(
            mlp_grads[0][1].astype(jnp.bfloat16), "seq", scatter_dimension=0, tiled=True
        ).astype(jnp.float32),
        lax.psum_scatter(
            mlp_grads[0][2].astype(jnp.bfloat16), "seq", scatter_dimension=1, tiled=True
        ).astype(jnp.float32),
        lax.psum_scatter(
            attn_gain_grads[1].astype(jnp.bfloat16), "seq", scatter_dimension=0, tiled=True
        ).astype(jnp.float32),
        lax.psum_scatter(
            attn_grads[1][0].astype(jnp.bfloat16), "seq", scatter_dimension=0, tiled=True
        ).astype(jnp.float32),
        lax.psum_scatter(
            out_grads[1].astype(jnp.bfloat16), "seq", scatter_dimension=1, tiled=True
        ).astype(jnp.float32),
        lax.psum_scatter(
            mlp_gain_grads[1].astype(jnp.bfloat16), "seq", scatter_dimension=0, tiled=True
        ).astype(jnp.float32),
        lax.psum_scatter(
            mlp_grads[1][0].astype(jnp.bfloat16), "seq", scatter_dimension=0, tiled=True
        ).astype(jnp.float32),
        lax.psum_scatter(
            mlp_grads[1][1].astype(jnp.bfloat16), "seq", scatter_dimension=0, tiled=True
        ).astype(jnp.float32),
        lax.psum_scatter(
            mlp_grads[1][2].astype(jnp.bfloat16), "seq", scatter_dimension=1, tiled=True
        ).astype(jnp.float32),
    )
    kv_grads = (
        lax.psum_scatter(attn_grads[0][1], ("seq", "tp"), scatter_dimension=0, tiled=True),
        lax.psum_scatter(attn_grads[0][2], ("seq", "tp"), scatter_dimension=0, tiled=True),
        lax.psum_scatter(attn_grads[1][1], ("seq", "tp"), scatter_dimension=0, tiled=True),
        lax.psum_scatter(attn_grads[1][2], ("seq", "tp"), scatter_dimension=0, tiled=True),
    )
    return (
        outputs[0],
        outputs[1],
        input_grads[0],
        input_grads[1],
        seq_grads[0],
        seq_grads[1],
        kv_grads[0],
        kv_grads[1],
        seq_grads[2],
        seq_grads[3],
        seq_grads[4],
        seq_grads[5],
        seq_grads[6],
        seq_grads[7],
        seq_grads[8],
        kv_grads[2],
        kv_grads[3],
        seq_grads[9],
        seq_grads[10],
        seq_grads[11],
        seq_grads[12],
        seq_grads[13],
    )


def solution(mesh):
    placed = (
        P("seq", "tp"),
        P("seq", "tp"),
        P(),
        P("seq"),
        P("seq", "tp"),
        P("seq", None),
        P("seq", None),
        P("tp", "seq"),
        P("seq"),
        P("seq", "tp"),
        P("seq", "tp"),
        P("tp", "seq"),
        P("seq"),
        P("seq", "tp"),
        P("seq", None),
        P("seq", None),
        P("tp", "seq"),
        P("seq"),
        P("seq", "tp"),
        P("seq", "tp"),
        P("tp", "seq"),
        P("seq", None),
        P("seq", None),
    )
    return jax.shard_map(
        shards,
        mesh=mesh,
        in_specs=placed,
        out_specs=(
            P("seq", "tp"),
            P("seq", "tp"),
            P("seq", "tp"),
            P("seq", "tp"),
            P("seq"),
            P("seq", "tp"),
            P(("seq", "tp"), None),
            P(("seq", "tp"), None),
            P("tp", "seq"),
            P("seq"),
            P("seq", "tp"),
            P("seq", "tp"),
            P("tp", "seq"),
            P("seq"),
            P("seq", "tp"),
            P(("seq", "tp"), None),
            P(("seq", "tp"), None),
            P("tp", "seq"),
            P("seq"),
            P("seq", "tp"),
            P("seq", "tp"),
            P("tp", "seq"),
        ),
        check_vma=False,
    )
```

profile of v0, /device:TPU:0, one launch (start us, length us, event | category | flops | bytes accessed | tf_op | source)
XLA Modules:
  0.0 2161.4 jit_solution(13465242587920507447)
XLA Ops:
  10.6 10.3 all-gather.1
  21.6 8.7 all-gather
  30.4 13.6 all_gather.83
  44.0 9.8 all_gather.85
  55.7 10.2 all-gather.24.cloned.1.call-done
  68.8 9.8 all_gather.90
  79.6 11.7 all-gather.32.cloned.1.call-done
  97.5 19.1 all-gather.30.cloned.1.call-done
  118.1 28.1 %all-gather.28.cloned.1.call-done = bf16[2048,512]{1,0:T(8,128)(2,1)} async-done(((bf16[256,512]{1,0:T(8,128)(2,1)}), bf16[2048,512]{1,0:T(8,128)(2,1)}) %all-gather.28.cloned.1.call-update) | async-done | bytes 2097168 | tf_op jit(solution)/shard_map/all_gather | solution.py:90
  148.7 23.7 %all-gather.26.cloned.1.call-done = bf16[2176,256]{1,0:T(8,128)(2,1)} async-done(((bf16[272,256]{1,0:T(8,128)(2,1)}), bf16[2176,256]{1,0:T(8,128)(2,1)}) %all-gather.26.cloned.1.call-update) | async-done | bytes 1114128 | tf_op jit(solution)/shard_map/all_gather | solution.py:208
  172.4 26.3 %all-gather.34.cloned.1.call-done = bf16[2176,256]{1,0:T(8,128)(2,1)} async-done(((bf16[272,256]{1,0:T(8,128)(2,1)}), bf16[2176,256]{1,0:T(8,128)(2,1)}) %all-gather.34.cloned.1.call-update) | async-done | bytes 1114128 | tf_op jit(solution)/shard_map/all_gather | solution.py:209
  198.7 46.2 %while.31 = (s32[]{:T(128)}, f32[272,2]{0,1:T(2,128)S(1)}, f32[272,2]{0,1:T(2,128)S(1)}, f32[272,2,256]{2,0,1:T(8,128)S(1)}, s32[272]{0:T(512)S(1)}, /*index=5*/...) while((s32[]{:T(128)}, f32[272,2]{0,1:T(2,128)S(1)}, ...), condition=%wide.region_8.9_spmd, body=%wide.region_2.8_spmd.sunk | while | flops 153426496 | bytes 3787613 | solution.py:195
  249.6 35.5 %reduce-scatter.27.cloned.1.call-done = bf16[256,512]{1,0:T(8,128)(2,1)} async-done(((bf16[256,2048]{1,0:T(8,128)(2,1)}), bf16[256,512]{1,0:T(8,128)(2,1)}) %reduce-scatter.27.cloned.1.call-update) | async-done | bytes 262160 | tf_op jit(solution)/shard_map/reduce_scatter | solution.py:219
  288.8 20.4 all-gather.46.cloned.1.call-done
  312.6 9.4 all-gather.2
  322.0 17.4 all-gather.38.cloned.1.call-done
  340.9 89.8 %all-gather.40.cloned.1.call-done = bf16[2048,4096]{1,0:T(8,128)(2,1)} async-done(((bf16[256,4096]{1,0:T(8,128)(2,1)}), bf16[2048,4096]{1,0:T(8,128)(2,1)}) %all-gather.40.cloned.1.call-update) | async-done | bytes 16777232 | tf_op jit(solution)/shard_map/all_gather | solution.py:95
  430.7 12.8 fusion.106
  443.5 79.2 %all-gather.42.cloned.1.call-done = bf16[2048,4096]{1,0:T(8,128)(2,1)} async-done(((bf16[256,4096]{1,0:T(8,128)(2,1)}), bf16[2048,4096]{1,0:T(8,128)(2,1)}) %all-gather.42.cloned.1.call-update) | async-done | bytes 16777232 | tf_op jit(solution)/shard_map/all_gather | solution.py:96
  522.6 10.5 fusion.105
  533.1 84.5 %all-gather.44.cloned.1.call-done = bf16[4096,2048]{1,0:T(8,128)(2,1)} async-done(((bf16[4096,256]{1,0:T(8,128)(2,1)}), bf16[4096,2048]{1,0:T(8,128)(2,1)}) %all-gather.44.cloned.1.call-update) | async-done | bytes 16777232 | tf_op jit(solution)/shard_map/all_gather | solution.py:97
  617.7 14.0 multiply_convert_fusion
  631.7 12.3 fusion.111
  644.0 12.8 fusion.45
  657.6 8.7 all-gather.3
  667.0 13.1 all_gather.99
  682.3 14.6 all-gather.50.cloned.1.call-done
  699.5 52.0 %all-reduce.14.cloned.1.call-done = bf16[256,2048]{1,0:T(8,128)(2,1)} async-done(((bf16[256,2048]{1,0:T(8,128)(2,1)}), bf16[256,2048]{1,0:T(8,128)(2,1)}) %all-reduce.14.cloned.1.call-update) | async-done | bytes 1048592 | tf_op jit(solution)/shard_map/psum | solution.py:303
  757.2 24.0 %all-gather.52.cloned.1.call-done = bf16[1024,1024]{1,0:T(8,128)(2,1)} async-done(((bf16[1024,128]{1,0:T(8,128)(2,1)}), bf16[1024,1024]{1,0:T(8,128)(2,1)}) %all-gather.52.cloned.1.call-update) | async-done | bytes 2097168 | tf_op jit(solution)/shard_map/all_gather | solution.py:106
  784.9 19.8 psum.29
  806.8 13.1 all_gather.105
  835.9 11.9 convolution_convert_fusion.5
  852.8 70.2 %while.32 = (s32[]{:T(128)}, f32[272,2,256]{2,0,1:T(8,128)S(1)}, f32[8,272,256]{2,1,0:T(8,128)}, f32[8,272,256]{2,1,0:T(8,128)}, s32[272]{0:T(512)S(1)}, /*index...) while((s32[]{:T(128)}, f32[272,2,256]{2,0,1:T(8,128)S(1)}, ...), condition=%wide.region_24.25_spmd, body=%wide.region_20.24_spmd.sunk | while | flops 380477952 | bytes 8289021 | solution.py:394
  923.0 106.6 %fusion.107 = (f32[72,256]{1,0:T(8,128)S(1)}, f32[72,256]{1,0:T(8,128)S(1)}) fusion(f32[2176,256]{1,0:T(8,128)} %bitcast.147, f32[2176,256]{1,0:T(8,128)} %bitcast.146), kind=kCustom, calls=%all-reduce-scatter.2 | all-reduce-scatter fusion | flops 1179649 | bytes 4603904
  1055.5 9.9 convolution_convert_fusion.2
  1065.5 9.9 convolution_convert_fusion.1
  1077.0 9.5 convolution_convert_fusion
  1108.6 27.6 %psum.31 = bf16[16,1024]{1,0:T(8,128)(2,1)S(1)} all-reduce(bf16[16,1024]{1,0:T(8,128)(2,1)S(1)} %fusion.53), channel_id=1, replica_groups=mesh['seq'=8,'tp'=4] {'tp'}, use_global_device_ids=true, to_apply=%region_29.30 | all-reduce | flops 16384 | bytes 65536 | tf_op jit(solution)/shard_map/psum | solution.py:447
  1141.2 28.3 %all-reduce.9 = (bf16[2048]{0:T(1024)(128)(2,1)S(1)}, bf16[2048]{0:T(1024)(128)(2,1)S(1)}, bf16[1024]{0:T(1024)(128)(2,1)S(1)}, bf16[1024]{0:T(1024)(128)(2,1)S(1)}) all-reduce(bf16[2048]{0:T(1024)(128)(2,1)S(1)} %get-tuple-element.406, bf16[2048]{0:T(1024)(128)(2,1)S(1)} %copy-done.42, ...), channel_id=8, replica_groups=mesh['seq'=8,'tp'=4] {'seq'}, use_global_device_ids=true, to_apply=%region_32.33.clone | all-reduce | flops 6144 | bytes 24576
  1176.0 24.6 %reduce-scatter.35.cloned.1.call-done = bf16[256,512]{1,0:T(8,128)(2,1)} async-done(((bf16[2048,512]{1,0:T(8,128)(2,1)}), bf16[256,512]{1,0:T(8,128)(2,1)}) %reduce-scatter.35.cloned.1.call-update) | async-done | bytes 262160 | tf_op jit(solution)/shard_map/reduce_scatter | solution.py:470
  1202.4 42.6 %reduce-scatter.41.cloned.1.call-done = bf16[512,256]{1,0:T(8,128)(2,1)} async-done(((bf16[512,2048]{1,0:T(8,128)(2,1)}), bf16[512,256]{1,0:T(8,128)(2,1)}) %reduce-scatter.41.cloned.1.call-update) | async-done | bytes 262160 | tf_op jit(solution)/shard_map/reduce_scatter | solution.py:473
  1246.8 118.2 %reduce-scatter.43.cloned.1.call-done = bf16[256,4096]{1,0:T(8,128)(2,1)} async-done(((bf16[2048,4096]{1,0:T(8,128)(2,1)}), bf16[256,4096]{1,0:T(8,128)(2,1)}) %reduce-scatter.43.cloned.1.call-update) | async-done | bytes 2097168 | tf_op jit(solution)/shard_map/reduce_scatter | solution.py:479
  1369.1 115.9 %reduce-scatter.45.cloned.1.call-done = bf16[256,4096]{1,0:T(8,128)(2,1)} async-done(((bf16[2048,4096]{1,0:T(8,128)(2,1)}), bf16[256,4096]{1,0:T(8,128)(2,1)}) %reduce-scatter.45.cloned.1.call-update) | async-done | bytes 2097168 | tf_op jit(solution)/shard_map/reduce_scatter | solution.py:482
  1489.1 115.7 %reduce-scatter.47.cloned.1.call-done = bf16[4096,256]{1,0:T(8,128)(2,1)} async-done(((bf16[4096,2048]{1,0:T(8,128)(2,1)}), bf16[4096,256]{1,0:T(8,128)(2,1)}) %reduce-scatter.47.cloned.1.call-update) | async-done | bytes 2097168 | tf_op jit(solution)/shard_map/reduce_scatter | solution.py:485
  1608.7 134.4 %reduce-scatter.51.cloned.1.call-done = f32[32,256]{1,0:T(8,128)} async-done(((f32[1024,256]{1,0:T(8,128)}), f32[32,256]{1,0:T(8,128)}) %reduce-scatter.51.cloned.1.call-update) | async-done | bytes 32784 | tf_op jit(solution)/shard_map/reduce_scatter | solution.py:513
  1743.1 134.8 %reduce-scatter.53.cloned.1.call-done = f32[32,256]{1,0:T(8,128)} async-done(((f32[1024,256]{1,0:T(8,128)}), f32[32,256]{1,0:T(8,128)}) %reduce-scatter.53.cloned.1.call-update) | async-done | bytes 32784 | tf_op jit(solution)/shard_map/reduce_scatter | solution.py:514
  1877.8 137.5 %reduce-scatter.37.cloned.1.call-done = f32[64,256]{1,0:T(8,128)} async-done(((f32[2048,256]{1,0:T(8,128)}), f32[64,256]{1,0:T(8,128)}) %reduce-scatter.37.cloned.1.call-update) | async-done | bytes 65552 | tf_op jit(solution)/shard_map/reduce_scatter | solution.py:511
  2015.3 139.0 %reduce-scatter.39.cloned.1.call-done = f32[64,256]{1,0:T(8,128)} async-done(((f32[2048,256]{1,0:T(8,128)}), f32[64,256]{1,0:T(8,128)}) %reduce-scatter.39.cloned.1.call-update) | async-done | bytes 65552 | tf_op jit(solution)/shard_map/reduce_scatter | solution.py:512
  (471 shorter events, 272.0 us)
Async XLA Ops:
  7.2 46.9 %all-gather.22.cloned.1.call-start = ((), (), s32[]{:S(2)}) async-start(), calls=%async_computation.18 | async-start | bytes 1310720 | tf_op jit(solution)/shard_map/all_gather | solution.py:112
  7.9 58.0 %all-gather.24.cloned.1.call-start = ((), (), s32[]{:S(2)}) async-start(), calls=%async_computation.19 | async-start | bytes 1179648 | tf_op jit(solution)/shard_map/all_gather | solution.py:91
  8.7 82.7 %all-gather.32.cloned.1.call-start = ((), (), s32[]{:S(2)}) async-start(), calls=%async_computation.23 | async-start | bytes 1179648 | tf_op jit(solution)/shard_map/all_gather | solution.py:92
  9.4 107.2 %all-gather.30.cloned.1.call-start = ((), (), s32[]{:S(2)}) async-start(), calls=%async_computation.22 | async-start | bytes 1179648 | tf_op jit(solution)/shard_map/all_gather | solution.py:99
  10.0 136.3 %all-gather.28.cloned.1.call-start = ((), (), s32[]{:S(2)}) async-start(), calls=%async_computation.21 | async-start | bytes 2359296 | tf_op jit(solution)/shard_map/all_gather | solution.py:90
  10.6 161.8 %all-gather.26.cloned.1.call-start = ((), (), s32[]{:S(2)}) async-start(), calls=%async_computation.20 | async-start | bytes 1253376 | tf_op jit(solution)/shard_map/all_gather | solution.py:208
  53.9 62.7 %copy-start.38 = (f32[16]{0:T(128)}, f32[16]{0:T(128)S(1)}, u32[]{:S(2)}) copy-start(f32[16]{0:T(128)S(1)} %add_rsqrt_fusion.3) | copy-start | bytes 196
  55.7 90.6 %copy-start.35 = (f32[256]{0:T(256)}, f32[256]{0:T(256)S(1)}, u32[]{:S(2)}) copy-start(f32[256]{0:T(256)S(1)} %add_rsqrt_fusion.1) | copy-start | bytes 3076
  68.7 129.9 %all-gather.34.cloned.1.call-start = ((), (), s32[]{:S(2)}) async-start(), calls=%async_computation.24 | async-start | bytes 1253376 | tf_op jit(solution)/shard_map/all_gather | solution.py:209
  93.8 151.6 %all-gather.36.cloned.1.call-start = ((), (), s32[]{:S(2)}) async-start(), calls=%async_computation.25 | async-start | bytes 2359296 | tf_op jit(solution)/shard_map/all_gather | solution.py:93
  94.5 190.6 %reduce-scatter.27.cloned.1.call-start = ((), (), s32[]{:S(2)}) async-start(), calls=%async_computation.26 | async-start | bytes 1310720 | tf_op jit(solution)/shard_map/reduce_scatter | solution.py:219
  249.0 60.3 %all-gather.46.cloned.1.call-start = ((), (), s32[]{:S(2)}) async-start(), calls=%async_computation.32 | async-start | bytes 1179648 | tf_op jit(solution)/shard_map/all_gather | solution.py:102
  249.5 89.9 %all-gather.38.cloned.1.call-start = ((), (), s32[]{:S(2)}) async-start(), calls=%async_computation.27 | async-start | bytes 1310720 | tf_op jit(solution)/shard_map/all_gather | solution.py:231
  286.8 143.9 %all-gather.40.cloned.1.call-start = ((), (), s32[]{:S(2)}) async-start(), calls=%async_computation.28 | async-start | bytes 18874368 | tf_op jit(solution)/shard_map/all_gather | solution.py:95
  287.4 235.3 %all-gather.42.cloned.1.call-start = ((), (), s32[]{:S(2)}) async-start(), calls=%async_computation.29 | async-start | bytes 18874368 | tf_op jit(solution)/shard_map/all_gather | solution.py:96
  288.1 329.5 %all-gather.44.cloned.1.call-start = ((), (), s32[]{:S(2)}) async-start(), calls=%async_computation.30 | async-start | bytes 18874368 | tf_op jit(solution)/shard_map/all_gather | solution.py:97
  288.7 377.6 %reduce-scatter.31.cloned.1.call-start = ((), (), s32[]{:S(2)}) async-start(), calls=%async_computation.33 | async-start | bytes 40960 | tf_op jit(solution)/shard_map/reduce_scatter | solution.py:222
  311.4 368.9 %all-gather.48.cloned.1.call-start = ((), (), s32[]{:S(2)}) async-start(), calls=%async_computation.34 | async-start | bytes 2359296 | tf_op jit(solution)/shard_map/all_gather | solution.py:104
  311.9 384.9 %all-gather.50.cloned.1.call-start = ((), (), s32[]{:S(2)}) async-start(), calls=%async_computation.35 | async-start | bytes 2359296 | tf_op jit(solution)/shard_map/all_gather | solution.py:105
  312.5 439.0 %all-reduce.14.cloned.1.call-start = ((), (), s32[]{:S(2)}) async-start(), calls=%async_computation.38 | async-start | bytes 2097152 | tf_op jit(solution)/shard_map/psum | solution.py:303
  340.9 413.2 %copy-start.33 = (f32[256]{0:T(256)}, f32[256]{0:T(256)S(1)}, u32[]{:S(2)}) copy-start(f32[256]{0:T(256)S(1)} %add_rsqrt_fusion) | copy-start | bytes 3076
  430.7 91.9 %copy-start.1 = (bf16[256,2048]{1,0:T(8,128)(2,1)S(1)}, bf16[256,2048]{1,0:T(8,128)(2,1)}, u32[]{:S(2)}) copy-start(bf16[256,2048]{1,0:T(8,128)(2,1)} %all-gather.38.cloned.1.call-done) | copy-start | bytes 3145732
  443.5 174.2 %copy-start.16 = (bf16[256,2048]{1,0:T(8,128)(2,1)S(1)}, bf16[256,2048]{1,0:T(8,128)(2,1)}, u32[]{:S(2)}) copy-start(bf16[256,2048]{1,0:T(8,128)(2,1)} %param.52) | copy-start | bytes 3145732
  656.8 124.4 %all-gather.52.cloned.1.call-start = ((), (), s32[]{:S(2)}) async-start(), calls=%async_computation.36 | async-start | bytes 2359296 | tf_op jit(solution)/shard_map/all_gather | solution.py:106
  657.5 190.4 %all-gather.54.cloned.1.call-start = ((), (), s32[]{:S(2)}) async-start(), calls=%async_computation.39 | async-start | bytes 1310720 | tf_op jit(solution)/shard_map/all_gather | solution.py:327
  680.3 152.5 %copy-start.40 = (f32[16]{0:T(128)}, f32[16]{0:T(128)S(1)}, u32[]{:S(2)}) copy-start(f32[16]{0:T(128)S(1)} %add_rsqrt_fusion.2) | copy-start | bytes 196
  757.1 338.6 %reduce-scatter.33.cloned.1.call-start = ((), (), s32[]{:S(2)}) async-start(), calls=%async_computation.37 | async-start | bytes 40960 | tf_op jit(solution)/shard_map/reduce_scatter | solution.py:262
  822.5 274.5 %reduce-scatter.59.cloned.1.call-start = ((), (), s32[]{:S(2)}) async-start(), calls=%async_computation.53 | async-start | bytes 1179648
  824.3 274.5 %reduce-scatter.61.cloned.1.call-start = ((), (), s32[]{:S(2)}) async-start(), calls=%async_computation.54 | async-start | bytes 2359296
  830.4 270.3 %reduce-scatter.55.cloned.1.call-start = ((), (), s32[]{:S(2)}) async-start(), calls=%async_computation.51 | async-start | bytes 2359296 | tf_op jit(solution)/shard_map/reduce_scatter | solution.py:500
  832.7 270.0 %reduce-scatter.57.cloned.1.call-start = ((), (), s32[]{:S(2)}) async-start(), calls=%async_computation.52 | async-start | bytes 2359296 | tf_op jit(solution)/shard_map/reduce_scatter | solution.py:503
  834.9 269.5 %reduce-scatter.29.cloned.1.call-start = ((), (), s32[]{:S(2)}) async-start(), calls=%async_computation.31 | async-start | bytes 1310720 | tf_op jit(solution)/shard_map/reduce_scatter | solution.py:259
  847.9 290.0 %all-reduce.16.cloned.1.call-start = ((), (), s32[]{:S(2)}) async-start(), calls=%async_computation.40 | async-start | bytes 2097152 | tf_op jit(solution)/shard_map/psum | solution.py:446
  1029.7 9.4 collective-permute-start.2
  1031.7 7.4 collective-permute-start.3
  1033.1 7.3 collective-permute-start.1
  1035.0 5.7 collective-permute-start
  1040.4 51.4 %copy-start.23 = (bf16[272,256]{1,0:T(8,128)(2,1)}, bf16[272,256]{1,0:T(8,128)(2,1)S(1)}, u32[]{:S(2)}) copy-start(bf16[272,256]{1,0:T(8,128)(2,1)S(1)} %dynamic_update_slice.14) | copy-start | bytes 417796
  1048.1 126.3 %reduce-scatter.49.cloned.1.call-start = ((), (), s32[]{:S(2)}) async-start(), calls=%async_computation.48 | async-start | bytes 1179648 | tf_op jit(solution)/shard_map/reduce_scatter | solution.py:491
  1049.8 150.8 %reduce-scatter.35.cloned.1.call-start = ((), (), s32[]{:S(2)}) async-start(), calls=%async_computation.41 | async-start | bytes 2359296 | tf_op jit(solution)/shard_map/reduce_scatter | solution.py:470
  1052.1 192.9 %reduce-scatter.41.cloned.1.call-start = ((), (), s32[]{:S(2)}) async-start(), calls=%async_computation.44 | async-start | bytes 2359296 | tf_op jit(solution)/shard_map/reduce_scatter | solution.py:473
  1055.5 309.5 %reduce-scatter.43.cloned.1.call-start = ((), (), s32[]{:S(2)}) async-start(), calls=%async_computation.45 | async-start | bytes 18874368 | tf_op jit(solution)/shard_map/reduce_scatter | solution.py:479
  1065.4 419.5 %reduce-scatter.45.cloned.1.call-start = ((), (), s32[]{:S(2)}) async-start(), calls=%async_computation.46 | async-start | bytes 18874368 | tf_op jit(solution)/shard_map/reduce_scatter | solution.py:482
  1075.4 529.4 %reduce-scatter.47.cloned.1.call-start = ((), (), s32[]{:S(2)}) async-start(), calls=%async_computation.47 | async-start | bytes 18874368 | tf_op jit(solution)/shard_map/reduce_scatter | solution.py:485
  1086.4 656.6 %reduce-scatter.51.cloned.1.call-start = ((), (), s32[]{:S(2)}) async-start(), calls=%async_computation.49 | async-start | bytes 1081344 | tf_op jit(solution)/shard_map/reduce_scatter | solution.py:513
  1087.9 789.9 %reduce-scatter.53.cloned.1.call-start = ((), (), s32[]{:S(2)}) async-start(), calls=%async_computation.50 | async-start | bytes 1081344 | tf_op jit(solution)/shard_map/reduce_scatter | solution.py:514
  1089.5 925.9 %reduce-scatter.37.cloned.1.call-start = ((), (), s32[]{:S(2)}) async-start(), calls=%async_computation.42 | async-start | bytes 2162688 | tf_op jit(solution)/shard_map/reduce_scatter | solution.py:511
  1091.7 1062.6 %reduce-scatter.39.cloned.1.call-start = ((), (), s32[]{:S(2)}) async-start(), calls=%async_computation.43 | async-start | bytes 2162688 | tf_op jit(solution)/shard_map/reduce_scatter | solution.py:512
  (48 other events, 464.1 us)
Sparse Core Ops, SparseCore 0:
  9.6 31.0 all-gather.21
  42.6 23.2 all-gather.23
  67.8 23.4 all-gather.31
  93.1 23.4 all-gather.29
  118.3 27.8 all-gather.27
  148.6 23.7 all-gather.25
  174.9 23.7 all-gather.33
  200.6 28.1 all-gather.35
  249.1 35.9 reduce-scatter.26
  286.9 22.2 all-gather.45
  311.4 27.9 all-gather.37
  341.3 89.3 all-gather.39
  432.7 89.8 all-gather.41
  524.5 93.1 all-gather.43
  620.4 18.9 reduce-scatter.30
  641.1 26.0 all-gather.47
  668.9 27.8 all-gather.49
  699.7 51.8 all-reduce.13
  753.5 27.5 all-gather.51
  783.2 29.3 all-gather.53
  822.6 16.3 reduce-scatter.32
  842.2 34.1 reduce-scatter.58
  879.6 41.1 reduce-scatter.60
  924.4 44.1 reduce-scatter.54
  971.8 44.2 reduce-scatter.56
  1018.4 29.3 reduce-scatter.28
  1050.5 65.4 all-reduce.15
  1119.5 35.5 reduce-scatter.48
  1159.3 41.2 reduce-scatter.34
  1203.7 41.2 reduce-scatter.40
  1249.0 115.9 reduce-scatter.42
  1369.0 115.9 reduce-scatter.44
  1488.8 115.9 reduce-scatter.46
  1607.7 135.3 reduce-scatter.50
  1745.9 131.9 reduce-scatter.52
  1880.6 134.6 reduce-scatter.36
  2018.0 136.2 reduce-scatter.38
where the time goes:
time: 2170 us; the launch traced here: 2160 us
  waiting for transfers between devices  1510 us (70%)
  blocking collectives  279 us (13%)
  matrix products  188 us (9%)
  local copies, waits for them, and re-layouts  69 us (3%)
  other arithmetic  68.5 us (3%)
  loops' own time  21.9 us (1%)
    reduce_scatter x1, waiting for transfers between devices, shards(): lax.psum_scatter(attn_grads[0][2], ('seq', 'tp'), scatter_dimension=0, ti...  139 us
    reduce_scatter x1, waiting for transfers between devices, shards(): lax.psum_scatter(attn_grads[0][1], ('seq', 'tp'), scatter_dimension=0, ti...  137 us
    unnamed x2, blocking collectives  135 us
    reduce_scatter x1, waiting for transfers between devices, shards(): lax.psum_scatter(attn_grads[1][2], ('seq', 'tp'), scatter_dimension=0, ti...  135 us
    reduce_scatter x1, waiting for transfers between devices, shards(): lax.psum_scatter(attn_grads[1][1], ('seq', 'tp'), scatter_dimension=0, ti...  134 us
    reduce_scatter x1, waiting for transfers between devices, shards(): lax.psum_scatter(mlp_grads[0][0].astype(jnp.bfloat16), 'seq', scatter_dim...  118 us
    reduce_scatter x1, waiting for transfers between devices, shards(): lax.psum_scatter(mlp_grads[0][1].astype(jnp.bfloat16), 'seq', scatter_dim...  116 us
    reduce_scatter x1, waiting for transfers between devices, shards(): lax.psum_scatter(mlp_grads[0][2].astype(jnp.bfloat16), 'seq', scatter_dim...  116 us
  transfers between devices with their start and end apart: 41, of which 25 were waited for; matrix products, arithmetic and copies ran while one was open for 20% of the time, Pallas kernels for 0%

commit v1 on v0

v1 whole, which is shorter than its diff:
```python
import functools

import jax
import jax.numpy as jnp
from jax import lax
from jax.experimental import pallas as pl
from jax.experimental.pallas import tpu as pltpu
from jax.sharding import PartitionSpec as P

HD = 256
IMG = 768
TXT = 48
ACT = 50
EPS = 1e-06
NEG = -1e30
BF = jnp.bfloat16
F32 = jnp.float32


def swap(value, axis, mask):
    count = lax.axis_size(axis)
    return lax.ppermute(value, axis, [(i, i ^ mask) for i in range(count)])


def gather_seq(halves):
    count = lax.axis_size("seq")
    masks = [1 << b for b in range(count.bit_length() - 1)]
    far = masks[1:]
    results = []
    for number, half in enumerate(halves):
        blocks = {0: half}
        for mask in far if number % 2 == 0 else far[::-1]:
            keys = sorted(blocks)
            got = swap(jnp.stack([blocks[k] for k in keys]), "seq", mask)
            for place, k in enumerate(keys):
                blocks[k ^ mask] = got[place]
        results.append(blocks)
    whole = []
    for blocks in results:
        keys = sorted(blocks)
        got = swap(jnp.stack([blocks[k] for k in keys]), "seq", 1)
        for place, k in enumerate(keys):
            blocks[k ^ 1] = got[place]
        whole.append([blocks[k] for k in range(count)])
    return whole


def scatter_seq(halves):
    count = lax.axis_size("seq")
    masks = [1 << b for b in range(count.bit_length() - 1)]
    far = masks[1:]
    results = []
    for number, half in enumerate(halves):
        blocks = dict(enumerate(half))
        for mask in [1] + (far if number % 2 == 0 else far[::-1]):
            keys = sorted(blocks)
            sent = [k for k in keys if k & mask]
            got = swap(jnp.stack([blocks[k].astype(BF) for k in sent]), "seq", mask)
            blocks = {k: blocks[k] for k in keys if not k & mask}
            for place, k in enumerate(sent):
                blocks[k ^ mask] = blocks[k ^ mask].astype(F32) + got[place].astype(F32)
        results.append(blocks[0])
    return results


def scatter_tp(make_piece):
    count = lax.axis_size("tp")
    rank = lax.axis_index("tp")
    total = make_piece(rank).astype(F32)
    for k in range(1, count):
        total = total + swap(make_piece(rank ^ k).astype(BF), "tp", k).astype(F32)
    return total


def gather_tp(piece):
    count = lax.axis_size("tp")
    rank = lax.axis_index("tp")
    return [(rank, piece)] + [(rank ^ k, swap(piece, "tp", k)) for k in range(1, count)]


def columns_of(pieces, rows, width, dtype):
    count = len(pieces)
    whole = jnp.zeros((rows, count * width), dtype)
    for place, piece in pieces:
        whole = lax.dynamic_update_slice(whole, piece, (0, place * width))
    return whole


def fold_action(piece, width):
    count = width // piece.shape[1]
    return jnp.concatenate(jnp.split(piece, count, axis=0), axis=1)


def unfold_action(piece, width):
    count = piece.shape[1] // width
    return jnp.concatenate(jnp.split(piece, count, axis=1), axis=0)


def normalized_rows(values):
    inverse = lax.rsqrt(jnp.mean(values * values, axis=1, keepdims=True) + EPS)
    return values * inverse, inverse


def gated(gate_in, up_in):
    return jax.nn.gelu(gate_in, approximate=True) * up_in


def dot(left, right):
    return jnp.dot(left, right, preferred_element_type=F32)


def dot_t(left, right):
    return lax.dot_general(left, right, (((1,), (1,)), ((), ())), preferred_element_type=F32)


def t_dot(left, right):
    return lax.dot_general(left, right, (((0,), (0,)), ((), ())), preferred_element_type=F32)


def token_codes(prefix_segment, seq_count, suf_rows):
    items_all = prefix_segment.shape[0] // (IMG + TXT)
    places = jnp.arange(seq_count * suf_rows, dtype=jnp.int32)
    items_of = places // (ACT + 1)
    suffix_seg = jnp.where(items_of < items_all, items_of, items_all)
    suffix_lvl = jnp.where((items_of < items_all) & (places % (ACT + 1) == 0), 1, 2)
    suffix = (suffix_seg * 4 + suffix_lvl).astype(jnp.int32)
    return jnp.concatenate(
        [(prefix_segment * 4).reshape(seq_count, -1), suffix.reshape(seq_count, -1)], axis=1
    )


def key_step(count):
    for step in (2176, 1088, 544, 272):
        if count % step == 0:
            return step
    return count


def attend_kernel(q_ref, k_ref, v_ref, qc_ref, kc_ref, att_ref, lse_ref):
    rows = q_ref.shape[0]
    heads = q_ref.shape[1] // HD
    count = k_ref.shape[0]
    step = key_step(count)
    code = qc_ref[...]
    low = code - code % 4
    for h in range(heads):
        query = q_ref[:, h * HD : (h + 1) * HD] * BF(HD**-0.5)
        top = jnp.full((rows, 1), NEG, F32)
        mass = jnp.zeros((rows, 1), F32)
        total = jnp.zeros((rows, HD), F32)
        for begin in range(0, count, step):
            keys = k_ref[begin : begin + step, :]
            marks = kc_ref[:, begin : begin + step]
            allowed = (marks >= low) & (marks <= code)
            scores = jnp.where(allowed, dot_t(query, keys), NEG)
            new_top = jnp.maximum(top, jnp.max(scores, axis=1, keepdims=True))
            expo = jnp.where(allowed, jnp.exp(scores - new_top), 0.0)
            shrink = jnp.exp(top - new_top)
            mass = mass * shrink + jnp.sum(expo, axis=1, keepdims=True)
            total = total * shrink + dot(expo.astype(BF), v_ref[begin : begin + step, :])
            top = new_top
        att_ref[:, h * HD : (h + 1) * HD] = total / mass
        lse_ref[:, h * 128 : (h + 1) * 128] = jnp.broadcast_to(top + jnp.log(mass), (rows, 128))


def attend(queries, keys, values, query_code, key_code):
    rows, width = queries.shape
    heads = width // HD
    count = keys.shape[0]
    return pl.pallas_call(
        attend_kernel,
        out_shape=(
            jax.ShapeDtypeStruct((rows, width), F32),
            jax.ShapeDtypeStruct((rows, heads * 128), F32),
        ),
        compiler_params=pltpu.CompilerParams(vmem_limit_bytes=48 << 20),
        cost_estimate=pl.CostEstimate(
            flops=4 * rows * width * count,
            bytes_accessed=4 * count * HD + 8 * rows * width,
            transcendentals=rows * heads * count,
        ),
    )(queries, keys, values, query_code, key_code)


def attend_back_kernel(
    q_ref, k_ref, v_ref, qc_ref, kc_ref, att_ref, lse_ref, dm_ref, dq_ref, dk_ref, dv_ref
):
    rows = q_ref.shape[0]
    heads = q_ref.shape[1] // HD
    count = k_ref.shape[0]
    step = key_step(count)
    code = qc_ref[...]
    low = code - code % 4
    dq = [jnp.zeros((rows, HD), F32) for _ in range(heads)]
    for begin in range(0, count, step):
        keys = k_ref[begin : begin + step, :]
        vals = v_ref[begin : begin + step, :]
        marks = kc_ref[:, begin : begin + step]
        allowed = (marks >= low) & (marks <= code)
        dk = jnp.zeros((step, HD), F32)
        dv = jnp.zeros((step, HD), F32)
        for h in range(heads):
            span = slice(h * HD, (h + 1) * HD)
            query = q_ref[:, span] * BF(HD**-0.5)
            dmix = dm_ref[:, span]
            delta = jnp.sum(dmix.astype(F32) * att_ref[:, span], axis=1, keepdims=True)
            scores = dot_t(query, keys)
            probs = jnp.where(allowed, jnp.exp(scores - lse_ref[:, h * 128 : h * 128 + 1]), 0.0)
            dscores = (probs * (dot_t(dmix, vals) - delta)).astype(BF)
            dq[h] = dq[h] + dot(dscores, keys)
            dk = dk + t_dot(dscores, query)
            dv = dv + t_dot(probs.astype(BF), dmix)
        dk_ref[begin : begin + step, :] = dk.astype(BF)
        dv_ref[begin : begin + step, :] = dv.astype(BF)
    for h in range(heads):
        dq_ref[:, h * HD : (h + 1) * HD] = (dq[h] * HD**-0.5).astype(BF)


def attend_back(queries, keys, values, query_code, key_code, attended, log_sum, dmixed):
    rows, width = queries.shape
    count = keys.shape[0]
    return pl.pallas_call(
        attend_back_kernel,
        out_shape=(
            jax.ShapeDtypeStruct((rows, width), BF),
            jax.ShapeDtypeStruct((count, HD), BF),
            jax.ShapeDtypeStruct((count, HD), BF),
        ),
        compiler_params=pltpu.CompilerParams(vmem_limit_bytes=56 << 20),
        cost_estimate=pl.CostEstimate(
            flops=10 * rows * width * count,
            bytes_accessed=8 * count * HD + 12 * rows * width,
            transcendentals=rows * width // HD * count,
        ),
    )(queries, keys, values, query_code, key_code, attended, log_sum, dmixed)


def shards(
    x_prefix,
    x_action,
    prefix_segment,
    prefix_attn_gain,
    prefix_query,
    prefix_key,
    prefix_value,
    prefix_out,
    prefix_mlp_gain,
    prefix_gate,
    prefix_up,
    prefix_down,
    action_attn_gain,
    action_query,
    action_key,
    action_value,
    action_out,
    action_mlp_gain,
    action_gate,
    action_up,
    action_down,
    cot_prefix,
    cot_action,
):
    n = lax.axis_size("seq")
    tp = lax.axis_size("tp")
    s = lax.axis_index("seq")
    t = lax.axis_index("tp")
    rp, cp = x_prefix.shape
    ra, ca = x_action.shape
    rows = rp + ra
    dp, da = cp * tp, ca * tp
    kp, ka = dp // n, da // n
    width = prefix_query.shape[1]
    fp, fa = prefix_gate.shape[1] // n, action_gate.shape[1] // n

    def pack_columns(prefix_part, action_part):
        return jnp.concatenate([prefix_part, fold_action(action_part, prefix_part.shape[1])], 0)

    def unpack_columns(packed):
        return packed[:rp], unfold_action(packed[rp:], ca)

    def full_rows(packed_pieces):
        parts = [(place, unpack_columns(piece)) for place, piece in packed_pieces]
        return (
            columns_of([(p, v[0]) for p, v in parts], rp, cp, packed_pieces[0][1].dtype),
            columns_of([(p, v[1]) for p, v in parts], ra, ca, packed_pieces[0][1].dtype),
        )

    def halves_of(prefix_rows, action_rows):
        return [
            jnp.concatenate([prefix_rows[:, : dp // 2], action_rows[: ra // 2]], axis=0),
            jnp.concatenate([prefix_rows[:, dp // 2 :], action_rows[ra // 2 :]], axis=0),
        ]

    def tokens_of(halves):
        prefix_all = jnp.concatenate(
            [
                jnp.concatenate([halves[0][k][:rp], halves[1][k][:rp]], axis=1)
                for k in range(n)
            ],
            axis=0,
        )
        action_all = jnp.concatenate(
            [x for k in range(n) for x in (halves[0][k][rp:], halves[1][k][rp:])], axis=0
        )
        return prefix_all, action_all

    def reduce_tokens(prefix_all, action_all):
        halves = [[], []]
        for k in range(n):
            pair = halves_of(prefix_all[k * rp : (k + 1) * rp], action_all[k * ra : (k + 1) * ra])
            for half, part in zip(halves, pair):
                half.append(part)
        left, right = scatter_seq(halves)
        prefix_sum = jnp.concatenate([left[:rp], right[:rp]], axis=1)
        action_sum = jnp.concatenate([left[rp:], right[rp:]], axis=0)
        return prefix_sum, action_sum

    def own_columns(prefix_rows, action_rows, rank):
        return (
            lax.dynamic_slice_in_dim(prefix_rows, rank * cp, cp, 1),
            lax.dynamic_slice_in_dim(action_rows, rank * ca, ca, 1),
        )

    def reduce_columns(prefix_rows, action_rows):
        return unpack_columns(
            scatter_tp(lambda rank: pack_columns(*own_columns(prefix_rows, action_rows, rank)))
        )

    gains = jnp.concatenate(
        [prefix_attn_gain, prefix_mlp_gain, action_attn_gain, action_mlp_gain]
    )
    qkv_width = width + 2 * HD
    gain_rows = -(-gains.shape[0] // qkv_width)
    gains = jnp.pad(gains, (0, 8 * qkv_width - gains.shape[0])).reshape(8, qkv_width)
    pack_qkv = jnp.concatenate(
        [
            jnp.concatenate([prefix_query, prefix_key, prefix_value], axis=1),
            jnp.concatenate([action_query, action_key, action_value], axis=1),
            gains,
        ],
        axis=0,
    )
    got_qkv = lax.all_gather(pack_qkv, "seq", axis=0)
    qkv_prefix = got_qkv[:, :kp].reshape(dp, qkv_width)
    qkv_action = got_qkv[:, kp : kp + ka].reshape(da, qkv_width)
    got_gains = got_qkv[:, kp + ka : kp + ka + gain_rows].reshape(n, -1).astype(F32)
    attn_gain_p = got_gains[:, :kp].reshape(dp)
    mlp_gain_p = got_gains[:, kp : 2 * kp].reshape(dp)
    attn_gain_a = got_gains[:, 2 * kp : 2 * kp + ka].reshape(da)
    mlp_gain_a = got_gains[:, 2 * kp + ka : 2 * kp + 2 * ka].reshape(da)
    pack_out = jnp.concatenate([prefix_out.T, action_out.T], axis=0)
    got_out = lax.all_gather(pack_out, "seq", axis=0)
    out_prefix_t = got_out[:, :kp].reshape(dp, width)
    out_action_t = got_out[:, kp:].reshape(da, width)

    down_prefix_t = prefix_down.T
    down_action_t = action_down.T

    def ff_piece(rank):
        prefix_part = jnp.concatenate(
            [
                lax.dynamic_slice_in_dim(w, rank * fp, fp, 1)
                for w in (prefix_gate, prefix_up, down_prefix_t)
            ],
            axis=1,
        )
        action_part = jnp.concatenate(
            [
                lax.dynamic_slice_in_dim(w, rank * fa, fa, 1)
                for w in (action_gate, action_up, down_action_t)
            ],
            axis=1,
        )
        return jnp.concatenate([prefix_part, fold_action(action_part, 3 * fp)], axis=0)

    ff_prefix = jnp.zeros((dp, 3 * fp), BF)
    ff_action = jnp.zeros((da, 3 * fa), BF)
    for k in range(n):
        piece = ff_piece(s ^ k)
        if k:
            piece = swap(piece, "seq", k)
        ff_prefix = lax.dynamic_update_slice(ff_prefix, piece[:kp], ((s ^ k) * kp, 0))
        ff_action = lax.dynamic_update_slice(
            ff_action, unfold_action(piece[kp:], 3 * fa), ((s ^ k) * ka, 0)
        )

    x_parts = full_rows(gather_tp(pack_columns(x_prefix, x_action)))
    norms1 = []
    projected = []
    for part, gain, weights in zip(
        x_parts, (attn_gain_p, attn_gain_a), (qkv_prefix, qkv_action)
    ):
        centered, inverse = normalized_rows(part.astype(F32))
        normed = (centered * gain).astype(BF)
        norms1.append((centered, inverse, gain, normed))
        projected.append(dot(normed, weights).astype(BF))
    qkv = jnp.concatenate(projected, axis=0)
    queries = qkv[:, :width]
    key_blocks, value_blocks = gather_seq([qkv[:, width : width + HD], qkv[:, width + HD :]])
    keys = jnp.concatenate(key_blocks, axis=0)
    values = jnp.concatenate(value_blocks, axis=0)
    codes = token_codes(prefix_segment, n, ra)
    query_code = lax.dynamic_slice_in_dim(codes, s, 1, 0).reshape(rows, 1)
    key_code = jnp.concatenate(
        [lax.dynamic_slice_in_dim(codes, s ^ k, 1, 0) for k in range(n)], axis=1
    )
    attended, log_sum = attend(queries, keys, values, query_code, key_code)
    mixed = attended.astype(BF)
    mixed_parts = (mixed[:rp], mixed[rp:])
    branch = reduce_columns(
        dot_t(mixed_parts[0], out_prefix_t), dot_t(mixed_parts[1], out_action_t)
    )
    residuals = (x_prefix.astype(F32) + branch[0], x_action.astype(F32) + branch[1])
    mids = full_rows(
        gather_tp(pack_columns(residuals[0].astype(BF), residuals[1].astype(BF)))
    )
    norms2 = []
    for part, gain in zip(mids, (mlp_gain_p, mlp_gain_a)):
        centered, inverse = normalized_rows(part.astype(F32))
        norms2.append((centered, inverse, gain, (centered * gain).astype(BF)))

    cot_all = tokens_of(gather_seq(halves_of(cot_prefix, cot_action)))
    normed_all = tokens_of(gather_seq(halves_of(norms2[0][3], norms2[1][3])))
    lifted = []
    dnormed = []
    ff_grads = []
    for rows_in, cot_rows, weights, f in zip(
        normed_all, cot_all, (ff_prefix, ff_action), (fp, fa)
    ):
        gate, up, down_t = weights[:, :f], weights[:, f : 2 * f], weights[:, 2 * f :]
        gate_out = dot(rows_in, gate)
        up_out = dot(rows_in, up)
        hidden, pull = jax.vjp(gated, gate_out, up_out)
        hidden = hidden.astype(BF)
        dhidden = dot(cot_rows, down_t)
        dgate, dup = (g.astype(BF) for g in pull(dhidden))
        dnormed.append((dot_t(dgate, gate) + dot_t(dup, up)).astype(BF))
        lifted.append(dot_t(hidden, down_t).astype(BF))
        ff_grads.append(
            (
                t_dot(rows_in, dgate).astype(BF),
                t_dot(rows_in, dup).astype(BF),
                t_dot(cot_rows, hidden).astype(BF),
            )
        )
    dnormed2 = reduce_columns(*reduce_tokens(*dnormed))
    lifted_own = reduce_columns(*reduce_tokens(*lifted))
    outputs = [(r + m).astype(BF) for r, m in zip(residuals, lifted_own)]

    def ff_grad_piece(rank):
        prefix_part = jnp.concatenate(
            [lax.dynamic_slice_in_dim(g, rank * kp, kp, 0) for g in ff_grads[0]], axis=1
        )
        action_part = jnp.concatenate(
            [lax.dynamic_slice_in_dim(g, rank * ka, ka, 0) for g in ff_grads[1]], axis=1
        )
        return jnp.concatenate([prefix_part, fold_action(action_part, 3 * fp)], axis=0)

    home_prefix = [jnp.zeros((kp, n * fp), F32) for _ in range(3)]
    home_action = [jnp.zeros((ka, n * fa), F32) for _ in range(3)]
    for k in range(n):
        piece = ff_grad_piece(s ^ k)
        if k:
            piece = swap(piece, "seq", k)
        action_piece = unfold_action(piece[kp:], 3 * fa)
        for i in range(3):
            home_prefix[i] = lax.dynamic_update_slice(
                home_prefix[i],
                piece[:kp, i * fp : (i + 1) * fp].astype(F32),
                (0, (s ^ k) * fp),
            )
            home_action[i] = lax.dynamic_update_slice(
                home_action[i],
                action_piece[:, i * fa : (i + 1) * fa].astype(F32),
                (0, (s ^ k) * fa),
            )

    dnormed2_full = full_rows(gather_tp(pack_columns(*(d.astype(BF) for d in dnormed2))))
    dresids = []
    dbranches = []
    mlp_gain_grads = []
    for part, cot_rows, (centered, inverse, gain, _), cols in zip(
        dnormed2_full, (cot_prefix, cot_action), norms2, (cp, ca)
    ):
        gradient = part.astype(F32)
        inner = gradient * gain
        moved = inverse * (
            inner - centered * jnp.mean(inner * centered, axis=1, keepdims=True)
        )
        dresid = cot_rows.astype(F32) + moved
        mlp_gain_grads.append(jnp.sum(gradient * centered, axis=0))
        dbranches.append(dresid.astype(BF))
        dresids.append(lax.dynamic_slice_in_dim(dresid, t * cols, cols, 1))

    dmixed = jnp.concatenate(
        [dot(dbranches[0], out_prefix_t), dot(dbranches[1], out_action_t)], axis=0
    ).astype(BF)
    out_grads = jnp.concatenate(
        [
            t_dot(dbranches[0], mixed_parts[0]).astype(BF).reshape(n, kp, width),
            t_dot(dbranches[1], mixed_parts[1]).astype(BF).reshape(n, ka, width),
        ],
        axis=1,
    )
    out_home = lax.psum_scatter(out_grads, "seq", scatter_dimension=0).astype(F32)
    dquery, dkey_all, dvalue_all = attend_back(
        queries, keys, values, query_code, key_code, attended, log_sum, dmixed
    )
    dkey, dvalue = scatter_seq(
        [
            [part[k * rows : (k + 1) * rows] for k in range(n)]
            for part in (dkey_all, dvalue_all)
        ]
    )
    dqkv = jnp.concatenate([dquery, dkey.astype(BF), dvalue.astype(BF)], axis=1)
    dqkv_parts = (dqkv[:rp], dqkv[rp:])
    qkv_grads = []
    dnormed1 = []
    dots = []
    attn_gain_grads = []
    for part, weights, (centered, inverse, gain, normed) in zip(
        dqkv_parts, (qkv_prefix, qkv_action), norms1
    ):
        qkv_grads.append(t_dot(normed, part).astype(BF))
        partial = dot_t(part, weights)
        product = partial * centered
        dots.append(jnp.sum(product * gain, axis=1))
        attn_gain_grads.append(jnp.sum(product, axis=0))
        dnormed1.append(partial)
    row_dots = jnp.pad(jnp.concatenate(dots), (0, cp * (-(-rows // cp)) - rows)).reshape(-1, cp)
    dots_high = row_dots.astype(BF)
    dots_low = (row_dots - dots_high.astype(F32)).astype(BF)
    dot_rows = jnp.concatenate([dots_high, dots_low], axis=0)
    dot_count = row_dots.shape[0]
    dot_rows = jnp.pad(dot_rows, ((0, 8 - dot_rows.shape[0]), (0, 0)))
    own = pack_columns(*own_columns(*dnormed1, t))
    packed_own = jnp.concatenate([own, dot_rows.astype(F32)], axis=0)
    total = packed_own
    for k in range(1, tp):
        message = pack_columns(*own_columns(*dnormed1, t ^ k)).astype(BF)
        total = total + swap(jnp.concatenate([message, dot_rows], axis=0), "tp", k).astype(F32)
    columns1 = unpack_columns(total[: own.shape[0]])
    dot_totals = total[own.shape[0] : own.shape[0] + 2 * dot_count].reshape(2, -1).sum(axis=0)
    dot_parts = (dot_totals[:rp, None], dot_totals[rp:rows, None])
    grad_x = []
    for gradient, row_dot, dresid, (centered, inverse, gain, _), cols in zip(
        columns1, dot_parts, dresids, norms1, (cp, ca)
    ):
        own_centered = lax.dynamic_slice_in_dim(centered, t * cols, cols, 1)
        own_gain = lax.dynamic_slice_in_dim(gain, t * cols, cols, 0)
        mean = row_dot / (cols * tp)
        moved = inverse * (gradient * own_gain - own_centered * mean)
        grad_x.append((dresid + moved).astype(BF))

    gain_rows_sent = jnp.concatenate(
        [
            mlp_gain_grads[0].reshape(n, kp),
            mlp_gain_grads[1].reshape(n, ka),
            attn_gain_grads[0].reshape(n, kp),
            attn_gain_grads[1].reshape(n, ka),
        ],
        axis=1,
    ).astype(BF)
    gain_rows_sent = jnp.pad(
        gain_rows_sent, ((0, 0), (0, 8 * qkv_width - gain_rows_sent.shape[1]))
    ).reshape(n, 8, qkv_width)
    qkv_sent = jnp.concatenate(
        [
            qkv_grads[0].reshape(n, kp, qkv_width),
            qkv_grads[1].reshape(n, ka, qkv_width),
            gain_rows_sent,
        ],
        axis=1,
    )
    qkv_home = lax.psum_scatter(qkv_sent, "seq", scatter_dimension=0).astype(F32)
    gains_home = qkv_home[kp + ka :].reshape(-1)
    shared = qkv_home[: kp + ka, width:]
    qp, qa = kp // tp, ka // tp
    attn_gains_partial = jnp.pad(
        gains_home[kp + ka : 2 * (kp + ka)], (0, (-(kp + ka)) % (2 * HD))
    ).reshape(-1, 2 * HD)
    attn_gains_partial = jnp.pad(
        attn_gains_partial, ((0, (-attn_gains_partial.shape[0]) % 8), (0, 0))
    )

    def shared_piece(rank):
        return jnp.concatenate(
            [
                lax.dynamic_slice_in_dim(shared, rank * qp, qp, 0),
                lax.dynamic_slice_in_dim(shared, kp + rank * qa, qa, 0),
                attn_gains_partial,
            ],
            axis=0,
        )

    shared_home = scatter_tp(shared_piece)
    attn_gains_home = shared_home[qp + qa :].reshape(-1)
    return (
        outputs[0],
        outputs[1],
        grad_x[0],
        grad_x[1],
        attn_gains_home[:kp],
        qkv_home[:kp, :width],
        shared_home[:qp, :HD],
        shared_home[:qp, HD:],
        out_home[:kp].T,
        gains_home[:kp],
        home_prefix[0],
        home_prefix[1],
        home_prefix[2].T,
        attn_gains_home[kp : kp + ka],
        qkv_home[kp : kp + ka, :width],
        shared_home[qp : qp + qa, :HD],
        shared_home[qp : qp + qa, HD:],
        out_home[kp:].T,
        gains_home[kp : kp + ka],
        home_action[0],
        home_action[1],
        home_action[2].T,
    )


def solution(mesh):
    split = P("seq", "tp")
    turned = P("tp", "seq")
    both = P(("seq", "tp"), None)
    one = P("seq")
    rows = P("seq", None)
    stream_in = (one, split, rows, rows, turned, one, split, split, turned)
    stream_out = (one, split, both, both, turned, one, split, split, turned)
    return jax.shard_map(
        shards,
        mesh=mesh,
        in_specs=(split, split, P()) + stream_in + stream_in + (rows, rows),
        out_specs=(split, split, split, split) + stream_out + stream_out,
        check_vma=False,
    )
```

time: 2170 us -> 952 us (0.44)
  waiting for transfers between devices: 1510 us -> 354 us
  blocking collectives: 279 us -> 0 us
  local copies, waits for them, and re-layouts: 69 us -> 234 us
  matrix products: 188 us -> 103 us
  starting transfers between devices: 10.8 us -> 87.8 us
  other arithmetic: 68.5 us -> 134 us
  loops' own time: 21.9 us -> 0 us
    reduce_scatter x16 -> x2, waiting for transfers between devices: 998 us -> 0.01 us  [the longest x1 0.01 us: shards(): lax.psum_scatter(out_grads, 'seq', scatter_dimension=0).astype(F32)]
    all_gather x17 -> x2, waiting for transfers between devices: 449 us -> 0.01 us  [the longest x1 0.01 us: shards(): got_qkv = lax.all_gather(pack_qkv, 'seq', axis=0)]
    ppermute x0 -> x74, waiting for transfers between devices: none -> 354 us  [swap(): return lax.ppermute(value, axis, [(i, i ^ mask) for i in range(count)])]
    unnamed x2 -> x0, blocking collectives: 135 us -> none
    all_gather x9 -> x0, blocking collectives: 96.6 us -> none  [the longest x1 13.6 us: shards(): lax.all_gather(x_action, 'tp', axis=1, tiled=True)]
    ppermute x0 -> x74, starting transfers between devices: none -> 87.5 us  [swap(): return lax.ppermute(value, axis, [(i, i ^ mask) for i in range(count)])]
    dot_general x70 -> x30, matrix products: 188 us -> 103 us  [the longest x10 46 us: dot_t(): lax.dot_general(left, right, (((1,), (1,)), ((), ())), preferred_element_...]
    psum x2 -> x0, waiting for transfers between devices: 52 us -> none  [the longest x1 52 us: shards(): lax.psum(mlp_grads[0][3].astype(jnp.bfloat16), 'tp').astype(jnp.float32)]
  transfers between devices with their start and end apart: 41 -> 78, of which waited for: 25 -> 32; matrix products, arithmetic and copies ran while one was open for 20% -> 37% of each run, Pallas kernels for 0% -> 0%
where the time goes in v1:
time: 952 us; the launch traced here: 944 us
  waiting for transfers between devices  354 us (37%)
  local copies, waits for them, and re-layouts  234 us (25%)
  other arithmetic  134 us (14%)
  matrix products  103 us (11%)
  starting transfers between devices  87.8 us (9%)
  between operations  19.1 us (2%)
  Pallas kernels  12 us (1%)
    ppermute x74, waiting for transfers between devices, swap(): return lax.ppermute(value, axis, [(i, i ^ mask) for i in range(count)])  354 us
    ppermute x74, starting transfers between devices, swap(): return lax.ppermute(value, axis, [(i, i ^ mask) for i in range(count)])  87.5 us
    unnamed x605, local copies, waits for them, and re-layouts  53.9 us
    dot_general x10, matrix products, dot_t(): lax.dot_general(left, right, (((1,), (1,)), ((), ())), preferred_element_...  46 us
    convert_element_type x21, local copies, waits for them, and re-layouts, shards(): piece[:kp, i * fp:(i + 1) * fp].astype(F32)  34.9 us
    dot_general x10, matrix products, dot(): return jnp.dot(left, right, preferred_element_type=F32)  30.1 us
    dot_general x10, matrix products, t_dot(): lax.dot_general(left, right, (((0,), (0,)), ((), ())), preferred_element_...  27.3 us
    another operation x32, other arithmetic, scatter_seq(): got = swap(jnp.stack([blocks[k].astype(BF) for k in sent]), 'seq', mask)  22.8 us
  transfers between devices with their start and end apart: 78, of which 32 were waited for; matrix products, arithmetic and copies ran while one was open for 37% of the time, Pallas kernels for 0%

profile of v1, /device:TPU:0, one launch (start us, length us, event | category | flops | bytes accessed | tf_op | source)
XLA Modules:
  0.0 944.1 jit_solution(10290508319126192246)
XLA Ops:
  65.9 37.2 %collective-permute-done.37 = bf16[1,264,1024]{2,1,0:T(8,128)(2,1)S(1)} collective-permute-done((bf16[1,264,1024]{2,1,0:T(8,128)(2,1)S(1)}, bf16[1,264,1024]{2,1,0:T(8,128)(2,1)S(1)}, u32[]{:S(2)}, u32[]{:S(2)}) %collective-permute-start.37) | collective-permute-done | bytes 540704 | tf_op jit(solution)/shard_map/ppermute | solution.py:22
  112.1 58.2 %collective-permute-done.24 = bf16[288,1536]{1,0:T(8,128)(2,1)S(1)} collective-permute-done((bf16[288,1536]{1,0:T(8,128)(2,1)S(1)}, bf16[288,1536]{1,0:T(8,128)(2,1)S(1)}, u32[]{:S(2)}, u32[]{:S(2)}) %collective-permute-start.24) | collective-permute-done | bytes 884768 | tf_op jit(solution)/shard_map/ppermute | solution.py:22
  171.8 16.6 %collective-permute-done.25 = bf16[288,1536]{1,0:T(8,128)(2,1)S(1)} collective-permute-done((bf16[288,1536]{1,0:T(8,128)(2,1)S(1)}, bf16[288,1536]{1,0:T(8,128)(2,1)S(1)}, u32[]{:S(2)}, u32[]{:S(2)}) %collective-permute-start.25) | collective-permute-done | bytes 884768 | tf_op jit(solution)/shard_map/ppermute | solution.py:22
  194.7 17.3 %collective-permute-done.38 = bf16[2,264,1024]{2,1,0:T(8,128)(2,1)S(1)} collective-permute-done((bf16[2,264,1024]{2,1,0:T(8,128)(2,1)S(1)}, bf16[2,264,1024]{2,1,0:T(8,128)(2,1)S(1)}, u32[]{:S(2)}, u32[]{:S(2)}) %collective-permute-start.38) | collective-permute-done | bytes 1081376 | tf_op jit(solution)/shard_map/ppermute | solution.py:22
  231.0 3.3 slice.1762
  248.0 4.3 collective-permute-done.4
  263.5 3.9 shard_map.390
  268.7 3.4 collective-permute-start.11
  274.7 5.3 collective-permute-done.11
  280.1 15.5 %collective-permute-done.10 = bf16[264,512]{1,0:T(8,128)(2,1)S(1)} collective-permute-done((bf16[264,512]{1,0:T(8,128)(2,1)S(1)}, bf16[264,512]{1,0:T(8,128)(2,1)S(1)}, u32[]{:S(2)}, u32[]{:S(2)}) %collective-permute-start.10) | collective-permute-done | bytes 270368 | tf_op jit(solution)/shard_map/ppermute | solution.py:22
  303.8 4.7 collective-permute-done.12
  308.4 11.5 %collective-permute-done.13 = bf16[264,512]{1,0:T(8,128)(2,1)S(1)} collective-permute-done((bf16[264,512]{1,0:T(8,128)(2,1)S(1)}, bf16[264,512]{1,0:T(8,128)(2,1)S(1)}, u32[]{:S(2)}, u32[]{:S(2)}) %collective-permute-start.13) | collective-permute-done | bytes 270368 | tf_op jit(solution)/shard_map/ppermute | solution.py:22
  325.9 7.4 collective-permute-done.15
  342.5 13.0 %collective-permute-done.16 = bf16[2,264,1024]{2,1,0:T(8,128)(2,1)S(1)} collective-permute-done((bf16[2,264,1024]{2,1,0:T(8,128)(2,1)S(1)}, bf16[2,264,1024]{2,1,0:T(8,128)(2,1)S(1)}, u32[]{:S(2)}, u32[]{:S(2)}) %collective-permute-start.16) | collective-permute-done | bytes 1081376 | tf_op jit(solution)/shard_map/ppermute | solution.py:22
  356.7 7.9 fusion.18
  372.6 7.6 fusion.23
  380.2 10.0 %fusion.6 = (bf16[2048,512]{1,0:T(8,128)(2,1)S(1)}, bf16[2048,512]{1,0:T(8,128)(2,1)S(1)}, bf16[2048,512]{1,0:T(8,128)(2,1)S(1)}) fusion(f32[2048,512]{1,0:T(8,128)S(1)} %fusion.18, f32[2048,512]{1,0:T(8,128)} %fusion.23, bf16[2048,2048]{1,0:T(8,128)(2,1)S(1)} %maximum_dynamic-update-slice_fusion, bf16[2048,1536]{1,0:T(8,128)(2,1)} %slice_dynamic-update-slice_fusion), kind=kOutput, calls=%fused_computation.11 | convolution fusion | flops 4322230272 | bytes 25165824 | tf_op jit(solution)/shard_map/dot_general | solution.py:109
  390.2 9.2 convolution_convert_fusion
  399.4 9.3 convolution_convert_fusion.3
  408.7 9.7 %fusion.21 = f32[2048,2048]{1,0:T(8,128)} fusion(bf16[2048,512]{1,0:T(8,128)(2,1)S(1)} %get-tuple-element.155, bf16[2048,1536]{1,0:T(8,128)(2,1)} %slice_dynamic-update-slice_fusion), kind=kOutput, calls=%fused_computation.68 | convolution fusion | flops 4294967296 | bytes 20971520 | tf_op jit(solution)/shard_map/dot_general | solution.py:113
  418.4 4.9 convolution_convert_fusion.4
  424.8 6.0 convolution_convert_fusion.5
  430.8 14.8 %add_convert_fusion = bf16[2048,2048]{1,0:T(8,128)(2,1)} fusion(f32[2048,2048]{1,0:T(8,128)} %fusion.21, bf16[2048,512]{1,0:T(8,128)(2,1)} %copy-done.265, bf16[2048,1536]{1,0:T(8,128)(2,1)} %slice_dynamic-update-slice_fusion), kind=kOutput, calls=%fused_computation | convolution fusion | flops 4303355904 | bytes 29360128 | tf_op jit(solution)/shard_map/dot_general | solution.py:113
  445.6 5.3 slice_bitcast_fusion.9
  453.6 6.2 slice_bitcast_fusion.29
  529.6 23.6 %collective-permute-done.71 = bf16[288,1536]{1,0:T(8,128)(2,1)} collective-permute-done((bf16[288,1536]{1,0:T(8,128)(2,1)}, bf16[288,1536]{1,0:T(8,128)(2,1)}, u32[]{:S(2)}, u32[]{:S(2)}) %collective-permute-start.71) | collective-permute-done | bytes 884768 | tf_op jit(solution)/shard_map/ppermute | solution.py:22
  627.4 35.4 %collective-permute-done.29 = bf16[2,264,1024]{2,1,0:T(8,128)(2,1)} collective-permute-done((bf16[2,264,1024]{2,1,0:T(8,128)(2,1)}, bf16[2,264,1024]{2,1,0:T(8,128)(2,1)}, u32[]{:S(2)}, u32[]{:S(2)}) %collective-permute-start.29) | collective-permute-done | bytes 1081376 | tf_op jit(solution)/shard_map/ppermute | solution.py:22
  673.7 8.9 collective-permute-done.30
  686.7 6.5 collective-permute-done.45
  699.0 3.5 collective-permute-start.51
  702.6 5.5 collective-permute-start.50
  708.4 17.3 %collective-permute-done.50 = bf16[264,512]{1,0:T(8,128)(2,1)S(1)} collective-permute-done((bf16[264,512]{1,0:T(8,128)(2,1)S(1)}, bf16[264,512]{1,0:T(8,128)(2,1)S(1)}, u32[]{:S(2)}, u32[]{:S(2)}) %collective-permute-start.50) | collective-permute-done | bytes 270368 | tf_op jit(solution)/shard_map/ppermute | solution.py:22
  726.6 3.4 collective-permute-start.53
  730.6 7.9 collective-permute-done.52
  738.5 10.4 %collective-permute-done.53 = bf16[264,512]{1,0:T(8,128)(2,1)S(1)} collective-permute-done((bf16[264,512]{1,0:T(8,128)(2,1)S(1)}, bf16[264,512]{1,0:T(8,128)(2,1)S(1)}, u32[]{:S(2)}, u32[]{:S(2)}) %collective-permute-start.53) | collective-permute-done | bytes 270368 | tf_op jit(solution)/shard_map/ppermute | solution.py:22
  756.5 8.1 shard_map.391
  769.9 4.2 copy.257
  774.1 3.6 pad_maximum_fusion.1
  784.0 5.7 copy.308
  803.2 6.3 multiply_reduce_fusion.1
  811.6 3.6 multiply_reduce_fusion.3
  818.8 3.6 pad_maximum_fusion
  824.3 5.7 copy.309
  864.6 6.7 collective-permute-start.35
  871.7 15.5 %collective-permute-done.35 = bf16[264,512]{1,0:T(8,128)(2,1)S(1)} collective-permute-done((bf16[264,512]{1,0:T(8,128)(2,1)S(1)}, bf16[264,512]{1,0:T(8,128)(2,1)S(1)}, u32[]{:S(2)}, u32[]{:S(2)}) %collective-permute-start.35) | collective-permute-done | bytes 270368 | tf_op jit(solution)/shard_map/ppermute | solution.py:22
  893.7 6.4 collective-permute-done.63
  900.1 13.7 %collective-permute-done.62 = bf16[272,512]{1,0:T(8,128)(2,1)S(1)} collective-permute-done((bf16[272,512]{1,0:T(8,128)(2,1)S(1)}, bf16[272,512]{1,0:T(8,128)(2,1)S(1)}, u32[]{:S(2)}, u32[]{:S(2)}) %collective-permute-start.62) | collective-permute-done | bytes 278560 | tf_op jit(solution)/shard_map/ppermute | solution.py:22
  928.8 3.4 collective-permute-done.66
  (1246 shorter events, 423.5 us)
Async XLA Ops:
  7.2 221.1 %all-gather.5.cloned.1.call-start = ((), (), s32[]{:S(2)}) async-start(), calls=%async_computation.4 | async-start | bytes 7225344 | tf_op jit(solution)/shard_map/all_gather | solution.py:343
  10.4 244.1 %all-gather.7.cloned.1.call-start = ((), (), s32[]{:S(2)}) async-start(), calls=%async_computation.5 | async-start | bytes 3538944 | tf_op jit(solution)/shard_map/all_gather | solution.py:352
  11.2 45.3 %collective-permute-start = (bf16[264,512]{1,0:T(8,128)(2,1)}, bf16[264,512]{1,0:T(8,128)(2,1)}, u32[]{:S(2)}, u32[]{:S(2)}) collective-permute-start(bf16[264,512]{1,0:T(8,128)(2,1)} %maximum_maximum_fusion.14), channel_id=1, source_target_pairs={{0,1},{1,0},{2,3},{3,2},{4,5},{5,4},{6,7},{7,6},{8,9},{9,8},{10,11... | collective-permute-start | bytes 811016 | tf_op jit(solution)/shard_map/ppermute | solution.py:22
  14.2 43.5 %collective-permute-start.1 = (bf16[264,512]{1,0:T(8,128)(2,1)}, bf16[264,512]{1,0:T(8,128)(2,1)}, u32[]{:S(2)}, u32[]{:S(2)}) collective-permute-start(bf16[264,512]{1,0:T(8,128)(2,1)} %maximum_maximum_fusion.14), channel_id=1, source_target_pairs={{0,2},{1,3},{2,0},{3,1},{4,6},{5,7},{6,4},{7,5},{8,10},{9,11},{10,... | collective-permute-start | bytes 811016 | tf_op jit(solution)/shard_map/ppermute | solution.py:22
  16.8 43.7 %collective-permute-start.2 = (bf16[264,512]{1,0:T(8,128)(2,1)}, bf16[264,512]{1,0:T(8,128)(2,1)}, u32[]{:S(2)}, u32[]{:S(2)}) collective-permute-start(bf16[264,512]{1,0:T(8,128)(2,1)} %maximum_maximum_fusion.14), channel_id=1, source_target_pairs={{0,3},{1,2},{2,1},{3,0},{4,7},{5,6},{6,5},{7,4},{8,11},{9,10},{10,... | collective-permute-start | bytes 811016 | tf_op jit(solution)/shard_map/ppermute | solution.py:22
  26.8 79.1 %collective-permute-start.21 = (bf16[288,1536]{1,0:T(8,128)(2,1)}, bf16[288,1536]{1,0:T(8,128)(2,1)}, u32[]{:S(2)}, u32[]{:S(2)}) collective-permute-start(bf16[288,1536]{1,0:T(8,128)(2,1)} %maximum_maximum_fusion.7), channel_id=1, source_target_pairs={{0,4},{4,0},{8,12},{12,8},{16,20},{20,16},{24,28},{28,24},{1,5},{5... | collective-permute-start | bytes 2654216 | tf_op jit(solution)/shard_map/ppermute | solution.py:22
  28.1 80.0 %collective-permute-start.22 = (bf16[288,1536]{1,0:T(8,128)(2,1)}, bf16[288,1536]{1,0:T(8,128)(2,1)}, u32[]{:S(2)}, u32[]{:S(2)}) collective-permute-start(bf16[288,1536]{1,0:T(8,128)(2,1)} %maximum_maximum_fusion.8), channel_id=1, source_target_pairs={{0,8},{4,12},{8,0},{12,4},{16,24},{20,28},{24,16},{28,20},{1,9},{5... | collective-permute-start | bytes 2654216 | tf_op jit(solution)/shard_map/ppermute | solution.py:22
  30.7 886.7 %reduce-scatter.5.cloned.1.call-start = ((), (), s32[]{:S(2)}) async-start(), calls=%async_computation.3 | async-start | bytes 3538944 | tf_op jit(solution)/shard_map/reduce_scatter | solution.py:505
  56.5 54.0 %collective-permute-start.23 = (bf16[288,1536]{1,0:T(8,128)(2,1)}, bf16[288,1536]{1,0:T(8,128)(2,1)S(1)}, u32[]{:S(2)}, u32[]{:S(2)}) collective-permute-start(bf16[288,1536]{1,0:T(8,128)(2,1)} %maximum_maximum_fusion.9), channel_id=1, source_target_pairs={{0,12},{4,8},{8,4},{12,0},{16,28},{20,24},{24,20},{28,16},{1,13},{... | collective-permute-start | bytes 2654216 | tf_op jit(solution)/shard_map/ppermute | solution.py:22
  57.7 45.4 %collective-permute-start.37 = (bf16[1,264,1024]{2,1,0:T(8,128)(2,1)S(1)}, bf16[1,264,1024]{2,1,0:T(8,128)(2,1)S(1)}, u32[]{:S(2)}, u32[]{:S(2)}) collective-permute-start(bf16[1,264,1024]{2,1,0:T(8,128)(2,1)S(1)} %maximum_bitcast_fusion.10), channel_id=1, source_target_pairs={{0,8},{4,12},{8,0},{12,4},{16,24},{20,28},{24,16},{28,20},{1,9},{5... | collective-permute-start | bytes 1622024 | tf_op jit(solution)/shard_map/ppermute | solution.py:22
  60.5 44.2 %collective-permute-start.40 = (bf16[1,264,1024]{2,1,0:T(8,128)(2,1)S(1)}, bf16[1,264,1024]{2,1,0:T(8,128)(2,1)S(1)}, u32[]{:S(2)}, u32[]{:S(2)}) collective-permute-start(bf16[1,264,1024]{2,1,0:T(8,128)(2,1)S(1)} %maximum_bitcast_fusion.11), channel_id=1, source_target_pairs={{0,16},{4,20},{8,24},{12,28},{16,0},{20,4},{24,8},{28,12},{1,17},{... | collective-permute-start | bytes 1622024 | tf_op jit(solution)/shard_map/ppermute | solution.py:22
  103.1 67.2 %collective-permute-start.24 = (bf16[288,1536]{1,0:T(8,128)(2,1)S(1)}, bf16[288,1536]{1,0:T(8,128)(2,1)S(1)}, u32[]{:S(2)}, u32[]{:S(2)}) collective-permute-start(bf16[288,1536]{1,0:T(8,128)(2,1)S(1)} %copy-done.146), channel_id=1, source_target_pairs={{0,16},{4,20},{8,24},{12,28},{16,0},{20,4},{24,8},{28,12},{1,17},{... | collective-permute-start | bytes 2654216 | tf_op jit(solution)/shard_map/ppermute | solution.py:22
  104.8 83.6 %collective-permute-start.25 = (bf16[288,1536]{1,0:T(8,128)(2,1)S(1)}, bf16[288,1536]{1,0:T(8,128)(2,1)S(1)}, u32[]{:S(2)}, u32[]{:S(2)}) collective-permute-start(bf16[288,1536]{1,0:T(8,128)(2,1)S(1)} %copy-done.145), channel_id=1, source_target_pairs={{0,20},{4,16},{8,28},{12,24},{16,4},{20,0},{24,12},{28,8},{1,21},{... | collective-permute-start | bytes 2654216 | tf_op jit(solution)/shard_map/ppermute | solution.py:22
  106.2 82.2 %collective-permute-start.26 = (bf16[288,1536]{1,0:T(8,128)(2,1)S(1)}, bf16[288,1536]{1,0:T(8,128)(2,1)S(1)}, u32[]{:S(2)}, u32[]{:S(2)}) collective-permute-start(bf16[288,1536]{1,0:T(8,128)(2,1)S(1)} %copy-done.144), channel_id=1, source_target_pairs={{0,24},{4,28},{8,16},{12,20},{16,8},{20,12},{24,0},{28,4},{1,25},{... | collective-permute-start | bytes 2654216 | tf_op jit(solution)/shard_map/ppermute | solution.py:22
  108.1 80.4 %collective-permute-start.27 = (bf16[288,1536]{1,0:T(8,128)(2,1)S(1)}, bf16[288,1536]{1,0:T(8,128)(2,1)S(1)}, u32[]{:S(2)}, u32[]{:S(2)}) collective-permute-start(bf16[288,1536]{1,0:T(8,128)(2,1)S(1)} %copy-done.143), channel_id=1, source_target_pairs={{0,28},{4,24},{8,20},{12,16},{16,12},{20,8},{24,4},{28,0},{1,29},{... | collective-permute-start | bytes 2654216 | tf_op jit(solution)/shard_map/ppermute | solution.py:22
  110.5 101.5 %collective-permute-start.38 = (bf16[2,264,1024]{2,1,0:T(8,128)(2,1)S(1)}, bf16[2,264,1024]{2,1,0:T(8,128)(2,1)S(1)}, u32[]{:S(2)}, u32[]{:S(2)}) collective-permute-start(bf16[2,264,1024]{2,1,0:T(8,128)(2,1)S(1)} %pad_maximum_fusion.14), channel_id=1, source_target_pairs={{0,16},{4,20},{8,24},{12,28},{16,0},{20,4},{24,8},{28,12},{1,17},{... | collective-permute-start | bytes 3244040 | tf_op jit(solution)/shard_map/ppermute | solution.py:22
  170.3 42.0 %collective-permute-start.41 = (bf16[2,264,1024]{2,1,0:T(8,128)(2,1)S(1)}, bf16[2,264,1024]{2,1,0:T(8,128)(2,1)S(1)}, u32[]{:S(2)}, u32[]{:S(2)}) collective-permute-start(bf16[2,264,1024]{2,1,0:T(8,128)(2,1)S(1)} %pad_maximum_fusion.15), channel_id=1, source_target_pairs={{0,8},{4,12},{8,0},{12,4},{16,24},{20,28},{24,16},{28,20},{1,9},{5... | collective-permute-start | bytes 3244040 | tf_op jit(solution)/shard_map/ppermute | solution.py:22
  272.1 23.4 %collective-permute-start.10 = (bf16[264,512]{1,0:T(8,128)(2,1)S(1)}, bf16[264,512]{1,0:T(8,128)(2,1)S(1)}, u32[]{:S(2)}, u32[]{:S(2)}) collective-permute-start(bf16[264,512]{1,0:T(8,128)(2,1)S(1)} %maximum_maximum_fusion.16), channel_id=1, source_target_pairs={{0,2},{1,3},{2,0},{3,1},{4,6},{5,7},{6,4},{7,5},{8,10},{9,11},{10,... | collective-permute-start | bytes 811016 | tf_op jit(solution)/shard_map/ppermute | solution.py:22
  272.3 23.3 %collective-permute-start.9 = (bf16[264,512]{1,0:T(8,128)(2,1)S(1)}, bf16[264,512]{1,0:T(8,128)(2,1)S(1)}, u32[]{:S(2)}, u32[]{:S(2)}) collective-permute-start(bf16[264,512]{1,0:T(8,128)(2,1)S(1)} %maximum_maximum_fusion.15), channel_id=1, source_target_pairs={{0,1},{1,0},{2,3},{3,2},{4,5},{5,4},{6,7},{7,6},{8,9},{9,8},{10,11... | collective-permute-start | bytes 811016 | tf_op jit(solution)/shard_map/ppermute | solution.py:22
  298.0 21.9 %collective-permute-start.13 = (bf16[264,512]{1,0:T(8,128)(2,1)S(1)}, bf16[264,512]{1,0:T(8,128)(2,1)S(1)}, u32[]{:S(2)}, u32[]{:S(2)}) collective-permute-start(bf16[264,512]{1,0:T(8,128)(2,1)S(1)} %maximum_maximum_fusion.18), channel_id=1, source_target_pairs={{0,2},{1,3},{2,0},{3,1},{4,6},{5,7},{6,4},{7,5},{8,10},{9,11},{10,... | collective-permute-start | bytes 811016 | tf_op jit(solution)/shard_map/ppermute | solution.py:22
  302.3 17.7 %collective-permute-start.14 = (bf16[264,512]{1,0:T(8,128)(2,1)S(1)}, bf16[264,512]{1,0:T(8,128)(2,1)S(1)}, u32[]{:S(2)}, u32[]{:S(2)}) collective-permute-start(bf16[264,512]{1,0:T(8,128)(2,1)S(1)} %maximum_maximum_fusion.18), channel_id=1, source_target_pairs={{0,3},{1,2},{2,1},{3,0},{4,7},{5,6},{6,5},{7,4},{8,11},{9,10},{10,... | collective-permute-start | bytes 811016 | tf_op jit(solution)/shard_map/ppermute | solution.py:22
  333.4 22.0 %collective-permute-start.16 = (bf16[2,264,1024]{2,1,0:T(8,128)(2,1)S(1)}, bf16[2,264,1024]{2,1,0:T(8,128)(2,1)S(1)}, u32[]{:S(2)}, u32[]{:S(2)}) collective-permute-start(bf16[2,264,1024]{2,1,0:T(8,128)(2,1)S(1)} %pad_maximum_fusion.10), channel_id=1, source_target_pairs={{0,16},{4,20},{8,24},{12,28},{16,0},{20,4},{24,8},{28,12},{1,17},{... | collective-permute-start | bytes 3244040 | tf_op jit(solution)/shard_map/ppermute | solution.py:22
  336.6 19.2 %collective-permute-start.19 = (bf16[2,264,1024]{2,1,0:T(8,128)(2,1)S(1)}, bf16[2,264,1024]{2,1,0:T(8,128)(2,1)S(1)}, u32[]{:S(2)}, u32[]{:S(2)}) collective-permute-start(bf16[2,264,1024]{2,1,0:T(8,128)(2,1)S(1)} %pad_maximum_fusion.11), channel_id=1, source_target_pairs={{0,8},{4,12},{8,0},{12,4},{16,24},{20,28},{24,16},{28,20},{1,9},{5... | collective-permute-start | bytes 3244040 | tf_op jit(solution)/shard_map/ppermute | solution.py:22
  452.8 157.5 %collective-permute-start.43 = (bf16[4,264,1024]{2,1,0:T(8,128)(2,1)}, bf16[4,264,1024]{2,1,0:T(8,128)(2,1)}, u32[]{:S(2)}, u32[]{:S(2)}) collective-permute-start(bf16[4,264,1024]{2,1,0:T(8,128)(2,1)} %pad_maximum_fusion.8), channel_id=1, source_target_pairs={{0,4},{4,0},{8,12},{12,8},{16,20},{20,16},{24,28},{28,24},{1,5},{5... | collective-permute-start | bytes 6488072 | tf_op jit(solution)/shard_map/ppermute | solution.py:22
  468.3 44.2 %collective-permute-start.67 = (bf16[288,1536]{1,0:T(8,128)(2,1)}, bf16[288,1536]{1,0:T(8,128)(2,1)}, u32[]{:S(2)}, u32[]{:S(2)}) collective-permute-start(bf16[288,1536]{1,0:T(8,128)(2,1)} %copy.259), channel_id=1, source_target_pairs={{0,4},{4,0},{8,12},{12,8},{16,20},{20,16},{24,28},{28,24},{1,5},{5... | collective-permute-start | bytes 2654216 | tf_op jit(solution)/shard_map/ppermute | solution.py:22
  472.4 44.1 %collective-permute-start.68 = (bf16[288,1536]{1,0:T(8,128)(2,1)}, bf16[288,1536]{1,0:T(8,128)(2,1)}, u32[]{:S(2)}, u32[]{:S(2)}) collective-permute-start(bf16[288,1536]{1,0:T(8,128)(2,1)} %copy.261), channel_id=1, source_target_pairs={{0,8},{4,12},{8,0},{12,4},{16,24},{20,28},{24,16},{28,20},{1,9},{5... | collective-permute-start | bytes 2654216 | tf_op jit(solution)/shard_map/ppermute | solution.py:22
  477.1 43.2 %collective-permute-start.69 = (bf16[288,1536]{1,0:T(8,128)(2,1)}, bf16[288,1536]{1,0:T(8,128)(2,1)}, u32[]{:S(2)}, u32[]{:S(2)}) collective-permute-start(bf16[288,1536]{1,0:T(8,128)(2,1)} %copy.263), channel_id=1, source_target_pairs={{0,12},{4,8},{8,4},{12,0},{16,28},{20,24},{24,20},{28,16},{1,13},{... | collective-permute-start | bytes 2654216 | tf_op jit(solution)/shard_map/ppermute | solution.py:22
  481.0 43.8 %collective-permute-start.70 = (bf16[288,1536]{1,0:T(8,128)(2,1)}, bf16[288,1536]{1,0:T(8,128)(2,1)}, u32[]{:S(2)}, u32[]{:S(2)}) collective-permute-start(bf16[288,1536]{1,0:T(8,128)(2,1)} %copy.265), channel_id=1, source_target_pairs={{0,16},{4,20},{8,24},{12,28},{16,0},{20,4},{24,8},{28,12},{1,17},{... | collective-permute-start | bytes 2654216 | tf_op jit(solution)/shard_map/ppermute | solution.py:22
  512.6 40.6 %collective-permute-start.71 = (bf16[288,1536]{1,0:T(8,128)(2,1)}, bf16[288,1536]{1,0:T(8,128)(2,1)}, u32[]{:S(2)}, u32[]{:S(2)}) collective-permute-start(bf16[288,1536]{1,0:T(8,128)(2,1)} %copy.267), channel_id=1, source_target_pairs={{0,20},{4,16},{8,28},{12,24},{16,4},{20,0},{24,12},{28,8},{1,21},{... | collective-permute-start | bytes 2654216 | tf_op jit(solution)/shard_map/ppermute | solution.py:22
  516.5 41.5 %collective-permute-start.72 = (bf16[288,1536]{1,0:T(8,128)(2,1)}, bf16[288,1536]{1,0:T(8,128)(2,1)}, u32[]{:S(2)}, u32[]{:S(2)}) collective-permute-start(bf16[288,1536]{1,0:T(8,128)(2,1)} %copy.269), channel_id=1, source_target_pairs={{0,24},{4,28},{8,16},{12,20},{16,8},{20,12},{24,0},{28,4},{1,25},{... | collective-permute-start | bytes 2654216 | tf_op jit(solution)/shard_map/ppermute | solution.py:22
  520.3 101.3 %collective-permute-start.46 = (bf16[4,264,1024]{2,1,0:T(8,128)(2,1)}, bf16[4,264,1024]{2,1,0:T(8,128)(2,1)S(1)}, u32[]{:S(2)}, u32[]{:S(2)}) collective-permute-start(bf16[4,264,1024]{2,1,0:T(8,128)(2,1)} %pad_maximum_fusion.9), channel_id=1, source_target_pairs={{0,4},{4,0},{8,12},{12,8},{16,20},{20,16},{24,28},{28,24},{1,5},{5... | collective-permute-start | bytes 6488072 | tf_op jit(solution)/shard_map/ppermute | solution.py:22
  524.7 93.3 %collective-permute-start.31 = (bf16[4,264,1024]{2,1,0:T(8,128)(2,1)}, bf16[4,264,1024]{2,1,0:T(8,128)(2,1)}, u32[]{:S(2)}, u32[]{:S(2)}) collective-permute-start(bf16[4,264,1024]{2,1,0:T(8,128)(2,1)} %pad_maximum_fusion.5), channel_id=1, source_target_pairs={{0,4},{4,0},{8,12},{12,8},{16,20},{20,16},{24,28},{28,24},{1,5},{5... | collective-permute-start | bytes 6488072 | tf_op jit(solution)/shard_map/ppermute | solution.py:22
  553.2 61.0 %collective-permute-start.28 = (bf16[4,264,1024]{2,1,0:T(8,128)(2,1)}, bf16[4,264,1024]{2,1,0:T(8,128)(2,1)}, u32[]{:S(2)}, u32[]{:S(2)}) collective-permute-start(bf16[4,264,1024]{2,1,0:T(8,128)(2,1)} %pad_maximum_fusion.4), channel_id=1, source_target_pairs={{0,4},{4,0},{8,12},{12,8},{16,20},{20,16},{24,28},{28,24},{1,5},{5... | collective-permute-start | bytes 6488072 | tf_op jit(solution)/shard_map/ppermute | solution.py:22
  558.0 49.9 %collective-permute-start.73 = (bf16[288,1536]{1,0:T(8,128)(2,1)}, bf16[288,1536]{1,0:T(8,128)(2,1)}, u32[]{:S(2)}, u32[]{:S(2)}) collective-permute-start(bf16[288,1536]{1,0:T(8,128)(2,1)} %copy.271), channel_id=1, source_target_pairs={{0,28},{4,24},{8,20},{12,16},{16,12},{20,8},{24,4},{28,0},{1,29},{... | collective-permute-start | bytes 2654216 | tf_op jit(solution)/shard_map/ppermute | solution.py:22
  613.1 52.0 %collective-permute-start.44 = (bf16[2,264,1024]{2,1,0:T(8,128)(2,1)}, bf16[2,264,1024]{2,1,0:T(8,128)(2,1)}, u32[]{:S(2)}, u32[]{:S(2)}) collective-permute-start(bf16[2,264,1024]{2,1,0:T(8,128)(2,1)} %pad_maximum_fusion.16), channel_id=1, source_target_pairs={{0,8},{4,12},{8,0},{12,4},{16,24},{20,28},{24,16},{28,20},{1,9},{5... | collective-permute-start | bytes 3244040 | tf_op jit(solution)/shard_map/ppermute | solution.py:22
  617.2 45.7 %collective-permute-start.29 = (bf16[2,264,1024]{2,1,0:T(8,128)(2,1)}, bf16[2,264,1024]{2,1,0:T(8,128)(2,1)}, u32[]{:S(2)}, u32[]{:S(2)}) collective-permute-start(bf16[2,264,1024]{2,1,0:T(8,128)(2,1)} %pad_maximum_fusion.12), channel_id=1, source_target_pairs={{0,8},{4,12},{8,0},{12,4},{16,24},{20,28},{24,16},{28,20},{1,9},{5... | collective-permute-start | bytes 3244040 | tf_op jit(solution)/shard_map/ppermute | solution.py:22
  621.0 47.2 %collective-permute-start.32 = (bf16[2,264,1024]{2,1,0:T(8,128)(2,1)}, bf16[2,264,1024]{2,1,0:T(8,128)(2,1)}, u32[]{:S(2)}, u32[]{:S(2)}) collective-permute-start(bf16[2,264,1024]{2,1,0:T(8,128)(2,1)} %pad_maximum_fusion.13), channel_id=1, source_target_pairs={{0,16},{4,20},{8,24},{12,28},{16,0},{20,4},{24,8},{28,12},{1,17},{... | collective-permute-start | bytes 3244040 | tf_op jit(solution)/shard_map/ppermute | solution.py:22
  623.3 47.9 %collective-permute-start.47 = (bf16[2,264,1024]{2,1,0:T(8,128)(2,1)}, bf16[2,264,1024]{2,1,0:T(8,128)(2,1)}, u32[]{:S(2)}, u32[]{:S(2)}) collective-permute-start(bf16[2,264,1024]{2,1,0:T(8,128)(2,1)} %pad_maximum_fusion.17), channel_id=1, source_target_pairs={{0,16},{4,20},{8,24},{12,28},{16,0},{20,4},{24,8},{28,12},{1,17},{... | collective-permute-start | bytes 3244040 | tf_op jit(solution)/shard_map/ppermute | solution.py:22
  664.4 18.2 %collective-permute-start.30 = (bf16[1,264,1024]{2,1,0:T(8,128)(2,1)S(1)}, bf16[1,264,1024]{2,1,0:T(8,128)(2,1)S(1)}, u32[]{:S(2)}, u32[]{:S(2)}) collective-permute-start(bf16[1,264,1024]{2,1,0:T(8,128)(2,1)S(1)} %add_convert_fusion.10), channel_id=1, source_target_pairs={{0,16},{4,20},{8,24},{12,28},{16,0},{20,4},{24,8},{28,12},{1,17},{... | collective-permute-start | bytes 1622024 | tf_op jit(solution)/shard_map/ppermute | solution.py:22
  666.6 26.6 %collective-permute-start.45 = (bf16[1,264,1024]{2,1,0:T(8,128)(2,1)S(1)}, bf16[1,264,1024]{2,1,0:T(8,128)(2,1)S(1)}, u32[]{:S(2)}, u32[]{:S(2)}) collective-permute-start(bf16[1,264,1024]{2,1,0:T(8,128)(2,1)S(1)} %add_convert_fusion.4), channel_id=1, source_target_pairs={{0,16},{4,20},{8,24},{12,28},{16,0},{20,4},{24,8},{28,12},{1,17},{... | collective-permute-start | bytes 1622024 | tf_op jit(solution)/shard_map/ppermute | solution.py:22
  672.5 22.4 %collective-permute-start.48 = (bf16[1,264,1024]{2,1,0:T(8,128)(2,1)S(1)}, bf16[1,264,1024]{2,1,0:T(8,128)(2,1)S(1)}, u32[]{:S(2)}, u32[]{:S(2)}) collective-permute-start(bf16[1,264,1024]{2,1,0:T(8,128)(2,1)S(1)} %add_convert_fusion.1), channel_id=1, source_target_pairs={{0,8},{4,12},{8,0},{12,4},{16,24},{20,28},{24,16},{28,20},{1,9},{5... | collective-permute-start | bytes 1622024 | tf_op jit(solution)/shard_map/ppermute | solution.py:22
  702.6 23.1 %collective-permute-start.50 = (bf16[264,512]{1,0:T(8,128)(2,1)S(1)}, bf16[264,512]{1,0:T(8,128)(2,1)S(1)}, u32[]{:S(2)}, u32[]{:S(2)}) collective-permute-start(bf16[264,512]{1,0:T(8,128)(2,1)S(1)} %maximum_maximum_fusion.23), channel_id=1, source_target_pairs={{0,2},{1,3},{2,0},{3,1},{4,6},{5,7},{6,4},{7,5},{8,10},{9,11},{10,... | collective-permute-start | bytes 811016 | tf_op jit(solution)/shard_map/ppermute | solution.py:22
  726.6 22.3 %collective-permute-start.53 = (bf16[264,512]{1,0:T(8,128)(2,1)S(1)}, bf16[264,512]{1,0:T(8,128)(2,1)S(1)}, u32[]{:S(2)}, u32[]{:S(2)}) collective-permute-start(bf16[264,512]{1,0:T(8,128)(2,1)S(1)} %fusion.42), channel_id=1, source_target_pairs={{0,2},{1,3},{2,0},{3,1},{4,6},{5,7},{6,4},{7,5},{8,10},{9,11},{10,... | collective-permute-start | bytes 811016 | tf_op jit(solution)/shard_map/ppermute | solution.py:22
  730.0 19.0 %collective-permute-start.54 = (bf16[264,512]{1,0:T(8,128)(2,1)S(1)}, bf16[264,512]{1,0:T(8,128)(2,1)S(1)}, u32[]{:S(2)}, u32[]{:S(2)}) collective-permute-start(bf16[264,512]{1,0:T(8,128)(2,1)S(1)} %fusion.42), channel_id=1, source_target_pairs={{0,3},{1,2},{2,1},{3,0},{4,7},{5,6},{6,5},{7,4},{8,11},{9,10},{10,... | collective-permute-start | bytes 811016 | tf_op jit(solution)/shard_map/ppermute | solution.py:22
  777.7 142.2 %reduce-scatter.3.cloned.1.call-start = ((), (), s32[]{:S(2)}) async-start(), calls=%async_computation.2 | async-start | bytes 7225344 | tf_op jit(solution)/shard_map/reduce_scatter | solution.py:575
  864.6 22.6 %collective-permute-start.35 = (bf16[264,512]{1,0:T(8,128)(2,1)S(1)}, bf16[264,512]{1,0:T(8,128)(2,1)S(1)}, u32[]{:S(2)}, u32[]{:S(2)}) collective-permute-start(bf16[264,512]{1,0:T(8,128)(2,1)S(1)} %maximum_maximum_fusion.20), channel_id=1, source_target_pairs={{0,2},{1,3},{2,0},{3,1},{4,6},{5,7},{6,4},{7,5},{8,10},{9,11},{10,... | collective-permute-start | bytes 811016 | tf_op jit(solution)/shard_map/ppermute | solution.py:22
  890.7 23.1 %collective-permute-start.62 = (bf16[272,512]{1,0:T(8,128)(2,1)S(1)}, bf16[272,512]{1,0:T(8,128)(2,1)S(1)}, u32[]{:S(2)}, u32[]{:S(2)}) collective-permute-start(bf16[272,512]{1,0:T(8,128)(2,1)S(1)} %get-tuple-element.601), channel_id=1, source_target_pairs={{0,2},{1,3},{2,0},{3,1},{4,6},{5,7},{6,4},{7,5},{8,10},{9,11},{10,... | collective-permute-start | bytes 835592 | tf_op jit(solution)/shard_map/ppermute | solution.py:22
  890.7 23.1 %collective-permute-start.61 = (bf16[272,512]{1,0:T(8,128)(2,1)S(1)}, bf16[272,512]{1,0:T(8,128)(2,1)S(1)}, u32[]{:S(2)}, u32[]{:S(2)}) collective-permute-start(bf16[272,512]{1,0:T(8,128)(2,1)S(1)} %get-tuple-element.599), channel_id=1, source_target_pairs={{0,1},{1,0},{2,3},{3,2},{4,5},{5,4},{6,7},{7,6},{8,9},{9,8},{10,11... | collective-permute-start | bytes 835592 | tf_op jit(solution)/shard_map/ppermute | solution.py:22
  (296 other events, 3648.0 us)
Sparse Core Ops, SparseCore 0:
  10.5 65.8 all-gather.4
  78.3 82.2 all-gather.6
  777.8 48.9 reduce-scatter.4
  830.5 62.4 reduce-scatter.2

commit v2 on v1

v2 whole, which is shorter than its diff:
```python
import jax
import jax.numpy as jnp
from jax import lax
from jax.experimental import pallas as pl
from jax.experimental.pallas import tpu as pltpu
from jax.sharding import PartitionSpec as P

HD = 256
IMG = 768
TXT = 48
ACT = 50
EPS = 1e-06
NEG = -1e30
BF = jnp.bfloat16
F32 = jnp.float32
MIB = 1 << 20


def swap(value, axis, mask):
    count = lax.axis_size(axis)
    return lax.ppermute(value, axis, [(i, i ^ mask) for i in range(count)])


def after(values, *tokens):
    return lax.optimization_barrier((values, tokens))[0]


def far_masks():
    count = lax.axis_size("seq")
    masks = [1 << b for b in range(1, count.bit_length() - 1)]
    return masks, masks[::-1]


def block_order(number):
    order = [0]
    for mask in far_masks()[number]:
        order = order + [k ^ mask for k in order]
    return order


def gather_far(halves):
    results = []
    for half, masks in zip(halves, far_masks()):
        blocks = [half]
        for mask in masks:
            blocks = blocks + [swap(b, "seq", mask) for b in blocks]
        results.append(blocks)
    return results


def gather_rows(halves):
    even = jnp.concatenate([b for blocks in gather_far(halves) for b in blocks], axis=0)
    return swap(even, "seq", 1), even


def scatter_far(halves):
    results = []
    for half, masks in zip(halves, far_masks()):
        blocks = half
        for mask in masks[:0:-1]:
            keep = blocks.shape[0] // 2
            got = swap(blocks[keep:].astype(BF), "seq", mask)
            blocks = blocks[:keep].astype(F32) + got.astype(F32)
        got = swap(blocks[1].astype(BF), "seq", masks[0])
        results.append((blocks[0], got))
    return results


def gather_tp(piece):
    return [piece] + [swap(piece, "tp", k) for k in range(1, lax.axis_size("tp"))]


def sum_tp(pieces):
    total = pieces[0].astype(F32)
    for k in range(1, len(pieces)):
        total = total + swap(pieces[k].astype(BF), "tp", k).astype(F32)
    return total


def dot(left, right):
    return jnp.dot(left, right, preferred_element_type=F32)


def dot_t(left, right):
    return lax.dot_general(left, right, (((1,), (1,)), ((), ())), preferred_element_type=F32)


def t_dot(left, right):
    return lax.dot_general(left, right, (((0,), (0,)), ((), ())), preferred_element_type=F32)


def whole_call(kernel, outs, args, flops, scratch=(), limit=48, transcendentals=0):
    specs = [
        pl.BlockSpec(memory_space=pltpu.SMEM if a.ndim == 1 else pltpu.VMEM) for a in args
    ]
    outs = tuple(jax.ShapeDtypeStruct(shape, dtype) for shape, dtype in outs)
    moved = sum(a.size * a.dtype.itemsize for a in args)
    moved += sum(o.size * o.dtype.itemsize for o in outs)
    return pl.pallas_call(
        kernel,
        out_shape=outs,
        in_specs=specs,
        out_specs=tuple(pl.BlockSpec(memory_space=pltpu.VMEM) for _ in outs),
        scratch_shapes=list(scratch),
        compiler_params=pltpu.CompilerParams(vmem_limit_bytes=limit * MIB),
        cost_estimate=pl.CostEstimate(
            flops=int(flops), bytes_accessed=int(moved), transcendentals=int(transcendentals)
        ),
    )(*args)


def inverse_rms(values):
    return lax.rsqrt(jnp.mean(values * values, axis=1, keepdims=True) + EPS)


def place(rank, width):
    return pl.ds(pl.multiple_of(rank * width, width), width)


def token_codes(prefix_segment, seq_count, suf_rows):
    items_all = prefix_segment.shape[0] // (IMG + TXT)
    places = jnp.arange(seq_count * suf_rows, dtype=jnp.int32)
    items_of = places // (ACT + 1)
    suffix_seg = jnp.where(items_of < items_all, items_of, items_all)
    suffix_lvl = jnp.where((items_of < items_all) & (places % (ACT + 1) == 0), 1, 2)
    suffix = (suffix_seg * 4 + suffix_lvl).astype(jnp.int32)
    return jnp.concatenate(
        [(prefix_segment * 4).reshape(seq_count, -1), suffix.reshape(seq_count, -1)], axis=1
    )


def front_kernel(t_ref, *refs):
    tp = lax.axis_size("tp")
    xs = refs[:tp]
    w_ref, gp_ref, ga_ref, q_ref, kva_ref, kvb_ref, xp_ref, xa_ref, inv_ref = refs[tp:]
    rp, dp = xp_ref.shape
    ra, da = xa_ref.shape
    cp, ca = dp // tp, da // tp
    kp, ka = dp // w_ref.shape[0], da // w_ref.shape[0]
    width = q_ref.shape[1]
    half = kva_ref.shape[0]
    for k in range(tp):
        xp_ref[:, place(t_ref[0] ^ k, cp)] = xs[k][:rp, :]
        xa_ref[:, place(t_ref[0] ^ k, ca)] = xs[k][rp:, :ca]
    parts = []
    inverses = []
    for x_ref, g_ref, first, last, size in (
        (xp_ref, gp_ref, 0, kp, dp),
        (xa_ref, ga_ref, kp, kp + ka, da),
    ):
        rows = x_ref[...].astype(F32)
        inverse = inverse_rms(rows)
        normed = (rows * inverse * g_ref[...]).astype(BF)
        parts.append(dot(normed, w_ref[:, first:last, :].reshape(size, -1)))
        inverses.append(inverse)
    qkv = jnp.concatenate(parts, axis=0)
    q_ref[...] = qkv[:, :width].astype(BF)
    kva_ref[...] = qkv[:half, width:].astype(BF)
    kvb_ref[...] = qkv[half:, width:].astype(BF)
    inv_ref[...] = jnp.broadcast_to(jnp.concatenate(inverses, axis=0), inv_ref.shape)


def key_step(count):
    for step in (2176, 1088, 544, 272):
        if count % step == 0:
            return step
    return count


def attend_kernel(q_ref, kv_ref, qc_ref, kc_ref, att_ref, mix_ref, lse_ref):
    rows = q_ref.shape[0]
    heads = q_ref.shape[1] // HD
    count = kv_ref.shape[0]
    step = key_step(count)
    code = qc_ref[...]
    low = code - code % 4
    for h in range(heads):
        query = q_ref[:, h * HD : (h + 1) * HD] * BF(HD**-0.5)
        top = jnp.full((rows, 1), NEG, F32)
        mass = jnp.zeros((rows, 1), F32)
        total = jnp.zeros((rows, HD), F32)
        for begin in range(0, count, step):
            keys = kv_ref[begin : begin + step, :HD]
            marks = kc_ref[:, begin : begin + step]
            allowed = (marks >= low) & (marks <= code)
            scores = jnp.where(allowed, dot_t(query, keys), NEG)
            new_top = jnp.maximum(top, jnp.max(scores, axis=1, keepdims=True))
            expo = jnp.where(allowed, jnp.exp(scores - new_top), 0.0)
            shrink = jnp.exp(top - new_top)
            mass = mass * shrink + jnp.sum(expo, axis=1, keepdims=True)
            total = total * shrink + dot(expo.astype(BF), kv_ref[begin : begin + step, HD:])
            top = new_top
        attended = total / mass
        att_ref[:, h * HD : (h + 1) * HD] = attended
        mix_ref[:, h * HD : (h + 1) * HD] = attended.astype(BF)
        lse_ref[:, h * 128 : (h + 1) * 128] = jnp.broadcast_to(top + jnp.log(mass), (rows, 128))


def attend_back_kernel(
    q_ref, kv_ref, qc_ref, kc_ref, att_ref, lse_ref, dm_ref, dq_ref, *dkv_refs
):
    rows = q_ref.shape[0]
    heads = q_ref.shape[1] // HD
    count = kv_ref.shape[0]
    step = key_step(count)
    each = dkv_refs[0].shape[0]
    code = qc_ref[...]
    low = code - code % 4
    dq = [jnp.zeros((rows, HD), F32) for _ in range(heads)]
    for begin in range(0, count, step):
        keys = kv_ref[begin : begin + step, :HD]
        vals = kv_ref[begin : begin + step, HD:]
        marks = kc_ref[:, begin : begin + step]
        allowed = (marks >= low) & (marks <= code)
        dk = jnp.zeros((step, HD), F32)
        dv = jnp.zeros((step, HD), F32)
        for h in range(heads):
            span = slice(h * HD, (h + 1) * HD)
            query = q_ref[:, span] * BF(HD**-0.5)
            dmix = dm_ref[:, span]
            delta = jnp.sum(dmix.astype(F32) * att_ref[:, span], axis=1, keepdims=True)
            scores = dot_t(query, keys)
            probs = jnp.where(allowed, jnp.exp(scores - lse_ref[:, h * 128 : h * 128 + 1]), 0.0)
            dscores = (probs * (dot_t(dmix, vals) - delta)).astype(BF)
            dq[h] = dq[h] + dot(dscores, keys)
            dk = dk + t_dot(dscores, query)
            dv = dv + t_dot(probs.astype(BF), dmix)
        dkv = jnp.concatenate([dk, dv], axis=1).astype(BF)
        for part in range(len(dkv_refs)):
            first, last = max(begin, part * each), min(begin + step, (part + 1) * each)
            if first < last:
                dkv_refs[part][first - part * each : last - part * each, :] = dkv[
                    first - begin : last - begin
                ]
    for h in range(heads):
        dq_ref[:, h * HD : (h + 1) * HD] = (dq[h] * HD**-0.5).astype(BF)


def branch_kernel(t_ref, mix_ref, w_ref, *outs):
    tp = len(outs)
    n = w_ref.shape[0]
    cp = outs[0].shape[1]
    ra = mix_ref.shape[0] - (outs[0].shape[0] - 16)
    rp = mix_ref.shape[0] - ra
    kp = cp * tp // n
    for k in range(tp):
        rank = t_ref[0] ^ k
        blocks = w_ref[pl.ds(rank * (n // tp), n // tp)]
        prefix = dot_t(mix_ref[:rp, :], blocks[:, :kp].reshape(cp, -1))
        action = dot_t(mix_ref[rp:, :], blocks[:, kp:].reshape(-1, mix_ref.shape[1]))
        outs[k][:rp, :] = prefix.astype(BF)
        outs[k][rp:, :] = jnp.concatenate(
            [action, jnp.zeros((ra, cp - action.shape[1]), F32)], axis=1
        ).astype(BF)


def middle_kernel(t_ref, *refs):
    tp = lax.axis_size("tp")
    mids = refs[:tp]
    gp_ref, ga_ref, mp_ref, ma_ref, a_ref, b_ref = refs[tp:]
    rp, dp = mp_ref.shape
    ra, da = ma_ref.shape
    cp, ca = dp // tp, da // tp
    for k in range(tp):
        mp_ref[:, place(t_ref[0] ^ k, cp)] = mids[k][:rp, :]
        ma_ref[:, place(t_ref[0] ^ k, ca)] = mids[k][rp:, :ca]
    rows = mp_ref[...].astype(F32)
    prefix = rows * inverse_rms(rows) * gp_ref[...]
    rows = ma_ref[...].astype(F32)
    action = rows * inverse_rms(rows) * ga_ref[...]
    action = jnp.concatenate([action, jnp.zeros((ra, dp - da), F32)], axis=1)
    for number, out in enumerate((a_ref, b_ref)):
        out[...] = jnp.concatenate(
            [
                prefix[number * (rp // 2) : (number + 1) * (rp // 2)],
                action[number * (ra // 2) : (number + 1) * (ra // 2)],
            ],
            axis=0,
        ).astype(BF)


def gelu_parts(value):
    scale = 0.7978845608028654
    square = value * value
    bent = jnp.tanh(scale * (value + 0.044715 * value * square))
    gelu = 0.5 * value * (1.0 + bent)
    slope = 0.5 * (1.0 + bent) + 0.5 * value * (1.0 - bent * bent) * scale * (
        1.0 + 3.0 * 0.044715 * square
    )
    return gelu, slope


def forward_back(rows, cot_rows, gate_up, down):
    f = down.shape[0]
    both = dot(rows, gate_up)
    gelu, slope = gelu_parts(both[:, :f])
    up = both[:, f:]
    dhidden = dot_t(cot_rows, down)
    return gelu * up, jnp.concatenate([dhidden * up * slope, dhidden * gelu], axis=1)


def feed_kernel(pair, x_ref, c_ref, w_ref, d_ref, act_ref, *refs):
    near_ref = refs[0] if len(refs) == 4 else None
    h_ref, g_ref, dn_ref = refs[-3:]
    rows, dp = x_ref.shape
    each = rows // pair
    prefix = each - act_ref.shape[0] // pair
    hidden, dgate_up = forward_back(x_ref[...], c_ref[...], w_ref[...], d_ref[...])
    inside = lax.broadcasted_iota(jnp.int32, (rows, 1), 0) % each < prefix
    dgate_up = jnp.where(inside, dgate_up, 0.0).astype(BF)
    h_ref[...] = jnp.where(inside, hidden, 0.0).astype(BF)
    g_ref[...] = dgate_up
    dn = dot_t(dgate_up, w_ref[...])
    action = act_ref[...]
    action = jnp.concatenate(
        [action, jnp.zeros((action.shape[0], dp - action.shape[1]), F32)], axis=1
    )
    pieces = []
    for i in range(pair):
        pieces.append(dn[i * each : i * each + prefix])
        pieces.append(action[i * (each - prefix) : (i + 1) * (each - prefix)])
    dn = jnp.concatenate(pieces, axis=0)
    if near_ref is not None:
        dn = dn + near_ref[...].astype(F32)
    dn_ref[...] = dn.astype(BF)


def feed(rows_in, cot_rows, gate_up, down, dn_action, near, each):
    total, dp = rows_in.shape
    pair = 2
    step = pair * each
    f = down.shape[0]
    act_step = dn_action.shape[0] * step // total
    row_spec = pl.BlockSpec((step, dp), lambda i: (i, 0))
    in_specs = [
        row_spec,
        row_spec,
        pl.BlockSpec(gate_up.shape, lambda i: (0, 0)),
        pl.BlockSpec(down.shape, lambda i: (0, 0)),
        pl.BlockSpec((act_step, dn_action.shape[1]), lambda i: (i, 0)),
    ]
    args = [rows_in, cot_rows, gate_up, down, dn_action]
    if near is not None:
        in_specs.append(row_spec)
        args.append(near)
    return pl.pallas_call(
        lambda *refs: feed_kernel(pair, *refs),
        grid=(total // step,),
        in_specs=in_specs,
        out_specs=(
            pl.BlockSpec((step, f), lambda i: (i, 0)),
            pl.BlockSpec((step, 2 * f), lambda i: (i, 0)),
            row_spec,
        ),
        out_shape=(
            jax.ShapeDtypeStruct((total, f), BF),
            jax.ShapeDtypeStruct((total, 2 * f), BF),
            jax.ShapeDtypeStruct((total, dp), BF),
        ),
        compiler_params=pltpu.CompilerParams(vmem_limit_bytes=48 * MIB),
        cost_estimate=pl.CostEstimate(
            flops=10 * total * dp * f,
            bytes_accessed=8 * total * dp + 6 * f * dp,
            transcendentals=total * f,
        ),
    )(*args)


def feed_action_kernel(x_ref, c_ref, w_ref, d_ref, dn_ref, lift_ref, gw_ref, gd_ref):
    rows, cot_rows = x_ref[...], c_ref[...]
    hidden, dgate_up = forward_back(rows, cot_rows, w_ref[...], d_ref[...])
    hidden, dgate_up = hidden.astype(BF), dgate_up.astype(BF)
    dn_ref[...] = dot_t(dgate_up, w_ref[...])
    lift_ref[...] = dot(hidden, d_ref[...])
    gw_ref[...] = t_dot(rows, dgate_up).astype(BF)
    gd_ref[...] = t_dot(hidden, cot_rows).astype(BF)


def weights_kernel(
    xo_ref, xe_ref, co_ref, ce_ref, ho_ref, he_ref, go_ref, ge_ref, act_ref, gw_ref, gd_ref
):
    f = ho_ref.shape[1]
    kp = gd_ref.shape[2]
    gw_ref[...] = (t_dot(xo_ref[...], go_ref[...]) + t_dot(xe_ref[...], ge_ref[...])).astype(BF)
    down = (t_dot(ho_ref[...], co_ref[...]) + t_dot(he_ref[...], ce_ref[...])).astype(BF)
    for i in range(gd_ref.shape[0]):
        gd_ref[i, :f, :] = down[:, i * kp : (i + 1) * kp]
        gd_ref[i, f:, :] = act_ref[i]


def weight_grads(x_odd, x_even, c_odd, c_even, h_odd, h_even, g_odd, g_even, action):
    total, dp = x_odd.shape
    f = h_odd.shape[1]
    n, extra, kp = action.shape
    wide = 256
    cols = pl.BlockSpec((total, wide), lambda i: (0, i))
    h_spec = pl.BlockSpec((total, f), lambda i: (0, 0))
    g_spec = pl.BlockSpec((total, 2 * f), lambda i: (0, 0))
    return pl.pallas_call(
        weights_kernel,
        grid=(dp // wide,),
        in_specs=[
            cols,
            cols,
            cols,
            cols,
            h_spec,
            h_spec,
            g_spec,
            g_spec,
            pl.BlockSpec((wide // kp, extra, kp), lambda i: (i, 0, 0)),
        ],
        out_specs=(
            pl.BlockSpec((wide, 2 * f), lambda i: (i, 0)),
            pl.BlockSpec((wide // kp, f + extra, kp), lambda i: (i, 0, 0)),
        ),
        out_shape=(
            jax.ShapeDtypeStruct((dp, 2 * f), BF),
            jax.ShapeDtypeStruct((n, f + extra, kp), BF),
        ),
        compiler_params=pltpu.CompilerParams(vmem_limit_bytes=48 * MIB),
        cost_estimate=pl.CostEstimate(
            flops=12 * total * dp * f, bytes_accessed=8 * total * dp, transcendentals=0
        ),
    )(x_odd, x_even, c_odd, c_even, h_odd, h_even, g_odd, g_even, action)


def lift_kernel(
    odd_ref, pa_ref, pb_ref, la_ref, lb_ref,
    oa_ref, ea_ref, ob_ref, eb_ref, aa_ref, ab_ref, d_ref, out_ref,
):
    odd = odd_ref[pl.program_id(0)] == 1
    dp = out_ref.shape[2]
    prefix = oa_ref.shape[0] - aa_ref.shape[0]
    outs = []
    for o_ref, e_ref in ((oa_ref, ea_ref), (ob_ref, eb_ref)):
        hidden = jnp.where(odd, o_ref[...].astype(F32), e_ref[...].astype(F32)).astype(BF)
        outs.append(dot(hidden, d_ref[...])[:prefix])
    action = jnp.concatenate([aa_ref[...], ab_ref[...]], axis=0)
    action = jnp.concatenate(
        [action, jnp.zeros((action.shape[0], dp - action.shape[1]), F32)], axis=1
    )
    out_ref[0] = jnp.concatenate(outs + [action], axis=0).astype(BF)


def lift(odd, place_a, place_b, lift_a, lift_b, h_odd, h_even, lifted_action, down, each, ra):
    n = odd.shape[0]
    f, dp = down.shape
    da = lifted_action.shape[1]
    a_spec = pl.BlockSpec((each, f), lambda j, o, a, b, la, lb: (a[j], 0))
    b_spec = pl.BlockSpec((each, f), lambda j, o, a, b, la, lb: (b[j], 0))
    rows = 2 * each
    return pl.pallas_call(
        lift_kernel,
        grid_spec=pltpu.PrefetchScalarGridSpec(
            num_scalar_prefetch=5,
            grid=(n,),
            in_specs=[
                a_spec,
                a_spec,
                b_spec,
                b_spec,
                pl.BlockSpec((ra // 2, da), lambda j, o, a, b, la, lb: (la[j], 0)),
                pl.BlockSpec((ra // 2, da), lambda j, o, a, b, la, lb: (lb[j], 0)),
                pl.BlockSpec((f, dp), lambda j, o, a, b, la, lb: (0, 0)),
            ],
            out_specs=pl.BlockSpec((1, rows, dp), lambda j, o, a, b, la, lb: (j, 0, 0)),
        ),
        out_shape=jax.ShapeDtypeStruct((n, rows, dp), BF),
        compiler_params=pltpu.CompilerParams(vmem_limit_bytes=32 * MIB),
        cost_estimate=pl.CostEstimate(
            flops=2 * n * rows * dp * f, bytes_accessed=2 * n * rows * dp, transcendentals=0
        ),
    )(odd, place_a, place_b, lift_a, lift_b, h_odd, h_even, h_odd, h_even,
      lifted_action, lifted_action, down)


def pieces_kernel(t_ref, ka_ref, ga_ref, kb_ref, gb_ref, *outs):
    tp = len(outs)
    each, dp = ka_ref.shape
    cp = dp // tp
    rp = outs[0].shape[0] * 2 * each // (2 * each)
    extra = 8
    prefix = each - extra
    ca = outs[0].shape[1] // 2
    del rp
    for k in range(tp):
        rank = t_ref[0] ^ k
        tops, ends = [], []
        for keep, got in ((ka_ref, ga_ref), (kb_ref, gb_ref)):
            wide = place(rank, cp)
            tops.append(keep[:prefix, wide].astype(F32) + got[:prefix, wide].astype(F32))
            slim = place(rank, ca)
            ends.append(
                keep[prefix:, slim].astype(F32) + got[prefix:, slim].astype(F32)
            )
        action = jnp.concatenate(ends, axis=0)
        action = jnp.concatenate(
            [action, jnp.zeros((action.shape[0], cp - ca), F32)], axis=1
        )
        outs[k][...] = jnp.concatenate(tops + [action], axis=0).astype(BF)


def middle_back_kernel(t_ref, *refs):
    tp = lax.axis_size("tp")
    ds = refs[:tp]
    mp_ref, ma_ref, gp_ref, ga_ref, cp_ref, ca_ref, w_ref = refs[tp : tp + 7]
    bp_ref, ba_ref, own_ref, lp_ref, la_ref, dm_ref, dp_scr, da_scr, rp_scr, ra_scr = refs[tp + 7 :]
    rp, dp = mp_ref.shape
    ra, da = ma_ref.shape
    cp, ca = dp // tp, da // tp
    n = w_ref.shape[0]
    kp = dp // n
    t = t_ref[0]
    for k in range(tp):
        dp_scr[:, place(t ^ k, cp)] = ds[k][:rp, :]
        da_scr[:, place(t ^ k, ca)] = ds[k][rp:, :ca]
    mixes = []
    for d_ref, m_ref, g_ref, c_ref, b_ref, r_ref, l_ref, first, last in (
        (dp_scr, mp_ref, gp_ref, cp_ref, bp_ref, rp_scr, lp_ref, 0, kp),
        (da_scr, ma_ref, ga_ref, ca_ref, ba_ref, ra_scr, la_ref, kp, w_ref.shape[1]),
    ):
        gradient = d_ref[...].astype(F32)
        rows = m_ref[...].astype(F32)
        inverse = inverse_rms(rows)
        centered = rows * inverse
        inner = gradient * g_ref[...]
        dresid = c_ref[...].astype(F32) + inverse * (
            inner - centered * jnp.mean(inner * centered, axis=1, keepdims=True)
        )
        l_ref[...] = jnp.sum(gradient * centered, axis=0, keepdims=True)
        r_ref[...] = dresid
        branch = dresid.astype(BF)
        b_ref[...] = branch
        mixes.append(dot(branch, w_ref[:, first:last, :].reshape(rows.shape[1], -1)))
    dm_ref[...] = jnp.concatenate(mixes, axis=0).astype(BF)
    own_ref[:rp, :] = rp_scr[:, place(t, cp)]
    own_ref[rp:, :] = jnp.concatenate(
        [ra_scr[:, place(t, ca)], jnp.zeros((ra, cp - ca), F32)], axis=1
    )


def out_grad_kernel(bp_ref, ba_ref, mix_ref, out_ref):
    rp, dp = bp_ref.shape
    n = out_ref.shape[0]
    kp = dp // n
    width = mix_ref.shape[1]
    out_ref[:, :kp, :] = t_dot(bp_ref[...], mix_ref[:rp, :]).astype(BF).reshape(n, kp, width)
    out_ref[:, kp:, :] = t_dot(ba_ref[...], mix_ref[rp:, :]).astype(BF).reshape(n, -1, width)


def front_back_kernel(heads_width, s_ref, t_ref, dq_ref, *refs):
    tp = lax.axis_size("tp")
    n = lax.axis_size("seq")
    (ka_ref, ra_ref, kb_ref, rb_ref, xp_ref, xa_ref, inv_ref, gp_ref, ga_ref, w_ref, lp_ref,
     la_ref) = refs[:12]
    groups = refs[12:16]
    pieces = refs[16 : 16 + tp]
    gwp_scr, gwa_scr, gain_scr, dp_scr, da_scr = refs[16 + tp :]
    rp, dp = xp_ref.shape
    ra, da = xa_ref.shape
    kp, ka = dp // n, da // n
    cp, ca = dp // tp, da // tp
    width = heads_width
    dkv = jnp.concatenate(
        [
            ka_ref[...].astype(F32) + ra_ref[...].astype(F32),
            kb_ref[...].astype(F32) + rb_ref[...].astype(F32),
        ],
        axis=0,
    )
    dqkv = jnp.concatenate([dq_ref[...].astype(F32), dkv], axis=1)
    gain_scr[...] = jnp.zeros(gain_scr.shape, F32)
    dots = []
    for x_ref, g_ref, d_scr, gw_scr, l_ref, begin, end, first, last, size, at in (
        (xp_ref, gp_ref, dp_scr, gwp_scr, lp_ref, 0, rp, 0, kp, kp, 0),
        (xa_ref, ga_ref, da_scr, gwa_scr, la_ref, rp, rp + ra, kp, kp + ka, ka, 256),
    ):
        grad_rows = dqkv[begin:end].astype(BF)
        centered = x_ref[...].astype(F32) * inv_ref[begin:end, :1]
        normed = (centered * g_ref[...]).astype(BF)
        gw_scr[...] = t_dot(normed, grad_rows).astype(BF)
        weights = w_ref[:, first:last, :].reshape(x_ref.shape[1], -1)
        partial = dot_t(grad_rows, weights)
        d_scr[...] = partial
        product = partial * centered
        gains = jnp.sum(product, axis=0, keepdims=True)
        mlp_gains = l_ref[...]
        for d in range(n):
            gain_scr[d, 0:1, at : at + size] = gains[:, d * size : (d + 1) * size]
            gain_scr[d, 0:1, at + 512 : at + 512 + size] = mlp_gains[
                :, d * size : (d + 1) * size
            ]
        dots.append(jnp.sum(product * g_ref[...], axis=1, keepdims=True))
    column = jnp.concatenate(dots, axis=0)
    lanes = lax.broadcasted_iota(jnp.int32, (rp + ra, cp), 1)
    rows = lax.broadcasted_iota(jnp.int32, (rp + ra, cp), 0)
    row = jnp.sum(jnp.where(lanes == rows, column, 0.0), axis=0, keepdims=True)
    high = row.astype(BF).astype(F32)
    tail = jnp.concatenate([high, row - high, jnp.zeros((6, cp), F32)], axis=0)
    for k in range(tp):
        rank = t_ref[0] ^ k
        action = jnp.concatenate(
            [da_scr[:, place(rank, ca)], jnp.zeros((ra, cp - ca), F32)], axis=1
        )
        pieces[k][...] = jnp.concatenate([dp_scr[:, place(rank, cp)], action, tail], axis=0).astype(
            BF
        )
    for odd in range(2):
        for number in range(2):
            out = groups[2 * odd + number]
            for i, k in enumerate(block_order(number)):
                d = s_ref[0] ^ (k ^ odd)
                hp, ha = kp // 2, ka // 2
                out[i, :hp, :] = gwp_scr[
                    pl.ds(pl.multiple_of(d * kp + number * hp, hp), hp), :
                ]
                out[i, hp : hp + ha, :] = gwa_scr[
                    pl.ds(pl.multiple_of(d * ka + number * ha, ha), ha), :
                ]
                out[i, hp + ha :, :] = gain_scr[d].astype(BF) * BF(1 - number)


def grad_x_kernel(t_ref, *refs):
    tp = lax.axis_size("tp")
    ds = refs[:tp]
    x_ref, inv_ref, gp_ref, ga_ref, r_ref, op_ref, oa_ref = refs[tp:]
    rp, cp = op_ref.shape
    ra, ca = oa_ref.shape
    t = t_ref[0]
    total = ds[0][...].astype(F32)
    for k in range(1, tp):
        total = total + ds[k][...].astype(F32)
    row = total[rp + ra : rp + ra + 1] + total[rp + ra + 1 : rp + ra + 2]
    lanes = lax.broadcasted_iota(jnp.int32, (rp + ra, cp), 1)
    rows = lax.broadcasted_iota(jnp.int32, (rp + ra, cp), 0)
    column = jnp.sum(jnp.where(lanes == rows, row, 0.0), axis=1, keepdims=True)
    for o_ref, g_ref, begin, end, wide in (
        (op_ref, gp_ref, 0, rp, cp),
        (oa_ref, ga_ref, rp, rp + ra, ca),
    ):
        inverse = inv_ref[begin:end, :1]
        centered = x_ref[begin:end, :wide].astype(F32) * inverse
        mean = column[begin:end] / (wide * tp)
        moved = inverse * (
            total[begin:end, :wide] * g_ref[:, place(t, wide)] - centered * mean
        )
        o_ref[...] = (r_ref[begin:end, :wide] + moved).astype(BF)


def home_kernel(in_ref, gate_ref, up_ref):
    f = gate_ref.shape[1]
    gate_ref[...] = in_ref[0, :, :f].astype(F32)
    up_ref[...] = in_ref[0, :, f:].astype(F32)


def home(got):
    n, kp, both = got.shape
    f = both // 2
    out = pl.BlockSpec((kp, f), lambda j: (0, j))
    return pl.pallas_call(
        home_kernel,
        grid=(n,),
        in_specs=[pl.BlockSpec((1, kp, both), lambda j: (j, 0, 0))],
        out_specs=(out, out),
        out_shape=(jax.ShapeDtypeStruct((kp, n * f), F32),) * 2,
        cost_estimate=pl.CostEstimate(
            flops=0, bytes_accessed=6 * n * kp * both, transcendentals=0
        ),
    )(got)


def shards(
    x_prefix,
    x_action,
    prefix_segment,
    prefix_attn_gain,
    prefix_query,
    prefix_key,
    prefix_value,
    prefix_out,
    prefix_mlp_gain,
    prefix_gate,
    prefix_up,
    prefix_down,
    action_attn_gain,
    action_query,
    action_key,
    action_value,
    action_out,
    action_mlp_gain,
    action_gate,
    action_up,
    action_down,
    cot_prefix,
    cot_action,
):
    n = lax.axis_size("seq")
    tp = lax.axis_size("tp")
    s = lax.axis_index("seq")
    t = lax.axis_index("tp")
    rank_t = t.astype(jnp.int32).reshape(1)
    rank_s = s.astype(jnp.int32).reshape(1)
    rp, cp = x_prefix.shape
    ra, ca = x_action.shape
    rows = rp + ra
    half = rows // 2
    dp, da = cp * tp, ca * tp
    kp, ka = dp // n, da // n
    width = prefix_query.shape[1]
    qkv_width = width + 2 * HD
    fp, fa = prefix_gate.shape[1] // n, action_gate.shape[1] // n

    x_pack = jnp.concatenate(
        [x_prefix, jnp.pad(x_action, ((0, 0), (0, cp - ca)))], axis=0
    )
    x_pieces = gather_tp(x_pack)
    gains = jnp.concatenate(
        [prefix_attn_gain, prefix_mlp_gain, action_attn_gain, action_mlp_gain]
    )
    gain_rows = -(-gains.shape[0] // qkv_width)
    gains = jnp.pad(gains, (0, 8 * qkv_width - gains.shape[0])).reshape(8, qkv_width)
    pack_qkv = jnp.concatenate(
        [
            jnp.concatenate([prefix_query, prefix_key, prefix_value], axis=1),
            jnp.concatenate([action_query, action_key, action_value], axis=1),
            gains,
        ],
        axis=0,
    )
    got_qkv = lax.all_gather(pack_qkv, "seq", axis=0)
    got_gains = got_qkv[:, kp + ka : kp + ka + gain_rows].reshape(n, -1).astype(F32)
    attn_gain_p = got_gains[:, :kp].reshape(1, dp)
    mlp_gain_p = got_gains[:, kp : 2 * kp].reshape(1, dp)
    attn_gain_a = got_gains[:, 2 * kp : 2 * kp + ka].reshape(1, da)
    mlp_gain_a = got_gains[:, 2 * kp + ka : 2 * kp + 2 * ka].reshape(1, da)
    pack_out = jnp.concatenate([prefix_out.T, action_out.T], axis=0)
    cot_wide = jnp.pad(cot_action, ((0, 0), (0, dp - da)))
    cot_odd, cot_even = gather_rows(
        [
            jnp.concatenate(
                [
                    cot_prefix[i * (rp // 2) : (i + 1) * (rp // 2)],
                    cot_wide[i * (ra // 2) : (i + 1) * (ra // 2)],
                ],
                axis=0,
            )
            for i in range(2)
        ]
    )

    def by_units(w, f):
        return w.reshape(w.shape[0], n, f).transpose(1, 0, 2)

    gate_up_sent = jnp.concatenate([by_units(prefix_gate, fp), by_units(prefix_up, fp)], axis=2)
    action_sent = jnp.concatenate(
        [
            by_units(action_gate, fa),
            by_units(action_up, fa),
            action_down.reshape(n, fa, ka).transpose(0, 2, 1),
        ],
        axis=2,
    ).reshape(n, -1, kp)
    extra = action_sent.shape[1]
    down_sent = jnp.concatenate([prefix_down.reshape(n, fp, kp), action_sent], axis=1)

    queries, kv_a, kv_b, x_full_p, x_full_a, inverse1 = whole_call(
        front_kernel,
        (
            ((rows, width), BF),
            ((half, 2 * HD), BF),
            ((half, 2 * HD), BF),
            ((rp, dp), BF),
            ((ra, da), BF),
            ((rows, 128), F32),
        ),
        [rank_t, *x_pieces, got_qkv, attn_gain_p, attn_gain_a],
        2 * rp * dp * qkv_width,
    )
    kv_even = [jnp.concatenate(blocks, axis=0) for blocks in gather_far([kv_a, kv_b])]
    kv_odd = [swap(e, "seq", 1) for e in kv_even]
    keys_values = jnp.concatenate([kv_even[0], kv_odd[0], kv_even[1], kv_odd[1]], axis=0)
    codes = token_codes(prefix_segment, n, ra)
    query_code = lax.dynamic_slice_in_dim(codes, s, 1, 0).reshape(rows, 1)
    key_code = jnp.concatenate(
        [
            lax.dynamic_slice(codes, (s ^ k ^ odd, number * half), (1, half))
            for number in range(2)
            for odd in range(2)
            for k in block_order(number)
        ],
        axis=1,
    )
    attended, mixed, log_sum = whole_call(
        attend_kernel,
        (
            ((rows, width), F32),
            ((rows, width), BF),
            ((rows, width // HD * 128), F32),
        ),
        [queries, keys_values, query_code, key_code],
        4 * rows * width * n * rows,
        transcendentals=rows * width // HD * n * rows,
    )
    got_out = lax.all_gather(after(pack_out, queries), "seq", axis=0)
    gate_up_sent, down_sent = after((gate_up_sent, down_sent), keys_values)
    gate_up = lax.all_to_all(gate_up_sent, "seq", 0, 0).reshape(dp, 2 * fp)
    down_got = lax.all_to_all(down_sent, "seq", 0, 0)

    piece = (((rows, cp), BF),)
    branch = sum_tp(
        whole_call(
            branch_kernel, piece * tp, [rank_t, mixed, got_out], 2 * rows * dp * width
        )
    )
    residual = x_pack.astype(F32) + branch
    block = (((half, dp), BF),)
    mid_p, mid_a, normed_a, normed_b = whole_call(
        middle_kernel,
        (((rp, dp), BF), ((ra, da), BF)) + block * 2,
        [rank_t, *gather_tp(residual.astype(BF)), mlp_gain_p, mlp_gain_a],
        rp * dp,
    )

    normed_odd, normed_even = gather_rows([normed_a, normed_b])
    down = down_got[:, :fp].transpose(1, 0, 2).reshape(fp, dp)
    action_got = down_got[:, fp:].reshape(da, 3 * fa)
    gate_up_action = action_got[:, : 2 * fa]
    down_action = action_got[:, 2 * fa :].T

    def action_rows(blocks):
        return blocks.reshape(n, half, dp)[:, rp // 2 :, :da].reshape(-1, da)

    normed_action = jnp.concatenate([action_rows(normed_odd), action_rows(normed_even)], axis=0)
    cot_action_all = jnp.concatenate([action_rows(cot_odd), action_rows(cot_even)], axis=0)
    tokens = n * ra
    dn_action, lifted_action, grad_gu_action, grad_down_action = whole_call(
        feed_action_kernel,
        (
            ((tokens, da), F32),
            ((tokens, da), F32),
            ((da, 2 * fa), BF),
            ((fa, da), BF),
        ),
        [normed_action, cot_action_all, gate_up_action, down_action],
        18 * tokens * da * fa,
    )
    h_odd, g_odd, dn_odd = feed(
        normed_odd, cot_odd, gate_up, down, dn_action[: tokens // 2], None, half
    )
    h_even, g_even, dn_even = feed(
        normed_even,
        cot_even,
        gate_up,
        down,
        dn_action[tokens // 2 :],
        swap(dn_odd, "seq", 1),
        half,
    )
    dn_blocks = dn_even.reshape(2, n // 2, half, dp)
    (keep_a, got_a), (keep_b, got_b) = scatter_far([dn_blocks[0], dn_blocks[1]])
    dn_own = sum_tp(
        whole_call(
            pieces_kernel, piece * tp, [rank_t, keep_a, got_a, keep_b, got_b], rp * dp
        )
    )
    dn_pieces = gather_tp(dn_own.astype(BF))

    action_grads = jnp.concatenate(
        [
            grad_gu_action.reshape(n, ka, 2 * fa),
            grad_down_action.reshape(fa, n, ka).transpose(1, 2, 0),
        ],
        axis=2,
    ).reshape(n, extra, kp)
    grad_gu, grad_down = weight_grads(
        normed_odd, normed_even, cot_odd, cot_even, h_odd, h_even, g_odd, g_even, action_grads
    )
    ranks = s ^ jnp.arange(n, dtype=jnp.int32)
    odd_bits = ranks & 1
    places = []
    for number in range(2):
        table = [0] * n
        for i, k in enumerate(block_order(number)):
            table[k] = table[k ^ 1] = number * (n // 2) + i
        places.append(jnp.array(table, jnp.int32)[ranks])
    lift_places = [p + (1 - odd_bits) * n for p in places]
    lifted = lift(
        odd_bits, *places, *lift_places, h_odd, h_even, lifted_action, down, half, ra
    )
    lifted_home = lax.psum_scatter(after(lifted, got_a), "seq", scatter_dimension=0)
    grad_gu, grad_down = after((grad_gu, grad_down), got_a)
    grad_gu_home = lax.all_to_all(grad_gu.reshape(n, kp, 2 * fp), "seq", 0, 0)
    grad_down_home = lax.all_to_all(grad_down, "seq", 0, 0)

    row = ((1, dp), F32)
    row_a = ((1, da), F32)
    dbranch_p, dbranch_a, dresid, mlp_gains_p, mlp_gains_a, dmixed = whole_call(
        middle_back_kernel,
        (((rp, dp), BF), ((ra, da), BF), ((rows, cp), F32), row, row_a, ((rows, width), BF)),
        [rank_t, *dn_pieces, mid_p, mid_a, mlp_gain_p, mlp_gain_a, cot_prefix, cot_action, got_out],
        2 * rows * dp * width,
        scratch=(
            pltpu.VMEM((rp, dp), BF),
            pltpu.VMEM((ra, da), BF),
            pltpu.VMEM((rp, dp), F32),
            pltpu.VMEM((ra, da), F32),
        ),
    )
    dquery, *dkv_parts = whole_call(
        attend_back_kernel,
        (((rows, width), BF),) + (((n * rows // 4, 2 * HD), BF),) * 4,
        [queries, keys_values, query_code, key_code, attended, log_sum, dmixed],
        10 * rows * width * n * rows,
        limit=56,
        transcendentals=rows * width // HD * n * rows,
    )
    dkv_even = [
        (e.astype(F32) + swap(o, "seq", 1).astype(F32)).astype(BF).reshape(n // 2, half, 2 * HD)
        for e, o in ((dkv_parts[0], dkv_parts[1]), (dkv_parts[2], dkv_parts[3]))
    ]
    dkv = [part for pair in scatter_far(dkv_even) for part in pair]
    (out_grads,) = whole_call(
        out_grad_kernel,
        (((n, kp + ka, width), BF),),
        [dbranch_p, dbranch_a, mixed],
        2 * rows * dp * width,
    )
    out_home = lax.psum_scatter(out_grads, "seq", scatter_dimension=0).astype(F32)
    tall = (kp + ka) // 2 + 8
    *groups_and_pieces, = whole_call(
        lambda *refs: front_back_kernel(width, *refs),
        (((n // 2, tall, qkv_width), BF),) * 4 + (((rows + 8, cp), BF),) * tp,
        [
            rank_s, rank_t, dquery, *dkv, x_full_p, x_full_a, inverse1, attn_gain_p, attn_gain_a,
            got_qkv, mlp_gains_p, mlp_gains_a,
        ],
        4 * rows * dp * qkv_width,
        scratch=(
            pltpu.VMEM((dp, qkv_width), BF),
            pltpu.VMEM((da, qkv_width), BF),
            pltpu.VMEM((n, 8, qkv_width), F32),
            pltpu.VMEM((rp, dp), F32),
            pltpu.VMEM((ra, da), F32),
        ),
    )
    groups, pieces = groups_and_pieces[:4], groups_and_pieces[4:]
    grad_x_p, grad_x_a = whole_call(
        grad_x_kernel,
        (((rp, cp), BF), ((ra, ca), BF)),
        [
            rank_t, pieces[0], *[swap(pieces[k], "tp", k) for k in range(1, tp)], x_pack,
            inverse1, attn_gain_p, attn_gain_a, dresid,
        ],
        rp * dp,
    )
    group_even = [
        (e.astype(F32) + swap(o, "seq", 1).astype(F32)).astype(BF)
        for e, o in ((groups[2 * 0], groups[2]), (groups[1], groups[3]))
    ]
    qkv_a, qkv_b = [
        keep.astype(F32) + got.astype(F32) for keep, got in scatter_far(group_even)
    ]
    hp, ha = kp // 2, ka // 2
    qkv_home_p = jnp.concatenate([qkv_a[:hp], qkv_b[:hp]], axis=0)
    qkv_home_a = jnp.concatenate([qkv_a[hp : hp + ha], qkv_b[hp : hp + ha]], axis=0)
    gains_home = qkv_a[hp + ha :]
    qp, qa = kp // tp, ka // tp
    attn_gains = jnp.pad(gains_home[:1, :512], ((0, 7), (0, 0)))

    def shared_piece(rank):
        return jnp.concatenate(
            [
                lax.dynamic_slice_in_dim(qkv_home_p[:, width:], rank * qp, qp, 0),
                lax.dynamic_slice_in_dim(qkv_home_a[:, width:], rank * qa, qa, 0),
                attn_gains,
            ],
            axis=0,
        )

    shared_home = sum_tp([shared_piece(t ^ k) for k in range(tp)])
    attn_gains_home = shared_home[qp + qa]

    def own_piece(rank):
        return jnp.concatenate(
            [
                lax.dynamic_slice(lifted_home, (0, rank * cp), (rp, cp)),
                jnp.pad(
                    lax.dynamic_slice(lifted_home, (rp, rank * ca), (ra, ca)),
                    ((0, 0), (0, cp - ca)),
                ),
            ],
            axis=0,
        )

    output = (residual + sum_tp([own_piece(t ^ k) for k in range(tp)])).astype(BF)
    grad_gate_p, grad_up_p = home(grad_gu_home)
    grad_down_p = grad_down_home[:, :fp].astype(F32).reshape(n * fp, kp)
    action_home = grad_down_home[:, fp:].reshape(n, ka, 3 * fa).astype(F32)

    def units(part):
        return part.transpose(1, 0, 2).reshape(ka, n * fa)

    grad_gate_a = units(action_home[:, :, :fa])
    grad_up_a = units(action_home[:, :, fa : 2 * fa])
    grad_down_a = action_home[:, :, 2 * fa :].transpose(0, 2, 1).reshape(n * fa, ka)
    return (
        output[:rp],
        output[rp:, :ca],
        grad_x_p,
        grad_x_a,
        attn_gains_home[:kp],
        qkv_home_p[:, :width],
        shared_home[:qp, :HD],
        shared_home[:qp, HD:],
        out_home[:kp].T,
        gains_home[0, 512 : 512 + kp],
        grad_gate_p,
        grad_up_p,
        grad_down_p,
        attn_gains_home[256 : 256 + ka],
        qkv_home_a[:, :width],
        shared_home[qp : qp + qa, :HD],
        shared_home[qp : qp + qa, HD:],
        out_home[kp:].T,
        gains_home[0, 768 : 768 + ka],
        grad_gate_a,
        grad_up_a,
        grad_down_a,
    )


def solution(mesh):
    split = P("seq", "tp")
    turned = P("tp", "seq")
    both = P(("seq", "tp"), None)
    one = P("seq")
    rows = P("seq", None)
    stream_in = (one, split, rows, rows, turned, one, split, split, turned)
    stream_out = (one, split, both, both, turned, one, split, split, turned)
    return jax.shard_map(
        shards,
        mesh=mesh,
        in_specs=(split, split, P()) + stream_in + stream_in + (rows, rows),
        out_specs=(split, split, split, split) + stream_out + stream_out,
        check_vma=False,
    )
```

time: 952 us -> 767 us (0.81)
  local copies, waits for them, and re-layouts: 234 us -> 90.8 us
  matrix products: 103 us -> 0 us
  other arithmetic: 134 us -> 32.3 us
  Pallas kernels: 12 us -> 110 us
  waiting for transfers between devices: 354 us -> 398 us
  starting transfers between devices: 87.8 us -> 112 us
    dot_general x30 -> x0, matrix products: 103 us -> none  [the longest x10 46 us: dot_t(): lax.dot_general(left, right, (((1,), (1,)), ((), ())), preferred_element_...]
    pallas_call x2 -> x16, Pallas kernels: 12 us -> 110 us  [the longest x11 38.1 us: whole_call(): pl.pallas_call(kernel, out_shape=outs, in_specs=specs, out_specs=tuple((p...]
    convert_element_type x44 -> x7, local copies, waits for them, and re-layouts: 45.5 us -> 2.92 us  [the longest x1 2.64 us: shards(): action_home = grad_down_home[:, fp:].reshape(n, ka, 3 * fa).astype(F32)]
    all_gather x1, waiting for transfers between devices: 0.01 us -> 42.4 us  [shards(): got_qkv = lax.all_gather(pack_qkv, 'seq', axis=0)]
    dynamic_update_slice x61 -> x0, local copies, waits for them, and re-layouts: 41.2 us -> none  [the longest x20 18 us: shards(): lax.dynamic_update_slice(home_prefix[i], piece[:kp, i * fp:(i + 1) * fp]....]
    all_to_all x0 -> x4, waiting for transfers between devices: none -> 38.9 us  [the longest x1 38.9 us: shards(): gate_up = lax.all_to_all(gate_up_sent, 'seq', 0, 0).reshape(dp, 2 * fp)]
    ppermute x74 -> x63, waiting for transfers between devices: 354 us -> 316 us  [swap(): return lax.ppermute(value, axis, [(i, i ^ mask) for i in range(count)])]
    convert_element_type x32 -> x8, other arithmetic: 41.4 us -> 8.77 us  [the longest x4 4.56 us: shards(): (e.astype(F32) + swap(o, 'seq', 1).astype(F32)).astype(BF)]
  transfers between devices with their start and end apart: 78 -> 71, of which waited for: 32 -> 34; matrix products, arithmetic and copies ran while one was open for 37% -> 11% of each run, Pallas kernels for 0% -> 8%
where the time goes in v2:
time: 767 us; the launch traced here: 758 us
  waiting for transfers between devices  398 us (52%)
  starting transfers between devices  112 us (15%)
  Pallas kernels  110 us (14%)
  local copies, waits for them, and re-layouts  90.8 us (12%)
  other arithmetic  32.3 us (4%)
  between operations  15.5 us (2%)
    ppermute x63, waiting for transfers between devices, swap(): return lax.ppermute(value, axis, [(i, i ^ mask) for i in range(count)])  316 us
    ppermute x63, starting transfers between devices, swap(): return lax.ppermute(value, axis, [(i, i ^ mask) for i in range(count)])  93.4 us
    unnamed x206, local copies, waits for them, and re-layouts  45.4 us
    all_gather x1, waiting for transfers between devices, shards(): got_qkv = lax.all_gather(pack_qkv, 'seq', axis=0)  42.4 us
    all_to_all x1, waiting for transfers between devices, shards(): gate_up = lax.all_to_all(gate_up_sent, 'seq', 0, 0).reshape(dp, 2 * fp)  38.9 us
    pallas_call x11, Pallas kernels, whole_call(): pl.pallas_call(kernel, out_shape=outs, in_specs=specs, out_specs=tuple((p...  38.1 us
    pallas_call x2, Pallas kernels, feed(): pl.pallas_call(lambda *refs: feed_kernel(pair, *refs), grid=(total // ste...  36.3 us
    pallas_call x1, Pallas kernels, weight_grads(): pl.pallas_call(weights_kernel, grid=(dp // wide,), in_specs=[cols, cols,...  21.3 us
  transfers between devices with their start and end apart: 71, of which 34 were waited for; matrix products, arithmetic and copies ran while one was open for 11% of the time, Pallas kernels for 8%

profile of v2, /device:TPU:0, one launch (start us, length us, event | category | flops | bytes accessed | tf_op | source)
XLA Modules:
  0.0 758.4 jit_solution(14136385695771570646)
XLA Ops:
  16.9 42.4 %all-gather.5.cloned.1.call-done = bf16[3136,1024]{1,0:T(8,128)(2,1)} async-done(((bf16[392,1024]{1,0:T(8,128)(2,1)}), bf16[3136,1024]{1,0:T(8,128)(2,1)}) %all-gather.5.cloned.1.call-update) | async-done | bytes 6422544 | tf_op jit(solution)/shard_map/all_gather | solution.py:731
  61.5 4.8 shard_map.408
  74.1 4.9 bitcast_bitcast_fusion
  79.9 8.9 %collective-permute-done.24 = bf16[136,2048]{1,0:T(8,128)(2,1)S(1)} collective-permute-done((bf16[136,2048]{1,0:T(8,128)(2,1)S(1)}, bf16[136,2048]{1,0:T(8,128)(2,1)S(1)}, u32[]{:S(2)}, u32[]{:S(2)}) %collective-permute-start.24) | collective-permute-done | bytes 557088 | tf_op jit(solution)/shard_map/ppermute | solution.py:21
  93.1 18.4 %collective-permute-done.26 = bf16[136,2048]{1,0:T(8,128)(2,1)} collective-permute-done((bf16[136,2048]{1,0:T(8,128)(2,1)S(1)}, bf16[136,2048]{1,0:T(8,128)(2,1)}, u32[]{:S(2)}, u32[]{:S(2)}) %collective-permute-start.26) | collective-permute-done | bytes 557088 | tf_op jit(solution)/shard_map/ppermute | solution.py:21
  126.5 3.8 collective-permute-done.9
  132.5 3.8 shard_map.409
  139.9 3.5 copy.61
  159.6 9.8 %collective-permute-done.12 = bf16[272,512]{1,0:T(8,128)(2,1)S(1)} collective-permute-done((bf16[272,512]{1,0:T(8,128)(2,1)S(1)}, bf16[272,512]{1,0:T(8,128)(2,1)S(1)}, u32[]{:S(2)}, u32[]{:S(2)}) %collective-permute-start.12) | collective-permute-done | bytes 278560 | tf_op jit(solution)/shard_map/ppermute | solution.py:21
  169.7 5.5 collective-permute-start.14
  179.5 3.4 pad_maximum_fusion.1
  185.8 11.8 %collective-permute-done.15.refs_2_ = bf16[272,512]{1,0:T(8,128)(2,1)S(1)} collective-permute-done((bf16[272,512]{1,0:T(8,128)(2,1)S(1)}, bf16[272,512]{1,0:T(8,128)(2,1)S(1)}, u32[]{:S(2)}, u32[]{:S(2)}) %collective-permute-start.15) | collective-permute-done | bytes 278560 | tf_op jit(solution)/shard_map/ppermute | solution.py:21
  207.1 4.4 all-to-all-start.1
  217.8 8.6 %collective-permute-start.22 = (bf16[136,2048]{1,0:T(8,128)(2,1)S(1)}, bf16[136,2048]{1,0:T(8,128)(2,1)S(1)}, u32[]{:S(2)}, u32[]{:S(2)}) collective-permute-start(bf16[136,2048]{1,0:T(8,128)(2,1)S(1)} %collective-permute-done.20), channel_id=1, source_target_pairs={{0,8},{4,12},{8,0},{12,4},{16,24},{20,28},{24,16},{28,20},{1,9},{5... | collective-permute-start | bytes 1671176 | tf_op jit(solution)/shard_map/ppermute | solution.py:21
  227.2 10.2 %collective-permute-done.18 = bf16[136,2048]{1,0:T(8,128)(2,1)S(1)} collective-permute-done((bf16[136,2048]{1,0:T(8,128)(2,1)S(1)}, bf16[136,2048]{1,0:T(8,128)(2,1)S(1)}, u32[]{:S(2)}, u32[]{:S(2)}) %collective-permute-start.18) | collective-permute-done | bytes 557088 | tf_op jit(solution)/shard_map/ppermute | solution.py:21
  238.3 28.6 %collective-permute-done.19 = bf16[136,2048]{1,0:T(8,128)(2,1)S(1)} collective-permute-done((bf16[136,2048]{1,0:T(8,128)(2,1)S(1)}, bf16[136,2048]{1,0:T(8,128)(2,1)S(1)}, u32[]{:S(2)}, u32[]{:S(2)}) %collective-permute-start.19) | collective-permute-done | bytes 557088 | tf_op jit(solution)/shard_map/ppermute | solution.py:21
  271.3 4.6 all-to-all-start
  286.0 38.9 %all-to-all-done = bf16[8,256,1024]{2,1,0:T(8,128)(2,1)} async-done(((bf16[8,256,1024]{2,1,0:T(8,128)(2,1)}), bf16[8,256,1024]{2,1,0:T(8,128)(2,1)}, u32[]{:S(2)}, u32[]{:S(2)}) %all-to-all-start) | async-done | bytes 4194336 | tf_op jit(solution)/shard_map/all_to_all | solution.py:807
  325.0 17.8 %shard_map.413 = (bf16[1088,512]{1,0:T(8,128)(2,1)S(1)}, bf16[1088,1024]{1,0:T(8,128)(2,1)S(1)}, bf16[1088,2048]{1,0:T(8,128)(2,1)}) custom-call(bf16[1088,2048]{1,0:T(8,128)(2,1)} %collective-permute-done.23.refs_0_.xo_ref, bf16[1088,2048]{1,0:T(8,128)(2,1)} %collective-permute-done.30.refs_1_.co_ref, bf16[2048,1024]{1,0:T(8,128)(2,1)} %bitcast.16.refs_2_, ...), custom_call_target="tpu_custom_call" | custom-call | flops 11408506880 | bytes 24117248 | tf_op jit(solution)/shard_map/pallas_call | solution.py:346
  344.1 7.7 %collective-permute-done.31.refs_5_ = bf16[1088,2048]{1,0:T(8,128)(2,1)S(1)} collective-permute-done((bf16[1088,2048]{1,0:T(8,128)(2,1)}, bf16[1088,2048]{1,0:T(8,128)(2,1)S(1)}, u32[]{:S(2)}, u32[]{:S(2)}) %collective-permute-start.31) | collective-permute-done | bytes 4456480 | tf_op jit(solution)/shard_map/ppermute | solution.py:21
  353.9 18.5 %shard_map.414 = (bf16[1088,512]{1,0:T(8,128)(2,1)S(1)}, bf16[1088,1024]{1,0:T(8,128)(2,1)S(1)}, bf16[1088,2048]{1,0:T(8,128)(2,1)}) custom-call(bf16[1088,2048]{1,0:T(8,128)(2,1)} %constant_dynamic-update-slice_fusion.10.refs_0_.xe_ref, bf16[1088,2048]{1,0:T(8,128)(2,1)} %constant_dynamic-update-slice_fusion.18.refs_1_.ce_ref, ...), custom_call_target="tpu_custom_call" | custom-call | flops 11408506880 | bytes 24117248 | tf_op jit(solution)/shard_map/pallas_call | solution.py:346
  372.4 4.1 fusion.63
  377.8 25.5 %collective-permute-done.32 = bf16[2,136,2048]{2,1,0:T(8,128)(2,1)S(1)} collective-permute-done((bf16[2,136,2048]{2,1,0:T(8,128)(2,1)S(1)}, bf16[2,136,2048]{2,1,0:T(8,128)(2,1)S(1)}, u32[]{:S(2)}, u32[]{:S(2)}) %collective-permute-start.32) | collective-permute-done | bytes 1114144 | tf_op jit(solution)/shard_map/ppermute | solution.py:21
  405.8 11.8 %collective-permute-done.33.ga_ref = bf16[136,2048]{1,0:T(8,128)(2,1)S(1)} collective-permute-done((bf16[136,2048]{1,0:T(8,128)(2,1)S(1)}, bf16[136,2048]{1,0:T(8,128)(2,1)S(1)}, u32[]{:S(2)}, u32[]{:S(2)}) %collective-permute-start.33) | collective-permute-done | bytes 557088 | tf_op jit(solution)/shard_map/ppermute | solution.py:21
  418.6 6.6 collective-permute-start.39
  427.7 6.6 collective-permute-done.39
  434.3 13.2 %collective-permute-done.40 = bf16[272,512]{1,0:T(8,128)(2,1)S(1)} collective-permute-done((bf16[272,512]{1,0:T(8,128)(2,1)S(1)}, bf16[272,512]{1,0:T(8,128)(2,1)S(1)}, u32[]{:S(2)}, u32[]{:S(2)}) %collective-permute-start.40) | collective-permute-done | bytes 278560 | tf_op jit(solution)/shard_map/ppermute | solution.py:21
  447.7 3.6 collective-permute-start.42
  453.7 4.9 collective-permute-done.42.refs_1_
  458.6 13.7 %collective-permute-done.43.refs_2_ = bf16[272,512]{1,0:T(8,128)(2,1)S(1)} collective-permute-done((bf16[272,512]{1,0:T(8,128)(2,1)S(1)}, bf16[272,512]{1,0:T(8,128)(2,1)S(1)}, u32[]{:S(2)}, u32[]{:S(2)}) %collective-permute-start.43) | collective-permute-done | bytes 278560 | tf_op jit(solution)/shard_map/ppermute | solution.py:21
  472.3 4.4 shard_map.417
  485.6 7.2 shard_map.415
  492.8 3.4 copy-done.3
  497.9 8.4 %shard_map.418 = (bf16[272,512]{1,0:T(8,128)(2,1)}, bf16[544,512]{1,0:T(8,128)(2,1)}, bf16[544,512]{1,0:T(8,128)(2,1)}, bf16[544,512]{1,0:T(8,128)(2,1)}, bf16[544,512]{1,0:T(8,128)(2,1)}) custom-call(bf16[272,512]{1,0:T(8,128)(2,1)} %copy-done.39, bf16[2176,512]{1,0:T(8,128)(2,1)} %copy-done.35, s32[272,1]{1,0:T(8,128)} %copy-done.24, ...), custom_call_target="tpu_custom_call" | custom-call | flops 3030384640 | bytes 6137408 | tf_op jit(solution)/shard_map/pallas_call | solution.py:99
  506.9 21.3 %shard_map.422 = (bf16[2048,1024]{1,0:T(8,128)(2,1)}, bf16[8,704,256]{2,1,0:T(8,128)(2,1)}) custom-call(bf16[1088,2048]{1,0:T(8,128)(2,1)} %collective-permute-done.23.refs_0_.xo_ref, bf16[1088,2048]{1,0:T(8,128)(2,1)} %constant_dynamic-update-slice_fusion.10.refs_0_.xe_ref, bf16[1088,2048]{1,0:T(8,128)(2,1)} %collective-permute-done.30.refs_1_.co_ref, ...), custom_call_target="tpu_custom_call" | custom-call | flops 13690208256 | bytes 17825792 | tf_op jit(solution)/shard_map/pallas_call | solution.py:399
  528.3 4.6 all-to-all-start.3
  536.8 49.3 %collective-permute-done.49 = bf16[2,136,512]{2,1,0:T(8,128)(2,1)S(1)} collective-permute-done((bf16[2,136,512]{2,1,0:T(8,128)(2,1)S(1)}, bf16[2,136,512]{2,1,0:T(8,128)(2,1)S(1)}, u32[]{:S(2)}, u32[]{:S(2)}) %collective-permute-start.49) | collective-permute-done | bytes 278560 | tf_op jit(solution)/shard_map/ppermute | solution.py:21
  588.7 6.4 collective-permute-done.50.refs_6_
  596.7 9.3 %shard_map.419 = (bf16[4,200,1024]{2,1,0:T(8,128)(2,1)S(1)}, bf16[4,200,1024]{2,1,0:T(8,128)(2,1)}, bf16[4,200,1024]{2,1,0:T(8,128)(2,1)}, bf16[4,200,1024]{2,1,...) custom-call(s32[1]{0:T(128)} %bitcast.38.refs_0_, ...), custom_call_target="tpu_custom_call" | custom-call | flops 2281701376 | bytes 16482312 | tf_op jit(solution)/shard_map/pallas_call | solution.py:99
  606.0 5.7 collective-permute-start.51
  616.0 4.9 all-to-all-start.2
  621.4 4.2 collective-permute-done.51.refs_1_
  625.6 10.2 %collective-permute-done.53.refs_3_ = bf16[280,512]{1,0:T(8,128)(2,1)} collective-permute-done((bf16[280,512]{1,0:T(8,128)(2,1)}, bf16[280,512]{1,0:T(8,128)(2,1)}, u32[]{:S(2)}, u32[]{:S(2)}) %collective-permute-start.53) | collective-permute-done | bytes 286752 | tf_op jit(solution)/shard_map/ppermute | solution.py:21
  656.1 30.5 %collective-permute-done.58 = bf16[2,200,1024]{2,1,0:T(8,128)(2,1)S(1)} collective-permute-done((bf16[2,200,1024]{2,1,0:T(8,128)(2,1)}, bf16[2,200,1024]{2,1,0:T(8,128)(2,1)S(1)}, u32[]{:S(2)}, u32[]{:S(2)}) %collective-permute-start.58) | collective-permute-done | bytes 819232 | tf_op jit(solution)/shard_map/ppermute | solution.py:21
  694.7 7.3 shard_map.423
  711.3 6.0 collective-permute-done.61
  731.4 3.8 collective-permute-done.34
  735.2 13.6 %collective-permute-done.35 = bf16[272,512]{1,0:T(8,128)(2,1)} collective-permute-done((bf16[272,512]{1,0:T(8,128)(2,1)}, bf16[272,512]{1,0:T(8,128)(2,1)}, u32[]{:S(2)}, u32[]{:S(2)}) %collective-permute-start.35) | collective-permute-done | bytes 278560 | tf_op jit(solution)/shard_map/ppermute | solution.py:21
  (443 shorter events, 191.9 us)
Async XLA Ops:
  7.3 52.1 %all-gather.5.cloned.1.call-start = ((), (), s32[]{:S(2)}) async-start(), calls=%async_computation.8 | async-start | bytes 7225344 | tf_op jit(solution)/shard_map/all_gather | solution.py:731
  10.3 129.5 %all-gather.7.cloned.1.call-start = ((), (), s32[]{:S(2)}) async-start(), calls=%async_computation.9 | async-start | bytes 3538944 | tf_op jit(solution)/shard_map/all_gather | solution.py:805
  10.5 51.1 %collective-permute-start = (bf16[272,512]{1,0:T(8,128)(2,1)S(1)}, bf16[272,512]{1,0:T(8,128)(2,1)S(1)}, u32[]{:S(2)}, u32[]{:S(2)}) collective-permute-start(bf16[272,512]{1,0:T(8,128)(2,1)S(1)} %fusion.12.refs_0_.refs_4_), channel_id=1, source_target_pairs={{0,1},{1,0},{2,3},{3,2},{4,5},{5,4},{6,7},{7,6},{8,9},{9,8},{10,11... | collective-permute-start | bytes 835592 | tf_op jit(solution)/shard_map/ppermute | solution.py:21
  13.5 48.0 %collective-permute-start.1 = (bf16[272,512]{1,0:T(8,128)(2,1)S(1)}, bf16[272,512]{1,0:T(8,128)(2,1)S(1)}, u32[]{:S(2)}, u32[]{:S(2)}) collective-permute-start(bf16[272,512]{1,0:T(8,128)(2,1)S(1)} %fusion.12.refs_0_.refs_4_), channel_id=1, source_target_pairs={{0,2},{1,3},{2,0},{3,1},{4,6},{5,7},{6,4},{7,5},{8,10},{9,11},{10,... | collective-permute-start | bytes 835592 | tf_op jit(solution)/shard_map/ppermute | solution.py:21
  16.1 45.4 %collective-permute-start.2 = (bf16[272,512]{1,0:T(8,128)(2,1)S(1)}, bf16[272,512]{1,0:T(8,128)(2,1)S(1)}, u32[]{:S(2)}, u32[]{:S(2)}) collective-permute-start(bf16[272,512]{1,0:T(8,128)(2,1)S(1)} %fusion.12.refs_0_.refs_4_), channel_id=1, source_target_pairs={{0,3},{1,2},{2,1},{3,0},{4,7},{5,6},{6,5},{7,4},{8,11},{9,10},{10,... | collective-permute-start | bytes 835592 | tf_op jit(solution)/shard_map/ppermute | solution.py:21
  69.8 19.1 %collective-permute-start.24 = (bf16[136,2048]{1,0:T(8,128)(2,1)S(1)}, bf16[136,2048]{1,0:T(8,128)(2,1)S(1)}, u32[]{:S(2)}, u32[]{:S(2)}) collective-permute-start(bf16[136,2048]{1,0:T(8,128)(2,1)S(1)} %pad_maximum_fusion.7), channel_id=1, source_target_pairs={{0,8},{4,12},{8,0},{12,4},{16,24},{20,28},{24,16},{28,20},{1,9},{5... | collective-permute-start | bytes 1671176 | tf_op jit(solution)/shard_map/ppermute | solution.py:21
  71.3 19.8 %collective-permute-start.25 = (bf16[136,2048]{1,0:T(8,128)(2,1)S(1)}, bf16[136,2048]{1,0:T(8,128)(2,1)}, u32[]{:S(2)}, u32[]{:S(2)}) collective-permute-start(bf16[136,2048]{1,0:T(8,128)(2,1)S(1)} %pad_maximum_fusion.7), channel_id=1, source_target_pairs={{0,16},{4,20},{8,24},{12,28},{16,0},{20,4},{24,8},{28,12},{1,17},{... | collective-permute-start | bytes 1671176 | tf_op jit(solution)/shard_map/ppermute | solution.py:21
  88.8 22.6 %collective-permute-start.26 = (bf16[136,2048]{1,0:T(8,128)(2,1)S(1)}, bf16[136,2048]{1,0:T(8,128)(2,1)}, u32[]{:S(2)}, u32[]{:S(2)}) collective-permute-start(bf16[136,2048]{1,0:T(8,128)(2,1)S(1)} %collective-permute-done.24), channel_id=1, source_target_pairs={{0,16},{4,20},{8,24},{12,28},{16,0},{20,4},{24,8},{28,12},{1,17},{... | collective-permute-start | bytes 1671176 | tf_op jit(solution)/shard_map/ppermute | solution.py:21
  145.5 14.1 %collective-permute-start.11 = (bf16[272,512]{1,0:T(8,128)(2,1)S(1)}, bf16[272,512]{1,0:T(8,128)(2,1)S(1)}, u32[]{:S(2)}, u32[]{:S(2)}) collective-permute-start(bf16[272,512]{1,0:T(8,128)(2,1)S(1)} %get-tuple-element.90), channel_id=1, source_target_pairs={{0,1},{1,0},{2,3},{3,2},{4,5},{5,4},{6,7},{7,6},{8,9},{9,8},{10,11... | collective-permute-start | bytes 835592 | tf_op jit(solution)/shard_map/ppermute | solution.py:21
  147.1 22.4 %collective-permute-start.12 = (bf16[272,512]{1,0:T(8,128)(2,1)S(1)}, bf16[272,512]{1,0:T(8,128)(2,1)S(1)}, u32[]{:S(2)}, u32[]{:S(2)}) collective-permute-start(bf16[272,512]{1,0:T(8,128)(2,1)S(1)} %get-tuple-element.91), channel_id=1, source_target_pairs={{0,2},{1,3},{2,0},{3,1},{4,6},{5,7},{6,4},{7,5},{8,10},{9,11},{10,... | collective-permute-start | bytes 835592 | tf_op jit(solution)/shard_map/ppermute | solution.py:21
  149.5 20.0 %collective-permute-start.13 = (bf16[272,512]{1,0:T(8,128)(2,1)S(1)}, bf16[272,512]{1,0:T(8,128)(2,1)S(1)}, u32[]{:S(2)}, u32[]{:S(2)}) collective-permute-start(bf16[272,512]{1,0:T(8,128)(2,1)S(1)} %get-tuple-element.92), channel_id=1, source_target_pairs={{0,3},{1,2},{2,1},{3,0},{4,7},{5,6},{6,5},{7,4},{8,11},{9,10},{10,... | collective-permute-start | bytes 835592 | tf_op jit(solution)/shard_map/ppermute | solution.py:21
  151.9 26.4 %collective-permute-start.27 = (bf16[136,2048]{1,0:T(8,128)(2,1)}, bf16[136,2048]{1,0:T(8,128)(2,1)}, u32[]{:S(2)}, u32[]{:S(2)}) collective-permute-start(bf16[136,2048]{1,0:T(8,128)(2,1)} %pad_maximum_fusion.8), channel_id=1, source_target_pairs={{0,16},{4,20},{8,24},{12,28},{16,0},{20,4},{24,8},{28,12},{1,17},{... | collective-permute-start | bytes 1671176 | tf_op jit(solution)/shard_map/ppermute | solution.py:21
  155.7 47.7 %collective-permute-start.28 = (bf16[136,2048]{1,0:T(8,128)(2,1)}, bf16[136,2048]{1,0:T(8,128)(2,1)}, u32[]{:S(2)}, u32[]{:S(2)}) collective-permute-start(bf16[136,2048]{1,0:T(8,128)(2,1)} %pad_maximum_fusion.8), channel_id=1, source_target_pairs={{0,8},{4,12},{8,0},{12,4},{16,24},{20,28},{24,16},{28,20},{1,9},{5... | collective-permute-start | bytes 1671176 | tf_op jit(solution)/shard_map/ppermute | solution.py:21
  169.7 16.1 %collective-permute-start.14 = (bf16[272,512]{1,0:T(8,128)(2,1)S(1)}, bf16[272,512]{1,0:T(8,128)(2,1)S(1)}, u32[]{:S(2)}, u32[]{:S(2)}) collective-permute-start(bf16[272,512]{1,0:T(8,128)(2,1)S(1)} %fusion.33.refs_0_), channel_id=1, source_target_pairs={{0,1},{1,0},{2,3},{3,2},{4,5},{5,4},{6,7},{7,6},{8,9},{9,8},{10,11... | collective-permute-start | bytes 835592 | tf_op jit(solution)/shard_map/ppermute | solution.py:21
  175.2 22.4 %collective-permute-start.15 = (bf16[272,512]{1,0:T(8,128)(2,1)S(1)}, bf16[272,512]{1,0:T(8,128)(2,1)S(1)}, u32[]{:S(2)}, u32[]{:S(2)}) collective-permute-start(bf16[272,512]{1,0:T(8,128)(2,1)S(1)} %fusion.33.refs_0_), channel_id=1, source_target_pairs={{0,2},{1,3},{2,0},{3,1},{4,6},{5,7},{6,4},{7,5},{8,10},{9,11},{10,... | collective-permute-start | bytes 835592 | tf_op jit(solution)/shard_map/ppermute | solution.py:21
  176.2 21.4 %collective-permute-start.16 = (bf16[272,512]{1,0:T(8,128)(2,1)S(1)}, bf16[272,512]{1,0:T(8,128)(2,1)S(1)}, u32[]{:S(2)}, u32[]{:S(2)}) collective-permute-start(bf16[272,512]{1,0:T(8,128)(2,1)S(1)} %fusion.33.refs_0_), channel_id=1, source_target_pairs={{0,3},{1,2},{2,1},{3,0},{4,7},{5,6},{6,5},{7,4},{8,11},{9,10},{10,... | collective-permute-start | bytes 835592 | tf_op jit(solution)/shard_map/ppermute | solution.py:21
  178.3 27.9 %collective-permute-start.29 = (bf16[136,2048]{1,0:T(8,128)(2,1)}, bf16[136,2048]{1,0:T(8,128)(2,1)S(1)}, u32[]{:S(2)}, u32[]{:S(2)}) collective-permute-start(bf16[136,2048]{1,0:T(8,128)(2,1)} %collective-permute-done.27), channel_id=1, source_target_pairs={{0,8},{4,12},{8,0},{12,4},{16,24},{20,28},{24,16},{28,20},{1,9},{5... | collective-permute-start | bytes 1671176 | tf_op jit(solution)/shard_map/ppermute | solution.py:21
  202.3 15.6 %collective-permute-start.20 = (bf16[136,2048]{1,0:T(8,128)(2,1)S(1)}, bf16[136,2048]{1,0:T(8,128)(2,1)S(1)}, u32[]{:S(2)}, u32[]{:S(2)}) collective-permute-start(bf16[136,2048]{1,0:T(8,128)(2,1)S(1)} %get-tuple-element.94), channel_id=1, source_target_pairs={{0,16},{4,20},{8,24},{12,28},{16,0},{20,4},{24,8},{28,12},{1,17},{... | collective-permute-start | bytes 1671176 | tf_op jit(solution)/shard_map/ppermute | solution.py:21
  205.3 32.2 %collective-permute-start.18 = (bf16[136,2048]{1,0:T(8,128)(2,1)S(1)}, bf16[136,2048]{1,0:T(8,128)(2,1)S(1)}, u32[]{:S(2)}, u32[]{:S(2)}) collective-permute-start(bf16[136,2048]{1,0:T(8,128)(2,1)S(1)} %get-tuple-element.93), channel_id=1, source_target_pairs={{0,16},{4,20},{8,24},{12,28},{16,0},{20,4},{24,8},{28,12},{1,17},{... | collective-permute-start | bytes 1671176 | tf_op jit(solution)/shard_map/ppermute | solution.py:21
  207.1 69.7 %collective-permute-start.30 = (bf16[1088,2048]{1,0:T(8,128)(2,1)}, bf16[1088,2048]{1,0:T(8,128)(2,1)}, u32[]{:S(2)}, u32[]{:S(2)}) collective-permute-start(bf16[1088,2048]{1,0:T(8,128)(2,1)} %constant_dynamic-update-slice_fusion.18.refs_1_.ce_ref), channel_id=1, source_target_pairs={{0,4},{4,0},{8,12},{12,8},{16,20},{20,16},{24,28},{28,24},{1,5},{5... | collective-permute-start | bytes 13369352 | tf_op jit(solution)/shard_map/ppermute | solution.py:21
  207.1 64.2 %all-to-all-start.1 = ((bf16[8,704,256]{2,1,0:T(8,128)(2,1)}), bf16[8,704,256]{2,1,0:T(8,128)(2,1)}, u32[]{:S(2)}, u32[]{:S(2)}) async-start(bf16[8,704,256]{2,1,0:T(8,128)(2,1)} %pad_maximum_fusion.1), calls=%async_computation.1 | async-start | bytes 5767168 | tf_op jit(solution)/shard_map/all_to_all | solution.py:808
  211.5 55.4 %collective-permute-start.19 = (bf16[136,2048]{1,0:T(8,128)(2,1)S(1)}, bf16[136,2048]{1,0:T(8,128)(2,1)S(1)}, u32[]{:S(2)}, u32[]{:S(2)}) collective-permute-start(bf16[136,2048]{1,0:T(8,128)(2,1)S(1)} %collective-permute-done.17), channel_id=1, source_target_pairs={{0,16},{4,20},{8,24},{12,28},{16,0},{20,4},{24,8},{28,12},{1,17},{... | collective-permute-start | bytes 1671176 | tf_op jit(solution)/shard_map/ppermute | solution.py:21
  214.3 55.3 %collective-permute-start.21 = (bf16[136,2048]{1,0:T(8,128)(2,1)S(1)}, bf16[136,2048]{1,0:T(8,128)(2,1)S(1)}, u32[]{:S(2)}, u32[]{:S(2)}) collective-permute-start(bf16[136,2048]{1,0:T(8,128)(2,1)S(1)} %get-tuple-element.94), channel_id=1, source_target_pairs={{0,8},{4,12},{8,0},{12,4},{16,24},{20,28},{24,16},{28,20},{1,9},{5... | collective-permute-start | bytes 1671176 | tf_op jit(solution)/shard_map/ppermute | solution.py:21
  217.8 52.6 %collective-permute-start.22 = (bf16[136,2048]{1,0:T(8,128)(2,1)S(1)}, bf16[136,2048]{1,0:T(8,128)(2,1)S(1)}, u32[]{:S(2)}, u32[]{:S(2)}) collective-permute-start(bf16[136,2048]{1,0:T(8,128)(2,1)S(1)} %collective-permute-done.20), channel_id=1, source_target_pairs={{0,8},{4,12},{8,0},{12,4},{16,24},{20,28},{24,16},{28,20},{1,9},{5... | collective-permute-start | bytes 1671176 | tf_op jit(solution)/shard_map/ppermute | solution.py:21
  271.3 53.7 %all-to-all-start = ((bf16[8,256,1024]{2,1,0:T(8,128)(2,1)}), bf16[8,256,1024]{2,1,0:T(8,128)(2,1)}, u32[]{:S(2)}, u32[]{:S(2)}) async-start(bf16[8,256,1024]{2,1,0:T(8,128)(2,1)} %pad_maximum_fusion), calls=%async_computation | async-start | bytes 8388608 | tf_op jit(solution)/shard_map/all_to_all | solution.py:807
  275.8 443.8 %reduce-scatter.5.cloned.1.call-start = ((), (), s32[]{:S(2)}) async-start(), calls=%async_computation.7 | async-start | bytes 3538944 | tf_op jit(solution)/shard_map/reduce_scatter | solution.py:929
  376.6 26.7 %collective-permute-start.32 = (bf16[2,136,2048]{2,1,0:T(8,128)(2,1)S(1)}, bf16[2,136,2048]{2,1,0:T(8,128)(2,1)S(1)}, u32[]{:S(2)}, u32[]{:S(2)}) collective-permute-start(bf16[2,136,2048]{2,1,0:T(8,128)(2,1)S(1)} %bitcast.188), channel_id=1, source_target_pairs={{0,16},{4,20},{8,24},{12,28},{16,0},{20,4},{24,8},{28,12},{1,17},{... | collective-permute-start | bytes 3342344 | tf_op jit(solution)/shard_map/ppermute | solution.py:21
  377.2 27.1 %collective-permute-start.37 = (bf16[2,136,2048]{2,1,0:T(8,128)(2,1)S(1)}, bf16[2,136,2048]{2,1,0:T(8,128)(2,1)S(1)}, u32[]{:S(2)}, u32[]{:S(2)}) collective-permute-start(bf16[2,136,2048]{2,1,0:T(8,128)(2,1)S(1)} %bitcast.187), channel_id=1, source_target_pairs={{0,8},{4,12},{8,0},{12,4},{16,24},{20,28},{24,16},{28,20},{1,9},{5... | collective-permute-start | bytes 3342344 | tf_op jit(solution)/shard_map/ppermute | solution.py:21
  418.6 15.7 %collective-permute-start.39 = (bf16[272,512]{1,0:T(8,128)(2,1)S(1)}, bf16[272,512]{1,0:T(8,128)(2,1)S(1)}, u32[]{:S(2)}, u32[]{:S(2)}) collective-permute-start(bf16[272,512]{1,0:T(8,128)(2,1)S(1)} %get-tuple-element.107), channel_id=1, source_target_pairs={{0,1},{1,0},{2,3},{3,2},{4,5},{5,4},{6,7},{7,6},{8,9},{9,8},{10,11... | collective-permute-start | bytes 835592 | tf_op jit(solution)/shard_map/ppermute | solution.py:21
  425.3 22.3 %collective-permute-start.40 = (bf16[272,512]{1,0:T(8,128)(2,1)S(1)}, bf16[272,512]{1,0:T(8,128)(2,1)S(1)}, u32[]{:S(2)}, u32[]{:S(2)}) collective-permute-start(bf16[272,512]{1,0:T(8,128)(2,1)S(1)} %get-tuple-element.108), channel_id=1, source_target_pairs={{0,2},{1,3},{2,0},{3,1},{4,6},{5,7},{6,4},{7,5},{8,10},{9,11},{10,... | collective-permute-start | bytes 835592 | tf_op jit(solution)/shard_map/ppermute | solution.py:21
  426.3 21.3 %collective-permute-start.41 = (bf16[272,512]{1,0:T(8,128)(2,1)S(1)}, bf16[272,512]{1,0:T(8,128)(2,1)S(1)}, u32[]{:S(2)}, u32[]{:S(2)}) collective-permute-start(bf16[272,512]{1,0:T(8,128)(2,1)S(1)} %get-tuple-element.109), channel_id=1, source_target_pairs={{0,3},{1,2},{2,1},{3,0},{4,7},{5,6},{6,5},{7,4},{8,11},{9,10},{10,... | collective-permute-start | bytes 835592 | tf_op jit(solution)/shard_map/ppermute | solution.py:21
  451.3 21.0 %collective-permute-start.43 = (bf16[272,512]{1,0:T(8,128)(2,1)S(1)}, bf16[272,512]{1,0:T(8,128)(2,1)S(1)}, u32[]{:S(2)}, u32[]{:S(2)}) collective-permute-start(bf16[272,512]{1,0:T(8,128)(2,1)S(1)} %add_convert_fusion.4.refs_0_), channel_id=1, source_target_pairs={{0,2},{1,3},{2,0},{3,1},{4,6},{5,7},{6,4},{7,5},{8,10},{9,11},{10,... | collective-permute-start | bytes 835592 | tf_op jit(solution)/shard_map/ppermute | solution.py:21
  452.3 20.0 %collective-permute-start.44 = (bf16[272,512]{1,0:T(8,128)(2,1)S(1)}, bf16[272,512]{1,0:T(8,128)(2,1)S(1)}, u32[]{:S(2)}, u32[]{:S(2)}) collective-permute-start(bf16[272,512]{1,0:T(8,128)(2,1)S(1)} %add_convert_fusion.4.refs_0_), channel_id=1, source_target_pairs={{0,3},{1,2},{2,1},{3,0},{4,7},{5,6},{6,5},{7,4},{8,11},{9,10},{10,... | collective-permute-start | bytes 835592 | tf_op jit(solution)/shard_map/ppermute | solution.py:21
  480.1 240.6 %reduce-scatter.3.cloned.1.call-start = ((), (), s32[]{:S(2)}) async-start(), calls=%async_computation.6 | async-start | bytes 10027008 | tf_op jit(solution)/shard_map/reduce_scatter | solution.py:891
  506.4 26.4 %collective-permute-start.48 = (bf16[544,512]{1,0:T(8,128)(2,1)}, bf16[544,512]{1,0:T(8,128)(2,1)S(1)}, u32[]{:S(2)}, u32[]{:S(2)}) collective-permute-start(bf16[544,512]{1,0:T(8,128)(2,1)} %get-tuple-element.117), channel_id=1, source_target_pairs={{0,4},{4,0},{8,12},{12,8},{16,20},{20,16},{24,28},{28,24},{1,5},{5... | collective-permute-start | bytes 1671176 | tf_op jit(solution)/shard_map/ppermute | solution.py:21
  506.4 28.6 %collective-permute-start.45 = (bf16[544,512]{1,0:T(8,128)(2,1)}, bf16[544,512]{1,0:T(8,128)(2,1)S(1)}, u32[]{:S(2)}, u32[]{:S(2)}) collective-permute-start(bf16[544,512]{1,0:T(8,128)(2,1)} %get-tuple-element.115), channel_id=1, source_target_pairs={{0,4},{4,0},{8,12},{12,8},{16,20},{20,16},{24,28},{28,24},{1,5},{5... | collective-permute-start | bytes 1671176 | tf_op jit(solution)/shard_map/ppermute | solution.py:21
  528.3 87.7 %all-to-all-start.3 = ((bf16[8,704,256]{2,1,0:T(8,128)(2,1)}), bf16[8,704,256]{2,1,0:T(8,128)(2,1)}, u32[]{:S(2)}, u32[]{:S(2)}) async-start(bf16[8,704,256]{2,1,0:T(8,128)(2,1)} %get-tuple-element.145), calls=%async_computation.5 | async-start | bytes 5767168 | tf_op jit(solution)/shard_map/all_to_all | solution.py:894
  533.0 53.1 %collective-permute-start.49 = (bf16[2,136,512]{2,1,0:T(8,128)(2,1)S(1)}, bf16[2,136,512]{2,1,0:T(8,128)(2,1)S(1)}, u32[]{:S(2)}, u32[]{:S(2)}) collective-permute-start(bf16[2,136,512]{2,1,0:T(8,128)(2,1)S(1)} %bitcast.196), channel_id=1, source_target_pairs={{0,8},{4,12},{8,0},{12,4},{16,24},{20,28},{24,16},{28,20},{1,9},{5... | collective-permute-start | bytes 835592 | tf_op jit(solution)/shard_map/ppermute | solution.py:21
  535.2 52.6 %collective-permute-start.46 = (bf16[2,136,512]{2,1,0:T(8,128)(2,1)S(1)}, bf16[2,136,512]{2,1,0:T(8,128)(2,1)S(1)}, u32[]{:S(2)}, u32[]{:S(2)}) collective-permute-start(bf16[2,136,512]{2,1,0:T(8,128)(2,1)S(1)} %bitcast.197), channel_id=1, source_target_pairs={{0,16},{4,20},{8,24},{12,28},{16,0},{20,4},{24,8},{28,12},{1,17},{... | collective-permute-start | bytes 835592 | tf_op jit(solution)/shard_map/ppermute | solution.py:21
  606.0 33.9 %collective-permute-start.57 = (bf16[4,200,1024]{2,1,0:T(8,128)(2,1)}, bf16[4,200,1024]{2,1,0:T(8,128)(2,1)}, u32[]{:S(2)}, u32[]{:S(2)}) collective-permute-start(bf16[4,200,1024]{2,1,0:T(8,128)(2,1)} %get-tuple-element.133), channel_id=1, source_target_pairs={{0,4},{4,0},{8,12},{12,8},{16,20},{20,16},{24,28},{28,24},{1,5},{5... | collective-permute-start | bytes 4915208 | tf_op jit(solution)/shard_map/ppermute | solution.py:21
  606.0 19.6 %collective-permute-start.51 = (bf16[280,512]{1,0:T(8,128)(2,1)}, bf16[280,512]{1,0:T(8,128)(2,1)}, u32[]{:S(2)}, u32[]{:S(2)}) collective-permute-start(bf16[280,512]{1,0:T(8,128)(2,1)} %get-tuple-element.124), channel_id=1, source_target_pairs={{0,1},{1,0},{2,3},{3,2},{4,5},{5,4},{6,7},{7,6},{8,9},{9,8},{10,11... | collective-permute-start | bytes 860168 | tf_op jit(solution)/shard_map/ppermute | solution.py:21
  614.6 21.3 %collective-permute-start.53 = (bf16[280,512]{1,0:T(8,128)(2,1)}, bf16[280,512]{1,0:T(8,128)(2,1)}, u32[]{:S(2)}, u32[]{:S(2)}) collective-permute-start(bf16[280,512]{1,0:T(8,128)(2,1)} %get-tuple-element.126), channel_id=1, source_target_pairs={{0,3},{1,2},{2,1},{3,0},{4,7},{5,6},{6,5},{7,4},{8,11},{9,10},{10,... | collective-permute-start | bytes 860168 | tf_op jit(solution)/shard_map/ppermute | solution.py:21
  616.0 78.7 %all-to-all-start.2 = ((bf16[8,256,1024]{2,1,0:T(8,128)(2,1)}), bf16[8,256,1024]{2,1,0:T(8,128)(2,1)}, u32[]{:S(2)}, u32[]{:S(2)}) async-start(bf16[8,256,1024]{2,1,0:T(8,128)(2,1)} %bitcast.183), calls=%async_computation.4 | async-start | bytes 8388608 | tf_op jit(solution)/shard_map/all_to_all | solution.py:893
  620.9 25.3 %collective-permute-start.54 = (bf16[4,200,1024]{2,1,0:T(8,128)(2,1)}, bf16[4,200,1024]{2,1,0:T(8,128)(2,1)}, u32[]{:S(2)}, u32[]{:S(2)}) collective-permute-start(bf16[4,200,1024]{2,1,0:T(8,128)(2,1)} %get-tuple-element.131), channel_id=1, source_target_pairs={{0,4},{4,0},{8,12},{12,8},{16,20},{20,16},{24,28},{28,24},{1,5},{5... | collective-permute-start | bytes 4915208 | tf_op jit(solution)/shard_map/ppermute | solution.py:21
  643.3 43.2 %collective-permute-start.58 = (bf16[2,200,1024]{2,1,0:T(8,128)(2,1)}, bf16[2,200,1024]{2,1,0:T(8,128)(2,1)S(1)}, u32[]{:S(2)}, u32[]{:S(2)}) collective-permute-start(bf16[2,200,1024]{2,1,0:T(8,128)(2,1)} %slice.376), channel_id=1, source_target_pairs={{0,8},{4,12},{8,0},{12,4},{16,24},{20,28},{24,16},{28,20},{1,9},{5... | collective-permute-start | bytes 2457608 | tf_op jit(solution)/shard_map/ppermute | solution.py:21
  650.5 39.2 %collective-permute-start.55 = (bf16[2,200,1024]{2,1,0:T(8,128)(2,1)}, bf16[2,200,1024]{2,1,0:T(8,128)(2,1)}, u32[]{:S(2)}, u32[]{:S(2)}) collective-permute-start(bf16[2,200,1024]{2,1,0:T(8,128)(2,1)} %slice.371), channel_id=1, source_target_pairs={{0,16},{4,20},{8,24},{12,28},{16,0},{20,4},{24,8},{28,12},{1,17},{... | collective-permute-start | bytes 2457608 | tf_op jit(solution)/shard_map/ppermute | solution.py:21
  726.0 22.8 %collective-permute-start.35 = (bf16[272,512]{1,0:T(8,128)(2,1)}, bf16[272,512]{1,0:T(8,128)(2,1)}, u32[]{:S(2)}, u32[]{:S(2)}) collective-permute-start(bf16[272,512]{1,0:T(8,128)(2,1)} %fusion.15), channel_id=1, source_target_pairs={{0,2},{1,3},{2,0},{3,1},{4,6},{5,7},{6,4},{7,5},{8,10},{9,11},{10,... | collective-permute-start | bytes 835592 | tf_op jit(solution)/shard_map/ppermute | solution.py:21
  728.3 20.5 %collective-permute-start.36 = (bf16[272,512]{1,0:T(8,128)(2,1)}, bf16[272,512]{1,0:T(8,128)(2,1)}, u32[]{:S(2)}, u32[]{:S(2)}) collective-permute-start(bf16[272,512]{1,0:T(8,128)(2,1)} %fusion.16), channel_id=1, source_target_pairs={{0,3},{1,2},{2,1},{3,0},{4,7},{5,6},{6,5},{7,4},{8,11},{9,10},{10,... | collective-permute-start | bytes 835592 | tf_op jit(solution)/shard_map/ppermute | solution.py:21
  (111 other events, 1850.0 us)
Sparse Core Ops, SparseCore 0:
  10.5 48.7 all-gather.4
  68.1 44.8 all-gather.6
  480.3 48.2 reduce-scatter.4
  532.4 91.8 reduce-scatter.2

commit v3 on v2

--- a/solution.py
+++ b/solution.py
@@ -48,21 +48,27 @@
     return results
 
 
-def gather_rows(halves):
-    even = jnp.concatenate([b for blocks in gather_far(halves) for b in blocks], axis=0)
+def near_rows(far):
+    even = jnp.concatenate([b for blocks in far for b in blocks], axis=0)
     return swap(even, "seq", 1), even
 
 
-def scatter_far(halves):
+def add(left, right):
+    return left.astype(F32) + right.astype(F32)
+
+
+def scatter_rows(halves, token=None):
     results = []
-    for half, masks in zip(halves, far_masks()):
-        blocks = half
+    for (mine, other), masks in zip(halves, far_masks()):
         for mask in masks[:0:-1]:
-            keep = blocks.shape[0] // 2
-            got = swap(blocks[keep:].astype(BF), "seq", mask)
-            blocks = blocks[:keep].astype(F32) + got.astype(F32)
-        got = swap(blocks[1].astype(BF), "seq", masks[0])
-        results.append((blocks[0], got))
+            keep = mine.shape[0] // 2
+            got = swap(add(mine[keep:], other[keep:]).astype(BF), "seq", mask)
+            mine, other = add(mine[:keep], other[:keep]), got
+        sent = add(mine[1], other[1]).astype(BF)
+        if token is not None:
+            sent = after(sent, token)
+        got = swap(sent, "seq", masks[0])
+        results.append((add(mine[0], other[0]), got))
     return results
 
 
@@ -299,9 +305,7 @@
     return gelu * up, jnp.concatenate([dhidden * up * slope, dhidden * gelu], axis=1)
 
 
-def feed_kernel(pair, x_ref, c_ref, w_ref, d_ref, act_ref, *refs):
-    near_ref = refs[0] if len(refs) == 4 else None
-    h_ref, g_ref, dn_ref = refs[-3:]
+def feed_kernel(pair, x_ref, c_ref, w_ref, d_ref, act_ref, h_ref, g_ref, dn_ref):
     rows, dp = x_ref.shape
     each = rows // pair
     prefix = each - act_ref.shape[0] // pair
@@ -319,13 +323,10 @@
     for i in range(pair):
         pieces.append(dn[i * each : i * each + prefix])
         pieces.append(action[i * (each - prefix) : (i + 1) * (each - prefix)])
-    dn = jnp.concatenate(pieces, axis=0)
-    if near_ref is not None:
-        dn = dn + near_ref[...].astype(F32)
-    dn_ref[...] = dn.astype(BF)
-
-
-def feed(rows_in, cot_rows, gate_up, down, dn_action, near, each):
+    dn_ref[...] = jnp.concatenate(pieces, axis=0).astype(BF)
+
+
+def feed(rows_in, cot_rows, gate_up, down, dn_action, each):
     total, dp = rows_in.shape
     pair = 2
     step = pair * each
@@ -339,10 +340,6 @@
         pl.BlockSpec(down.shape, lambda i: (0, 0)),
         pl.BlockSpec((act_step, dn_action.shape[1]), lambda i: (i, 0)),
     ]
-    args = [rows_in, cot_rows, gate_up, down, dn_action]
-    if near is not None:
-        in_specs.append(row_spec)
-        args.append(near)
     return pl.pallas_call(
         lambda *refs: feed_kernel(pair, *refs),
         grid=(total // step,),
@@ -363,7 +360,7 @@
             bytes_accessed=8 * total * dp + 6 * f * dp,
             transcendentals=total * f,
         ),
-    )(*args)
+    )(rows_in, cot_rows, gate_up, down, dn_action)
 
 
 def feed_action_kernel(x_ref, c_ref, w_ref, d_ref, dn_ref, lift_ref, gw_ref, gd_ref):
@@ -736,7 +733,7 @@
     mlp_gain_a = got_gains[:, 2 * kp + ka : 2 * kp + 2 * ka].reshape(1, da)
     pack_out = jnp.concatenate([prefix_out.T, action_out.T], axis=0)
     cot_wide = jnp.pad(cot_action, ((0, 0), (0, dp - da)))
-    cot_odd, cot_even = gather_rows(
+    cot_far = gather_far(
         [
             jnp.concatenate(
                 [
@@ -748,6 +745,7 @@
             for i in range(2)
         ]
     )
+    cot_odd, cot_even = near_rows(cot_far)
 
     def by_units(w, f):
         return w.reshape(w.shape[0], n, f).transpose(1, 0, 2)
@@ -774,7 +772,7 @@
             ((ra, da), BF),
             ((rows, 128), F32),
         ),
-        [rank_t, *x_pieces, got_qkv, attn_gain_p, attn_gain_a],
+        [after(rank_t, cot_far[0][1], cot_far[1][1]), *x_pieces, got_qkv, attn_gain_p, attn_gain_a],
         2 * rp * dp * qkv_width,
     )
     kv_even = [jnp.concatenate(blocks, axis=0) for blocks in gather_far([kv_a, kv_b])]
@@ -803,26 +801,26 @@
         transcendentals=rows * width // HD * n * rows,
     )
     got_out = lax.all_gather(after(pack_out, queries), "seq", axis=0)
-    gate_up_sent, down_sent = after((gate_up_sent, down_sent), keys_values)
-    gate_up = lax.all_to_all(gate_up_sent, "seq", 0, 0).reshape(dp, 2 * fp)
-    down_got = lax.all_to_all(down_sent, "seq", 0, 0)
+    down_got = lax.all_to_all(after(down_sent, keys_values), "seq", 0, 0)
 
     piece = (((rows, cp), BF),)
     branch = sum_tp(
         whole_call(
-            branch_kernel, piece * tp, [rank_t, mixed, got_out], 2 * rows * dp * width
+            branch_kernel, piece * tp, [after(rank_t, cot_far[0][-1], cot_far[1][-1]), mixed, got_out], 2 * rows * dp * width
         )
     )
     residual = x_pack.astype(F32) + branch
+    mid_own = after(residual.astype(BF), down_got)
+    gate_up = lax.all_to_all(after(gate_up_sent, branch), "seq", 0, 0).reshape(dp, 2 * fp)
     block = (((half, dp), BF),)
     mid_p, mid_a, normed_a, normed_b = whole_call(
         middle_kernel,
         (((rp, dp), BF), ((ra, da), BF)) + block * 2,
-        [rank_t, *gather_tp(residual.astype(BF)), mlp_gain_p, mlp_gain_a],
+        [after(rank_t, gate_up), *gather_tp(mid_own), mlp_gain_p, mlp_gain_a],
         rp * dp,
     )
 
-    normed_odd, normed_even = gather_rows([normed_a, normed_b])
+    normed_odd, normed_even = near_rows(gather_far([normed_a, normed_b]))
     down = down_got[:, :fp].transpose(1, 0, 2).reshape(fp, dp)
     action_got = down_got[:, fp:].reshape(da, 3 * fa)
     gate_up_action = action_got[:, : 2 * fa]
@@ -846,25 +844,14 @@
         18 * tokens * da * fa,
     )
     h_odd, g_odd, dn_odd = feed(
-        normed_odd, cot_odd, gate_up, down, dn_action[: tokens // 2], None, half
+        normed_odd, cot_odd, gate_up, down, dn_action[: tokens // 2], half
     )
     h_even, g_even, dn_even = feed(
-        normed_even,
-        cot_even,
-        gate_up,
-        down,
-        dn_action[tokens // 2 :],
-        swap(dn_odd, "seq", 1),
-        half,
-    )
-    dn_blocks = dn_even.reshape(2, n // 2, half, dp)
-    (keep_a, got_a), (keep_b, got_b) = scatter_far([dn_blocks[0], dn_blocks[1]])
-    dn_own = sum_tp(
-        whole_call(
-            pieces_kernel, piece * tp, [rank_t, keep_a, got_a, keep_b, got_b], rp * dp
-        )
-    )
-    dn_pieces = gather_tp(dn_own.astype(BF))
+        normed_even, cot_even, gate_up, down, dn_action[tokens // 2 :], half
+    )
+    dn_blocks = [
+        d.reshape(2, n // 2, half, dp) for d in (dn_even, swap(dn_odd, "seq", 1))
+    ]
 
     action_grads = jnp.concatenate(
         [
@@ -888,8 +875,20 @@
     lifted = lift(
         odd_bits, *places, *lift_places, h_odd, h_even, lifted_action, down, half, ra
     )
-    lifted_home = lax.psum_scatter(after(lifted, got_a), "seq", scatter_dimension=0)
-    grad_gu, grad_down = after((grad_gu, grad_down), got_a)
+    (keep_a, got_a), (keep_b, got_b) = scatter_rows(
+        [(dn_blocks[0][i], dn_blocks[1][i]) for i in range(2)], grad_gu
+    )
+    dn_own = sum_tp(
+        whole_call(
+            pieces_kernel,
+            piece * tp,
+            [after(rank_t, lifted), keep_a, got_a, keep_b, got_b],
+            rp * dp,
+        )
+    )
+    dn_pieces = gather_tp(dn_own.astype(BF))
+    lifted_home = lax.psum_scatter(after(lifted, got_a, got_b), "seq", scatter_dimension=0)
+    grad_gu, grad_down = after((grad_gu, grad_down), got_a, got_b)
     grad_gu_home = lax.all_to_all(grad_gu.reshape(n, kp, 2 * fp), "seq", 0, 0)
     grad_down_home = lax.all_to_all(grad_down, "seq", 0, 0)
 
@@ -898,7 +897,7 @@
     dbranch_p, dbranch_a, dresid, mlp_gains_p, mlp_gains_a, dmixed = whole_call(
         middle_back_kernel,
         (((rp, dp), BF), ((ra, da), BF), ((rows, cp), F32), row, row_a, ((rows, width), BF)),
-        [rank_t, *dn_pieces, mid_p, mid_a, mlp_gain_p, mlp_gain_a, cot_prefix, cot_action, got_out],
+        [after(rank_t, grad_down_home), *dn_pieces, mid_p, mid_a, mlp_gain_p, mlp_gain_a, cot_prefix, cot_action, got_out],
         2 * rows * dp * width,
         scratch=(
             pltpu.VMEM((rp, dp), BF),
@@ -915,15 +914,15 @@
         limit=56,
         transcendentals=rows * width // HD * n * rows,
     )
-    dkv_even = [
-        (e.astype(F32) + swap(o, "seq", 1).astype(F32)).astype(BF).reshape(n // 2, half, 2 * HD)
+    dkv_halves = [
+        [d.reshape(n // 2, half, 2 * HD) for d in (e, swap(o, "seq", 1))]
         for e, o in ((dkv_parts[0], dkv_parts[1]), (dkv_parts[2], dkv_parts[3]))
     ]
-    dkv = [part for pair in scatter_far(dkv_even) for part in pair]
+    dkv = [part for pair in scatter_rows(dkv_halves) for part in pair]
     (out_grads,) = whole_call(
         out_grad_kernel,
         (((n, kp + ka, width), BF),),
-        [dbranch_p, dbranch_a, mixed],
+        [dbranch_p, dbranch_a, after(mixed, dquery)],
         2 * rows * dp * width,
     )
     out_home = lax.psum_scatter(out_grads, "seq", scatter_dimension=0).astype(F32)
@@ -932,7 +931,7 @@
         lambda *refs: front_back_kernel(width, *refs),
         (((n // 2, tall, qkv_width), BF),) * 4 + (((rows + 8, cp), BF),) * tp,
         [
-            rank_s, rank_t, dquery, *dkv, x_full_p, x_full_a, inverse1, attn_gain_p, attn_gain_a,
+            after(rank_s, grad_gu_home), rank_t, dquery, *dkv, x_full_p, x_full_a, inverse1, attn_gain_p, attn_gain_a,
             got_qkv, mlp_gains_p, mlp_gains_a,
         ],
         4 * rows * dp * qkv_width,
@@ -954,33 +953,6 @@
         ],
         rp * dp,
     )
-    group_even = [
-        (e.astype(F32) + swap(o, "seq", 1).astype(F32)).astype(BF)
-        for e, o in ((groups[2 * 0], groups[2]), (groups[1], groups[3]))
-    ]
-    qkv_a, qkv_b = [
-        keep.astype(F32) + got.astype(F32) for keep, got in scatter_far(group_even)
-    ]
-    hp, ha = kp // 2, ka // 2
-    qkv_home_p = jnp.concatenate([qkv_a[:hp], qkv_b[:hp]], axis=0)
-    qkv_home_a = jnp.concatenate([qkv_a[hp : hp + ha], qkv_b[hp : hp + ha]], axis=0)
-    gains_home = qkv_a[hp + ha :]
-    qp, qa = kp // tp, ka // tp
-    attn_gains = jnp.pad(gains_home[:1, :512], ((0, 7), (0, 0)))
-
-    def shared_piece(rank):
-        return jnp.concatenate(
-            [
-                lax.dynamic_slice_in_dim(qkv_home_p[:, width:], rank * qp, qp, 0),
-                lax.dynamic_slice_in_dim(qkv_home_a[:, width:], rank * qa, qa, 0),
-                attn_gains,
-            ],
-            axis=0,
-        )
-
-    shared_home = sum_tp([shared_piece(t ^ k) for k in range(tp)])
-    attn_gains_home = shared_home[qp + qa]
-
     def own_piece(rank):
         return jnp.concatenate(
             [
@@ -994,6 +966,33 @@
         )
 
     output = (residual + sum_tp([own_piece(t ^ k) for k in range(tp)])).astype(BF)
+    qkv_a, qkv_b = [
+        add(keep, got)
+        for keep, got in scatter_rows(
+            [(e, swap(o, "seq", 1)) for e, o in ((groups[0], groups[2]), (groups[1], groups[3]))],
+            output,
+        )
+    ]
+    hp, ha = kp // 2, ka // 2
+    qkv_home_p = jnp.concatenate([qkv_a[:hp], qkv_b[:hp]], axis=0)
+    qkv_home_a = jnp.concatenate([qkv_a[hp : hp + ha], qkv_b[hp : hp + ha]], axis=0)
+    gains_home = qkv_a[hp + ha :]
+    qp, qa = kp // tp, ka // tp
+
+    attn_gains = jnp.pad(gains_home[:1, :512], ((0, 7), (0, 0)))
+
+    def shared_piece(rank):
+        return jnp.concatenate(
+            [
+                lax.dynamic_slice_in_dim(qkv_home_p[:, width:], rank * qp, qp, 0),
+                lax.dynamic_slice_in_dim(qkv_home_a[:, width:], rank * qa, qa, 0),
+                attn_gains,
+            ],
+            axis=0,
+        )
+
+    shared_home = sum_tp([shared_piece(t ^ k) for k in range(tp)])
+    attn_gains_home = shared_home[qp + qa]
     grad_gate_p, grad_up_p = home(grad_gu_home)
     grad_down_p = grad_down_home[:, :fp].astype(F32).reshape(n * fp, kp)
     action_home = grad_down_home[:, fp:].reshape(n, ka, 3 * fa).astype(F32)

time: 767 us -> 706 us (0.920)
  waiting for transfers between devices: 398 us -> 283 us
  blocking collectives: 0 us -> 47.8 us
  other arithmetic: 32.3 us -> 48.1 us
  local copies, waits for them, and re-layouts: 90.8 us -> 76.8 us
    ppermute x63, waiting for transfers between devices: 316 us -> 241 us  [swap(): return lax.ppermute(value, axis, [(i, i ^ mask) for i in range(count)])]
    all_to_all x0 -> x1, blocking collectives: none -> 47.8 us  [shards(): grad_down_home = lax.all_to_all(grad_down, 'seq', 0, 0)]
    all_gather x1, waiting for transfers between devices: 42.4 us -> 2.17 us  [shards(): got_qkv = lax.all_gather(pack_qkv, 'seq', axis=0)]
    convert_element_type x5 -> x10, other arithmetic: 4.74 us -> 17.9 us  [the longest x5 12.9 us: scatter_rows(): got = swap(add(mine[keep:], other[keep:]).astype(BF), 'seq', mask)]
    reduce_scatter x1, starting transfers between devices: 0.04 us -> 8.79 us  [shards(): lax.psum_scatter(out_grads, 'seq', scatter_dimension=0).astype(F32)]
    slice x8 -> x0, local copies, waits for them, and re-layouts: 8.6 us -> none  [the longest x5 6.21 us: scatter_far(): got = swap(blocks[keep:].astype(BF), 'seq', mask)]
    unnamed x206 -> x185, local copies, waits for them, and re-layouts: 45.4 us -> 38.9 us
    all_to_all x3 -> x2, waiting for transfers between devices: 38.9 us -> 39.8 us  [the longest x1 39.8 us: shards(): lax.all_to_all(after(gate_up_sent, branch), 'seq', 0, 0).reshape(dp, 2 * fp)]
  transfers between devices with their start and end apart: 71 -> 70, of which waited for: 34 -> 37; matrix products, arithmetic and copies ran while one was open for 11% -> 12% of each run, Pallas kernels for 8% -> 12%
where the time goes in v3:
time: 706 us; the launch traced here: 700 us
  waiting for transfers between devices  283 us (40%)
  starting transfers between devices  119 us (17%)
  Pallas kernels  110 us (16%)
  local copies, waits for them, and re-layouts  76.8 us (11%)
  other arithmetic  48.1 us (7%)
  blocking collectives  47.8 us (7%)
  between operations  15.3 us (2%)
    ppermute x63, waiting for transfers between devices, swap(): return lax.ppermute(value, axis, [(i, i ^ mask) for i in range(count)])  241 us
    ppermute x63, starting transfers between devices, swap(): return lax.ppermute(value, axis, [(i, i ^ mask) for i in range(count)])  96 us
    all_to_all x1, blocking collectives, shards(): grad_down_home = lax.all_to_all(grad_down, 'seq', 0, 0)  47.8 us
    all_to_all x1, waiting for transfers between devices, shards(): lax.all_to_all(after(gate_up_sent, branch), 'seq', 0, 0).reshape(dp, 2 * fp)  39.8 us
    pallas_call x11, Pallas kernels, whole_call(): pl.pallas_call(kernel, out_shape=outs, in_specs=specs, out_specs=tuple((p...  39.7 us
    unnamed x185, local copies, waits for them, and re-layouts  38.9 us
    pallas_call x2, Pallas kernels, feed(): pl.pallas_call(lambda *refs: feed_kernel(pair, *refs), grid=(total // ste...  34.7 us
    pallas_call x1, Pallas kernels, weight_grads(): pl.pallas_call(weights_kernel, grid=(dp // wide,), in_specs=[cols, cols,...  21.3 us
  transfers between devices with their start and end apart: 70, of which 37 were waited for; matrix products, arithmetic and copies ran while one was open for 12% of the time, Pallas kernels for 12%

profile of v3, /device:TPU:0, one launch (start us, length us, event | category | flops | bytes accessed | tf_op | source)
XLA Modules:
  0.0 700.2 jit_solution(7804713031198139674)
XLA Ops:
  15.1 15.5 %collective-permute-done = bf16[136,2048]{1,0:T(8,128)(2,1)S(1)} collective-permute-done((bf16[136,2048]{1,0:T(8,128)(2,1)S(1)}, bf16[136,2048]{1,0:T(8,128)(2,1)S(1)}, u32[]{:S(2)}, u32[]{:S(2)}) %collective-permute-start) | collective-permute-done | bytes 557088 | tf_op jit(solution)/shard_map/ppermute | solution.py:21
  34.4 16.0 %collective-permute-done.1 = bf16[136,2048]{1,0:T(8,128)(2,1)S(1)} collective-permute-done((bf16[136,2048]{1,0:T(8,128)(2,1)S(1)}, bf16[136,2048]{1,0:T(8,128)(2,1)S(1)}, u32[]{:S(2)}, u32[]{:S(2)}) %collective-permute-start.1) | collective-permute-done | bytes 557088 | tf_op jit(solution)/shard_map/ppermute | solution.py:21
  59.5 17.6 %collective-permute-done.2 = bf16[136,2048]{1,0:T(8,128)(2,1)S(1)} collective-permute-done((bf16[136,2048]{1,0:T(8,128)(2,1)S(1)}, bf16[136,2048]{1,0:T(8,128)(2,1)S(1)}, u32[]{:S(2)}, u32[]{:S(2)}) %collective-permute-start.2) | collective-permute-done | bytes 557088 | tf_op jit(solution)/shard_map/ppermute | solution.py:21
  80.9 4.7 shard_map.408
  94.6 3.4 pad_maximum_fusion.1
  101.2 4.9 collective-permute-done.11
  108.0 3.2 collective-permute-done.13
  113.8 4.6 all-to-all-start.1
  121.1 44.1 %collective-permute-done.3 = bf16[136,2048]{1,0:T(8,128)(2,1)} collective-permute-done((bf16[136,2048]{1,0:T(8,128)(2,1)S(1)}, bf16[136,2048]{1,0:T(8,128)(2,1)}, u32[]{:S(2)}, u32[]{:S(2)}) %collective-permute-start.3) | collective-permute-done | bytes 557088 | tf_op jit(solution)/shard_map/ppermute | solution.py:21
  165.2 3.8 shard_map.409
  185.7 4.6 collective-permute-done.15
  190.3 10.2 %collective-permute-done.16 = bf16[272,512]{1,0:T(8,128)(2,1)S(1)} collective-permute-done((bf16[272,512]{1,0:T(8,128)(2,1)S(1)}, bf16[272,512]{1,0:T(8,128)(2,1)S(1)}, u32[]{:S(2)}, u32[]{:S(2)}) %collective-permute-start.16) | collective-permute-done | bytes 278560 | tf_op jit(solution)/shard_map/ppermute | solution.py:21
  201.6 4.7 all-to-all-start
  208.5 5.2 collective-permute-start.18
  216.1 39.8 %all-to-all-done = bf16[8,256,1024]{2,1,0:T(8,128)(2,1)} async-done(((bf16[8,256,1024]{2,1,0:T(8,128)(2,1)}), bf16[8,256,1024]{2,1,0:T(8,128)(2,1)}, u32[]{:S(2)}, u32[]{:S(2)}) %all-to-all-start) | async-done | bytes 4194336 | tf_op jit(solution)/shard_map/all_to_all | solution.py:814
  258.5 8.3 %collective-permute-done.29 = bf16[136,2048]{1,0:T(8,128)(2,1)S(1)} collective-permute-done((bf16[136,2048]{1,0:T(8,128)(2,1)S(1)}, bf16[136,2048]{1,0:T(8,128)(2,1)S(1)}, u32[]{:S(2)}, u32[]{:S(2)}) %collective-permute-start.29) | collective-permute-done | bytes 557088 | tf_op jit(solution)/shard_map/ppermute | solution.py:21
  271.0 7.2 %collective-permute-done.21 = bf16[136,2048]{1,0:T(8,128)(2,1)S(1)} collective-permute-done((bf16[136,2048]{1,0:T(8,128)(2,1)S(1)}, bf16[136,2048]{1,0:T(8,128)(2,1)S(1)}, u32[]{:S(2)}, u32[]{:S(2)}) %collective-permute-start.21) | collective-permute-done | bytes 557088 | tf_op jit(solution)/shard_map/ppermute | solution.py:21
  285.8 9.7 %collective-permute-done.23 = bf16[136,2048]{1,0:T(8,128)(2,1)S(1)} collective-permute-done((bf16[136,2048]{1,0:T(8,128)(2,1)S(1)}, bf16[136,2048]{1,0:T(8,128)(2,1)S(1)}, u32[]{:S(2)}, u32[]{:S(2)}) %collective-permute-start.23) | collective-permute-done | bytes 557088 | tf_op jit(solution)/shard_map/ppermute | solution.py:21
  299.0 7.4 %collective-permute-done.26 = bf16[136,2048]{1,0:T(8,128)(2,1)S(1)} collective-permute-done((bf16[136,2048]{1,0:T(8,128)(2,1)S(1)}, bf16[136,2048]{1,0:T(8,128)(2,1)S(1)}, u32[]{:S(2)}, u32[]{:S(2)}) %collective-permute-start.26) | collective-permute-done | bytes 557088 | tf_op jit(solution)/shard_map/ppermute | solution.py:21
  318.8 17.4 %shard_map.413 = (bf16[1088,512]{1,0:T(8,128)(2,1)S(1)}, bf16[1088,1024]{1,0:T(8,128)(2,1)S(1)}, bf16[1088,2048]{1,0:T(8,128)(2,1)}) custom-call(bf16[1088,2048]{1,0:T(8,128)(2,1)} %collective-permute-done.27.refs_0_.xo_ref, bf16[1088,2048]{1,0:T(8,128)(2,1)} %copy-done.75, bf16[2048,1024]{1,0:T(8,128)(2,1)} %bitcast.10.refs_2_, ...), custom_call_target="tpu_custom_call" | custom-call | flops 11408506880 | bytes 24117248 | tf_op jit(solution)/shard_map/pallas_call | solution.py:343
  344.7 17.3 %shard_map.414 = (bf16[1088,512]{1,0:T(8,128)(2,1)S(1)}, bf16[1088,1024]{1,0:T(8,128)(2,1)S(1)}, bf16[1088,2048]{1,0:T(8,128)(2,1)}) custom-call(bf16[1088,2048]{1,0:T(8,128)(2,1)} %constant_dynamic-update-slice_fusion.10.refs_0_.xe_ref, bf16[1088,2048]{1,0:T(8,128)(2,1)} %constant_dynamic-update-slice_fusion.18.refs_1_.ce_ref, ...), custom_call_target="tpu_custom_call" | custom-call | flops 11408506880 | bytes 24117248 | tf_op jit(solution)/shard_map/pallas_call | solution.py:343
  363.4 4.6 add_convert_fusion
  369.2 21.3 %shard_map.416 = (bf16[2048,1024]{1,0:T(8,128)(2,1)}, bf16[8,704,256]{2,1,0:T(8,128)(2,1)}) custom-call(bf16[1088,2048]{1,0:T(8,128)(2,1)} %collective-permute-done.27.refs_0_.xo_ref, bf16[1088,2048]{1,0:T(8,128)(2,1)} %constant_dynamic-update-slice_fusion.10.refs_0_.xe_ref, bf16[1088,2048]{1,0:T(8,128)(2,1)} %copy-done.75, ...), custom_call_target="tpu_custom_call" | custom-call | flops 13690208256 | bytes 17825792 | tf_op jit(solution)/shard_map/pallas_call | solution.py:396
  390.5 3.9 collective-permute-done.34
  398.0 7.0 shard_map.415
  404.9 3.4 copy-done.3
  410.9 47.8 %all_to_all.20 = bf16[8,704,256]{2,1,0:T(8,128)(2,1)} all-to-all(bf16[8,704,256]{2,1,0:T(8,128)(2,1)} %get-tuple-element.132), channel_id=1, replica_groups=mesh['seq'=8,'tp'=4] {'seq'}, dimensions={0} | all-to-all | bytes 5767168 | tf_op jit(solution)/shard_map/all_to_all | solution.py:893
  458.8 4.6 all-to-all-start.2
  463.4 8.8 %reduce-scatter.5.cloned.1.call-start = ((), (), s32[]{:S(2)}) async-start(), calls=%async_computation.7 | async-start | bytes 3538944 | tf_op jit(solution)/shard_map/reduce_scatter | solution.py:928
  473.6 8.9 %collective-permute-start.39 = (bf16[272,512]{1,0:T(8,128)(2,1)S(1)}, bf16[272,512]{1,0:T(8,128)(2,1)S(1)}, u32[]{:S(2)}, u32[]{:S(2)}) collective-permute-start(bf16[272,512]{1,0:T(8,128)(2,1)S(1)} %get-tuple-element.136), channel_id=1, source_target_pairs={{0,1},{1,0},{2,3},{3,2},{4,5},{5,4},{6,7},{7,6},{8,9},{9,8},{10,11... | collective-permute-start | bytes 835592 | tf_op jit(solution)/shard_map/ppermute | solution.py:21
  485.0 9.8 %collective-permute-done.39 = bf16[272,512]{1,0:T(8,128)(2,1)S(1)} collective-permute-done((bf16[272,512]{1,0:T(8,128)(2,1)S(1)}, bf16[272,512]{1,0:T(8,128)(2,1)S(1)}, u32[]{:S(2)}, u32[]{:S(2)}) %collective-permute-start.39) | collective-permute-done | bytes 278560 | tf_op jit(solution)/shard_map/ppermute | solution.py:21
  494.8 10.2 %collective-permute-done.40 = bf16[272,512]{1,0:T(8,128)(2,1)S(1)} collective-permute-done((bf16[272,512]{1,0:T(8,128)(2,1)S(1)}, bf16[272,512]{1,0:T(8,128)(2,1)S(1)}, u32[]{:S(2)}, u32[]{:S(2)}) %collective-permute-start.40) | collective-permute-done | bytes 278560 | tf_op jit(solution)/shard_map/ppermute | solution.py:21
  505.1 5.5 collective-permute-start.42
  513.0 8.3 %collective-permute-done.42.refs_1_ = bf16[272,512]{1,0:T(8,128)(2,1)S(1)} collective-permute-done((bf16[272,512]{1,0:T(8,128)(2,1)S(1)}, bf16[272,512]{1,0:T(8,128)(2,1)S(1)}, u32[]{:S(2)}, u32[]{:S(2)}) %collective-permute-start.42) | collective-permute-done | bytes 278560 | tf_op jit(solution)/shard_map/ppermute | solution.py:21
  521.2 11.7 %collective-permute-done.43.refs_2_ = bf16[272,512]{1,0:T(8,128)(2,1)S(1)} collective-permute-done((bf16[272,512]{1,0:T(8,128)(2,1)S(1)}, bf16[272,512]{1,0:T(8,128)(2,1)S(1)}, u32[]{:S(2)}, u32[]{:S(2)}) %collective-permute-start.43) | collective-permute-done | bytes 278560 | tf_op jit(solution)/shard_map/ppermute | solution.py:21
  533.0 4.3 shard_map.418
  538.9 8.3 %shard_map.419 = (bf16[272,512]{1,0:T(8,128)(2,1)}, bf16[544,512]{1,0:T(8,128)(2,1)}, bf16[544,512]{1,0:T(8,128)(2,1)}, bf16[544,512]{1,0:T(8,128)(2,1)}, bf16[544,512]{1,0:T(8,128)(2,1)}) custom-call(bf16[272,512]{1,0:T(8,128)(2,1)} %copy-done.38, bf16[2176,512]{1,0:T(8,128)(2,1)} %copy-done.34, s32[272,1]{1,0:T(8,128)} %copy-done.33, ...), custom_call_target="tpu_custom_call" | custom-call | flops 3030384640 | bytes 6137408 | tf_op jit(solution)/shard_map/pallas_call | solution.py:105
  557.0 3.2 collective-permute-done.49
  573.7 10.0 %shard_map.420 = (bf16[4,200,1024]{2,1,0:T(8,128)(2,1)S(1)}, bf16[4,200,1024]{2,1,0:T(8,128)(2,1)}, bf16[4,200,1024]{2,1,0:T(8,128)(2,1)}, bf16[4,200,1024]{2,1,...) custom-call(s32[1]{0:T(128)} %bitcast.44.refs_0_, ...), custom_call_target="tpu_custom_call" | custom-call | flops 2281701376 | bytes 16482312 | tf_op jit(solution)/shard_map/pallas_call | solution.py:105
  588.5 3.9 collective-permute-start.51
  602.9 7.3 %shard_map.423 = (f32[256,4096]{1,0:T(8,128)}, f32[256,4096]{1,0:T(8,128)}) custom-call(bf16[8,256,1024]{2,1,0:T(8,128)(2,1)} %all-to-all-done.2.in_ref), custom_call_target="tpu_custom_call" | custom-call | bytes 12582912 | tf_op jit(solution)/shard_map/pallas_call | solution.py:658
  610.2 5.4 collective-permute-done.52.refs_2_
  617.8 3.5 add_convert_fusion.2
  621.5 3.5 add_convert_fusion.3
  630.2 5.9 collective-permute-start.36
  647.1 12.5 %collective-permute-done.37 = bf16[272,512]{1,0:T(8,128)(2,1)} collective-permute-done((bf16[272,512]{1,0:T(8,128)(2,1)}, bf16[272,512]{1,0:T(8,128)(2,1)}, u32[]{:S(2)}, u32[]{:S(2)}) %collective-permute-start.37) | collective-permute-done | bytes 278560 | tf_op jit(solution)/shard_map/ppermute | solution.py:21
  677.9 5.2 collective-permute-start.60
  686.9 4.1 collective-permute-done.61
  (407 shorter events, 202.3 us)
Async XLA Ops:
  7.2 72.0 %all-gather.5.cloned.1.call-start = ((), (), s32[]{:S(2)}) async-start(), calls=%async_computation.8 | async-start | bytes 7225344 | tf_op jit(solution)/shard_map/all_gather | solution.py:728
  10.3 160.9 %all-gather.7.cloned.1.call-start = ((), (), s32[]{:S(2)}) async-start(), calls=%async_computation.9 | async-start | bytes 3538944 | tf_op jit(solution)/shard_map/all_gather | solution.py:803
  10.6 20.0 %collective-permute-start = (bf16[136,2048]{1,0:T(8,128)(2,1)S(1)}, bf16[136,2048]{1,0:T(8,128)(2,1)S(1)}, u32[]{:S(2)}, u32[]{:S(2)}) collective-permute-start(bf16[136,2048]{1,0:T(8,128)(2,1)S(1)} %pad_maximum_fusion.5), channel_id=1, source_target_pairs={{0,8},{4,12},{8,0},{12,4},{16,24},{20,28},{24,16},{28,20},{1,9},{5... | collective-permute-start | bytes 1671176 | tf_op jit(solution)/shard_map/ppermute | solution.py:21
  13.6 20.7 %collective-permute-start.28 = (bf16[136,2048]{1,0:T(8,128)(2,1)S(1)}, bf16[136,2048]{1,0:T(8,128)(2,1)S(1)}, u32[]{:S(2)}, u32[]{:S(2)}) collective-permute-start(bf16[136,2048]{1,0:T(8,128)(2,1)S(1)} %pad_maximum_fusion.5), channel_id=1, source_target_pairs={{0,16},{4,20},{8,24},{12,28},{16,0},{20,4},{24,8},{28,12},{1,17},{... | collective-permute-start | bytes 1671176 | tf_op jit(solution)/shard_map/ppermute | solution.py:21
  30.6 19.9 %collective-permute-start.1 = (bf16[136,2048]{1,0:T(8,128)(2,1)S(1)}, bf16[136,2048]{1,0:T(8,128)(2,1)S(1)}, u32[]{:S(2)}, u32[]{:S(2)}) collective-permute-start(bf16[136,2048]{1,0:T(8,128)(2,1)S(1)} %collective-permute-done), channel_id=1, source_target_pairs={{0,16},{4,20},{8,24},{12,28},{16,0},{20,4},{24,8},{28,12},{1,17},{... | collective-permute-start | bytes 1671176 | tf_op jit(solution)/shard_map/ppermute | solution.py:21
  50.7 26.4 %collective-permute-start.2 = (bf16[136,2048]{1,0:T(8,128)(2,1)S(1)}, bf16[136,2048]{1,0:T(8,128)(2,1)S(1)}, u32[]{:S(2)}, u32[]{:S(2)}) collective-permute-start(bf16[136,2048]{1,0:T(8,128)(2,1)S(1)} %pad_maximum_fusion.6), channel_id=1, source_target_pairs={{0,16},{4,20},{8,24},{12,28},{16,0},{20,4},{24,8},{28,12},{1,17},{... | collective-permute-start | bytes 1671176 | tf_op jit(solution)/shard_map/ppermute | solution.py:21
  53.3 27.5 %collective-permute-start.4 = (bf16[272,512]{1,0:T(8,128)(2,1)S(1)}, bf16[272,512]{1,0:T(8,128)(2,1)S(1)}, u32[]{:S(2)}, u32[]{:S(2)}) collective-permute-start(bf16[272,512]{1,0:T(8,128)(2,1)S(1)} %fusion.25.refs_0_.refs_4_), channel_id=1, source_target_pairs={{0,1},{1,0},{2,3},{3,2},{4,5},{5,4},{6,7},{7,6},{8,9},{9,8},{10,11... | collective-permute-start | bytes 835592 | tf_op jit(solution)/shard_map/ppermute | solution.py:21
  54.6 26.2 %collective-permute-start.5 = (bf16[272,512]{1,0:T(8,128)(2,1)S(1)}, bf16[272,512]{1,0:T(8,128)(2,1)S(1)}, u32[]{:S(2)}, u32[]{:S(2)}) collective-permute-start(bf16[272,512]{1,0:T(8,128)(2,1)S(1)} %fusion.25.refs_0_.refs_4_), channel_id=1, source_target_pairs={{0,2},{1,3},{2,0},{3,1},{4,6},{5,7},{6,4},{7,5},{8,10},{9,11},{10,... | collective-permute-start | bytes 835592 | tf_op jit(solution)/shard_map/ppermute | solution.py:21
  57.4 23.4 %collective-permute-start.6 = (bf16[272,512]{1,0:T(8,128)(2,1)S(1)}, bf16[272,512]{1,0:T(8,128)(2,1)S(1)}, u32[]{:S(2)}, u32[]{:S(2)}) collective-permute-start(bf16[272,512]{1,0:T(8,128)(2,1)S(1)} %fusion.25.refs_0_.refs_4_), channel_id=1, source_target_pairs={{0,3},{1,2},{2,1},{3,0},{4,7},{5,6},{6,5},{7,4},{8,11},{9,10},{10,... | collective-permute-start | bytes 835592 | tf_op jit(solution)/shard_map/ppermute | solution.py:21
  113.8 87.7 %all-to-all-start.1 = ((bf16[8,704,256]{2,1,0:T(8,128)(2,1)}), bf16[8,704,256]{2,1,0:T(8,128)(2,1)}, u32[]{:S(2)}, u32[]{:S(2)}) async-start(bf16[8,704,256]{2,1,0:T(8,128)(2,1)} %pad_maximum_fusion.1), calls=%async_computation.1 | async-start | bytes 5767168 | tf_op jit(solution)/shard_map/all_to_all | solution.py:804
  118.5 46.7 %collective-permute-start.3 = (bf16[136,2048]{1,0:T(8,128)(2,1)S(1)}, bf16[136,2048]{1,0:T(8,128)(2,1)}, u32[]{:S(2)}, u32[]{:S(2)}) collective-permute-start(bf16[136,2048]{1,0:T(8,128)(2,1)S(1)} %copy-done.63), channel_id=1, source_target_pairs={{0,8},{4,12},{8,0},{12,4},{16,24},{20,28},{24,16},{28,20},{1,9},{5... | collective-permute-start | bytes 1671176 | tf_op jit(solution)/shard_map/ppermute | solution.py:21
  178.1 22.4 %collective-permute-start.16 = (bf16[272,512]{1,0:T(8,128)(2,1)S(1)}, bf16[272,512]{1,0:T(8,128)(2,1)S(1)}, u32[]{:S(2)}, u32[]{:S(2)}) collective-permute-start(bf16[272,512]{1,0:T(8,128)(2,1)S(1)} %get-tuple-element.105), channel_id=1, source_target_pairs={{0,2},{1,3},{2,0},{3,1},{4,6},{5,7},{6,4},{7,5},{8,10},{9,11},{10,... | collective-permute-start | bytes 835592 | tf_op jit(solution)/shard_map/ppermute | solution.py:21
  180.5 20.0 %collective-permute-start.17 = (bf16[272,512]{1,0:T(8,128)(2,1)S(1)}, bf16[272,512]{1,0:T(8,128)(2,1)S(1)}, u32[]{:S(2)}, u32[]{:S(2)}) collective-permute-start(bf16[272,512]{1,0:T(8,128)(2,1)S(1)} %get-tuple-element.106), channel_id=1, source_target_pairs={{0,3},{1,2},{2,1},{3,0},{4,7},{5,6},{6,5},{7,4},{8,11},{9,10},{10,... | collective-permute-start | bytes 835592 | tf_op jit(solution)/shard_map/ppermute | solution.py:21
  201.6 54.3 %all-to-all-start = ((bf16[8,256,1024]{2,1,0:T(8,128)(2,1)}), bf16[8,256,1024]{2,1,0:T(8,128)(2,1)}, u32[]{:S(2)}, u32[]{:S(2)}) async-start(bf16[8,256,1024]{2,1,0:T(8,128)(2,1)} %pad_maximum_fusion), calls=%async_computation | async-start | bytes 8388608 | tf_op jit(solution)/shard_map/all_to_all | solution.py:814
  206.3 420.3 %reduce-scatter.3.cloned.1.call-start = ((), (), s32[]{:S(2)}) async-start(), calls=%async_computation.6 | async-start | bytes 10027008 | tf_op jit(solution)/shard_map/reduce_scatter | solution.py:890
  206.6 60.2 %collective-permute-start.29 = (bf16[136,2048]{1,0:T(8,128)(2,1)S(1)}, bf16[136,2048]{1,0:T(8,128)(2,1)S(1)}, u32[]{:S(2)}, u32[]{:S(2)}) collective-permute-start(bf16[136,2048]{1,0:T(8,128)(2,1)S(1)} %copy-done.61), channel_id=1, source_target_pairs={{0,8},{4,12},{8,0},{12,4},{16,24},{20,28},{24,16},{28,20},{1,9},{5... | collective-permute-start | bytes 1671176 | tf_op jit(solution)/shard_map/ppermute | solution.py:21
  208.5 47.4 %collective-permute-start.18 = (bf16[272,512]{1,0:T(8,128)(2,1)S(1)}, bf16[272,512]{1,0:T(8,128)(2,1)S(1)}, u32[]{:S(2)}, u32[]{:S(2)}) collective-permute-start(bf16[272,512]{1,0:T(8,128)(2,1)S(1)} %get-tuple-element.110.refs_0_), channel_id=1, source_target_pairs={{0,1},{1,0},{2,3},{3,2},{4,5},{5,4},{6,7},{7,6},{8,9},{9,8},{10,11... | collective-permute-start | bytes 835592 | tf_op jit(solution)/shard_map/ppermute | solution.py:21
  213.7 42.2 %collective-permute-start.19 = (bf16[272,512]{1,0:T(8,128)(2,1)S(1)}, bf16[272,512]{1,0:T(8,128)(2,1)S(1)}, u32[]{:S(2)}, u32[]{:S(2)}) collective-permute-start(bf16[272,512]{1,0:T(8,128)(2,1)S(1)} %get-tuple-element.110.refs_0_), channel_id=1, source_target_pairs={{0,2},{1,3},{2,0},{3,1},{4,6},{5,7},{6,4},{7,5},{8,10},{9,11},{10,... | collective-permute-start | bytes 835592 | tf_op jit(solution)/shard_map/ppermute | solution.py:21
  214.6 41.3 %collective-permute-start.20 = (bf16[272,512]{1,0:T(8,128)(2,1)S(1)}, bf16[272,512]{1,0:T(8,128)(2,1)S(1)}, u32[]{:S(2)}, u32[]{:S(2)}) collective-permute-start(bf16[272,512]{1,0:T(8,128)(2,1)S(1)} %get-tuple-element.110.refs_0_), channel_id=1, source_target_pairs={{0,3},{1,2},{2,1},{3,0},{4,7},{5,6},{6,5},{7,4},{8,11},{9,10},{10,... | collective-permute-start | bytes 835592 | tf_op jit(solution)/shard_map/ppermute | solution.py:21
  256.4 21.8 %collective-permute-start.21 = (bf16[136,2048]{1,0:T(8,128)(2,1)S(1)}, bf16[136,2048]{1,0:T(8,128)(2,1)S(1)}, u32[]{:S(2)}, u32[]{:S(2)}) collective-permute-start(bf16[136,2048]{1,0:T(8,128)(2,1)S(1)} %get-tuple-element.111), channel_id=1, source_target_pairs={{0,8},{4,12},{8,0},{12,4},{16,24},{20,28},{24,16},{28,20},{1,9},{5... | collective-permute-start | bytes 1671176 | tf_op jit(solution)/shard_map/ppermute | solution.py:21
  257.5 23.7 %collective-permute-start.24 = (bf16[136,2048]{1,0:T(8,128)(2,1)S(1)}, bf16[136,2048]{1,0:T(8,128)(2,1)S(1)}, u32[]{:S(2)}, u32[]{:S(2)}) collective-permute-start(bf16[136,2048]{1,0:T(8,128)(2,1)S(1)} %get-tuple-element.112), channel_id=1, source_target_pairs={{0,16},{4,20},{8,24},{12,28},{16,0},{20,4},{24,8},{28,12},{1,17},{... | collective-permute-start | bytes 1671176 | tf_op jit(solution)/shard_map/ppermute | solution.py:21
  267.6 17.3 %collective-permute-start.22 = (bf16[136,2048]{1,0:T(8,128)(2,1)S(1)}, bf16[136,2048]{1,0:T(8,128)(2,1)S(1)}, u32[]{:S(2)}, u32[]{:S(2)}) collective-permute-start(bf16[136,2048]{1,0:T(8,128)(2,1)S(1)} %get-tuple-element.111), channel_id=1, source_target_pairs={{0,16},{4,20},{8,24},{12,28},{16,0},{20,4},{24,8},{28,12},{1,17},{... | collective-permute-start | bytes 1671176 | tf_op jit(solution)/shard_map/ppermute | solution.py:21
  271.0 37.2 %collective-permute-start.30 = (bf16[1088,2048]{1,0:T(8,128)(2,1)}, bf16[1088,2048]{1,0:T(8,128)(2,1)S(1)}, u32[]{:S(2)}, u32[]{:S(2)}) collective-permute-start(bf16[1088,2048]{1,0:T(8,128)(2,1)} %constant_dynamic-update-slice_fusion.18.refs_1_.ce_ref), channel_id=1, source_target_pairs={{0,4},{4,0},{8,12},{12,8},{16,20},{20,16},{24,28},{28,24},{1,5},{5... | collective-permute-start | bytes 13369352 | tf_op jit(solution)/shard_map/ppermute | solution.py:21
  278.2 17.3 %collective-permute-start.23 = (bf16[136,2048]{1,0:T(8,128)(2,1)S(1)}, bf16[136,2048]{1,0:T(8,128)(2,1)S(1)}, u32[]{:S(2)}, u32[]{:S(2)}) collective-permute-start(bf16[136,2048]{1,0:T(8,128)(2,1)S(1)} %collective-permute-done.21), channel_id=1, source_target_pairs={{0,16},{4,20},{8,24},{12,28},{16,0},{20,4},{24,8},{28,12},{1,17},{... | collective-permute-start | bytes 1671176 | tf_op jit(solution)/shard_map/ppermute | solution.py:21
  280.6 17.5 %collective-permute-start.25 = (bf16[136,2048]{1,0:T(8,128)(2,1)S(1)}, bf16[136,2048]{1,0:T(8,128)(2,1)S(1)}, u32[]{:S(2)}, u32[]{:S(2)}) collective-permute-start(bf16[136,2048]{1,0:T(8,128)(2,1)S(1)} %get-tuple-element.112), channel_id=1, source_target_pairs={{0,8},{4,12},{8,0},{12,4},{16,24},{20,28},{24,16},{28,20},{1,9},{5... | collective-permute-start | bytes 1671176 | tf_op jit(solution)/shard_map/ppermute | solution.py:21
  281.2 25.2 %collective-permute-start.26 = (bf16[136,2048]{1,0:T(8,128)(2,1)S(1)}, bf16[136,2048]{1,0:T(8,128)(2,1)S(1)}, u32[]{:S(2)}, u32[]{:S(2)}) collective-permute-start(bf16[136,2048]{1,0:T(8,128)(2,1)S(1)} %collective-permute-done.24), channel_id=1, source_target_pairs={{0,8},{4,12},{8,0},{12,4},{16,24},{20,28},{24,16},{28,20},{1,9},{5... | collective-permute-start | bytes 1671176 | tf_op jit(solution)/shard_map/ppermute | solution.py:21
  338.5 24.9 %collective-permute-start.31 = (bf16[1088,2048]{1,0:T(8,128)(2,1)}, bf16[1088,2048]{1,0:T(8,128)(2,1)}, u32[]{:S(2)}, u32[]{:S(2)}) collective-permute-start(bf16[1088,2048]{1,0:T(8,128)(2,1)} %get-tuple-element.118), channel_id=1, source_target_pairs={{0,4},{4,0},{8,12},{12,8},{16,20},{20,16},{24,28},{28,24},{1,5},{5... | collective-permute-start | bytes 13369352 | tf_op jit(solution)/shard_map/ppermute | solution.py:21
  368.0 26.5 %collective-permute-start.34 = (bf16[2,136,2048]{2,1,0:T(8,128)(2,1)S(1)}, bf16[2,136,2048]{2,1,0:T(8,128)(2,1)S(1)}, u32[]{:S(2)}, u32[]{:S(2)}) collective-permute-start(bf16[2,136,2048]{2,1,0:T(8,128)(2,1)S(1)} %bitcast.234), channel_id=1, source_target_pairs={{0,8},{4,12},{8,0},{12,4},{16,24},{20,28},{24,16},{28,20},{1,9},{5... | collective-permute-start | bytes 3342344 | tf_op jit(solution)/shard_map/ppermute | solution.py:21
  368.6 27.5 %collective-permute-start.32 = (bf16[2,136,2048]{2,1,0:T(8,128)(2,1)S(1)}, bf16[2,136,2048]{2,1,0:T(8,128)(2,1)S(1)}, u32[]{:S(2)}, u32[]{:S(2)}) collective-permute-start(bf16[2,136,2048]{2,1,0:T(8,128)(2,1)S(1)} %bitcast.233), channel_id=1, source_target_pairs={{0,16},{4,20},{8,24},{12,28},{16,0},{20,4},{24,8},{28,12},{1,17},{... | collective-permute-start | bytes 3342344 | tf_op jit(solution)/shard_map/ppermute | solution.py:21
  395.6 13.9 %collective-permute-start.35 = (bf16[136,2048]{1,0:T(8,128)(2,1)}, bf16[136,2048]{1,0:T(8,128)(2,1)S(1)}, u32[]{:S(2)}, u32[]{:S(2)}) collective-permute-start(bf16[136,2048]{1,0:T(8,128)(2,1)} %get-tuple-element.125), channel_id=1, source_target_pairs={{0,16},{4,20},{8,24},{12,28},{16,0},{20,4},{24,8},{28,12},{1,17},{... | collective-permute-start | bytes 1671176 | tf_op jit(solution)/shard_map/ppermute | solution.py:21
  458.8 106.4 %all-to-all-start.2 = ((bf16[8,256,1024]{2,1,0:T(8,128)(2,1)}), bf16[8,256,1024]{2,1,0:T(8,128)(2,1)}, u32[]{:S(2)}, u32[]{:S(2)}) async-start(bf16[8,256,1024]{2,1,0:T(8,128)(2,1)} %bitcast.229), calls=%async_computation.3 | async-start | bytes 8388608 | tf_op jit(solution)/shard_map/all_to_all | solution.py:892
  463.4 182.7 %reduce-scatter.5.cloned.1.call-start = ((), (), s32[]{:S(2)}) async-start(), calls=%async_computation.7 | async-start | bytes 3538944 | tf_op jit(solution)/shard_map/reduce_scatter | solution.py:928
  473.6 21.1 %collective-permute-start.39 = (bf16[272,512]{1,0:T(8,128)(2,1)S(1)}, bf16[272,512]{1,0:T(8,128)(2,1)S(1)}, u32[]{:S(2)}, u32[]{:S(2)}) collective-permute-start(bf16[272,512]{1,0:T(8,128)(2,1)S(1)} %get-tuple-element.136), channel_id=1, source_target_pairs={{0,1},{1,0},{2,3},{3,2},{4,5},{5,4},{6,7},{7,6},{8,9},{9,8},{10,11... | collective-permute-start | bytes 835592 | tf_op jit(solution)/shard_map/ppermute | solution.py:21
  482.5 22.4 %collective-permute-start.40 = (bf16[272,512]{1,0:T(8,128)(2,1)S(1)}, bf16[272,512]{1,0:T(8,128)(2,1)S(1)}, u32[]{:S(2)}, u32[]{:S(2)}) collective-permute-start(bf16[272,512]{1,0:T(8,128)(2,1)S(1)} %get-tuple-element.137), channel_id=1, source_target_pairs={{0,2},{1,3},{2,0},{3,1},{4,6},{5,7},{6,4},{7,5},{8,10},{9,11},{10,... | collective-permute-start | bytes 835592 | tf_op jit(solution)/shard_map/ppermute | solution.py:21
  483.5 21.4 %collective-permute-start.41 = (bf16[272,512]{1,0:T(8,128)(2,1)S(1)}, bf16[272,512]{1,0:T(8,128)(2,1)S(1)}, u32[]{:S(2)}, u32[]{:S(2)}) collective-permute-start(bf16[272,512]{1,0:T(8,128)(2,1)S(1)} %get-tuple-element.138), channel_id=1, source_target_pairs={{0,3},{1,2},{2,1},{3,0},{4,7},{5,6},{6,5},{7,4},{8,11},{9,10},{10,... | collective-permute-start | bytes 835592 | tf_op jit(solution)/shard_map/ppermute | solution.py:21
  505.1 16.2 %collective-permute-start.42 = (bf16[272,512]{1,0:T(8,128)(2,1)S(1)}, bf16[272,512]{1,0:T(8,128)(2,1)S(1)}, u32[]{:S(2)}, u32[]{:S(2)}) collective-permute-start(bf16[272,512]{1,0:T(8,128)(2,1)S(1)} %add_convert_fusion.6.refs_0_), channel_id=1, source_target_pairs={{0,1},{1,0},{2,3},{3,2},{4,5},{5,4},{6,7},{7,6},{8,9},{9,8},{10,11... | collective-permute-start | bytes 835592 | tf_op jit(solution)/shard_map/ppermute | solution.py:21
  510.5 22.4 %collective-permute-start.43 = (bf16[272,512]{1,0:T(8,128)(2,1)S(1)}, bf16[272,512]{1,0:T(8,128)(2,1)S(1)}, u32[]{:S(2)}, u32[]{:S(2)}) collective-permute-start(bf16[272,512]{1,0:T(8,128)(2,1)S(1)} %add_convert_fusion.6.refs_0_), channel_id=1, source_target_pairs={{0,2},{1,3},{2,0},{3,1},{4,6},{5,7},{6,4},{7,5},{8,10},{9,11},{10,... | collective-permute-start | bytes 835592 | tf_op jit(solution)/shard_map/ppermute | solution.py:21
  511.5 21.4 %collective-permute-start.44 = (bf16[272,512]{1,0:T(8,128)(2,1)S(1)}, bf16[272,512]{1,0:T(8,128)(2,1)S(1)}, u32[]{:S(2)}, u32[]{:S(2)}) collective-permute-start(bf16[272,512]{1,0:T(8,128)(2,1)S(1)} %add_convert_fusion.6.refs_0_), channel_id=1, source_target_pairs={{0,3},{1,2},{2,1},{3,0},{4,7},{5,6},{6,5},{7,4},{8,11},{9,10},{10,... | collective-permute-start | bytes 835592 | tf_op jit(solution)/shard_map/ppermute | solution.py:21
  584.4 33.4 %collective-permute-start.57 = (bf16[4,200,1024]{2,1,0:T(8,128)(2,1)}, bf16[4,200,1024]{2,1,0:T(8,128)(2,1)}, u32[]{:S(2)}, u32[]{:S(2)}) collective-permute-start(bf16[4,200,1024]{2,1,0:T(8,128)(2,1)} %get-tuple-element.163), channel_id=1, source_target_pairs={{0,4},{4,0},{8,12},{12,8},{16,20},{20,16},{24,28},{28,24},{1,5},{5... | collective-permute-start | bytes 4915208 | tf_op jit(solution)/shard_map/ppermute | solution.py:21
  584.4 37.1 %collective-permute-start.54 = (bf16[4,200,1024]{2,1,0:T(8,128)(2,1)}, bf16[4,200,1024]{2,1,0:T(8,128)(2,1)}, u32[]{:S(2)}, u32[]{:S(2)}) collective-permute-start(bf16[4,200,1024]{2,1,0:T(8,128)(2,1)} %get-tuple-element.160), channel_id=1, source_target_pairs={{0,4},{4,0},{8,12},{12,8},{16,20},{20,16},{24,28},{28,24},{1,5},{5... | collective-permute-start | bytes 4915208 | tf_op jit(solution)/shard_map/ppermute | solution.py:21
  588.5 21.7 %collective-permute-start.51 = (bf16[280,512]{1,0:T(8,128)(2,1)}, bf16[280,512]{1,0:T(8,128)(2,1)S(1)}, u32[]{:S(2)}, u32[]{:S(2)}) collective-permute-start(bf16[280,512]{1,0:T(8,128)(2,1)} %get-tuple-element.153), channel_id=1, source_target_pairs={{0,1},{1,0},{2,3},{3,2},{4,5},{5,4},{6,7},{7,6},{8,9},{9,8},{10,11... | collective-permute-start | bytes 860168 | tf_op jit(solution)/shard_map/ppermute | solution.py:21
  592.4 23.2 %collective-permute-start.52 = (bf16[280,512]{1,0:T(8,128)(2,1)}, bf16[280,512]{1,0:T(8,128)(2,1)}, u32[]{:S(2)}, u32[]{:S(2)}) collective-permute-start(bf16[280,512]{1,0:T(8,128)(2,1)} %get-tuple-element.154), channel_id=1, source_target_pairs={{0,2},{1,3},{2,0},{3,1},{4,6},{5,7},{6,4},{7,5},{8,10},{9,11},{10,... | collective-permute-start | bytes 860168 | tf_op jit(solution)/shard_map/ppermute | solution.py:21
  593.3 22.3 %collective-permute-start.53 = (bf16[280,512]{1,0:T(8,128)(2,1)}, bf16[280,512]{1,0:T(8,128)(2,1)}, u32[]{:S(2)}, u32[]{:S(2)}) collective-permute-start(bf16[280,512]{1,0:T(8,128)(2,1)} %get-tuple-element.155), channel_id=1, source_target_pairs={{0,3},{1,2},{2,1},{3,0},{4,7},{5,6},{6,5},{7,4},{8,11},{9,10},{10,... | collective-permute-start | bytes 860168 | tf_op jit(solution)/shard_map/ppermute | solution.py:21
  621.2 19.2 %collective-permute-start.58 = (bf16[2,200,1024]{2,1,0:T(8,128)(2,1)}, bf16[2,200,1024]{2,1,0:T(8,128)(2,1)}, u32[]{:S(2)}, u32[]{:S(2)}) collective-permute-start(bf16[2,200,1024]{2,1,0:T(8,128)(2,1)} %get-tuple-element.224), channel_id=1, source_target_pairs={{0,8},{4,12},{8,0},{12,4},{16,24},{20,28},{24,16},{28,20},{1,9},{5... | collective-permute-start | bytes 2457608 | tf_op jit(solution)/shard_map/ppermute | solution.py:21
  625.0 19.1 %collective-permute-start.55 = (bf16[2,200,1024]{2,1,0:T(8,128)(2,1)}, bf16[2,200,1024]{2,1,0:T(8,128)(2,1)}, u32[]{:S(2)}, u32[]{:S(2)}) collective-permute-start(bf16[2,200,1024]{2,1,0:T(8,128)(2,1)} %get-tuple-element.226), channel_id=1, source_target_pairs={{0,16},{4,20},{8,24},{12,28},{16,0},{20,4},{24,8},{28,12},{1,17},{... | collective-permute-start | bytes 2457608 | tf_op jit(solution)/shard_map/ppermute | solution.py:21
  630.2 16.9 %collective-permute-start.36 = (bf16[272,512]{1,0:T(8,128)(2,1)}, bf16[272,512]{1,0:T(8,128)(2,1)}, u32[]{:S(2)}, u32[]{:S(2)}) collective-permute-start(bf16[272,512]{1,0:T(8,128)(2,1)} %fusion.27), channel_id=1, source_target_pairs={{0,1},{1,0},{2,3},{3,2},{4,5},{5,4},{6,7},{7,6},{8,9},{9,8},{10,11... | collective-permute-start | bytes 835592 | tf_op jit(solution)/shard_map/ppermute | solution.py:21
  636.8 22.8 %collective-permute-start.37 = (bf16[272,512]{1,0:T(8,128)(2,1)}, bf16[272,512]{1,0:T(8,128)(2,1)}, u32[]{:S(2)}, u32[]{:S(2)}) collective-permute-start(bf16[272,512]{1,0:T(8,128)(2,1)} %fusion.28), channel_id=1, source_target_pairs={{0,2},{1,3},{2,0},{3,1},{4,6},{5,7},{6,4},{7,5},{8,10},{9,11},{10,... | collective-permute-start | bytes 835592 | tf_op jit(solution)/shard_map/ppermute | solution.py:21
  638.5 21.1 %collective-permute-start.38 = (bf16[272,512]{1,0:T(8,128)(2,1)}, bf16[272,512]{1,0:T(8,128)(2,1)}, u32[]{:S(2)}, u32[]{:S(2)}) collective-permute-start(bf16[272,512]{1,0:T(8,128)(2,1)} %fusion.29), channel_id=1, source_target_pairs={{0,3},{1,2},{2,1},{3,0},{4,7},{5,6},{6,5},{7,4},{8,11},{9,10},{10,... | collective-permute-start | bytes 835592 | tf_op jit(solution)/shard_map/ppermute | solution.py:21
  (100 other events, 1269.0 us)
Sparse Core Ops, SparseCore 0:
  10.5 68.6 all-gather.4
  87.4 37.7 all-gather.6
  411.1 114.3 reduce-scatter.2
  550.6 49.3 reduce-scatter.4

commit v4 on v3

--- a/solution.py
+++ b/solution.py
@@ -48,8 +48,17 @@
     return results
 
 
-def near_rows(far):
-    even = jnp.concatenate([b for blocks in far for b in blocks], axis=0)
+def gather_stacked(halves):
+    stages = [list(halves)]
+    for step in range(len(far_masks()[0])):
+        got = [swap(b, "seq", masks[step]) for b, masks in zip(stages[-1], far_masks())]
+        got = lax.optimization_barrier(got)
+        stages.append([jnp.concatenate(pair, axis=0) for pair in zip(stages[-1], got)])
+    return stages[1:]
+
+
+def near_rows(blocks):
+    even = jnp.concatenate(blocks, axis=0)
     return swap(even, "seq", 1), even
 
 
@@ -59,17 +68,20 @@
 
 def scatter_rows(halves, token=None):
     results = []
+    firsts = []
     for (mine, other), masks in zip(halves, far_masks()):
         for mask in masks[:0:-1]:
             keep = mine.shape[0] // 2
-            got = swap(add(mine[keep:], other[keep:]).astype(BF), "seq", mask)
+            sent = add(mine[keep:], other[keep:]).astype(BF)
+            firsts.append(sent)
+            got = swap(sent, "seq", mask)
             mine, other = add(mine[:keep], other[:keep]), got
         sent = add(mine[1], other[1]).astype(BF)
         if token is not None:
             sent = after(sent, token)
         got = swap(sent, "seq", masks[0])
         results.append((add(mine[0], other[0]), got))
-    return results
+    return results, firsts[:: max(1, len(firsts) // 2)]
 
 
 def gather_tp(piece):
@@ -354,7 +366,7 @@
             jax.ShapeDtypeStruct((total, 2 * f), BF),
             jax.ShapeDtypeStruct((total, dp), BF),
         ),
-        compiler_params=pltpu.CompilerParams(vmem_limit_bytes=48 * MIB),
+        compiler_params=pltpu.CompilerParams(vmem_limit_bytes=58 * MIB),
         cost_estimate=pl.CostEstimate(
             flops=10 * total * dp * f,
             bytes_accessed=8 * total * dp + 6 * f * dp,
@@ -645,26 +657,44 @@
         o_ref[...] = (r_ref[begin:end, :wide] + moved).astype(BF)
 
 
-def home_kernel(in_ref, gate_ref, up_ref):
+def home_kernel(token_ref, gu_ref, down_in_ref, gate_ref, up_ref, down_ref, act_ref):
+    del token_ref
     f = gate_ref.shape[1]
-    gate_ref[...] = in_ref[0, :, :f].astype(F32)
-    up_ref[...] = in_ref[0, :, f:].astype(F32)
-
-
-def home(got):
-    n, kp, both = got.shape
+    gate_ref[...] = gu_ref[0, :, :f].astype(F32)
+    up_ref[...] = gu_ref[0, :, f:].astype(F32)
+    down_ref[...] = down_in_ref[0, :f, :].astype(F32)
+    act_ref[0] = down_in_ref[0, f:, :].astype(F32)
+
+
+def home(token, got_gu, got_down):
+    n, kp, both = got_gu.shape
     f = both // 2
+    tall = got_down.shape[1]
     out = pl.BlockSpec((kp, f), lambda j: (0, j))
     return pl.pallas_call(
         home_kernel,
         grid=(n,),
-        in_specs=[pl.BlockSpec((1, kp, both), lambda j: (j, 0, 0))],
-        out_specs=(out, out),
-        out_shape=(jax.ShapeDtypeStruct((kp, n * f), F32),) * 2,
+        in_specs=[
+            pl.BlockSpec(memory_space=pltpu.SMEM),
+            pl.BlockSpec((1, kp, both), lambda j: (j, 0, 0)),
+            pl.BlockSpec((1, tall, kp), lambda j: (j, 0, 0)),
+        ],
+        out_specs=(
+            out,
+            out,
+            pl.BlockSpec((f, kp), lambda j: (j, 0)),
+            pl.BlockSpec((1, tall - f, kp), lambda j: (j, 0, 0)),
+        ),
+        out_shape=(
+            jax.ShapeDtypeStruct((kp, n * f), F32),
+            jax.ShapeDtypeStruct((kp, n * f), F32),
+            jax.ShapeDtypeStruct((n * f, kp), F32),
+            jax.ShapeDtypeStruct((n, tall - f, kp), F32),
+        ),
         cost_estimate=pl.CostEstimate(
-            flops=0, bytes_accessed=6 * n * kp * both, transcendentals=0
-        ),
-    )(got)
+            flops=0, bytes_accessed=6 * n * kp * (both + tall), transcendentals=0
+        ),
+    )(token, got_gu, got_down)
 
 
 def shards(
@@ -733,7 +763,7 @@
     mlp_gain_a = got_gains[:, 2 * kp + ka : 2 * kp + 2 * ka].reshape(1, da)
     pack_out = jnp.concatenate([prefix_out.T, action_out.T], axis=0)
     cot_wide = jnp.pad(cot_action, ((0, 0), (0, dp - da)))
-    cot_far = gather_far(
+    cot_stages = gather_stacked(
         [
             jnp.concatenate(
                 [
@@ -745,7 +775,7 @@
             for i in range(2)
         ]
     )
-    cot_odd, cot_even = near_rows(cot_far)
+    cot_odd, cot_even = near_rows(cot_stages[-1])
 
     def by_units(w, f):
         return w.reshape(w.shape[0], n, f).transpose(1, 0, 2)
@@ -772,7 +802,7 @@
             ((ra, da), BF),
             ((rows, 128), F32),
         ),
-        [after(rank_t, cot_far[0][1], cot_far[1][1]), *x_pieces, got_qkv, attn_gain_p, attn_gain_a],
+        [after(rank_t, cot_even), *x_pieces, got_qkv, attn_gain_p, attn_gain_a],
         2 * rp * dp * qkv_width,
     )
     kv_even = [jnp.concatenate(blocks, axis=0) for blocks in gather_far([kv_a, kv_b])]
@@ -806,31 +836,34 @@
     piece = (((rows, cp), BF),)
     branch = sum_tp(
         whole_call(
-            branch_kernel, piece * tp, [after(rank_t, cot_far[0][-1], cot_far[1][-1]), mixed, got_out], 2 * rows * dp * width
+            branch_kernel, piece * tp, [rank_t, mixed, got_out], 2 * rows * dp * width
         )
     )
     residual = x_pack.astype(F32) + branch
     mid_own = after(residual.astype(BF), down_got)
     gate_up = lax.all_to_all(after(gate_up_sent, branch), "seq", 0, 0).reshape(dp, 2 * fp)
+    down = down_got[:, :fp].transpose(1, 0, 2).reshape(fp, dp)
+    action_got = down_got[:, fp:].reshape(da, 3 * fa)
+    gate_up_action = action_got[:, : 2 * fa]
+    down_action = action_got[:, 2 * fa :].T
+
+
+    def action_rows(blocks):
+        return blocks.reshape(n, half, dp)[:, rp // 2 :, :da].reshape(-1, da)
+
+    cot_action_all = jnp.concatenate([action_rows(cot_odd), action_rows(cot_even)], axis=0)
     block = (((half, dp), BF),)
     mid_p, mid_a, normed_a, normed_b = whole_call(
         middle_kernel,
         (((rp, dp), BF), ((ra, da), BF)) + block * 2,
-        [after(rank_t, gate_up), *gather_tp(mid_own), mlp_gain_p, mlp_gain_a],
+        [after(rank_t, gate_up, down, gate_up_action, down_action, cot_action_all), *gather_tp(mid_own), mlp_gain_p, mlp_gain_a],
         rp * dp,
     )
 
-    normed_odd, normed_even = near_rows(gather_far([normed_a, normed_b]))
-    down = down_got[:, :fp].transpose(1, 0, 2).reshape(fp, dp)
-    action_got = down_got[:, fp:].reshape(da, 3 * fa)
-    gate_up_action = action_got[:, : 2 * fa]
-    down_action = action_got[:, 2 * fa :].T
-
-    def action_rows(blocks):
-        return blocks.reshape(n, half, dp)[:, rp // 2 :, :da].reshape(-1, da)
-
+    normed_odd, normed_even = near_rows(
+        [b for blocks in gather_far([normed_a, normed_b]) for b in blocks]
+    )
     normed_action = jnp.concatenate([action_rows(normed_odd), action_rows(normed_even)], axis=0)
-    cot_action_all = jnp.concatenate([action_rows(cot_odd), action_rows(cot_even)], axis=0)
     tokens = n * ra
     dn_action, lifted_action, grad_gu_action, grad_down_action = whole_call(
         feed_action_kernel,
@@ -853,6 +886,7 @@
         d.reshape(2, n // 2, half, dp) for d in (dn_even, swap(dn_odd, "seq", 1))
     ]
 
+    grad_gu_action, grad_down_action = after((grad_gu_action, grad_down_action), dn_even)
     action_grads = jnp.concatenate(
         [
             grad_gu_action.reshape(n, ka, 2 * fa),
@@ -875,22 +909,19 @@
     lifted = lift(
         odd_bits, *places, *lift_places, h_odd, h_even, lifted_action, down, half, ra
     )
-    (keep_a, got_a), (keep_b, got_b) = scatter_rows(
+    ((keep_a, got_a), (keep_b, got_b)), _ = scatter_rows(
         [(dn_blocks[0][i], dn_blocks[1][i]) for i in range(2)], grad_gu
     )
-    dn_own = sum_tp(
-        whole_call(
-            pieces_kernel,
-            piece * tp,
-            [after(rank_t, lifted), keep_a, got_a, keep_b, got_b],
-            rp * dp,
-        )
-    )
+    sent_pieces = whole_call(
+        pieces_kernel,
+        piece * tp,
+        [after(rank_t, lifted), keep_a, got_a, keep_b, got_b],
+        rp * dp,
+    )
+    dn_own = sum_tp(sent_pieces)
     dn_pieces = gather_tp(dn_own.astype(BF))
     lifted_home = lax.psum_scatter(after(lifted, got_a, got_b), "seq", scatter_dimension=0)
-    grad_gu, grad_down = after((grad_gu, grad_down), got_a, got_b)
-    grad_gu_home = lax.all_to_all(grad_gu.reshape(n, kp, 2 * fp), "seq", 0, 0)
-    grad_down_home = lax.all_to_all(grad_down, "seq", 0, 0)
+    grad_down_home = lax.all_to_all(after(grad_down, sent_pieces[0]), "seq", 0, 0)
 
     row = ((1, dp), F32)
     row_a = ((1, da), F32)
@@ -906,6 +937,9 @@
             pltpu.VMEM((ra, da), F32),
         ),
     )
+    grad_gu_home = lax.all_to_all(
+        after(grad_gu, grad_down_home, dbranch_a).reshape(n, kp, 2 * fp), "seq", 0, 0
+    )
     dquery, *dkv_parts = whole_call(
         attend_back_kernel,
         (((rows, width), BF),) + (((n * rows // 4, 2 * HD), BF),) * 4,
@@ -918,7 +952,7 @@
         [d.reshape(n // 2, half, 2 * HD) for d in (e, swap(o, "seq", 1))]
         for e, o in ((dkv_parts[0], dkv_parts[1]), (dkv_parts[2], dkv_parts[3]))
     ]
-    dkv = [part for pair in scatter_rows(dkv_halves) for part in pair]
+    dkv = [part for pair in scatter_rows(dkv_halves)[0] for part in pair]
     (out_grads,) = whole_call(
         out_grad_kernel,
         (((n, kp + ka, width), BF),),
@@ -926,33 +960,6 @@
         2 * rows * dp * width,
     )
     out_home = lax.psum_scatter(out_grads, "seq", scatter_dimension=0).astype(F32)
-    tall = (kp + ka) // 2 + 8
-    *groups_and_pieces, = whole_call(
-        lambda *refs: front_back_kernel(width, *refs),
-        (((n // 2, tall, qkv_width), BF),) * 4 + (((rows + 8, cp), BF),) * tp,
-        [
-            after(rank_s, grad_gu_home), rank_t, dquery, *dkv, x_full_p, x_full_a, inverse1, attn_gain_p, attn_gain_a,
-            got_qkv, mlp_gains_p, mlp_gains_a,
-        ],
-        4 * rows * dp * qkv_width,
-        scratch=(
-            pltpu.VMEM((dp, qkv_width), BF),
-            pltpu.VMEM((da, qkv_width), BF),
-            pltpu.VMEM((n, 8, qkv_width), F32),
-            pltpu.VMEM((rp, dp), F32),
-            pltpu.VMEM((ra, da), F32),
-        ),
-    )
-    groups, pieces = groups_and_pieces[:4], groups_and_pieces[4:]
-    grad_x_p, grad_x_a = whole_call(
-        grad_x_kernel,
-        (((rp, cp), BF), ((ra, ca), BF)),
-        [
-            rank_t, pieces[0], *[swap(pieces[k], "tp", k) for k in range(1, tp)], x_pack,
-            inverse1, attn_gain_p, attn_gain_a, dresid,
-        ],
-        rp * dp,
-    )
     def own_piece(rank):
         return jnp.concatenate(
             [
@@ -966,13 +973,37 @@
         )
 
     output = (residual + sum_tp([own_piece(t ^ k) for k in range(tp)])).astype(BF)
-    qkv_a, qkv_b = [
-        add(keep, got)
-        for keep, got in scatter_rows(
-            [(e, swap(o, "seq", 1)) for e, o in ((groups[0], groups[2]), (groups[1], groups[3]))],
-            output,
-        )
-    ]
+    tall = (kp + ka) // 2 + 8
+    *groups_and_pieces, = whole_call(
+        lambda *refs: front_back_kernel(width, *refs),
+        (((n // 2, tall, qkv_width), BF),) * 4 + (((rows + 8, cp), BF),) * tp,
+        [
+            after(rank_s, output), rank_t, dquery, *dkv, x_full_p, x_full_a, inverse1, attn_gain_p, attn_gain_a,
+            got_qkv, mlp_gains_p, mlp_gains_a,
+        ],
+        4 * rows * dp * qkv_width,
+        scratch=(
+            pltpu.VMEM((dp, qkv_width), BF),
+            pltpu.VMEM((da, qkv_width), BF),
+            pltpu.VMEM((n, 8, qkv_width), F32),
+            pltpu.VMEM((rp, dp), F32),
+            pltpu.VMEM((ra, da), F32),
+        ),
+    )
+    groups, pieces = groups_and_pieces[:4], groups_and_pieces[4:]
+    tree, first_sent = scatter_rows(
+        [(e, swap(o, "seq", 1)) for e, o in ((groups[0], groups[2]), (groups[1], groups[3]))]
+    )
+    qkv_a, qkv_b = [add(keep, got) for keep, got in tree]
+    grad_x_p, grad_x_a = whole_call(
+        grad_x_kernel,
+        (((rp, cp), BF), ((ra, ca), BF)),
+        [
+            after(rank_t, first_sent), pieces[0], *[swap(pieces[k], "tp", k) for k in range(1, tp)], x_pack,
+            inverse1, attn_gain_p, attn_gain_a, dresid,
+        ],
+        rp * dp,
+    )
     hp, ha = kp // 2, ka // 2
     qkv_home_p = jnp.concatenate([qkv_a[:hp], qkv_b[:hp]], axis=0)
     qkv_home_a = jnp.concatenate([qkv_a[hp : hp + ha], qkv_b[hp : hp + ha]], axis=0)
@@ -993,9 +1024,10 @@
 
     shared_home = sum_tp([shared_piece(t ^ k) for k in range(tp)])
     attn_gains_home = shared_home[qp + qa]
-    grad_gate_p, grad_up_p = home(grad_gu_home)
-    grad_down_p = grad_down_home[:, :fp].astype(F32).reshape(n * fp, kp)
-    action_home = grad_down_home[:, fp:].reshape(n, ka, 3 * fa).astype(F32)
+    grad_gate_p, grad_up_p, grad_down_p, action_home = home(
+        after(rank_t, first_sent), grad_gu_home, grad_down_home
+    )
+    action_home = action_home.reshape(n, ka, 3 * fa)
 
     def units(part):
         return part.transpose(1, 0, 2).reshape(ka, n * fa)

time: 706 us -> 624 us (0.88)
  blocking collectives: 47.8 us -> 0 us
  waiting for transfers between devices: 283 us -> 261 us
  local copies, waits for them, and re-layouts: 76.8 us -> 69.1 us
    all_to_all x1 -> x0, blocking collectives: 47.8 us -> none  [shards(): grad_down_home = lax.all_to_all(grad_down, 'seq', 0, 0)]
    ppermute x63 -> x61, waiting for transfers between devices: 241 us -> 214 us  [swap(): return lax.ppermute(value, axis, [(i, i ^ mask) for i in range(count)])]
    all_to_all x1 -> x2, waiting for transfers between devices: 0.01 us -> 10.3 us  [the longest x1 10.3 us: shards(): lax.all_to_all(after(grad_down, sent_pieces[0]), 'seq', 0, 0)]
    reduce_scatter x1, starting transfers between devices: 8.79 us -> 0.21 us  [shards(): lax.psum_scatter(out_grads, 'seq', scatter_dimension=0).astype(F32)]
    convert_element_type x6 -> x3, other arithmetic: 14.2 us -> 6.25 us  [scatter_rows(): sent = add(mine[keep:], other[keep:]).astype(BF)]
    unnamed x185 -> x187, local copies, waits for them, and re-layouts: 38.9 us -> 33.7 us
    ppermute x63 -> x61, starting transfers between devices: 96 us -> 91.1 us  [swap(): return lax.ppermute(value, axis, [(i, i ^ mask) for i in range(count)])]
  transfers between devices with their start and end apart: 70 -> 69, of which waited for: 37 -> 30; matrix products, arithmetic and copies ran while one was open for 12% -> 12% of each run, Pallas kernels for 12% -> 14%
where the time goes in v4:
time: 624 us; the launch traced here: 614 us
  waiting for transfers between devices  261 us (42%)
  starting transfers between devices  116 us (19%)
  Pallas kernels  112 us (18%)
  local copies, waits for them, and re-layouts  69.1 us (11%)
  other arithmetic  41.2 us (7%)
  between operations  15.4 us (2%)
    ppermute x61, waiting for transfers between devices, swap(): return lax.ppermute(value, axis, [(i, i ^ mask) for i in range(count)])  214 us
    ppermute x61, starting transfers between devices, swap(): return lax.ppermute(value, axis, [(i, i ^ mask) for i in range(count)])  91.1 us
    pallas_call x11, Pallas kernels, whole_call(): pl.pallas_call(kernel, out_shape=outs, in_specs=specs, out_specs=tuple((p...  37.8 us
    pallas_call x2, Pallas kernels, feed(): pl.pallas_call(lambda *refs: feed_kernel(pair, *refs), grid=(total // ste...  36.6 us
    all_to_all x1, waiting for transfers between devices, shards(): lax.all_to_all(after(gate_up_sent, branch), 'seq', 0, 0).reshape(dp, 2 * fp)  34 us
    unnamed x187, local copies, waits for them, and re-layouts  33.7 us
    pallas_call x1, Pallas kernels, weight_grads(): pl.pallas_call(weights_kernel, grid=(dp // wide,), in_specs=[cols, cols,...  21.3 us
  transfers between devices with their start and end apart: 69, of which 30 were waited for; matrix products, arithmetic and copies ran while one was open for 12% of the time, Pallas kernels for 14%

profile of v4, /device:TPU:0, one launch (start us, length us, event | category | flops | bytes accessed | tf_op | source)
XLA Modules:
  0.0 613.8 jit_solution(3594347265444502362)
XLA Ops:
  12.0 3.0 collective-permute-start
  16.7 16.7 %collective-permute-done = bf16[136,2048]{1,0:T(8,128)(2,1)S(1)} collective-permute-done((bf16[136,2048]{1,0:T(8,128)(2,1)S(1)}, bf16[136,2048]{1,0:T(8,128)(2,1)S(1)}, u32[]{:S(2)}, u32[]{:S(2)}) %collective-permute-start) | collective-permute-done | bytes 557088 | tf_op jit(solution)/shard_map/ppermute | solution.py:21
  33.4 2.7 collective-permute-done.1
  42.4 2.8 collective-permute-start.5
  48.0 29.4 %collective-permute-done.3 = bf16[272,2048]{1,0:T(8,128)(2,1)} collective-permute-done((bf16[272,2048]{1,0:T(8,128)(2,1)}, bf16[272,2048]{1,0:T(8,128)(2,1)}, u32[]{:S(2)}, u32[]{:S(2)}) %collective-permute-start.3) | collective-permute-done | bytes 1114144 | tf_op jit(solution)/shard_map/ppermute | solution.py:21
  87.7 4.7 shard_map.408
  102.6 3.5 pad_maximum_fusion.1
  108.2 4.3 collective-permute-done.11
  114.0 3.5 collective-permute-done.13
  120.5 4.6 all-to-all-start.1
  126.2 3.8 shard_map.409
  134.1 3.2 copy.61
  146.0 2.6 pad_maximum_fusion
  148.6 5.2 collective-permute-done.15
  153.7 9.0 %collective-permute-done.16 = bf16[272,512]{1,0:T(8,128)(2,1)S(1)} collective-permute-done((bf16[272,512]{1,0:T(8,128)(2,1)S(1)}, bf16[272,512]{1,0:T(8,128)(2,1)S(1)}, u32[]{:S(2)}, u32[]{:S(2)}) %collective-permute-start.16) | collective-permute-done | bytes 278560 | tf_op jit(solution)/shard_map/ppermute | solution.py:21
  163.8 10.3 %all-to-all-start = ((bf16[8,256,1024]{2,1,0:T(8,128)(2,1)}), bf16[8,256,1024]{2,1,0:T(8,128)(2,1)}, u32[]{:S(2)}, u32[]{:S(2)}) async-start(bf16[8,256,1024]{2,1,0:T(8,128)(2,1)} %pad_maximum_fusion), calls=%async_computation | async-start | bytes 8388608 | tf_op jit(solution)/shard_map/all_to_all | solution.py:844
  177.7 5.6 collective-permute-start.19
  189.3 34.0 %all-to-all-done = bf16[8,256,1024]{2,1,0:T(8,128)(2,1)} async-done(((bf16[8,256,1024]{2,1,0:T(8,128)(2,1)}), bf16[8,256,1024]{2,1,0:T(8,128)(2,1)}, u32[]{:S(2)}, u32[]{:S(2)}) %all-to-all-start) | async-done | bytes 4194336 | tf_op jit(solution)/shard_map/all_to_all | solution.py:844
  229.7 10.8 %collective-permute-done.22 = bf16[136,2048]{1,0:T(8,128)(2,1)S(1)} collective-permute-done((bf16[136,2048]{1,0:T(8,128)(2,1)S(1)}, bf16[136,2048]{1,0:T(8,128)(2,1)S(1)}, u32[]{:S(2)}, u32[]{:S(2)}) %collective-permute-start.22) | collective-permute-done | bytes 557088 | tf_op jit(solution)/shard_map/ppermute | solution.py:21
  244.8 10.3 %collective-permute-done.23 = bf16[136,2048]{1,0:T(8,128)(2,1)S(1)} collective-permute-done((bf16[136,2048]{1,0:T(8,128)(2,1)S(1)}, bf16[136,2048]{1,0:T(8,128)(2,1)S(1)}, u32[]{:S(2)}, u32[]{:S(2)}) %collective-permute-start.23) | collective-permute-done | bytes 557088 | tf_op jit(solution)/shard_map/ppermute | solution.py:21
  255.2 10.6 %collective-permute-done.24 = bf16[136,2048]{1,0:T(8,128)(2,1)S(1)} collective-permute-done((bf16[136,2048]{1,0:T(8,128)(2,1)S(1)}, bf16[136,2048]{1,0:T(8,128)(2,1)S(1)}, u32[]{:S(2)}, u32[]{:S(2)}) %collective-permute-start.24) | collective-permute-done | bytes 557088 | tf_op jit(solution)/shard_map/ppermute | solution.py:21
  266.4 7.5 %collective-permute-done.28.refs_0_.xo_ref = bf16[1088,2048]{1,0:T(8,128)(2,1)S(1)} collective-permute-done((bf16[1088,2048]{1,0:T(8,128)(2,1)S(1)}, bf16[1088,2048]{1,0:T(8,128)(2,1)S(1)}, u32[]{:S(2)}, u32[]{:S(2)}) %collective-permute-start.28) | collective-permute-done | bytes 4456480 | tf_op jit(solution)/shard_map/ppermute | solution.py:21
  278.0 18.3 %shard_map.413 = (bf16[1088,512]{1,0:T(8,128)(2,1)}, bf16[1088,1024]{1,0:T(8,128)(2,1)}, bf16[1088,2048]{1,0:T(8,128)(2,1)}) custom-call(bf16[1088,2048]{1,0:T(8,128)(2,1)} %copy-done.78, bf16[1088,2048]{1,0:T(8,128)(2,1)} %collective-permute-done.18.refs_1_.co_ref, bf16[2048,1024]{1,0:T(8,128)(2,1)} %bitcast.10.refs_2_, bf16[512,2048]{1,0:T(8,128)(2,1)} %bitcast.208, ...), custom_call_target="tpu_custom_call" | custom-call | flops 11408506880 | bytes 24117248 | tf_op jit(solution)/shard_map/pallas_call | solution.py:355
  297.7 18.3 %shard_map.414 = (bf16[1088,512]{1,0:T(8,128)(2,1)}, bf16[1088,1024]{1,0:T(8,128)(2,1)}, bf16[1088,2048]{1,0:T(8,128)(2,1)}) custom-call(bf16[1088,2048]{1,0:T(8,128)(2,1)} %copy-done.74, bf16[1088,2048]{1,0:T(8,128)(2,1)} %constant_dynamic-update-slice_fusion.refs_1_.ce_ref, bf16[2048,1024]{1,0:T(8,128)(2,1)} %bitcast.10.refs_2_, ...), custom_call_target="tpu_custom_call" | custom-call | flops 11408506880 | bytes 24117248 | tf_op jit(solution)/shard_map/pallas_call | solution.py:355
  318.8 4.6 add_convert_fusion
  326.9 21.3 %shard_map.416 = (bf16[2048,1024]{1,0:T(8,128)(2,1)}, bf16[8,704,256]{2,1,0:T(8,128)(2,1)}) custom-call(bf16[1088,2048]{1,0:T(8,128)(2,1)} %copy-done.78, bf16[1088,2048]{1,0:T(8,128)(2,1)} %copy-done.74, bf16[1088,2048]{1,0:T(8,128)(2,1)} %collective-permute-done.18.refs_1_.co_ref, bf16[1088,2048]{1,0:T(8,128)(2,1)} %constant_dynamic-update-slice_fusion.refs_1_.ce_ref, ...), custom_call_target="tpu_custom_call" | custom-call | flops 13690208256 | bytes 17825792 | tf_op jit(solution)/shard_map/pallas_call | solution.py:408
  355.9 7.0 %shard_map.415 = bf16[8,272,2048]{2,1,0:T(8,128)(2,1)S(1)} custom-call(s32[8]{0:T(128)S(1)} %get-tuple-element.306.odd_ref, s32[8]{0:T(128)S(1)} %gather_fusion, s32[8]{0:T(128)S(1)} %gather_fusion.1, s32[8]{0:T(128)S(1)} %fusion.82.la_ref, s32[8]{0:T(128)S(1)} %get-tuple-element.307.lb_ref, bf16[1088,512]{1,0:T(8,128)(2,1)S(1)} %copy-done.50, ...), custom_call_target="tpu_custom_call" | custom-call | flops 4563402752 | bytes 8912896 | tf_op jit(solution)/shard_map/pallas_call | solution.py:462
  362.9 3.4 copy-done.3
  372.7 4.6 all-to-all-start.2
  377.5 5.8 collective-permute-start.37
  385.8 10.1 %collective-permute-done.37 = bf16[272,512]{1,0:T(8,128)(2,1)S(1)} collective-permute-done((bf16[272,512]{1,0:T(8,128)(2,1)S(1)}, bf16[272,512]{1,0:T(8,128)(2,1)S(1)}, u32[]{:S(2)}, u32[]{:S(2)}) %collective-permute-start.37) | collective-permute-done | bytes 278560 | tf_op jit(solution)/shard_map/ppermute | solution.py:21
  395.9 9.8 %collective-permute-done.38 = bf16[272,512]{1,0:T(8,128)(2,1)S(1)} collective-permute-done((bf16[272,512]{1,0:T(8,128)(2,1)S(1)}, bf16[272,512]{1,0:T(8,128)(2,1)S(1)}, u32[]{:S(2)}, u32[]{:S(2)}) %collective-permute-start.38) | collective-permute-done | bytes 278560 | tf_op jit(solution)/shard_map/ppermute | solution.py:21
  405.9 5.7 collective-permute-start.40
  414.0 10.3 %all-to-all-done.2.down_in_ref = bf16[8,704,256]{2,1,0:T(8,128)(2,1)} async-done(((bf16[8,704,256]{2,1,0:T(8,128)(2,1)}), bf16[8,704,256]{2,1,0:T(8,128)(2,1)}, u32[]{:S(2)}, u32[]{:S(2)}) %all-to-all-start.2) | async-done | bytes 2883616 | tf_op jit(solution)/shard_map/all_to_all | solution.py:924
  424.3 9.7 %collective-permute-done.41.refs_2_ = bf16[272,512]{1,0:T(8,128)(2,1)S(1)} collective-permute-done((bf16[272,512]{1,0:T(8,128)(2,1)S(1)}, bf16[272,512]{1,0:T(8,128)(2,1)S(1)}, u32[]{:S(2)}, u32[]{:S(2)}) %collective-permute-start.41) | collective-permute-done | bytes 278560 | tf_op jit(solution)/shard_map/ppermute | solution.py:21
  437.4 4.3 shard_map.418
  442.4 8.4 %shard_map.419 = (bf16[272,512]{1,0:T(8,128)(2,1)}, bf16[544,512]{1,0:T(8,128)(2,1)}, bf16[544,512]{1,0:T(8,128)(2,1)}, bf16[544,512]{1,0:T(8,128)(2,1)}, bf16[544,512]{1,0:T(8,128)(2,1)}) custom-call(bf16[272,512]{1,0:T(8,128)(2,1)} %copy-done.42, bf16[2176,512]{1,0:T(8,128)(2,1)} %copy-done.38, s32[272,1]{1,0:T(8,128)} %copy-done.29, ...), custom_call_target="tpu_custom_call" | custom-call | flops 3030384640 | bytes 6137408 | tf_op jit(solution)/shard_map/pallas_call | solution.py:117
  451.3 2.7 shard_map.422
  454.0 4.9 all-to-all-start.3
  466.2 4.7 collective-permute-start.34
  473.5 48.1 %collective-permute-done.47 = bf16[2,136,512]{2,1,0:T(8,128)(2,1)} collective-permute-done((bf16[2,136,512]{2,1,0:T(8,128)(2,1)}, bf16[2,136,512]{2,1,0:T(8,128)(2,1)}, u32[]{:S(2)}, u32[]{:S(2)}) %collective-permute-start.47) | collective-permute-done | bytes 278560 | tf_op jit(solution)/shard_map/ppermute | solution.py:21
  525.3 6.3 %collective-permute-done.48.refs_6_ = bf16[136,512]{1,0:T(8,128)(2,1)S(1)} collective-permute-done((bf16[136,512]{1,0:T(8,128)(2,1)S(1)}, bf16[136,512]{1,0:T(8,128)(2,1)S(1)}, u32[]{:S(2)}, u32[]{:S(2)}) %collective-permute-start.48) | collective-permute-done | bytes 139296 | tf_op jit(solution)/shard_map/ppermute | solution.py:21
  531.7 9.1 %shard_map.420 = (bf16[4,200,1024]{2,1,0:T(8,128)(2,1)S(1)}, bf16[4,200,1024]{2,1,0:T(8,128)(2,1)}, bf16[4,200,1024]{2,1,0:T(8,128)(2,1)}, bf16[4,200,1024]{2,1,...) custom-call(s32[1]{0:T(128)} %bitcast.44.refs_0_, ...), custom_call_target="tpu_custom_call" | custom-call | flops 2281701376 | bytes 16482312 | tf_op jit(solution)/shard_map/pallas_call | solution.py:117
  541.3 3.2 collective-permute-done.50
  544.5 3.5 convert_add_fusion.2
  562.6 9.1 %shard_map.423 = (f32[256,4096]{1,0:T(8,128)}, f32[256,4096]{1,0:T(8,128)}, f32[4096,256]{1,0:T(8,128)}, f32[8,192,256]{2,1,0:T(8,128)}) custom-call(s32[1]{0:T(128)} %bitcast.t_ref.refs_1_.token_ref, bf16[8,256,1024]{2,1,0:T(8,128)(2,1)} %all-to-all-done.3.gu_ref, bf16[8,704,256]{2,1,0:T(8,128)(2,1)} %all-to-all-done.2.down_in_ref), custom_call_target="tpu_custom_call" | custom-call | bytes 21233664 | tf_op jit(solution)/shard_map/pallas_call | solution.py:674
  571.8 2.6 reshape.313
  599.9 4.7 collective-permute-done.59
  (406 shorter events, 169.7 us)
Async XLA Ops:
  7.2 78.9 %all-gather.5.cloned.1.call-start = ((), (), s32[]{:S(2)}) async-start(), calls=%async_computation.8 | async-start | bytes 7225344 | tf_op jit(solution)/shard_map/all_gather | solution.py:758
  10.4 123.7 %all-gather.7.cloned.1.call-start = ((), (), s32[]{:S(2)}) async-start(), calls=%async_computation.9 | async-start | bytes 3538944 | tf_op jit(solution)/shard_map/all_gather | solution.py:833
  12.0 21.4 %collective-permute-start = (bf16[136,2048]{1,0:T(8,128)(2,1)S(1)}, bf16[136,2048]{1,0:T(8,128)(2,1)S(1)}, u32[]{:S(2)}, u32[]{:S(2)}) collective-permute-start(bf16[136,2048]{1,0:T(8,128)(2,1)S(1)} %pad_maximum_fusion.7), channel_id=1, source_target_pairs={{0,8},{4,12},{8,0},{12,4},{16,24},{20,28},{24,16},{28,20},{1,9},{5... | collective-permute-start | bytes 1671176 | tf_op jit(solution)/shard_map/ppermute | solution.py:21
  15.1 21.0 %collective-permute-start.1 = (bf16[136,2048]{1,0:T(8,128)(2,1)S(1)}, bf16[136,2048]{1,0:T(8,128)(2,1)S(1)}, u32[]{:S(2)}, u32[]{:S(2)}) collective-permute-start(bf16[136,2048]{1,0:T(8,128)(2,1)S(1)} %pad_maximum_fusion.8), channel_id=1, source_target_pairs={{0,16},{4,20},{8,24},{12,28},{16,0},{20,4},{24,8},{28,12},{1,17},{... | collective-permute-start | bytes 1671176 | tf_op jit(solution)/shard_map/ppermute | solution.py:21
  37.2 40.2 %collective-permute-start.3 = (bf16[272,2048]{1,0:T(8,128)(2,1)}, bf16[272,2048]{1,0:T(8,128)(2,1)}, u32[]{:S(2)}, u32[]{:S(2)}) collective-permute-start(bf16[272,2048]{1,0:T(8,128)(2,1)} %pad_maximum_fusion.3), channel_id=1, source_target_pairs={{0,8},{4,12},{8,0},{12,4},{16,24},{20,28},{24,16},{28,20},{1,9},{5... | collective-permute-start | bytes 3342344 | tf_op jit(solution)/shard_map/ppermute | solution.py:21
  38.3 40.7 %collective-permute-start.2 = (bf16[272,2048]{1,0:T(8,128)(2,1)}, bf16[272,2048]{1,0:T(8,128)(2,1)}, u32[]{:S(2)}, u32[]{:S(2)}) collective-permute-start(bf16[272,2048]{1,0:T(8,128)(2,1)} %pad_maximum_fusion.2), channel_id=1, source_target_pairs={{0,16},{4,20},{8,24},{12,28},{16,0},{20,4},{24,8},{28,12},{1,17},{... | collective-permute-start | bytes 3342344 | tf_op jit(solution)/shard_map/ppermute | solution.py:21
  40.9 46.8 %collective-permute-start.4 = (bf16[272,512]{1,0:T(8,128)(2,1)S(1)}, bf16[272,512]{1,0:T(8,128)(2,1)S(1)}, u32[]{:S(2)}, u32[]{:S(2)}) collective-permute-start(bf16[272,512]{1,0:T(8,128)(2,1)S(1)} %fusion.25.refs_0_.refs_4_), channel_id=1, source_target_pairs={{0,1},{1,0},{2,3},{3,2},{4,5},{5,4},{6,7},{7,6},{8,9},{9,8},{10,11... | collective-permute-start | bytes 835592 | tf_op jit(solution)/shard_map/ppermute | solution.py:21
  42.4 45.3 %collective-permute-start.5 = (bf16[272,512]{1,0:T(8,128)(2,1)S(1)}, bf16[272,512]{1,0:T(8,128)(2,1)S(1)}, u32[]{:S(2)}, u32[]{:S(2)}) collective-permute-start(bf16[272,512]{1,0:T(8,128)(2,1)S(1)} %fusion.25.refs_0_.refs_4_), channel_id=1, source_target_pairs={{0,2},{1,3},{2,0},{3,1},{4,6},{5,7},{6,4},{7,5},{8,10},{9,11},{10,... | collective-permute-start | bytes 835592 | tf_op jit(solution)/shard_map/ppermute | solution.py:21
  45.1 42.6 %collective-permute-start.6 = (bf16[272,512]{1,0:T(8,128)(2,1)S(1)}, bf16[272,512]{1,0:T(8,128)(2,1)S(1)}, u32[]{:S(2)}, u32[]{:S(2)}) collective-permute-start(bf16[272,512]{1,0:T(8,128)(2,1)S(1)} %fusion.25.refs_0_.refs_4_), channel_id=1, source_target_pairs={{0,3},{1,2},{2,1},{3,0},{4,7},{5,6},{6,5},{7,4},{8,11},{9,10},{10,... | collective-permute-start | bytes 835592 | tf_op jit(solution)/shard_map/ppermute | solution.py:21
  120.5 43.3 %all-to-all-start.1 = ((bf16[8,704,256]{2,1,0:T(8,128)(2,1)}), bf16[8,704,256]{2,1,0:T(8,128)(2,1)}, u32[]{:S(2)}, u32[]{:S(2)}) async-start(bf16[8,704,256]{2,1,0:T(8,128)(2,1)} %pad_maximum_fusion.1), calls=%async_computation.1 | async-start | bytes 5767168 | tf_op jit(solution)/shard_map/all_to_all | solution.py:834
  125.1 49.9 %collective-permute-start.18 = (bf16[1088,2048]{1,0:T(8,128)(2,1)}, bf16[1088,2048]{1,0:T(8,128)(2,1)}, u32[]{:S(2)}, u32[]{:S(2)}) collective-permute-start(bf16[1088,2048]{1,0:T(8,128)(2,1)} %constant_dynamic-update-slice_fusion.refs_1_.ce_ref), channel_id=1, source_target_pairs={{0,4},{4,0},{8,12},{12,8},{16,20},{20,16},{24,28},{28,24},{1,5},{5... | collective-permute-start | bytes 13369352 | tf_op jit(solution)/shard_map/ppermute | solution.py:21
  139.4 14.3 %collective-permute-start.15 = (bf16[272,512]{1,0:T(8,128)(2,1)S(1)}, bf16[272,512]{1,0:T(8,128)(2,1)S(1)}, u32[]{:S(2)}, u32[]{:S(2)}) collective-permute-start(bf16[272,512]{1,0:T(8,128)(2,1)S(1)} %get-tuple-element.113), channel_id=1, source_target_pairs={{0,1},{1,0},{2,3},{3,2},{4,5},{5,4},{6,7},{7,6},{8,9},{9,8},{10,11... | collective-permute-start | bytes 835592 | tf_op jit(solution)/shard_map/ppermute | solution.py:21
  140.4 22.4 %collective-permute-start.16 = (bf16[272,512]{1,0:T(8,128)(2,1)S(1)}, bf16[272,512]{1,0:T(8,128)(2,1)S(1)}, u32[]{:S(2)}, u32[]{:S(2)}) collective-permute-start(bf16[272,512]{1,0:T(8,128)(2,1)S(1)} %get-tuple-element.114), channel_id=1, source_target_pairs={{0,2},{1,3},{2,0},{3,1},{4,6},{5,7},{6,4},{7,5},{8,10},{9,11},{10,... | collective-permute-start | bytes 835592 | tf_op jit(solution)/shard_map/ppermute | solution.py:21
  142.8 20.0 %collective-permute-start.17 = (bf16[272,512]{1,0:T(8,128)(2,1)S(1)}, bf16[272,512]{1,0:T(8,128)(2,1)S(1)}, u32[]{:S(2)}, u32[]{:S(2)}) collective-permute-start(bf16[272,512]{1,0:T(8,128)(2,1)S(1)} %get-tuple-element.115), channel_id=1, source_target_pairs={{0,3},{1,2},{2,1},{3,0},{4,7},{5,6},{6,5},{7,4},{8,11},{9,10},{10,... | collective-permute-start | bytes 835592 | tf_op jit(solution)/shard_map/ppermute | solution.py:21
  163.8 59.5 %all-to-all-start = ((bf16[8,256,1024]{2,1,0:T(8,128)(2,1)}), bf16[8,256,1024]{2,1,0:T(8,128)(2,1)}, u32[]{:S(2)}, u32[]{:S(2)}) async-start(bf16[8,256,1024]{2,1,0:T(8,128)(2,1)} %pad_maximum_fusion), calls=%async_computation | async-start | bytes 8388608 | tf_op jit(solution)/shard_map/all_to_all | solution.py:844
  174.1 290.1 %reduce-scatter.3.cloned.1.call-start = ((), (), s32[]{:S(2)}) async-start(), calls=%async_computation.6 | async-start | bytes 10027008 | tf_op jit(solution)/shard_map/reduce_scatter | solution.py:923
  177.7 45.5 %collective-permute-start.19 = (bf16[272,512]{1,0:T(8,128)(2,1)S(1)}, bf16[272,512]{1,0:T(8,128)(2,1)S(1)}, u32[]{:S(2)}, u32[]{:S(2)}) collective-permute-start(bf16[272,512]{1,0:T(8,128)(2,1)S(1)} %get-tuple-element.119.refs_0_), channel_id=1, source_target_pairs={{0,1},{1,0},{2,3},{3,2},{4,5},{5,4},{6,7},{7,6},{8,9},{9,8},{10,11... | collective-permute-start | bytes 835592 | tf_op jit(solution)/shard_map/ppermute | solution.py:21
  183.4 39.9 %collective-permute-start.20 = (bf16[272,512]{1,0:T(8,128)(2,1)S(1)}, bf16[272,512]{1,0:T(8,128)(2,1)S(1)}, u32[]{:S(2)}, u32[]{:S(2)}) collective-permute-start(bf16[272,512]{1,0:T(8,128)(2,1)S(1)} %get-tuple-element.119.refs_0_), channel_id=1, source_target_pairs={{0,2},{1,3},{2,0},{3,1},{4,6},{5,7},{6,4},{7,5},{8,10},{9,11},{10,... | collective-permute-start | bytes 835592 | tf_op jit(solution)/shard_map/ppermute | solution.py:21
  184.4 39.6 %collective-permute-start.21 = (bf16[272,512]{1,0:T(8,128)(2,1)S(1)}, bf16[272,512]{1,0:T(8,128)(2,1)S(1)}, u32[]{:S(2)}, u32[]{:S(2)}) collective-permute-start(bf16[272,512]{1,0:T(8,128)(2,1)S(1)} %get-tuple-element.119.refs_0_), channel_id=1, source_target_pairs={{0,3},{1,2},{2,1},{3,0},{4,7},{5,6},{6,5},{7,4},{8,11},{9,10},{10,... | collective-permute-start | bytes 835592 | tf_op jit(solution)/shard_map/ppermute | solution.py:21
  227.7 15.5 %collective-permute-start.25 = (bf16[136,2048]{1,0:T(8,128)(2,1)S(1)}, bf16[136,2048]{1,0:T(8,128)(2,1)S(1)}, u32[]{:S(2)}, u32[]{:S(2)}) collective-permute-start(bf16[136,2048]{1,0:T(8,128)(2,1)S(1)} %get-tuple-element.121), channel_id=1, source_target_pairs={{0,16},{4,20},{8,24},{12,28},{16,0},{20,4},{24,8},{28,12},{1,17},{... | collective-permute-start | bytes 1671176 | tf_op jit(solution)/shard_map/ppermute | solution.py:21
  228.4 26.8 %collective-permute-start.23 = (bf16[136,2048]{1,0:T(8,128)(2,1)S(1)}, bf16[136,2048]{1,0:T(8,128)(2,1)S(1)}, u32[]{:S(2)}, u32[]{:S(2)}) collective-permute-start(bf16[136,2048]{1,0:T(8,128)(2,1)S(1)} %get-tuple-element.120), channel_id=1, source_target_pairs={{0,16},{4,20},{8,24},{12,28},{16,0},{20,4},{24,8},{28,12},{1,17},{... | collective-permute-start | bytes 1671176 | tf_op jit(solution)/shard_map/ppermute | solution.py:21
  240.5 25.3 %collective-permute-start.24 = (bf16[136,2048]{1,0:T(8,128)(2,1)S(1)}, bf16[136,2048]{1,0:T(8,128)(2,1)S(1)}, u32[]{:S(2)}, u32[]{:S(2)}) collective-permute-start(bf16[136,2048]{1,0:T(8,128)(2,1)S(1)} %collective-permute-done.22), channel_id=1, source_target_pairs={{0,16},{4,20},{8,24},{12,28},{16,0},{20,4},{24,8},{28,12},{1,17},{... | collective-permute-start | bytes 1671176 | tf_op jit(solution)/shard_map/ppermute | solution.py:21
  240.9 25.1 %collective-permute-start.26 = (bf16[136,2048]{1,0:T(8,128)(2,1)S(1)}, bf16[136,2048]{1,0:T(8,128)(2,1)S(1)}, u32[]{:S(2)}, u32[]{:S(2)}) collective-permute-start(bf16[136,2048]{1,0:T(8,128)(2,1)S(1)} %get-tuple-element.121), channel_id=1, source_target_pairs={{0,8},{4,12},{8,0},{12,4},{16,24},{20,28},{24,16},{28,20},{1,9},{5... | collective-permute-start | bytes 1671176 | tf_op jit(solution)/shard_map/ppermute | solution.py:21
  243.3 23.0 %collective-permute-start.27 = (bf16[136,2048]{1,0:T(8,128)(2,1)S(1)}, bf16[136,2048]{1,0:T(8,128)(2,1)S(1)}, u32[]{:S(2)}, u32[]{:S(2)}) collective-permute-start(bf16[136,2048]{1,0:T(8,128)(2,1)S(1)} %collective-permute-done.25), channel_id=1, source_target_pairs={{0,8},{4,12},{8,0},{12,4},{16,24},{20,28},{24,16},{28,20},{1,9},{5... | collective-permute-start | bytes 1671176 | tf_op jit(solution)/shard_map/ppermute | solution.py:21
  296.2 22.5 %collective-permute-start.29 = (bf16[1088,2048]{1,0:T(8,128)(2,1)}, bf16[1088,2048]{1,0:T(8,128)(2,1)}, u32[]{:S(2)}, u32[]{:S(2)}) collective-permute-start(bf16[1088,2048]{1,0:T(8,128)(2,1)} %get-tuple-element.127), channel_id=1, source_target_pairs={{0,4},{4,0},{8,12},{12,8},{16,20},{20,16},{24,28},{28,24},{1,5},{5... | collective-permute-start | bytes 13369352 | tf_op jit(solution)/shard_map/ppermute | solution.py:21
  323.3 26.9 %collective-permute-start.32 = (bf16[2,136,2048]{2,1,0:T(8,128)(2,1)S(1)}, bf16[2,136,2048]{2,1,0:T(8,128)(2,1)S(1)}, u32[]{:S(2)}, u32[]{:S(2)}) collective-permute-start(bf16[2,136,2048]{2,1,0:T(8,128)(2,1)S(1)} %bitcast.231), channel_id=1, source_target_pairs={{0,8},{4,12},{8,0},{12,4},{16,24},{20,28},{24,16},{28,20},{1,9},{5... | collective-permute-start | bytes 3342344 | tf_op jit(solution)/shard_map/ppermute | solution.py:21
  325.2 27.9 %collective-permute-start.30 = (bf16[2,136,2048]{2,1,0:T(8,128)(2,1)S(1)}, bf16[2,136,2048]{2,1,0:T(8,128)(2,1)S(1)}, u32[]{:S(2)}, u32[]{:S(2)}) collective-permute-start(bf16[2,136,2048]{2,1,0:T(8,128)(2,1)S(1)} %bitcast.230), channel_id=1, source_target_pairs={{0,16},{4,20},{8,24},{12,28},{16,0},{20,4},{24,8},{28,12},{1,17},{... | collective-permute-start | bytes 3342344 | tf_op jit(solution)/shard_map/ppermute | solution.py:21
  351.3 15.0 %collective-permute-start.33 = (bf16[136,2048]{1,0:T(8,128)(2,1)}, bf16[136,2048]{1,0:T(8,128)(2,1)}, u32[]{:S(2)}, u32[]{:S(2)}) collective-permute-start(bf16[136,2048]{1,0:T(8,128)(2,1)} %get-tuple-element.136), channel_id=1, source_target_pairs={{0,16},{4,20},{8,24},{12,28},{16,0},{20,4},{24,8},{28,12},{1,17},{... | collective-permute-start | bytes 1671176 | tf_op jit(solution)/shard_map/ppermute | solution.py:21
  354.2 14.1 %collective-permute-start.31 = (bf16[136,2048]{1,0:T(8,128)(2,1)}, bf16[136,2048]{1,0:T(8,128)(2,1)}, u32[]{:S(2)}, u32[]{:S(2)}) collective-permute-start(bf16[136,2048]{1,0:T(8,128)(2,1)} %get-tuple-element.135), channel_id=1, source_target_pairs={{0,8},{4,12},{8,0},{12,4},{16,24},{20,28},{24,16},{28,20},{1,9},{5... | collective-permute-start | bytes 1671176 | tf_op jit(solution)/shard_map/ppermute | solution.py:21
  372.7 51.6 %all-to-all-start.2 = ((bf16[8,704,256]{2,1,0:T(8,128)(2,1)}), bf16[8,704,256]{2,1,0:T(8,128)(2,1)}, u32[]{:S(2)}, u32[]{:S(2)}) async-start(bf16[8,704,256]{2,1,0:T(8,128)(2,1)} %get-tuple-element.144), calls=%async_computation.3 | async-start | bytes 5767168 | tf_op jit(solution)/shard_map/all_to_all | solution.py:924
  377.3 174.8 %reduce-scatter.5.cloned.1.call-start = ((), (), s32[]{:S(2)}) async-start(), calls=%async_computation.7 | async-start | bytes 3538944 | tf_op jit(solution)/shard_map/reduce_scatter | solution.py:962
  377.5 18.4 %collective-permute-start.37 = (bf16[272,512]{1,0:T(8,128)(2,1)S(1)}, bf16[272,512]{1,0:T(8,128)(2,1)S(1)}, u32[]{:S(2)}, u32[]{:S(2)}) collective-permute-start(bf16[272,512]{1,0:T(8,128)(2,1)S(1)} %copy-done.48), channel_id=1, source_target_pairs={{0,1},{1,0},{2,3},{3,2},{4,5},{5,4},{6,7},{7,6},{8,9},{9,8},{10,11... | collective-permute-start | bytes 835592 | tf_op jit(solution)/shard_map/ppermute | solution.py:21
  383.3 22.4 %collective-permute-start.38 = (bf16[272,512]{1,0:T(8,128)(2,1)S(1)}, bf16[272,512]{1,0:T(8,128)(2,1)S(1)}, u32[]{:S(2)}, u32[]{:S(2)}) collective-permute-start(bf16[272,512]{1,0:T(8,128)(2,1)S(1)} %copy-done.46), channel_id=1, source_target_pairs={{0,2},{1,3},{2,0},{3,1},{4,6},{5,7},{6,4},{7,5},{8,10},{9,11},{10,... | collective-permute-start | bytes 835592 | tf_op jit(solution)/shard_map/ppermute | solution.py:21
  384.3 21.4 %collective-permute-start.39 = (bf16[272,512]{1,0:T(8,128)(2,1)S(1)}, bf16[272,512]{1,0:T(8,128)(2,1)S(1)}, u32[]{:S(2)}, u32[]{:S(2)}) collective-permute-start(bf16[272,512]{1,0:T(8,128)(2,1)S(1)} %copy-done.44), channel_id=1, source_target_pairs={{0,3},{1,2},{2,1},{3,0},{4,7},{5,6},{6,5},{7,4},{8,11},{9,10},{10,... | collective-permute-start | bytes 835592 | tf_op jit(solution)/shard_map/ppermute | solution.py:21
  405.9 18.5 %collective-permute-start.40 = (bf16[272,512]{1,0:T(8,128)(2,1)S(1)}, bf16[272,512]{1,0:T(8,128)(2,1)S(1)}, u32[]{:S(2)}, u32[]{:S(2)}) collective-permute-start(bf16[272,512]{1,0:T(8,128)(2,1)S(1)} %add_convert_fusion.6.refs_0_), channel_id=1, source_target_pairs={{0,1},{1,0},{2,3},{3,2},{4,5},{5,4},{6,7},{7,6},{8,9},{9,8},{10,11... | collective-permute-start | bytes 835592 | tf_op jit(solution)/shard_map/ppermute | solution.py:21
  411.6 22.4 %collective-permute-start.41 = (bf16[272,512]{1,0:T(8,128)(2,1)S(1)}, bf16[272,512]{1,0:T(8,128)(2,1)S(1)}, u32[]{:S(2)}, u32[]{:S(2)}) collective-permute-start(bf16[272,512]{1,0:T(8,128)(2,1)S(1)} %add_convert_fusion.6.refs_0_), channel_id=1, source_target_pairs={{0,2},{1,3},{2,0},{3,1},{4,6},{5,7},{6,4},{7,5},{8,10},{9,11},{10,... | collective-permute-start | bytes 835592 | tf_op jit(solution)/shard_map/ppermute | solution.py:21
  412.6 22.1 %collective-permute-start.42 = (bf16[272,512]{1,0:T(8,128)(2,1)S(1)}, bf16[272,512]{1,0:T(8,128)(2,1)S(1)}, u32[]{:S(2)}, u32[]{:S(2)}) collective-permute-start(bf16[272,512]{1,0:T(8,128)(2,1)S(1)} %add_convert_fusion.6.refs_0_), channel_id=1, source_target_pairs={{0,3},{1,2},{2,1},{3,0},{4,7},{5,6},{6,5},{7,4},{8,11},{9,10},{10,... | collective-permute-start | bytes 835592 | tf_op jit(solution)/shard_map/ppermute | solution.py:21
  454.0 108.6 %all-to-all-start.3 = ((bf16[8,256,1024]{2,1,0:T(8,128)(2,1)}), bf16[8,256,1024]{2,1,0:T(8,128)(2,1)}, u32[]{:S(2)}, u32[]{:S(2)}) async-start(bf16[8,256,1024]{2,1,0:T(8,128)(2,1)} %bitcast.226), calls=%async_computation.5 | async-start | bytes 8388608 | tf_op jit(solution)/shard_map/all_to_all | solution.py:940
  459.9 61.7 %collective-permute-start.47 = (bf16[2,136,512]{2,1,0:T(8,128)(2,1)}, bf16[2,136,512]{2,1,0:T(8,128)(2,1)}, u32[]{:S(2)}, u32[]{:S(2)}) collective-permute-start(bf16[2,136,512]{2,1,0:T(8,128)(2,1)} %bitcast.55), channel_id=1, source_target_pairs={{0,8},{4,12},{8,0},{12,4},{16,24},{20,28},{24,16},{28,20},{1,9},{5... | collective-permute-start | bytes 835592 | tf_op jit(solution)/shard_map/ppermute | solution.py:21
  462.7 61.7 %collective-permute-start.44 = (bf16[2,136,512]{2,1,0:T(8,128)(2,1)}, bf16[2,136,512]{2,1,0:T(8,128)(2,1)S(1)}, u32[]{:S(2)}, u32[]{:S(2)}) collective-permute-start(bf16[2,136,512]{2,1,0:T(8,128)(2,1)} %bitcast.50), channel_id=1, source_target_pairs={{0,16},{4,20},{8,24},{12,28},{16,0},{20,4},{24,8},{28,12},{1,17},{... | collective-permute-start | bytes 835592 | tf_op jit(solution)/shard_map/ppermute | solution.py:21
  466.2 58.8 %collective-permute-start.34 = (bf16[272,512]{1,0:T(8,128)(2,1)S(1)}, bf16[272,512]{1,0:T(8,128)(2,1)S(1)}, u32[]{:S(2)}, u32[]{:S(2)}) collective-permute-start(bf16[272,512]{1,0:T(8,128)(2,1)S(1)} %fusion.27), channel_id=1, source_target_pairs={{0,1},{1,0},{2,3},{3,2},{4,5},{5,4},{6,7},{7,6},{8,9},{9,8},{10,11... | collective-permute-start | bytes 835592 | tf_op jit(solution)/shard_map/ppermute | solution.py:21
  470.9 54.1 %collective-permute-start.35 = (bf16[272,512]{1,0:T(8,128)(2,1)S(1)}, bf16[272,512]{1,0:T(8,128)(2,1)S(1)}, u32[]{:S(2)}, u32[]{:S(2)}) collective-permute-start(bf16[272,512]{1,0:T(8,128)(2,1)S(1)} %fusion.28), channel_id=1, source_target_pairs={{0,2},{1,3},{2,0},{3,1},{4,6},{5,7},{6,4},{7,5},{8,10},{9,11},{10,... | collective-permute-start | bytes 835592 | tf_op jit(solution)/shard_map/ppermute | solution.py:21
  472.0 53.1 %collective-permute-start.36 = (bf16[272,512]{1,0:T(8,128)(2,1)S(1)}, bf16[272,512]{1,0:T(8,128)(2,1)S(1)}, u32[]{:S(2)}, u32[]{:S(2)}) collective-permute-start(bf16[272,512]{1,0:T(8,128)(2,1)S(1)} %fusion.29), channel_id=1, source_target_pairs={{0,3},{1,2},{2,1},{3,0},{4,7},{5,6},{6,5},{7,4},{8,11},{9,10},{10,... | collective-permute-start | bytes 835592 | tf_op jit(solution)/shard_map/ppermute | solution.py:21
  548.0 26.4 %collective-permute-start.56 = (bf16[2,200,1024]{2,1,0:T(8,128)(2,1)}, bf16[2,200,1024]{2,1,0:T(8,128)(2,1)}, u32[]{:S(2)}, u32[]{:S(2)}) collective-permute-start(bf16[2,200,1024]{2,1,0:T(8,128)(2,1)} %get-tuple-element.237), channel_id=1, source_target_pairs={{0,8},{4,12},{8,0},{12,4},{16,24},{20,28},{24,16},{28,20},{1,9},{5... | collective-permute-start | bytes 2457608 | tf_op jit(solution)/shard_map/ppermute | solution.py:21
  550.5 27.2 %collective-permute-start.54 = (bf16[2,200,1024]{2,1,0:T(8,128)(2,1)}, bf16[2,200,1024]{2,1,0:T(8,128)(2,1)}, u32[]{:S(2)}, u32[]{:S(2)}) collective-permute-start(bf16[2,200,1024]{2,1,0:T(8,128)(2,1)} %get-tuple-element.239), channel_id=1, source_target_pairs={{0,16},{4,20},{8,24},{12,28},{16,0},{20,4},{24,8},{28,12},{1,17},{... | collective-permute-start | bytes 2457608 | tf_op jit(solution)/shard_map/ppermute | solution.py:21
  558.3 27.8 %collective-permute-start.51 = (bf16[280,512]{1,0:T(8,128)(2,1)S(1)}, bf16[280,512]{1,0:T(8,128)(2,1)S(1)}, u32[]{:S(2)}, u32[]{:S(2)}) collective-permute-start(bf16[280,512]{1,0:T(8,128)(2,1)S(1)} %get-tuple-element.168), channel_id=1, source_target_pairs={{0,1},{1,0},{2,3},{3,2},{4,5},{5,4},{6,7},{7,6},{8,9},{9,8},{10,11... | collective-permute-start | bytes 860168 | tf_op jit(solution)/shard_map/ppermute | solution.py:21
  559.8 26.2 %collective-permute-start.52 = (bf16[280,512]{1,0:T(8,128)(2,1)S(1)}, bf16[280,512]{1,0:T(8,128)(2,1)S(1)}, u32[]{:S(2)}, u32[]{:S(2)}) collective-permute-start(bf16[280,512]{1,0:T(8,128)(2,1)S(1)} %get-tuple-element.169), channel_id=1, source_target_pairs={{0,2},{1,3},{2,0},{3,1},{4,6},{5,7},{6,4},{7,5},{8,10},{9,11},{10,... | collective-permute-start | bytes 860168 | tf_op jit(solution)/shard_map/ppermute | solution.py:21
  561.7 24.4 %collective-permute-start.53 = (bf16[280,512]{1,0:T(8,128)(2,1)S(1)}, bf16[280,512]{1,0:T(8,128)(2,1)S(1)}, u32[]{:S(2)}, u32[]{:S(2)}) collective-permute-start(bf16[280,512]{1,0:T(8,128)(2,1)S(1)} %get-tuple-element.170), channel_id=1, source_target_pairs={{0,3},{1,2},{2,1},{3,0},{4,7},{5,6},{6,5},{7,4},{8,11},{9,10},{10,... | collective-permute-start | bytes 860168 | tf_op jit(solution)/shard_map/ppermute | solution.py:21
  (101 other events, 1298.6 us)
Sparse Core Ops, SparseCore 0:
  10.5 68.6 all-gather.4
  94.9 39.1 all-gather.6
  368.5 92.4 reduce-scatter.2
  464.8 68.0 reduce-scatter.4

commit v5 on v4

--- a/solution.py
+++ b/solution.py
@@ -54,7 +54,7 @@
         got = [swap(b, "seq", masks[step]) for b, masks in zip(stages[-1], far_masks())]
         got = lax.optimization_barrier(got)
         stages.append([jnp.concatenate(pair, axis=0) for pair in zip(stages[-1], got)])
-    return stages[1:]
+    return stages[1:], got
 
 
 def near_rows(blocks):
@@ -66,33 +66,43 @@
     return left.astype(F32) + right.astype(F32)
 
 
-def scatter_rows(halves, token=None):
-    results = []
-    firsts = []
-    for (mine, other), masks in zip(halves, far_masks()):
-        for mask in masks[:0:-1]:
-            keep = mine.shape[0] // 2
-            sent = add(mine[keep:], other[keep:]).astype(BF)
-            firsts.append(sent)
-            got = swap(sent, "seq", mask)
-            mine, other = add(mine[:keep], other[:keep]), got
-        sent = add(mine[1], other[1]).astype(BF)
-        if token is not None:
+def scatter_rows(halves, token=None, beside=((), ())):
+    parts = [list(half) for half in halves]
+    orders = [masks[::-1] for masks in far_masks()]
+    steps = len(orders[0])
+    history = []
+    beside = list(beside)
+    for step in range(steps):
+        keep = parts[0][0].shape[0] // 2
+        sent = [total_of([p[keep:] for p in part]).astype(BF) for part in parts]
+        if token is not None and step == steps - 1:
             sent = after(sent, token)
-        got = swap(sent, "seq", masks[0])
-        results.append((add(mine[0], other[0]), got))
-    return results, firsts[:: max(1, len(firsts) // 2)]
+        got = [swap(part, "seq", order[step]) for part, order in zip(sent, orders)]
+        for place, when in enumerate((0, steps - 1)):
+            if step == when and beside[place]:
+                got, beside[place] = lax.optimization_barrier((got, beside[place]))
+        parts = [[p[:keep] for p in part] + [g] for part, g in zip(parts, got)]
+        history.append(sent)
+    return [(total_of([p[0] for p in part[:-1]]), part[-1][0]) for part in parts], history, beside
 
 
 def gather_tp(piece):
     return [piece] + [swap(piece, "tp", k) for k in range(1, lax.axis_size("tp"))]
 
 
+def trade_tp(pieces):
+    return [pieces[0]] + [swap(pieces[k].astype(BF), "tp", k) for k in range(1, len(pieces))]
+
+
+def total_of(addends):
+    total = addends[0].astype(F32)
+    for part in addends[1:]:
+        total = total + part.astype(F32)
+    return total
+
+
 def sum_tp(pieces):
-    total = pieces[0].astype(F32)
-    for k in range(1, len(pieces)):
-        total = total + swap(pieces[k].astype(BF), "tp", k).astype(F32)
-    return total
+    return total_of(trade_tp(pieces))
 
 
 def dot(left, right):
@@ -263,10 +273,13 @@
     kp = cp * tp // n
     for k in range(tp):
         rank = t_ref[0] ^ k
-        blocks = w_ref[pl.ds(rank * (n // tp), n // tp)]
-        prefix = dot_t(mix_ref[:rp, :], blocks[:, :kp].reshape(cp, -1))
-        action = dot_t(mix_ref[rp:, :], blocks[:, kp:].reshape(-1, mix_ref.shape[1]))
-        outs[k][:rp, :] = prefix.astype(BF)
+        prefix, action = [], []
+        for i in range(n // tp):
+            block = w_ref[rank * (n // tp) + i]
+            prefix.append(dot(mix_ref[:rp, :], block[:, :kp]))
+            action.append(dot(mix_ref[rp:, :], block[:, kp:]))
+        action = jnp.concatenate(action, axis=1)
+        outs[k][:rp, :] = jnp.concatenate(prefix, axis=1).astype(BF)
         outs[k][rp:, :] = jnp.concatenate(
             [action, jnp.zeros((ra, cp - action.shape[1]), F32)], axis=1
         ).astype(BF)
@@ -331,11 +344,15 @@
     action = jnp.concatenate(
         [action, jnp.zeros((action.shape[0], dp - action.shape[1]), F32)], axis=1
     )
-    pieces = []
+    begin = 0
     for i in range(pair):
-        pieces.append(dn[i * each : i * each + prefix])
-        pieces.append(action[i * (each - prefix) : (i + 1) * (each - prefix)])
-    dn_ref[...] = jnp.concatenate(pieces, axis=0).astype(BF)
+        first, last = i * each + prefix, (i + 1) * each
+        low, high = first // 16 * 16, -(-last // 16) * 16
+        dn_ref[begin:low, :] = dn[begin:low].astype(BF)
+        piece = [dn[low:first], action[i * (each - prefix) : (i + 1) * (each - prefix)]]
+        piece = [p for p in piece + [dn[last:high]] if p.shape[0]]
+        dn_ref[low:high, :] = jnp.concatenate(piece, axis=0).astype(BF)
+        begin = high
 
 
 def feed(rows_in, cot_rows, gate_up, down, dn_action, each):
@@ -386,11 +403,14 @@
 
 
 def weights_kernel(
-    xo_ref, xe_ref, co_ref, ce_ref, ho_ref, he_ref, go_ref, ge_ref, act_ref, gw_ref, gd_ref
+    xo_ref, xe_ref, co_ref, ce_ref, ho_ref, he_ref, go_ref, ge_ref, act_ref, gg_ref, gu_ref,
+    gd_ref,
 ):
     f = ho_ref.shape[1]
     kp = gd_ref.shape[2]
-    gw_ref[...] = (t_dot(xo_ref[...], go_ref[...]) + t_dot(xe_ref[...], ge_ref[...])).astype(BF)
+    both = t_dot(xo_ref[...], go_ref[...]) + t_dot(xe_ref[...], ge_ref[...])
+    gg_ref[...] = both[:, :f].astype(BF)
+    gu_ref[...] = both[:, f:].astype(BF)
     down = (t_dot(ho_ref[...], co_ref[...]) + t_dot(he_ref[...], ce_ref[...])).astype(BF)
     for i in range(gd_ref.shape[0]):
         gd_ref[i, :f, :] = down[:, i * kp : (i + 1) * kp]
@@ -420,11 +440,13 @@
             pl.BlockSpec((wide // kp, extra, kp), lambda i: (i, 0, 0)),
         ],
         out_specs=(
-            pl.BlockSpec((wide, 2 * f), lambda i: (i, 0)),
+            pl.BlockSpec((wide, f), lambda i: (i, 0)),
+            pl.BlockSpec((wide, f), lambda i: (i, 0)),
             pl.BlockSpec((wide // kp, f + extra, kp), lambda i: (i, 0, 0)),
         ),
         out_shape=(
-            jax.ShapeDtypeStruct((dp, 2 * f), BF),
+            jax.ShapeDtypeStruct((dp, f), BF),
+            jax.ShapeDtypeStruct((dp, f), BF),
             jax.ShapeDtypeStruct((n, f + extra, kp), BF),
         ),
         compiler_params=pltpu.CompilerParams(vmem_limit_bytes=48 * MIB),
@@ -527,7 +549,7 @@
     mixes = []
     for d_ref, m_ref, g_ref, c_ref, b_ref, r_ref, l_ref, first, last in (
         (dp_scr, mp_ref, gp_ref, cp_ref, bp_ref, rp_scr, lp_ref, 0, kp),
-        (da_scr, ma_ref, ga_ref, ca_ref, ba_ref, ra_scr, la_ref, kp, w_ref.shape[1]),
+        (da_scr, ma_ref, ga_ref, ca_ref, ba_ref, ra_scr, la_ref, kp, w_ref.shape[2]),
     ):
         gradient = d_ref[...].astype(F32)
         rows = m_ref[...].astype(F32)
@@ -541,7 +563,11 @@
         r_ref[...] = dresid
         branch = dresid.astype(BF)
         b_ref[...] = branch
-        mixes.append(dot(branch, w_ref[:, first:last, :].reshape(rows.shape[1], -1)))
+        size = last - first
+        mix = jnp.zeros((rows.shape[0], dm_ref.shape[1]), F32)
+        for d in range(n):
+            mix = mix + dot_t(branch[:, d * size : (d + 1) * size], w_ref[d, :, first:last])
+        mixes.append(mix)
     dm_ref[...] = jnp.concatenate(mixes, axis=0).astype(BF)
     own_ref[:rp, :] = rp_scr[:, place(t, cp)]
     own_ref[rp:, :] = jnp.concatenate(
@@ -553,19 +579,20 @@
     rp, dp = bp_ref.shape
     n = out_ref.shape[0]
     kp = dp // n
-    width = mix_ref.shape[1]
-    out_ref[:, :kp, :] = t_dot(bp_ref[...], mix_ref[:rp, :]).astype(BF).reshape(n, kp, width)
-    out_ref[:, kp:, :] = t_dot(ba_ref[...], mix_ref[rp:, :]).astype(BF).reshape(n, -1, width)
+    ka = ba_ref.shape[1] // n
+    for d in range(n):
+        out_ref[d, :, :kp] = t_dot(mix_ref[:rp, :], bp_ref[:, d * kp : (d + 1) * kp]).astype(BF)
+        out_ref[d, :, kp:] = t_dot(mix_ref[rp:, :], ba_ref[:, d * ka : (d + 1) * ka]).astype(BF)
 
 
 def front_back_kernel(heads_width, s_ref, t_ref, dq_ref, *refs):
     tp = lax.axis_size("tp")
     n = lax.axis_size("seq")
     (ka_ref, ra_ref, kb_ref, rb_ref, xp_ref, xa_ref, inv_ref, gp_ref, ga_ref, w_ref, lp_ref,
-     la_ref) = refs[:12]
-    groups = refs[12:16]
-    pieces = refs[16 : 16 + tp]
-    gwp_scr, gwa_scr, gain_scr, dp_scr, da_scr = refs[16 + tp :]
+     la_ref, lifted_ref) = refs[:13]
+    groups = refs[13:17]
+    pieces = refs[17 : 17 + tp]
+    gwp_scr, gwa_scr, gain_scr, dp_scr, da_scr = refs[17 + tp :]
     rp, dp = xp_ref.shape
     ra, da = xa_ref.shape
     kp, ka = dp // n, da // n
@@ -612,9 +639,13 @@
         action = jnp.concatenate(
             [da_scr[:, place(rank, ca)], jnp.zeros((ra, cp - ca), F32)], axis=1
         )
-        pieces[k][...] = jnp.concatenate([dp_scr[:, place(rank, cp)], action, tail], axis=0).astype(
-            BF
+        lifted_action = jnp.concatenate(
+            [lifted_ref[rp:, place(rank, ca)].astype(F32), jnp.zeros((ra, cp - ca), F32)], axis=1
         )
+        lifted = lifted_ref[:rp, place(rank, cp)].astype(F32)
+        pieces[k][...] = jnp.concatenate(
+            [dp_scr[:, place(rank, cp)], action, tail, lifted, lifted_action], axis=0
+        ).astype(BF)
     for odd in range(2):
         for number in range(2):
             out = groups[2 * odd + number]
@@ -657,44 +688,57 @@
         o_ref[...] = (r_ref[begin:end, :wide] + moved).astype(BF)
 
 
-def home_kernel(token_ref, gu_ref, down_in_ref, gate_ref, up_ref, down_ref, act_ref):
+def home_kernel(token_ref, g_ref, d_ref, gate_ref, down_ref, act_ref):
     del token_ref
     f = gate_ref.shape[1]
-    gate_ref[...] = gu_ref[0, :, :f].astype(F32)
-    up_ref[...] = gu_ref[0, :, f:].astype(F32)
-    down_ref[...] = down_in_ref[0, :f, :].astype(F32)
-    act_ref[0] = down_in_ref[0, f:, :].astype(F32)
-
-
-def home(token, got_gu, got_down):
-    n, kp, both = got_gu.shape
-    f = both // 2
+    gate_ref[...] = g_ref[0].astype(F32)
+    down_ref[...] = d_ref[0, :f, :].astype(F32)
+    act_ref[0] = d_ref[0, f:, :].astype(F32)
+
+
+def home(token, got_gate, got_down):
+    n, kp, f = got_gate.shape
     tall = got_down.shape[1]
-    out = pl.BlockSpec((kp, f), lambda j: (0, j))
     return pl.pallas_call(
         home_kernel,
         grid=(n,),
         in_specs=[
             pl.BlockSpec(memory_space=pltpu.SMEM),
-            pl.BlockSpec((1, kp, both), lambda j: (j, 0, 0)),
+            pl.BlockSpec((1, kp, f), lambda j: (j, 0, 0)),
             pl.BlockSpec((1, tall, kp), lambda j: (j, 0, 0)),
         ],
         out_specs=(
-            out,
-            out,
+            pl.BlockSpec((kp, f), lambda j: (0, j)),
             pl.BlockSpec((f, kp), lambda j: (j, 0)),
             pl.BlockSpec((1, tall - f, kp), lambda j: (j, 0, 0)),
         ),
         out_shape=(
-            jax.ShapeDtypeStruct((kp, n * f), F32),
             jax.ShapeDtypeStruct((kp, n * f), F32),
             jax.ShapeDtypeStruct((n * f, kp), F32),
             jax.ShapeDtypeStruct((n, tall - f, kp), F32),
         ),
         cost_estimate=pl.CostEstimate(
-            flops=0, bytes_accessed=6 * n * kp * (both + tall), transcendentals=0
-        ),
-    )(token, got_gu, got_down)
+            flops=0, bytes_accessed=6 * n * kp * (f + tall), transcendentals=0
+        ),
+    )(token, got_gate, got_down)
+
+
+def home_up_kernel(u_ref, up_ref):
+    up_ref[...] = u_ref[0].astype(F32)
+
+
+def home_up(got):
+    n, kp, f = got.shape
+    return pl.pallas_call(
+        home_up_kernel,
+        grid=(n,),
+        in_specs=[pl.BlockSpec((1, kp, f), lambda j: (j, 0, 0))],
+        out_specs=pl.BlockSpec((kp, f), lambda j: (0, j)),
+        out_shape=jax.ShapeDtypeStruct((kp, n * f), F32),
+        cost_estimate=pl.CostEstimate(
+            flops=0, bytes_accessed=6 * n * kp * f, transcendentals=0
+        ),
+    )(got)
 
 
 def shards(
@@ -761,9 +805,9 @@
     mlp_gain_p = got_gains[:, kp : 2 * kp].reshape(1, dp)
     attn_gain_a = got_gains[:, 2 * kp : 2 * kp + ka].reshape(1, da)
     mlp_gain_a = got_gains[:, 2 * kp + ka : 2 * kp + 2 * ka].reshape(1, da)
-    pack_out = jnp.concatenate([prefix_out.T, action_out.T], axis=0)
+    pack_out = jnp.concatenate([prefix_out, action_out], axis=1)
     cot_wide = jnp.pad(cot_action, ((0, 0), (0, dp - da)))
-    cot_stages = gather_stacked(
+    cot_stages, cot_last = gather_stacked(
         [
             jnp.concatenate(
                 [
@@ -802,7 +846,7 @@
             ((ra, da), BF),
             ((rows, 128), F32),
         ),
-        [after(rank_t, cot_even), *x_pieces, got_qkv, attn_gain_p, attn_gain_a],
+        [after(rank_t, *cot_last), *x_pieces, got_qkv, attn_gain_p, attn_gain_a],
         2 * rp * dp * qkv_width,
     )
     kv_even = [jnp.concatenate(blocks, axis=0) for blocks in gather_far([kv_a, kv_b])]
@@ -894,7 +938,7 @@
         ],
         axis=2,
     ).reshape(n, extra, kp)
-    grad_gu, grad_down = weight_grads(
+    grad_gate, grad_up, grad_down = weight_grads(
         normed_odd, normed_even, cot_odd, cot_even, h_odd, h_even, g_odd, g_even, action_grads
     )
     ranks = s ^ jnp.arange(n, dtype=jnp.int32)
@@ -909,8 +953,8 @@
     lifted = lift(
         odd_bits, *places, *lift_places, h_odd, h_even, lifted_action, down, half, ra
     )
-    ((keep_a, got_a), (keep_b, got_b)), _ = scatter_rows(
-        [(dn_blocks[0][i], dn_blocks[1][i]) for i in range(2)], grad_gu
+    ((keep_a, got_a), (keep_b, got_b)), *_ = scatter_rows(
+        [(dn_blocks[0][i], dn_blocks[1][i]) for i in range(2)], grad_gate
     )
     sent_pieces = whole_call(
         pieces_kernel,
@@ -922,6 +966,10 @@
     dn_pieces = gather_tp(dn_own.astype(BF))
     lifted_home = lax.psum_scatter(after(lifted, got_a, got_b), "seq", scatter_dimension=0)
     grad_down_home = lax.all_to_all(after(grad_down, sent_pieces[0]), "seq", 0, 0)
+
+    grad_gate_home = lax.all_to_all(
+        after(grad_gate, grad_down_home).reshape(n, kp, fp), "seq", 0, 0
+    )
 
     row = ((1, dp), F32)
     row_a = ((1, da), F32)
@@ -937,9 +985,6 @@
             pltpu.VMEM((ra, da), F32),
         ),
     )
-    grad_gu_home = lax.all_to_all(
-        after(grad_gu, grad_down_home, dbranch_a).reshape(n, kp, 2 * fp), "seq", 0, 0
-    )
     dquery, *dkv_parts = whole_call(
         attend_back_kernel,
         (((rows, width), BF),) + (((n * rows // 4, 2 * HD), BF),) * 4,
@@ -952,34 +997,21 @@
         [d.reshape(n // 2, half, 2 * HD) for d in (e, swap(o, "seq", 1))]
         for e, o in ((dkv_parts[0], dkv_parts[1]), (dkv_parts[2], dkv_parts[3]))
     ]
-    dkv = [part for pair in scatter_rows(dkv_halves)[0] for part in pair]
+    dkv = [part for pair in scatter_rows(dkv_halves, grad_gate_home)[0] for part in pair]
     (out_grads,) = whole_call(
         out_grad_kernel,
-        (((n, kp + ka, width), BF),),
+        (((n, width, kp + ka), BF),),
         [dbranch_p, dbranch_a, after(mixed, dquery)],
         2 * rows * dp * width,
     )
-    out_home = lax.psum_scatter(out_grads, "seq", scatter_dimension=0).astype(F32)
-    def own_piece(rank):
-        return jnp.concatenate(
-            [
-                lax.dynamic_slice(lifted_home, (0, rank * cp), (rp, cp)),
-                jnp.pad(
-                    lax.dynamic_slice(lifted_home, (rp, rank * ca), (ra, ca)),
-                    ((0, 0), (0, cp - ca)),
-                ),
-            ],
-            axis=0,
-        )
-
-    output = (residual + sum_tp([own_piece(t ^ k) for k in range(tp)])).astype(BF)
+    out_home = lax.psum_scatter(out_grads, "seq", scatter_dimension=0)
     tall = (kp + ka) // 2 + 8
     *groups_and_pieces, = whole_call(
         lambda *refs: front_back_kernel(width, *refs),
-        (((n // 2, tall, qkv_width), BF),) * 4 + (((rows + 8, cp), BF),) * tp,
+        (((n // 2, tall, qkv_width), BF),) * 4 + (((2 * rows + 8, cp), BF),) * tp,
         [
-            after(rank_s, output), rank_t, dquery, *dkv, x_full_p, x_full_a, inverse1, attn_gain_p, attn_gain_a,
-            got_qkv, mlp_gains_p, mlp_gains_a,
+            rank_s, rank_t, dquery, *dkv, x_full_p, x_full_a, inverse1, attn_gain_p, attn_gain_a,
+            got_qkv, mlp_gains_p, mlp_gains_a, lifted_home,
         ],
         4 * rows * dp * qkv_width,
         scratch=(
@@ -991,15 +1023,22 @@
         ),
     )
     groups, pieces = groups_and_pieces[:4], groups_and_pieces[4:]
-    tree, first_sent = scatter_rows(
-        [(e, swap(o, "seq", 1)) for e, o in ((groups[0], groups[2]), (groups[1], groups[3]))]
+    tree, history, (tp_parts, _) = scatter_rows(
+        [(e, swap(o, "seq", 1)) for e, o in ((groups[0], groups[2]), (groups[1], groups[3]))],
+        None,
+        (trade_tp(pieces), ()),
+    )
+    lifted_parts = [part[rows + 8 :] for part in tp_parts]
+    grad_up_home = lax.all_to_all(
+        after(grad_up, grad_gate_home, groups[0]).reshape(n, kp, fp), "seq", 0, 0
     )
     qkv_a, qkv_b = [add(keep, got) for keep, got in tree]
+    output = (residual + total_of(lifted_parts)).astype(BF)
     grad_x_p, grad_x_a = whole_call(
         grad_x_kernel,
         (((rp, cp), BF), ((ra, ca), BF)),
         [
-            after(rank_t, first_sent), pieces[0], *[swap(pieces[k], "tp", k) for k in range(1, tp)], x_pack,
+            after(rank_t, history[-1]), *tp_parts, x_pack,
             inverse1, attn_gain_p, attn_gain_a, dresid,
         ],
         rp * dp,
@@ -1024,9 +1063,11 @@
 
     shared_home = sum_tp([shared_piece(t ^ k) for k in range(tp)])
     attn_gains_home = shared_home[qp + qa]
-    grad_gate_p, grad_up_p, grad_down_p, action_home = home(
-        after(rank_t, first_sent), grad_gu_home, grad_down_home
-    )
+    out_home = after(out_home, *history[-1]).astype(F32)
+    grad_gate_p, grad_down_p, action_home = home(
+        after(rank_t, history[0]), grad_gate_home, grad_down_home
+    )
+    grad_up_p = home_up(grad_up_home)
     action_home = action_home.reshape(n, ka, 3 * fa)
 
     def units(part):
@@ -1044,7 +1085,7 @@
         qkv_home_p[:, :width],
         shared_home[:qp, :HD],
         shared_home[:qp, HD:],
-        out_home[:kp].T,
+        out_home[:, :kp],
         gains_home[0, 512 : 512 + kp],
         grad_gate_p,
         grad_up_p,
@@ -1053,7 +1094,7 @@
         qkv_home_a[:, :width],
         shared_home[qp : qp + qa, :HD],
         shared_home[qp : qp + qa, HD:],
-        out_home[kp:].T,
+        out_home[:, kp:],
         gains_home[0, 768 : 768 + ka],
         grad_gate_a,
         grad_up_a,

time: 624 us -> 616 us (0.987)
  waiting for transfers between devices: 261 us -> 249 us
  starting transfers between devices: 116 us -> 105 us
  other arithmetic: 41.2 us -> 48.4 us
  Pallas kernels: 112 us -> 119 us
    ppermute x61 -> x58, waiting for transfers between devices: 214 us -> 193 us  [swap(): return lax.ppermute(value, axis, [(i, i ^ mask) for i in range(count)])]
    ppermute x61 -> x58, starting transfers between devices: 91.1 us -> 73.1 us  [swap(): return lax.ppermute(value, axis, [(i, i ^ mask) for i in range(count)])]
    convert_element_type x9 -> x11, other arithmetic: 13.2 us -> 23.8 us  [the longest x10 22.5 us: scatter_rows(): sent = [total_of([p[keep:] for p in part]).astype(BF) for part in parts]]
    all_to_all x1, waiting for transfers between devices: 10.3 us -> 20.6 us  [shards(): lax.all_to_all(after(grad_down, sent_pieces[0]), 'seq', 0, 0)]
    reduce_scatter x1, starting transfers between devices: 0.21 us -> 8.79 us  [shards(): out_home = lax.psum_scatter(out_grads, 'seq', scatter_dimension=0)]
    add x6 -> x2, other arithmetic: 10.4 us -> 3.26 us  [add(): return left.astype(F32) + right.astype(F32)]
    unnamed x187 -> x167, local copies, waits for them, and re-layouts: 33.7 us -> 31.8 us
  transfers between devices with their start and end apart: 69 -> 67, of which waited for: 30 -> 37; matrix products, arithmetic and copies ran while one was open for 12% -> 13% of each run, Pallas kernels for 14% -> 15%
where the time goes in v5:
time: 616 us; the launch traced here: 605 us
  waiting for transfers between devices  249 us (40%)
  Pallas kernels  119 us (19%)
  starting transfers between devices  105 us (17%)
  local copies, waits for them, and re-layouts  69 us (11%)
  other arithmetic  48.4 us (8%)
  between operations  15.3 us (2%)
    ppermute x58, waiting for transfers between devices, swap(): return lax.ppermute(value, axis, [(i, i ^ mask) for i in range(count)])  193 us
    ppermute x58, starting transfers between devices, swap(): return lax.ppermute(value, axis, [(i, i ^ mask) for i in range(count)])  73.1 us
    pallas_call x11, Pallas kernels, whole_call(): pl.pallas_call(kernel, out_shape=outs, in_specs=specs, out_specs=tuple((p...  39.6 us
    pallas_call x2, Pallas kernels, feed(): pl.pallas_call(lambda *refs: feed_kernel(pair, *refs), grid=(total // ste...  36.6 us
    all_to_all x1, waiting for transfers between devices, shards(): lax.all_to_all(after(gate_up_sent, branch), 'seq', 0, 0).reshape(dp, 2 * fp)  32.8 us
    unnamed x167, local copies, waits for them, and re-layouts  31.8 us
    convert_element_type x10, other arithmetic, scatter_rows(): sent = [total_of([p[keep:] for p in part]).astype(BF) for part in parts]  22.5 us
    pallas_call x1, Pallas kernels, weight_grads(): pl.pallas_call(weights_kernel, grid=(dp // wide,), in_specs=[cols, cols,...  22 us
  transfers between devices with their start and end apart: 67, of which 37 were waited for; matrix products, arithmetic and copies ran while one was open for 13% of the time, Pallas kernels for 15%

profile of v5, /device:TPU:0, one launch (start us, length us, event | category | flops | bytes accessed | tf_op | source)
XLA Modules:
  0.0 605.3 jit_solution(1044784226478099758)
XLA Ops:
  12.0 3.0 collective-permute-start
  16.7 16.7 %collective-permute-done = bf16[136,2048]{1,0:T(8,128)(2,1)S(1)} collective-permute-done((bf16[136,2048]{1,0:T(8,128)(2,1)S(1)}, bf16[136,2048]{1,0:T(8,128)(2,1)S(1)}, u32[]{:S(2)}, u32[]{:S(2)}) %collective-permute-start) | collective-permute-done | bytes 557088 | tf_op jit(solution)/shard_map/ppermute | solution.py:21
  33.4 2.8 collective-permute-done.1
  42.6 2.8 collective-permute-start.5
  46.3 32.8 %collective-permute-done.2 = bf16[272,2048]{1,0:T(8,128)(2,1)} collective-permute-done((bf16[272,2048]{1,0:T(8,128)(2,1)}, bf16[272,2048]{1,0:T(8,128)(2,1)}, u32[]{:S(2)}, u32[]{:S(2)}) %collective-permute-start.2) | collective-permute-done | bytes 1114144 | tf_op jit(solution)/shard_map/ppermute | solution.py:21
  81.5 4.7 shard_map.408
  92.3 3.7 pad_maximum_fusion.1
  98.8 5.7 collective-permute-done.7
  114.9 6.4 %collective-permute-done.13 = bf16[136,512]{1,0:T(8,128)(2,1)S(1)} collective-permute-done((bf16[136,512]{1,0:T(8,128)(2,1)S(1)}, bf16[136,512]{1,0:T(8,128)(2,1)S(1)}, u32[]{:S(2)}, u32[]{:S(2)}) %collective-permute-start.13) | collective-permute-done | bytes 139296 | tf_op jit(solution)/shard_map/ppermute | solution.py:21
  124.8 4.5 all-to-all-start.1
  136.7 3.8 shard_map.409
  144.8 3.8 collective-permute-start.17
  156.3 16.1 %collective-permute-done.16 = bf16[272,512]{1,0:T(8,128)(2,1)S(1)} collective-permute-done((bf16[272,512]{1,0:T(8,128)(2,1)S(1)}, bf16[272,512]{1,0:T(8,128)(2,1)S(1)}, u32[]{:S(2)}, u32[]{:S(2)}) %collective-permute-start.16) | collective-permute-done | bytes 278560 | tf_op jit(solution)/shard_map/ppermute | solution.py:21
  173.4 4.5 all-to-all-start
  185.4 3.1 collective-permute-start.20
  194.2 32.8 %all-to-all-done = bf16[8,256,1024]{2,1,0:T(8,128)(2,1)} async-done(((bf16[8,256,1024]{2,1,0:T(8,128)(2,1)}), bf16[8,256,1024]{2,1,0:T(8,128)(2,1)}, u32[]{:S(2)}, u32[]{:S(2)}) %all-to-all-start) | async-done | bytes 4194336 | tf_op jit(solution)/shard_map/all_to_all | solution.py:888
  231.3 10.8 %collective-permute-done.22 = bf16[136,2048]{1,0:T(8,128)(2,1)S(1)} collective-permute-done((bf16[136,2048]{1,0:T(8,128)(2,1)S(1)}, bf16[136,2048]{1,0:T(8,128)(2,1)S(1)}, u32[]{:S(2)}, u32[]{:S(2)}) %collective-permute-start.22) | collective-permute-done | bytes 557088 | tf_op jit(solution)/shard_map/ppermute | solution.py:21
  246.4 10.3 %collective-permute-done.23 = bf16[136,2048]{1,0:T(8,128)(2,1)S(1)} collective-permute-done((bf16[136,2048]{1,0:T(8,128)(2,1)S(1)}, bf16[136,2048]{1,0:T(8,128)(2,1)S(1)}, u32[]{:S(2)}, u32[]{:S(2)}) %collective-permute-start.23) | collective-permute-done | bytes 557088 | tf_op jit(solution)/shard_map/ppermute | solution.py:21
  256.7 10.7 %collective-permute-done.24 = bf16[136,2048]{1,0:T(8,128)(2,1)S(1)} collective-permute-done((bf16[136,2048]{1,0:T(8,128)(2,1)S(1)}, bf16[136,2048]{1,0:T(8,128)(2,1)S(1)}, u32[]{:S(2)}, u32[]{:S(2)}) %collective-permute-start.24) | collective-permute-done | bytes 557088 | tf_op jit(solution)/shard_map/ppermute | solution.py:21
  268.1 7.5 %collective-permute-done.28.refs_0_.xo_ref = bf16[1088,2048]{1,0:T(8,128)(2,1)S(1)} collective-permute-done((bf16[1088,2048]{1,0:T(8,128)(2,1)S(1)}, bf16[1088,2048]{1,0:T(8,128)(2,1)S(1)}, u32[]{:S(2)}, u32[]{:S(2)}) %collective-permute-start.28) | collective-permute-done | bytes 4456480 | tf_op jit(solution)/shard_map/ppermute | solution.py:21
  280.4 18.3 %shard_map.413 = (bf16[1088,512]{1,0:T(8,128)(2,1)}, bf16[1088,1024]{1,0:T(8,128)(2,1)}, bf16[1088,2048]{1,0:T(8,128)(2,1)}) custom-call(bf16[1088,2048]{1,0:T(8,128)(2,1)} %copy-done.68, bf16[1088,2048]{1,0:T(8,128)(2,1)} %collective-permute-done.18.refs_1_.co_ref, bf16[2048,1024]{1,0:T(8,128)(2,1)} %bitcast.8.refs_2_, bf16[512,2048]{1,0:T(8,128)(2,1)} %bitcast.151, ...), custom_call_target="tpu_custom_call" | custom-call | flops 11408506880 | bytes 24117248 | tf_op jit(solution)/shard_map/pallas_call | solution.py:372
  300.2 18.3 %shard_map.414 = (bf16[1088,512]{1,0:T(8,128)(2,1)}, bf16[1088,1024]{1,0:T(8,128)(2,1)}, bf16[1088,2048]{1,0:T(8,128)(2,1)}) custom-call(bf16[1088,2048]{1,0:T(8,128)(2,1)} %copy-done.65, bf16[1088,2048]{1,0:T(8,128)(2,1)} %constant_dynamic-update-slice_fusion.10.refs_1_.ce_ref, bf16[2048,1024]{1,0:T(8,128)(2,1)} %bitcast.8.refs_2_, ...), custom_call_target="tpu_custom_call" | custom-call | flops 11408506880 | bytes 24117248 | tf_op jit(solution)/shard_map/pallas_call | solution.py:372
  319.3 3.4 add_convert_fusion
  326.2 22.0 %shard_map.415 = (bf16[2048,512]{1,0:T(8,128)(2,1)S(1)}, bf16[2048,512]{1,0:T(8,128)(2,1)}, bf16[8,704,256]{2,1,0:T(8,128)(2,1)}) custom-call(bf16[1088,2048]{1,0:T(8,128)(2,1)} %copy-done.68, bf16[1088,2048]{1,0:T(8,128)(2,1)} %copy-done.65, bf16[1088,2048]{1,0:T(8,128)(2,1)} %collective-permute-done.18.refs_1_.co_ref, ...), custom_call_target="tpu_custom_call" | custom-call | flops 13690208256 | bytes 17825792 | tf_op jit(solution)/shard_map/pallas_call | solution.py:428
  351.0 3.6 fusion
  357.1 7.0 %shard_map.416 = bf16[8,272,2048]{2,1,0:T(8,128)(2,1)S(1)} custom-call(s32[8]{0:T(128)S(1)} %get-tuple-element.258.odd_ref, s32[8]{0:T(128)S(1)} %gather_fusion, s32[8]{0:T(128)S(1)} %gather_fusion.1, s32[8]{0:T(128)S(1)} %fusion.46.la_ref, s32[8]{0:T(128)S(1)} %get-tuple-element.259.lb_ref, bf16[1088,512]{1,0:T(8,128)(2,1)S(1)} %copy-done.42, ...), custom_call_target="tpu_custom_call" | custom-call | flops 4563402752 | bytes 8912896 | tf_op jit(solution)/shard_map/pallas_call | solution.py:484
  364.1 3.5 copy-done.3
  374.2 4.6 all-to-all-start.2
  383.3 7.0 %collective-permute-done.36 = bf16[272,512]{1,0:T(8,128)(2,1)S(1)} collective-permute-done((bf16[272,512]{1,0:T(8,128)(2,1)S(1)}, bf16[272,512]{1,0:T(8,128)(2,1)S(1)}, u32[]{:S(2)}, u32[]{:S(2)}) %collective-permute-start.36) | collective-permute-done | bytes 278560 | tf_op jit(solution)/shard_map/ppermute | solution.py:21
  390.3 14.6 %collective-permute-done.35 = bf16[272,512]{1,0:T(8,128)(2,1)S(1)} collective-permute-done((bf16[272,512]{1,0:T(8,128)(2,1)S(1)}, bf16[272,512]{1,0:T(8,128)(2,1)S(1)}, u32[]{:S(2)}, u32[]{:S(2)}) %collective-permute-start.35) | collective-permute-done | bytes 278560 | tf_op jit(solution)/shard_map/ppermute | solution.py:21
  409.5 20.6 %all-to-all-done.2.d_ref = bf16[8,704,256]{2,1,0:T(8,128)(2,1)} async-done(((bf16[8,704,256]{2,1,0:T(8,128)(2,1)}), bf16[8,704,256]{2,1,0:T(8,128)(2,1)}, u32[]{:S(2)}, u32[]{:S(2)}) %all-to-all-start.2) | async-done | bytes 2883616 | tf_op jit(solution)/shard_map/all_to_all | solution.py:968
  430.2 4.5 all-to-all-start.3
  434.7 8.8 %reduce-scatter.5.cloned.1.call-start = ((), (), s32[]{:S(2)}) async-start(), calls=%async_computation.8 | async-start | bytes 3538944 | tf_op jit(solution)/shard_map/reduce_scatter | solution.py:1007
  443.5 4.7 shard_map.418
  449.8 8.3 %shard_map.419 = (bf16[272,512]{1,0:T(8,128)(2,1)}, bf16[544,512]{1,0:T(8,128)(2,1)}, bf16[544,512]{1,0:T(8,128)(2,1)}, bf16[544,512]{1,0:T(8,128)(2,1)}, bf16[544,512]{1,0:T(8,128)(2,1)}) custom-call(bf16[272,512]{1,0:T(8,128)(2,1)} %copy-done.36, bf16[2176,512]{1,0:T(8,128)(2,1)} %copy-done.31, s32[272,1]{1,0:T(8,128)} %copy-done.22, ...), custom_call_target="tpu_custom_call" | custom-call | flops 3030384640 | bytes 6137408 | tf_op jit(solution)/shard_map/pallas_call | solution.py:127
  470.1 8.2 %collective-permute-done.41 = bf16[2,136,512]{2,1,0:T(8,128)(2,1)} collective-permute-done((bf16[2,136,512]{2,1,0:T(8,128)(2,1)}, bf16[2,136,512]{2,1,0:T(8,128)(2,1)}, u32[]{:S(2)}, u32[]{:S(2)}) %collective-permute-start.41) | collective-permute-done | bytes 278560 | tf_op jit(solution)/shard_map/ppermute | solution.py:21
  484.8 2.9 collective-permute-done.44
  490.0 10.9 %shard_map.420 = (bf16[4,200,1024]{2,1,0:T(8,128)(2,1)}, bf16[4,200,1024]{2,1,0:T(8,128)(2,1)}, bf16[4,200,1024]{2,1,0:T(8,128)(2,1)}, bf16[4,200,1024]{2,1,0:T(...) custom-call(s32[1]{0:T(128)} %bitcast.5.refs_0_, ...), custom_call_target="tpu_custom_call" | custom-call | flops 2281701376 | bytes 18710536 | tf_op jit(solution)/shard_map/pallas_call | solution.py:127
  501.4 4.5 all-to-all-start.4
  518.5 7.7 %shard_map.423 = (f32[256,4096]{1,0:T(8,128)}, f32[4096,256]{1,0:T(8,128)}, f32[8,192,256]{2,1,0:T(8,128)}) custom-call(s32[1]{0:T(128)} %bitcast.t_ref.refs_1_.token_ref, bf16[8,256,512]{2,1,0:T(8,128)(2,1)} %all-to-all-done.3.g_ref, bf16[8,704,256]{2,1,0:T(8,128)(2,1)} %all-to-all-done.2.d_ref), custom_call_target="tpu_custom_call" | custom-call | bytes 14942208 | tf_op jit(solution)/shard_map/pallas_call | solution.py:702
  526.3 2.7 reshape.318
  537.3 6.0 shard_map.424
  543.3 11.9 %collective-permute-done.51.refs_2_ = bf16[552,512]{1,0:T(8,128)(2,1)S(1)} collective-permute-done((bf16[552,512]{1,0:T(8,128)(2,1)}, bf16[552,512]{1,0:T(8,128)(2,1)S(1)}, u32[]{:S(2)}, u32[]{:S(2)}) %collective-permute-start.51) | collective-permute-done | bytes 565280 | tf_op jit(solution)/shard_map/ppermute | solution.py:21
  555.2 2.7 collective-permute-done.47
  574.2 3.6 collective-permute-done.53
  582.3 3.4 collective-permute-start.57
  585.7 4.6 collective-permute-start.56
  590.3 5.5 collective-permute-done.56
  (375 shorter events, 179.6 us)
Async XLA Ops:
  7.2 73.2 %all-gather.5.cloned.1.call-start = ((), (), s32[]{:S(2)}) async-start(), calls=%async_computation.9 | async-start | bytes 7225344 | tf_op jit(solution)/shard_map/all_gather | solution.py:802
  10.3 131.7 %all-gather.7.cloned.1.call-start = ((), (), s32[]{:S(2)}) async-start(), calls=%async_computation.10 | async-start | bytes 3538944 | tf_op jit(solution)/shard_map/all_gather | solution.py:877
  12.0 21.4 %collective-permute-start = (bf16[136,2048]{1,0:T(8,128)(2,1)S(1)}, bf16[136,2048]{1,0:T(8,128)(2,1)S(1)}, u32[]{:S(2)}, u32[]{:S(2)}) collective-permute-start(bf16[136,2048]{1,0:T(8,128)(2,1)S(1)} %pad_maximum_fusion.7), channel_id=1, source_target_pairs={{0,8},{4,12},{8,0},{12,4},{16,24},{20,28},{24,16},{28,20},{1,9},{5... | collective-permute-start | bytes 1671176 | tf_op jit(solution)/shard_map/ppermute | solution.py:21
  15.1 21.1 %collective-permute-start.1 = (bf16[136,2048]{1,0:T(8,128)(2,1)S(1)}, bf16[136,2048]{1,0:T(8,128)(2,1)S(1)}, u32[]{:S(2)}, u32[]{:S(2)}) collective-permute-start(bf16[136,2048]{1,0:T(8,128)(2,1)S(1)} %pad_maximum_fusion.8), channel_id=1, source_target_pairs={{0,16},{4,20},{8,24},{12,28},{16,0},{20,4},{24,8},{28,12},{1,17},{... | collective-permute-start | bytes 1671176 | tf_op jit(solution)/shard_map/ppermute | solution.py:21
  37.4 41.7 %collective-permute-start.2 = (bf16[272,2048]{1,0:T(8,128)(2,1)}, bf16[272,2048]{1,0:T(8,128)(2,1)}, u32[]{:S(2)}, u32[]{:S(2)}) collective-permute-start(bf16[272,2048]{1,0:T(8,128)(2,1)} %pad_maximum_fusion.2), channel_id=1, source_target_pairs={{0,16},{4,20},{8,24},{12,28},{16,0},{20,4},{24,8},{28,12},{1,17},{... | collective-permute-start | bytes 3342344 | tf_op jit(solution)/shard_map/ppermute | solution.py:21
  41.0 39.4 %collective-permute-start.3 = (bf16[272,2048]{1,0:T(8,128)(2,1)}, bf16[272,2048]{1,0:T(8,128)(2,1)}, u32[]{:S(2)}, u32[]{:S(2)}) collective-permute-start(bf16[272,2048]{1,0:T(8,128)(2,1)} %pad_maximum_fusion.3), channel_id=1, source_target_pairs={{0,8},{4,12},{8,0},{12,4},{16,24},{20,28},{24,16},{28,20},{1,9},{5... | collective-permute-start | bytes 3342344 | tf_op jit(solution)/shard_map/ppermute | solution.py:21
  41.1 40.4 %collective-permute-start.4 = (bf16[272,512]{1,0:T(8,128)(2,1)S(1)}, bf16[272,512]{1,0:T(8,128)(2,1)S(1)}, u32[]{:S(2)}, u32[]{:S(2)}) collective-permute-start(bf16[272,512]{1,0:T(8,128)(2,1)S(1)} %fusion.5.refs_0_.refs_4_), channel_id=1, source_target_pairs={{0,1},{1,0},{2,3},{3,2},{4,5},{5,4},{6,7},{7,6},{8,9},{9,8},{10,11... | collective-permute-start | bytes 835592 | tf_op jit(solution)/shard_map/ppermute | solution.py:21
  42.6 38.9 %collective-permute-start.5 = (bf16[272,512]{1,0:T(8,128)(2,1)S(1)}, bf16[272,512]{1,0:T(8,128)(2,1)S(1)}, u32[]{:S(2)}, u32[]{:S(2)}) collective-permute-start(bf16[272,512]{1,0:T(8,128)(2,1)S(1)} %fusion.5.refs_0_.refs_4_), channel_id=1, source_target_pairs={{0,2},{1,3},{2,0},{3,1},{4,6},{5,7},{6,4},{7,5},{8,10},{9,11},{10,... | collective-permute-start | bytes 835592 | tf_op jit(solution)/shard_map/ppermute | solution.py:21
  45.3 36.2 %collective-permute-start.6 = (bf16[272,512]{1,0:T(8,128)(2,1)S(1)}, bf16[272,512]{1,0:T(8,128)(2,1)S(1)}, u32[]{:S(2)}, u32[]{:S(2)}) collective-permute-start(bf16[272,512]{1,0:T(8,128)(2,1)S(1)} %fusion.5.refs_0_.refs_4_), channel_id=1, source_target_pairs={{0,3},{1,2},{2,1},{3,0},{4,7},{5,6},{6,5},{7,4},{8,11},{9,10},{10,... | collective-permute-start | bytes 835592 | tf_op jit(solution)/shard_map/ppermute | solution.py:21
  97.5 12.5 %collective-permute-start.8 = (bf16[136,512]{1,0:T(8,128)(2,1)S(1)}, bf16[136,512]{1,0:T(8,128)(2,1)S(1)}, u32[]{:S(2)}, u32[]{:S(2)}) collective-permute-start(bf16[136,512]{1,0:T(8,128)(2,1)S(1)} %get-tuple-element.118), channel_id=1, source_target_pairs={{0,16},{4,20},{8,24},{12,28},{16,0},{20,4},{24,8},{28,12},{1,17},{... | collective-permute-start | bytes 417800 | tf_op jit(solution)/shard_map/ppermute | solution.py:21
  124.8 48.6 %all-to-all-start.1 = ((bf16[8,704,256]{2,1,0:T(8,128)(2,1)}), bf16[8,704,256]{2,1,0:T(8,128)(2,1)}, u32[]{:S(2)}, u32[]{:S(2)}) async-start(bf16[8,704,256]{2,1,0:T(8,128)(2,1)} %pad_maximum_fusion.1), calls=%async_computation.1 | async-start | bytes 5767168 | tf_op jit(solution)/shard_map/all_to_all | solution.py:878
  134.1 45.1 %collective-permute-start.18 = (bf16[1088,2048]{1,0:T(8,128)(2,1)}, bf16[1088,2048]{1,0:T(8,128)(2,1)}, u32[]{:S(2)}, u32[]{:S(2)}) collective-permute-start(bf16[1088,2048]{1,0:T(8,128)(2,1)} %constant_dynamic-update-slice_fusion.10.refs_1_.ce_ref), channel_id=1, source_target_pairs={{0,4},{4,0},{8,12},{12,8},{16,20},{20,16},{24,28},{28,24},{1,5},{5... | collective-permute-start | bytes 13369352 | tf_op jit(solution)/shard_map/ppermute | solution.py:21
  144.8 11.5 %collective-permute-start.17 = (bf16[272,512]{1,0:T(8,128)(2,1)S(1)}, bf16[272,512]{1,0:T(8,128)(2,1)S(1)}, u32[]{:S(2)}, u32[]{:S(2)}) collective-permute-start(bf16[272,512]{1,0:T(8,128)(2,1)S(1)} %get-tuple-element.125), channel_id=1, source_target_pairs={{0,3},{1,2},{2,1},{3,0},{4,7},{5,6},{6,5},{7,4},{8,11},{9,10},{10,... | collective-permute-start | bytes 835592 | tf_op jit(solution)/shard_map/ppermute | solution.py:21
  148.6 23.8 %collective-permute-start.16 = (bf16[272,512]{1,0:T(8,128)(2,1)S(1)}, bf16[272,512]{1,0:T(8,128)(2,1)S(1)}, u32[]{:S(2)}, u32[]{:S(2)}) collective-permute-start(bf16[272,512]{1,0:T(8,128)(2,1)S(1)} %get-tuple-element.124), channel_id=1, source_target_pairs={{0,2},{1,3},{2,0},{3,1},{4,6},{5,7},{6,4},{7,5},{8,10},{9,11},{10,... | collective-permute-start | bytes 835592 | tf_op jit(solution)/shard_map/ppermute | solution.py:21
  148.6 23.8 %collective-permute-start.15 = (bf16[272,512]{1,0:T(8,128)(2,1)S(1)}, bf16[272,512]{1,0:T(8,128)(2,1)S(1)}, u32[]{:S(2)}, u32[]{:S(2)}) collective-permute-start(bf16[272,512]{1,0:T(8,128)(2,1)S(1)} %get-tuple-element.123), channel_id=1, source_target_pairs={{0,1},{1,0},{2,3},{3,2},{4,5},{5,4},{6,7},{7,6},{8,9},{9,8},{10,11... | collective-permute-start | bytes 835592 | tf_op jit(solution)/shard_map/ppermute | solution.py:21
  173.4 53.7 %all-to-all-start = ((bf16[8,256,1024]{2,1,0:T(8,128)(2,1)}), bf16[8,256,1024]{2,1,0:T(8,128)(2,1)}, u32[]{:S(2)}, u32[]{:S(2)}) async-start(bf16[8,256,1024]{2,1,0:T(8,128)(2,1)} %pad_maximum_fusion), calls=%async_computation | async-start | bytes 8388608 | tf_op jit(solution)/shard_map/all_to_all | solution.py:888
  177.9 310.7 %reduce-scatter.3.cloned.1.call-start = ((), (), s32[]{:S(2)}) async-start(), calls=%async_computation.7 | async-start | bytes 10027008 | tf_op jit(solution)/shard_map/reduce_scatter | solution.py:967
  185.4 41.6 %collective-permute-start.19 = (bf16[272,512]{1,0:T(8,128)(2,1)S(1)}, bf16[272,512]{1,0:T(8,128)(2,1)S(1)}, u32[]{:S(2)}, u32[]{:S(2)}) collective-permute-start(bf16[272,512]{1,0:T(8,128)(2,1)S(1)} %get-tuple-element.131.refs_0_), channel_id=1, source_target_pairs={{0,1},{1,0},{2,3},{3,2},{4,5},{5,4},{6,7},{7,6},{8,9},{9,8},{10,11... | collective-permute-start | bytes 835592 | tf_op jit(solution)/shard_map/ppermute | solution.py:21
  185.4 41.6 %collective-permute-start.20 = (bf16[272,512]{1,0:T(8,128)(2,1)S(1)}, bf16[272,512]{1,0:T(8,128)(2,1)}, u32[]{:S(2)}, u32[]{:S(2)}) collective-permute-start(bf16[272,512]{1,0:T(8,128)(2,1)S(1)} %get-tuple-element.131.refs_0_), channel_id=1, source_target_pairs={{0,2},{1,3},{2,0},{3,1},{4,6},{5,7},{6,4},{7,5},{8,10},{9,11},{10,... | collective-permute-start | bytes 835592 | tf_op jit(solution)/shard_map/ppermute | solution.py:21
  188.6 38.5 %collective-permute-start.21 = (bf16[272,512]{1,0:T(8,128)(2,1)S(1)}, bf16[272,512]{1,0:T(8,128)(2,1)}, u32[]{:S(2)}, u32[]{:S(2)}) collective-permute-start(bf16[272,512]{1,0:T(8,128)(2,1)S(1)} %get-tuple-element.131.refs_0_), channel_id=1, source_target_pairs={{0,3},{1,2},{2,1},{3,0},{4,7},{5,6},{6,5},{7,4},{8,11},{9,10},{10,... | collective-permute-start | bytes 835592 | tf_op jit(solution)/shard_map/ppermute | solution.py:21
  228.7 13.4 %collective-permute-start.22 = (bf16[136,2048]{1,0:T(8,128)(2,1)S(1)}, bf16[136,2048]{1,0:T(8,128)(2,1)S(1)}, u32[]{:S(2)}, u32[]{:S(2)}) collective-permute-start(bf16[136,2048]{1,0:T(8,128)(2,1)S(1)} %get-tuple-element.132), channel_id=1, source_target_pairs={{0,8},{4,12},{8,0},{12,4},{16,24},{20,28},{24,16},{28,20},{1,9},{5... | collective-permute-start | bytes 1671176 | tf_op jit(solution)/shard_map/ppermute | solution.py:21
  229.2 15.5 %collective-permute-start.25 = (bf16[136,2048]{1,0:T(8,128)(2,1)S(1)}, bf16[136,2048]{1,0:T(8,128)(2,1)S(1)}, u32[]{:S(2)}, u32[]{:S(2)}) collective-permute-start(bf16[136,2048]{1,0:T(8,128)(2,1)S(1)} %get-tuple-element.133), channel_id=1, source_target_pairs={{0,16},{4,20},{8,24},{12,28},{16,0},{20,4},{24,8},{28,12},{1,17},{... | collective-permute-start | bytes 1671176 | tf_op jit(solution)/shard_map/ppermute | solution.py:21
  229.9 26.8 %collective-permute-start.23 = (bf16[136,2048]{1,0:T(8,128)(2,1)S(1)}, bf16[136,2048]{1,0:T(8,128)(2,1)S(1)}, u32[]{:S(2)}, u32[]{:S(2)}) collective-permute-start(bf16[136,2048]{1,0:T(8,128)(2,1)S(1)} %get-tuple-element.132), channel_id=1, source_target_pairs={{0,16},{4,20},{8,24},{12,28},{16,0},{20,4},{24,8},{28,12},{1,17},{... | collective-permute-start | bytes 1671176 | tf_op jit(solution)/shard_map/ppermute | solution.py:21
  242.1 25.3 %collective-permute-start.24 = (bf16[136,2048]{1,0:T(8,128)(2,1)S(1)}, bf16[136,2048]{1,0:T(8,128)(2,1)S(1)}, u32[]{:S(2)}, u32[]{:S(2)}) collective-permute-start(bf16[136,2048]{1,0:T(8,128)(2,1)S(1)} %collective-permute-done.22), channel_id=1, source_target_pairs={{0,16},{4,20},{8,24},{12,28},{16,0},{20,4},{24,8},{28,12},{1,17},{... | collective-permute-start | bytes 1671176 | tf_op jit(solution)/shard_map/ppermute | solution.py:21
  242.5 25.1 %collective-permute-start.26 = (bf16[136,2048]{1,0:T(8,128)(2,1)S(1)}, bf16[136,2048]{1,0:T(8,128)(2,1)S(1)}, u32[]{:S(2)}, u32[]{:S(2)}) collective-permute-start(bf16[136,2048]{1,0:T(8,128)(2,1)S(1)} %get-tuple-element.133), channel_id=1, source_target_pairs={{0,8},{4,12},{8,0},{12,4},{16,24},{20,28},{24,16},{28,20},{1,9},{5... | collective-permute-start | bytes 1671176 | tf_op jit(solution)/shard_map/ppermute | solution.py:21
  244.8 23.2 %collective-permute-start.27 = (bf16[136,2048]{1,0:T(8,128)(2,1)S(1)}, bf16[136,2048]{1,0:T(8,128)(2,1)S(1)}, u32[]{:S(2)}, u32[]{:S(2)}) collective-permute-start(bf16[136,2048]{1,0:T(8,128)(2,1)S(1)} %collective-permute-done.25), channel_id=1, source_target_pairs={{0,8},{4,12},{8,0},{12,4},{16,24},{20,28},{24,16},{28,20},{1,9},{5... | collective-permute-start | bytes 1671176 | tf_op jit(solution)/shard_map/ppermute | solution.py:21
  298.7 20.6 %collective-permute-start.29 = (bf16[1088,2048]{1,0:T(8,128)(2,1)}, bf16[1088,2048]{1,0:T(8,128)(2,1)}, u32[]{:S(2)}, u32[]{:S(2)}) collective-permute-start(bf16[1088,2048]{1,0:T(8,128)(2,1)} %get-tuple-element.147), channel_id=1, source_target_pairs={{0,4},{4,0},{8,12},{12,8},{16,20},{20,16},{24,28},{28,24},{1,5},{5... | collective-permute-start | bytes 13369352 | tf_op jit(solution)/shard_map/ppermute | solution.py:21
  322.7 26.9 %collective-permute-start.31 = (bf16[2,136,2048]{2,1,0:T(8,128)(2,1)S(1)}, bf16[2,136,2048]{2,1,0:T(8,128)(2,1)S(1)}, u32[]{:S(2)}, u32[]{:S(2)}) collective-permute-start(bf16[2,136,2048]{2,1,0:T(8,128)(2,1)S(1)} %bitcast.184), channel_id=1, source_target_pairs={{0,8},{4,12},{8,0},{12,4},{16,24},{20,28},{24,16},{28,20},{1,9},{5... | collective-permute-start | bytes 3342344 | tf_op jit(solution)/shard_map/ppermute | solution.py:21
  324.5 26.6 %collective-permute-start.30 = (bf16[2,136,2048]{2,1,0:T(8,128)(2,1)S(1)}, bf16[2,136,2048]{2,1,0:T(8,128)(2,1)S(1)}, u32[]{:S(2)}, u32[]{:S(2)}) collective-permute-start(bf16[2,136,2048]{2,1,0:T(8,128)(2,1)S(1)} %bitcast.183), channel_id=1, source_target_pairs={{0,16},{4,20},{8,24},{12,28},{16,0},{20,4},{24,8},{28,12},{1,17},{... | collective-permute-start | bytes 3342344 | tf_op jit(solution)/shard_map/ppermute | solution.py:21
  354.6 14.1 %collective-permute-start.32 = (bf16[1,136,2048]{2,1,0:T(8,128)(2,1)}, bf16[1,136,2048]{2,1,0:T(8,128)(2,1)S(1)}, u32[]{:S(2)}, u32[]{:S(2)}) collective-permute-start(bf16[1,136,2048]{2,1,0:T(8,128)(2,1)} %get-tuple-element.149), channel_id=1, source_target_pairs={{0,8},{4,12},{8,0},{12,4},{16,24},{20,28},{24,16},{28,20},{1,9},{5... | collective-permute-start | bytes 1671176 | tf_op jit(solution)/shard_map/ppermute | solution.py:21
  355.4 14.0 %collective-permute-start.33 = (bf16[1,136,2048]{2,1,0:T(8,128)(2,1)}, bf16[1,136,2048]{2,1,0:T(8,128)(2,1)S(1)}, u32[]{:S(2)}, u32[]{:S(2)}) collective-permute-start(bf16[1,136,2048]{2,1,0:T(8,128)(2,1)} %get-tuple-element.150), channel_id=1, source_target_pairs={{0,16},{4,20},{8,24},{12,28},{16,0},{20,4},{24,8},{28,12},{1,17},{... | collective-permute-start | bytes 1671176 | tf_op jit(solution)/shard_map/ppermute | solution.py:21
  374.2 55.9 %all-to-all-start.2 = ((bf16[8,704,256]{2,1,0:T(8,128)(2,1)}), bf16[8,704,256]{2,1,0:T(8,128)(2,1)}, u32[]{:S(2)}, u32[]{:S(2)}) async-start(bf16[8,704,256]{2,1,0:T(8,128)(2,1)} %get-tuple-element.152), calls=%async_computation.2 | async-start | bytes 5767168 | tf_op jit(solution)/shard_map/all_to_all | solution.py:968
  381.4 23.5 %collective-permute-start.35 = (bf16[272,512]{1,0:T(8,128)(2,1)S(1)}, bf16[272,512]{1,0:T(8,128)(2,1)S(1)}, u32[]{:S(2)}, u32[]{:S(2)}) collective-permute-start(bf16[272,512]{1,0:T(8,128)(2,1)S(1)} %copy-done.38), channel_id=1, source_target_pairs={{0,2},{1,3},{2,0},{3,1},{4,6},{5,7},{6,4},{7,5},{8,10},{9,11},{10,... | collective-permute-start | bytes 835592 | tf_op jit(solution)/shard_map/ppermute | solution.py:21
  381.5 23.5 %collective-permute-start.34 = (bf16[272,512]{1,0:T(8,128)(2,1)S(1)}, bf16[272,512]{1,0:T(8,128)(2,1)S(1)}, u32[]{:S(2)}, u32[]{:S(2)}) collective-permute-start(bf16[272,512]{1,0:T(8,128)(2,1)S(1)} %get-tuple-element.154), channel_id=1, source_target_pairs={{0,1},{1,0},{2,3},{3,2},{4,5},{5,4},{6,7},{7,6},{8,9},{9,8},{10,11... | collective-permute-start | bytes 835592 | tf_op jit(solution)/shard_map/ppermute | solution.py:21
  405.1 38.4 %collective-permute-start.37 = (bf16[272,512]{1,0:T(8,128)(2,1)S(1)}, bf16[272,512]{1,0:T(8,128)(2,1)}, u32[]{:S(2)}, u32[]{:S(2)}) collective-permute-start(bf16[272,512]{1,0:T(8,128)(2,1)S(1)} %add_convert_fusion.9.refs_0_), channel_id=1, source_target_pairs={{0,1},{1,0},{2,3},{3,2},{4,5},{5,4},{6,7},{7,6},{8,9},{9,8},{10,11... | collective-permute-start | bytes 835592 | tf_op jit(solution)/shard_map/ppermute | solution.py:21
  405.2 38.3 %collective-permute-start.38 = (bf16[272,512]{1,0:T(8,128)(2,1)S(1)}, bf16[272,512]{1,0:T(8,128)(2,1)}, u32[]{:S(2)}, u32[]{:S(2)}) collective-permute-start(bf16[272,512]{1,0:T(8,128)(2,1)S(1)} %add_convert_fusion.9.refs_0_), channel_id=1, source_target_pairs={{0,2},{1,3},{2,0},{3,1},{4,6},{5,7},{6,4},{7,5},{8,10},{9,11},{10,... | collective-permute-start | bytes 835592 | tf_op jit(solution)/shard_map/ppermute | solution.py:21
  406.9 36.6 %collective-permute-start.39 = (bf16[272,512]{1,0:T(8,128)(2,1)S(1)}, bf16[272,512]{1,0:T(8,128)(2,1)}, u32[]{:S(2)}, u32[]{:S(2)}) collective-permute-start(bf16[272,512]{1,0:T(8,128)(2,1)S(1)} %add_convert_fusion.9.refs_0_), channel_id=1, source_target_pairs={{0,3},{1,2},{2,1},{3,0},{4,7},{5,6},{6,5},{7,4},{8,11},{9,10},{10,... | collective-permute-start | bytes 835592 | tf_op jit(solution)/shard_map/ppermute | solution.py:21
  430.2 51.7 %all-to-all-start.3 = ((bf16[8,256,512]{2,1,0:T(8,128)(2,1)}), bf16[8,256,512]{2,1,0:T(8,128)(2,1)}, u32[]{:S(2)}, u32[]{:S(2)}) async-start(bf16[8,256,512]{2,1,0:T(8,128)(2,1)} %bitcast.150), calls=%async_computation.3 | async-start | bytes 4194304 | tf_op jit(solution)/shard_map/all_to_all | solution.py:970
  434.7 132.3 %reduce-scatter.5.cloned.1.call-start = ((), (), s32[]{:S(2)}) async-start(), calls=%async_computation.8 | async-start | bytes 3538944 | tf_op jit(solution)/shard_map/reduce_scatter | solution.py:1007
  462.2 16.0 %collective-permute-start.41 = (bf16[2,136,512]{2,1,0:T(8,128)(2,1)}, bf16[2,136,512]{2,1,0:T(8,128)(2,1)}, u32[]{:S(2)}, u32[]{:S(2)}) collective-permute-start(bf16[2,136,512]{2,1,0:T(8,128)(2,1)} %bitcast.37), channel_id=1, source_target_pairs={{0,16},{4,20},{8,24},{12,28},{16,0},{20,4},{24,8},{28,12},{1,17},{... | collective-permute-start | bytes 835592 | tf_op jit(solution)/shard_map/ppermute | solution.py:21
  465.8 14.2 %collective-permute-start.43 = (bf16[2,136,512]{2,1,0:T(8,128)(2,1)}, bf16[2,136,512]{2,1,0:T(8,128)(2,1)S(1)}, u32[]{:S(2)}, u32[]{:S(2)}) collective-permute-start(bf16[2,136,512]{2,1,0:T(8,128)(2,1)} %bitcast.41), channel_id=1, source_target_pairs={{0,8},{4,12},{8,0},{12,4},{16,24},{20,28},{24,16},{28,20},{1,9},{5... | collective-permute-start | bytes 835592 | tf_op jit(solution)/shard_map/ppermute | solution.py:21
  501.4 35.9 %all-to-all-start.4 = ((bf16[8,256,512]{2,1,0:T(8,128)(2,1)}), bf16[8,256,512]{2,1,0:T(8,128)(2,1)}, u32[]{:S(2)}, u32[]{:S(2)}) async-start(bf16[8,256,512]{2,1,0:T(8,128)(2,1)} %bitcast.177), calls=%async_computation.6 | async-start | bytes 4194304 | tf_op jit(solution)/shard_map/all_to_all | solution.py:1032
  508.4 49.5 %collective-permute-start.47 = (bf16[2,200,1024]{2,1,0:T(8,128)(2,1)}, bf16[2,200,1024]{2,1,0:T(8,128)(2,1)}, u32[]{:S(2)}, u32[]{:S(2)}) collective-permute-start(bf16[2,200,1024]{2,1,0:T(8,128)(2,1)} %add_convert_fusion.3), channel_id=1, source_target_pairs={{0,16},{4,20},{8,24},{12,28},{16,0},{20,4},{24,8},{28,12},{1,17},{... | collective-permute-start | bytes 2457608 | tf_op jit(solution)/shard_map/ppermute | solution.py:21
  512.7 45.3 %collective-permute-start.49 = (bf16[2,200,1024]{2,1,0:T(8,128)(2,1)}, bf16[2,200,1024]{2,1,0:T(8,128)(2,1)}, u32[]{:S(2)}, u32[]{:S(2)}) collective-permute-start(bf16[2,200,1024]{2,1,0:T(8,128)(2,1)} %add_convert_fusion.2), channel_id=1, source_target_pairs={{0,8},{4,12},{8,0},{12,4},{16,24},{20,28},{24,16},{28,20},{1,9},{5... | collective-permute-start | bytes 2457608 | tf_op jit(solution)/shard_map/ppermute | solution.py:21
  514.1 29.2 %collective-permute-start.50 = (bf16[552,512]{1,0:T(8,128)(2,1)}, bf16[552,512]{1,0:T(8,128)(2,1)S(1)}, u32[]{:S(2)}, u32[]{:S(2)}) collective-permute-start(bf16[552,512]{1,0:T(8,128)(2,1)} %get-tuple-element.179), channel_id=1, source_target_pairs={{0,1},{1,0},{2,3},{3,2},{4,5},{5,4},{6,7},{7,6},{8,9},{9,8},{10,11... | collective-permute-start | bytes 1695752 | tf_op jit(solution)/shard_map/ppermute | solution.py:21
  514.1 41.1 %collective-permute-start.51 = (bf16[552,512]{1,0:T(8,128)(2,1)}, bf16[552,512]{1,0:T(8,128)(2,1)S(1)}, u32[]{:S(2)}, u32[]{:S(2)}) collective-permute-start(bf16[552,512]{1,0:T(8,128)(2,1)} %get-tuple-element.180), channel_id=1, source_target_pairs={{0,2},{1,3},{2,0},{3,1},{4,6},{5,7},{6,4},{7,5},{8,10},{9,11},{10,... | collective-permute-start | bytes 1695752 | tf_op jit(solution)/shard_map/ppermute | solution.py:21
  516.1 39.1 %collective-permute-start.52 = (bf16[552,512]{1,0:T(8,128)(2,1)}, bf16[552,512]{1,0:T(8,128)(2,1)S(1)}, u32[]{:S(2)}, u32[]{:S(2)}) collective-permute-start(bf16[552,512]{1,0:T(8,128)(2,1)} %get-tuple-element.181), channel_id=1, source_target_pairs={{0,3},{1,2},{2,1},{3,0},{4,7},{5,6},{6,5},{7,4},{8,11},{9,10},{10,... | collective-permute-start | bytes 1695752 | tf_op jit(solution)/shard_map/ppermute | solution.py:21
  560.2 12.3 %collective-permute-start.54 = (bf16[1,200,1024]{2,1,0:T(8,128)(2,1)}, bf16[1,200,1024]{2,1,0:T(8,128)(2,1)}, u32[]{:S(2)}, u32[]{:S(2)}) collective-permute-start(bf16[1,200,1024]{2,1,0:T(8,128)(2,1)} %add_convert_fusion.4), channel_id=1, source_target_pairs={{0,16},{4,20},{8,24},{12,28},{16,0},{20,4},{24,8},{28,12},{1,17},{... | collective-permute-start | bytes 1228808 | tf_op jit(solution)/shard_map/ppermute | solution.py:21
  (88 other events, 1060.7 us)
Sparse Core Ops, SparseCore 0:
  10.5 69.4 all-gather.4
  88.6 38.2 all-gather.6
  369.5 107.4 reduce-scatter.2
  480.3 69.5 reduce-scatter.4

commit v6 on v5

--- a/solution.py
+++ b/solution.py
@@ -497,7 +497,7 @@
             ],
             out_specs=pl.BlockSpec((1, rows, dp), lambda j, o, a, b, la, lb: (j, 0, 0)),
         ),
-        out_shape=jax.ShapeDtypeStruct((n, rows, dp), BF),
+        out_shape=pltpu.HBM((n, rows, dp), BF),
         compiler_params=pltpu.CompilerParams(vmem_limit_bytes=32 * MIB),
         cost_estimate=pl.CostEstimate(
             flops=2 * n * rows * dp * f, bytes_accessed=2 * n * rows * dp, transcendentals=0

time: 616 us -> 616 us (level)
    unnamed x167 -> x165, local copies, waits for them, and re-layouts: 31.8 us -> 28.2 us
  transfers between devices with their start and end apart: 67 -> 67, of which waited for: 37 -> 37; matrix products, arithmetic and copies ran while one was open for 13% -> 13% of each run, Pallas kernels for 15% -> 16%
where the time goes in v6:
time: 616 us; the launch traced here: 605 us
  waiting for transfers between devices  250 us (41%)
  Pallas kernels  121 us (20%)
  starting transfers between devices  105 us (17%)
  local copies, waits for them, and re-layouts  65.4 us (11%)
  other arithmetic  48.4 us (8%)
  between operations  15.3 us (2%)
    ppermute x58, waiting for transfers between devices, swap(): return lax.ppermute(value, axis, [(i, i ^ mask) for i in range(count)])  195 us
    ppermute x58, starting transfers between devices, swap(): return lax.ppermute(value, axis, [(i, i ^ mask) for i in range(count)])  73.3 us
    pallas_call x11, Pallas kernels, whole_call(): pl.pallas_call(kernel, out_shape=outs, in_specs=specs, out_specs=tuple((p...  39.6 us
    pallas_call x2, Pallas kernels, feed(): pl.pallas_call(lambda *refs: feed_kernel(pair, *refs), grid=(total // ste...  36.6 us
    all_to_all x1, waiting for transfers between devices, shards(): lax.all_to_all(after(gate_up_sent, branch), 'seq', 0, 0).reshape(dp, 2 * fp)  32.8 us
    unnamed x165, local copies, waits for them, and re-layouts  28.2 us
    convert_element_type x10, other arithmetic, scatter_rows(): sent = [total_of([p[keep:] for p in part]).astype(BF) for part in parts]  22.5 us
    pallas_call x1, Pallas kernels, weight_grads(): pl.pallas_call(weights_kernel, grid=(dp // wide,), in_specs=[cols, cols,...  22 us
  transfers between devices with their start and end apart: 67, of which 37 were waited for; matrix products, arithmetic and copies ran while one was open for 13% of the time, Pallas kernels for 16%

profile of v6, /device:TPU:0, one launch (start us, length us, event | category | flops | bytes accessed | tf_op | source)
XLA Modules:
  0.0 605.3 jit_solution(9778384223012261726)
XLA Ops:
  12.0 3.0 collective-permute-start
  16.7 16.7 %collective-permute-done = bf16[136,2048]{1,0:T(8,128)(2,1)S(1)} collective-permute-done((bf16[136,2048]{1,0:T(8,128)(2,1)S(1)}, bf16[136,2048]{1,0:T(8,128)(2,1)S(1)}, u32[]{:S(2)}, u32[]{:S(2)}) %collective-permute-start) | collective-permute-done | bytes 557088 | tf_op jit(solution)/shard_map/ppermute | solution.py:21
  33.4 2.8 collective-permute-done.1
  42.5 2.8 collective-permute-start.5
  46.3 32.8 %collective-permute-done.2 = bf16[272,2048]{1,0:T(8,128)(2,1)} collective-permute-done((bf16[272,2048]{1,0:T(8,128)(2,1)}, bf16[272,2048]{1,0:T(8,128)(2,1)}, u32[]{:S(2)}, u32[]{:S(2)}) %collective-permute-start.2) | collective-permute-done | bytes 1114144 | tf_op jit(solution)/shard_map/ppermute | solution.py:21
  81.5 4.7 shard_map.408
  92.3 3.7 pad_maximum_fusion.1
  98.8 5.7 collective-permute-done.7
  114.8 6.5 %collective-permute-done.13 = bf16[136,512]{1,0:T(8,128)(2,1)S(1)} collective-permute-done((bf16[136,512]{1,0:T(8,128)(2,1)S(1)}, bf16[136,512]{1,0:T(8,128)(2,1)S(1)}, u32[]{:S(2)}, u32[]{:S(2)}) %collective-permute-start.13) | collective-permute-done | bytes 139296 | tf_op jit(solution)/shard_map/ppermute | solution.py:21
  124.8 4.5 all-to-all-start.1
  136.7 3.8 shard_map.409
  144.8 3.7 collective-permute-start.17
  156.3 16.1 %collective-permute-done.16 = bf16[272,512]{1,0:T(8,128)(2,1)S(1)} collective-permute-done((bf16[272,512]{1,0:T(8,128)(2,1)S(1)}, bf16[272,512]{1,0:T(8,128)(2,1)S(1)}, u32[]{:S(2)}, u32[]{:S(2)}) %collective-permute-start.16) | collective-permute-done | bytes 278560 | tf_op jit(solution)/shard_map/ppermute | solution.py:21
  173.4 4.5 all-to-all-start
  185.4 3.1 collective-permute-start.20
  194.2 32.8 %all-to-all-done = bf16[8,256,1024]{2,1,0:T(8,128)(2,1)} async-done(((bf16[8,256,1024]{2,1,0:T(8,128)(2,1)}), bf16[8,256,1024]{2,1,0:T(8,128)(2,1)}, u32[]{:S(2)}, u32[]{:S(2)}) %all-to-all-start) | async-done | bytes 4194336 | tf_op jit(solution)/shard_map/all_to_all | solution.py:888
  231.2 10.8 %collective-permute-done.22 = bf16[136,2048]{1,0:T(8,128)(2,1)S(1)} collective-permute-done((bf16[136,2048]{1,0:T(8,128)(2,1)S(1)}, bf16[136,2048]{1,0:T(8,128)(2,1)S(1)}, u32[]{:S(2)}, u32[]{:S(2)}) %collective-permute-start.22) | collective-permute-done | bytes 557088 | tf_op jit(solution)/shard_map/ppermute | solution.py:21
  246.3 10.3 %collective-permute-done.23 = bf16[136,2048]{1,0:T(8,128)(2,1)S(1)} collective-permute-done((bf16[136,2048]{1,0:T(8,128)(2,1)S(1)}, bf16[136,2048]{1,0:T(8,128)(2,1)S(1)}, u32[]{:S(2)}, u32[]{:S(2)}) %collective-permute-start.23) | collective-permute-done | bytes 557088 | tf_op jit(solution)/shard_map/ppermute | solution.py:21
  256.7 10.7 %collective-permute-done.24 = bf16[136,2048]{1,0:T(8,128)(2,1)S(1)} collective-permute-done((bf16[136,2048]{1,0:T(8,128)(2,1)S(1)}, bf16[136,2048]{1,0:T(8,128)(2,1)S(1)}, u32[]{:S(2)}, u32[]{:S(2)}) %collective-permute-start.24) | collective-permute-done | bytes 557088 | tf_op jit(solution)/shard_map/ppermute | solution.py:21
  268.0 7.5 %collective-permute-done.28.refs_0_.xo_ref = bf16[1088,2048]{1,0:T(8,128)(2,1)S(1)} collective-permute-done((bf16[1088,2048]{1,0:T(8,128)(2,1)S(1)}, bf16[1088,2048]{1,0:T(8,128)(2,1)S(1)}, u32[]{:S(2)}, u32[]{:S(2)}) %collective-permute-start.28) | collective-permute-done | bytes 4456480 | tf_op jit(solution)/shard_map/ppermute | solution.py:21
  280.4 18.3 %shard_map.413 = (bf16[1088,512]{1,0:T(8,128)(2,1)}, bf16[1088,1024]{1,0:T(8,128)(2,1)}, bf16[1088,2048]{1,0:T(8,128)(2,1)}) custom-call(bf16[1088,2048]{1,0:T(8,128)(2,1)} %copy-done.67, bf16[1088,2048]{1,0:T(8,128)(2,1)} %collective-permute-done.18.refs_1_.co_ref, bf16[2048,1024]{1,0:T(8,128)(2,1)} %bitcast.8.refs_2_, bf16[512,2048]{1,0:T(8,128)(2,1)} %bitcast.151, ...), custom_call_target="tpu_custom_call" | custom-call | flops 11408506880 | bytes 24117248 | tf_op jit(solution)/shard_map/pallas_call | solution.py:372
  300.1 18.3 %shard_map.414 = (bf16[1088,512]{1,0:T(8,128)(2,1)}, bf16[1088,1024]{1,0:T(8,128)(2,1)}, bf16[1088,2048]{1,0:T(8,128)(2,1)}) custom-call(bf16[1088,2048]{1,0:T(8,128)(2,1)} %copy-done.64, bf16[1088,2048]{1,0:T(8,128)(2,1)} %constant_dynamic-update-slice_fusion.10.refs_1_.ce_ref, bf16[2048,1024]{1,0:T(8,128)(2,1)} %bitcast.8.refs_2_, ...), custom_call_target="tpu_custom_call" | custom-call | flops 11408506880 | bytes 24117248 | tf_op jit(solution)/shard_map/pallas_call | solution.py:372
  319.2 3.4 add_convert_fusion
  326.2 22.0 %shard_map.415 = (bf16[2048,512]{1,0:T(8,128)(2,1)S(1)}, bf16[2048,512]{1,0:T(8,128)(2,1)}, bf16[8,704,256]{2,1,0:T(8,128)(2,1)}) custom-call(bf16[1088,2048]{1,0:T(8,128)(2,1)} %copy-done.67, bf16[1088,2048]{1,0:T(8,128)(2,1)} %copy-done.64, bf16[1088,2048]{1,0:T(8,128)(2,1)} %collective-permute-done.18.refs_1_.co_ref, ...), custom_call_target="tpu_custom_call" | custom-call | flops 13690208256 | bytes 17825792 | tf_op jit(solution)/shard_map/pallas_call | solution.py:428
  351.0 3.6 fusion
  357.1 8.7 %shard_map.416 = bf16[8,272,2048]{2,1,0:T(8,128)(2,1)} custom-call(s32[8]{0:T(128)S(1)} %get-tuple-element.258.odd_ref, s32[8]{0:T(128)S(1)} %gather_fusion, s32[8]{0:T(128)S(1)} %gather_fusion.1, s32[8]{0:T(128)S(1)} %fusion.46.la_ref, s32[8]{0:T(128)S(1)} %get-tuple-element.259.lb_ref, bf16[1088,512]{1,0:T(8,128)(2,1)S(1)} %copy-done.41, ...), custom_call_target="tpu_custom_call" | custom-call | flops 4563402752 | bytes 8912896 | tf_op jit(solution)/shard_map/pallas_call | solution.py:484
  365.8 2.9 collective-permute-done.32
  374.2 4.6 all-to-all-start.2
  383.3 7.0 %collective-permute-done.36 = bf16[272,512]{1,0:T(8,128)(2,1)S(1)} collective-permute-done((bf16[272,512]{1,0:T(8,128)(2,1)S(1)}, bf16[272,512]{1,0:T(8,128)(2,1)S(1)}, u32[]{:S(2)}, u32[]{:S(2)}) %collective-permute-start.36) | collective-permute-done | bytes 278560 | tf_op jit(solution)/shard_map/ppermute | solution.py:21
  390.3 14.6 %collective-permute-done.35 = bf16[272,512]{1,0:T(8,128)(2,1)S(1)} collective-permute-done((bf16[272,512]{1,0:T(8,128)(2,1)S(1)}, bf16[272,512]{1,0:T(8,128)(2,1)S(1)}, u32[]{:S(2)}, u32[]{:S(2)}) %collective-permute-start.35) | collective-permute-done | bytes 278560 | tf_op jit(solution)/shard_map/ppermute | solution.py:21
  409.5 20.7 %all-to-all-done.2.d_ref = bf16[8,704,256]{2,1,0:T(8,128)(2,1)} async-done(((bf16[8,704,256]{2,1,0:T(8,128)(2,1)}), bf16[8,704,256]{2,1,0:T(8,128)(2,1)}, u32[]{:S(2)}, u32[]{:S(2)}) %all-to-all-start.2) | async-done | bytes 2883616 | tf_op jit(solution)/shard_map/all_to_all | solution.py:968
  430.2 4.5 all-to-all-start.3
  434.7 8.8 %reduce-scatter.5.cloned.1.call-start = ((), (), s32[]{:S(2)}) async-start(), calls=%async_computation.8 | async-start | bytes 3538944 | tf_op jit(solution)/shard_map/reduce_scatter | solution.py:1007
  443.5 4.7 shard_map.418
  449.8 8.3 %shard_map.419 = (bf16[272,512]{1,0:T(8,128)(2,1)}, bf16[544,512]{1,0:T(8,128)(2,1)}, bf16[544,512]{1,0:T(8,128)(2,1)}, bf16[544,512]{1,0:T(8,128)(2,1)}, bf16[544,512]{1,0:T(8,128)(2,1)}) custom-call(bf16[272,512]{1,0:T(8,128)(2,1)} %copy-done.35, bf16[2176,512]{1,0:T(8,128)(2,1)} %copy-done.30, s32[272,1]{1,0:T(8,128)} %copy-done.21, ...), custom_call_target="tpu_custom_call" | custom-call | flops 3030384640 | bytes 6137408 | tf_op jit(solution)/shard_map/pallas_call | solution.py:127
  467.3 2.7 shard_map.422
  470.0 8.2 %collective-permute-done.41 = bf16[2,136,512]{2,1,0:T(8,128)(2,1)} collective-permute-done((bf16[2,136,512]{2,1,0:T(8,128)(2,1)}, bf16[2,136,512]{2,1,0:T(8,128)(2,1)}, u32[]{:S(2)}, u32[]{:S(2)}) %collective-permute-start.41) | collective-permute-done | bytes 278560 | tf_op jit(solution)/shard_map/ppermute | solution.py:21
  484.8 2.9 collective-permute-done.44
  490.0 10.9 %shard_map.420 = (bf16[4,200,1024]{2,1,0:T(8,128)(2,1)}, bf16[4,200,1024]{2,1,0:T(8,128)(2,1)}, bf16[4,200,1024]{2,1,0:T(8,128)(2,1)}, bf16[4,200,1024]{2,1,0:T(...) custom-call(s32[1]{0:T(128)} %bitcast.5.refs_0_, ...), custom_call_target="tpu_custom_call" | custom-call | flops 2281701376 | bytes 18710536 | tf_op jit(solution)/shard_map/pallas_call | solution.py:127
  501.4 4.5 all-to-all-start.4
  518.5 7.7 %shard_map.423 = (f32[256,4096]{1,0:T(8,128)}, f32[4096,256]{1,0:T(8,128)}, f32[8,192,256]{2,1,0:T(8,128)}) custom-call(s32[1]{0:T(128)} %bitcast.t_ref.refs_1_.token_ref, bf16[8,256,512]{2,1,0:T(8,128)(2,1)} %all-to-all-done.3.g_ref, bf16[8,704,256]{2,1,0:T(8,128)(2,1)} %all-to-all-done.2.d_ref), custom_call_target="tpu_custom_call" | custom-call | bytes 14942208 | tf_op jit(solution)/shard_map/pallas_call | solution.py:702
  526.2 2.7 reshape.318
  537.2 6.0 shard_map.424
  543.2 12.0 %collective-permute-done.51.refs_2_ = bf16[552,512]{1,0:T(8,128)(2,1)S(1)} collective-permute-done((bf16[552,512]{1,0:T(8,128)(2,1)}, bf16[552,512]{1,0:T(8,128)(2,1)S(1)}, u32[]{:S(2)}, u32[]{:S(2)}) %collective-permute-start.51) | collective-permute-done | bytes 565280 | tf_op jit(solution)/shard_map/ppermute | solution.py:21
  574.1 3.6 collective-permute-done.53
  582.2 3.3 collective-permute-start.57
  585.6 4.7 collective-permute-start.56
  590.3 5.5 collective-permute-done.56
  (373 shorter events, 178.5 us)
Async XLA Ops:
  7.2 73.2 %all-gather.5.cloned.1.call-start = ((), (), s32[]{:S(2)}) async-start(), calls=%async_computation.9 | async-start | bytes 7225344 | tf_op jit(solution)/shard_map/all_gather | solution.py:802
  10.3 131.7 %all-gather.7.cloned.1.call-start = ((), (), s32[]{:S(2)}) async-start(), calls=%async_computation.10 | async-start | bytes 3538944 | tf_op jit(solution)/shard_map/all_gather | solution.py:877
  12.0 21.4 %collective-permute-start = (bf16[136,2048]{1,0:T(8,128)(2,1)S(1)}, bf16[136,2048]{1,0:T(8,128)(2,1)S(1)}, u32[]{:S(2)}, u32[]{:S(2)}) collective-permute-start(bf16[136,2048]{1,0:T(8,128)(2,1)S(1)} %pad_maximum_fusion.7), channel_id=1, source_target_pairs={{0,8},{4,12},{8,0},{12,4},{16,24},{20,28},{24,16},{28,20},{1,9},{5... | collective-permute-start | bytes 1671176 | tf_op jit(solution)/shard_map/ppermute | solution.py:21
  15.1 21.1 %collective-permute-start.1 = (bf16[136,2048]{1,0:T(8,128)(2,1)S(1)}, bf16[136,2048]{1,0:T(8,128)(2,1)S(1)}, u32[]{:S(2)}, u32[]{:S(2)}) collective-permute-start(bf16[136,2048]{1,0:T(8,128)(2,1)S(1)} %pad_maximum_fusion.8), channel_id=1, source_target_pairs={{0,16},{4,20},{8,24},{12,28},{16,0},{20,4},{24,8},{28,12},{1,17},{... | collective-permute-start | bytes 1671176 | tf_op jit(solution)/shard_map/ppermute | solution.py:21
  37.4 41.7 %collective-permute-start.2 = (bf16[272,2048]{1,0:T(8,128)(2,1)}, bf16[272,2048]{1,0:T(8,128)(2,1)}, u32[]{:S(2)}, u32[]{:S(2)}) collective-permute-start(bf16[272,2048]{1,0:T(8,128)(2,1)} %pad_maximum_fusion.2), channel_id=1, source_target_pairs={{0,16},{4,20},{8,24},{12,28},{16,0},{20,4},{24,8},{28,12},{1,17},{... | collective-permute-start | bytes 3342344 | tf_op jit(solution)/shard_map/ppermute | solution.py:21
  41.0 39.4 %collective-permute-start.3 = (bf16[272,2048]{1,0:T(8,128)(2,1)}, bf16[272,2048]{1,0:T(8,128)(2,1)}, u32[]{:S(2)}, u32[]{:S(2)}) collective-permute-start(bf16[272,2048]{1,0:T(8,128)(2,1)} %pad_maximum_fusion.3), channel_id=1, source_target_pairs={{0,8},{4,12},{8,0},{12,4},{16,24},{20,28},{24,16},{28,20},{1,9},{5... | collective-permute-start | bytes 3342344 | tf_op jit(solution)/shard_map/ppermute | solution.py:21
  41.0 40.4 %collective-permute-start.4 = (bf16[272,512]{1,0:T(8,128)(2,1)S(1)}, bf16[272,512]{1,0:T(8,128)(2,1)S(1)}, u32[]{:S(2)}, u32[]{:S(2)}) collective-permute-start(bf16[272,512]{1,0:T(8,128)(2,1)S(1)} %fusion.5.refs_0_.refs_4_), channel_id=1, source_target_pairs={{0,1},{1,0},{2,3},{3,2},{4,5},{5,4},{6,7},{7,6},{8,9},{9,8},{10,11... | collective-permute-start | bytes 835592 | tf_op jit(solution)/shard_map/ppermute | solution.py:21
  42.5 38.9 %collective-permute-start.5 = (bf16[272,512]{1,0:T(8,128)(2,1)S(1)}, bf16[272,512]{1,0:T(8,128)(2,1)S(1)}, u32[]{:S(2)}, u32[]{:S(2)}) collective-permute-start(bf16[272,512]{1,0:T(8,128)(2,1)S(1)} %fusion.5.refs_0_.refs_4_), channel_id=1, source_target_pairs={{0,2},{1,3},{2,0},{3,1},{4,6},{5,7},{6,4},{7,5},{8,10},{9,11},{10,... | collective-permute-start | bytes 835592 | tf_op jit(solution)/shard_map/ppermute | solution.py:21
  45.3 36.2 %collective-permute-start.6 = (bf16[272,512]{1,0:T(8,128)(2,1)S(1)}, bf16[272,512]{1,0:T(8,128)(2,1)S(1)}, u32[]{:S(2)}, u32[]{:S(2)}) collective-permute-start(bf16[272,512]{1,0:T(8,128)(2,1)S(1)} %fusion.5.refs_0_.refs_4_), channel_id=1, source_target_pairs={{0,3},{1,2},{2,1},{3,0},{4,7},{5,6},{6,5},{7,4},{8,11},{9,10},{10,... | collective-permute-start | bytes 835592 | tf_op jit(solution)/shard_map/ppermute | solution.py:21
  97.5 12.5 %collective-permute-start.8 = (bf16[136,512]{1,0:T(8,128)(2,1)S(1)}, bf16[136,512]{1,0:T(8,128)(2,1)S(1)}, u32[]{:S(2)}, u32[]{:S(2)}) collective-permute-start(bf16[136,512]{1,0:T(8,128)(2,1)S(1)} %get-tuple-element.118), channel_id=1, source_target_pairs={{0,16},{4,20},{8,24},{12,28},{16,0},{20,4},{24,8},{28,12},{1,17},{... | collective-permute-start | bytes 417800 | tf_op jit(solution)/shard_map/ppermute | solution.py:21
  124.8 48.5 %all-to-all-start.1 = ((bf16[8,704,256]{2,1,0:T(8,128)(2,1)}), bf16[8,704,256]{2,1,0:T(8,128)(2,1)}, u32[]{:S(2)}, u32[]{:S(2)}) async-start(bf16[8,704,256]{2,1,0:T(8,128)(2,1)} %pad_maximum_fusion.1), calls=%async_computation.1 | async-start | bytes 5767168 | tf_op jit(solution)/shard_map/all_to_all | solution.py:878
  134.1 45.1 %collective-permute-start.18 = (bf16[1088,2048]{1,0:T(8,128)(2,1)}, bf16[1088,2048]{1,0:T(8,128)(2,1)}, u32[]{:S(2)}, u32[]{:S(2)}) collective-permute-start(bf16[1088,2048]{1,0:T(8,128)(2,1)} %constant_dynamic-update-slice_fusion.10.refs_1_.ce_ref), channel_id=1, source_target_pairs={{0,4},{4,0},{8,12},{12,8},{16,20},{20,16},{24,28},{28,24},{1,5},{5... | collective-permute-start | bytes 13369352 | tf_op jit(solution)/shard_map/ppermute | solution.py:21
  144.8 11.5 %collective-permute-start.17 = (bf16[272,512]{1,0:T(8,128)(2,1)S(1)}, bf16[272,512]{1,0:T(8,128)(2,1)S(1)}, u32[]{:S(2)}, u32[]{:S(2)}) collective-permute-start(bf16[272,512]{1,0:T(8,128)(2,1)S(1)} %get-tuple-element.125), channel_id=1, source_target_pairs={{0,3},{1,2},{2,1},{3,0},{4,7},{5,6},{6,5},{7,4},{8,11},{9,10},{10,... | collective-permute-start | bytes 835592 | tf_op jit(solution)/shard_map/ppermute | solution.py:21
  148.5 23.9 %collective-permute-start.16 = (bf16[272,512]{1,0:T(8,128)(2,1)S(1)}, bf16[272,512]{1,0:T(8,128)(2,1)S(1)}, u32[]{:S(2)}, u32[]{:S(2)}) collective-permute-start(bf16[272,512]{1,0:T(8,128)(2,1)S(1)} %get-tuple-element.124), channel_id=1, source_target_pairs={{0,2},{1,3},{2,0},{3,1},{4,6},{5,7},{6,4},{7,5},{8,10},{9,11},{10,... | collective-permute-start | bytes 835592 | tf_op jit(solution)/shard_map/ppermute | solution.py:21
  148.5 23.9 %collective-permute-start.15 = (bf16[272,512]{1,0:T(8,128)(2,1)S(1)}, bf16[272,512]{1,0:T(8,128)(2,1)S(1)}, u32[]{:S(2)}, u32[]{:S(2)}) collective-permute-start(bf16[272,512]{1,0:T(8,128)(2,1)S(1)} %get-tuple-element.123), channel_id=1, source_target_pairs={{0,1},{1,0},{2,3},{3,2},{4,5},{5,4},{6,7},{7,6},{8,9},{9,8},{10,11... | collective-permute-start | bytes 835592 | tf_op jit(solution)/shard_map/ppermute | solution.py:21
  173.4 53.7 %all-to-all-start = ((bf16[8,256,1024]{2,1,0:T(8,128)(2,1)}), bf16[8,256,1024]{2,1,0:T(8,128)(2,1)}, u32[]{:S(2)}, u32[]{:S(2)}) async-start(bf16[8,256,1024]{2,1,0:T(8,128)(2,1)} %pad_maximum_fusion), calls=%async_computation | async-start | bytes 8388608 | tf_op jit(solution)/shard_map/all_to_all | solution.py:888
  177.9 310.7 %reduce-scatter.3.cloned.1.call-start = ((), (), s32[]{:S(2)}) async-start(), calls=%async_computation.7 | async-start | bytes 10027008 | tf_op jit(solution)/shard_map/reduce_scatter | solution.py:967
  185.4 41.6 %collective-permute-start.19 = (bf16[272,512]{1,0:T(8,128)(2,1)S(1)}, bf16[272,512]{1,0:T(8,128)(2,1)S(1)}, u32[]{:S(2)}, u32[]{:S(2)}) collective-permute-start(bf16[272,512]{1,0:T(8,128)(2,1)S(1)} %get-tuple-element.131.refs_0_), channel_id=1, source_target_pairs={{0,1},{1,0},{2,3},{3,2},{4,5},{5,4},{6,7},{7,6},{8,9},{9,8},{10,11... | collective-permute-start | bytes 835592 | tf_op jit(solution)/shard_map/ppermute | solution.py:21
  185.4 41.6 %collective-permute-start.20 = (bf16[272,512]{1,0:T(8,128)(2,1)S(1)}, bf16[272,512]{1,0:T(8,128)(2,1)}, u32[]{:S(2)}, u32[]{:S(2)}) collective-permute-start(bf16[272,512]{1,0:T(8,128)(2,1)S(1)} %get-tuple-element.131.refs_0_), channel_id=1, source_target_pairs={{0,2},{1,3},{2,0},{3,1},{4,6},{5,7},{6,4},{7,5},{8,10},{9,11},{10,... | collective-permute-start | bytes 835592 | tf_op jit(solution)/shard_map/ppermute | solution.py:21
  188.5 38.5 %collective-permute-start.21 = (bf16[272,512]{1,0:T(8,128)(2,1)S(1)}, bf16[272,512]{1,0:T(8,128)(2,1)}, u32[]{:S(2)}, u32[]{:S(2)}) collective-permute-start(bf16[272,512]{1,0:T(8,128)(2,1)S(1)} %get-tuple-element.131.refs_0_), channel_id=1, source_target_pairs={{0,3},{1,2},{2,1},{3,0},{4,7},{5,6},{6,5},{7,4},{8,11},{9,10},{10,... | collective-permute-start | bytes 835592 | tf_op jit(solution)/shard_map/ppermute | solution.py:21
  228.6 13.4 %collective-permute-start.22 = (bf16[136,2048]{1,0:T(8,128)(2,1)S(1)}, bf16[136,2048]{1,0:T(8,128)(2,1)S(1)}, u32[]{:S(2)}, u32[]{:S(2)}) collective-permute-start(bf16[136,2048]{1,0:T(8,128)(2,1)S(1)} %get-tuple-element.132), channel_id=1, source_target_pairs={{0,8},{4,12},{8,0},{12,4},{16,24},{20,28},{24,16},{28,20},{1,9},{5... | collective-permute-start | bytes 1671176 | tf_op jit(solution)/shard_map/ppermute | solution.py:21
  229.2 15.5 %collective-permute-start.25 = (bf16[136,2048]{1,0:T(8,128)(2,1)S(1)}, bf16[136,2048]{1,0:T(8,128)(2,1)S(1)}, u32[]{:S(2)}, u32[]{:S(2)}) collective-permute-start(bf16[136,2048]{1,0:T(8,128)(2,1)S(1)} %get-tuple-element.133), channel_id=1, source_target_pairs={{0,16},{4,20},{8,24},{12,28},{16,0},{20,4},{24,8},{28,12},{1,17},{... | collective-permute-start | bytes 1671176 | tf_op jit(solution)/shard_map/ppermute | solution.py:21
  229.8 26.8 %collective-permute-start.23 = (bf16[136,2048]{1,0:T(8,128)(2,1)S(1)}, bf16[136,2048]{1,0:T(8,128)(2,1)S(1)}, u32[]{:S(2)}, u32[]{:S(2)}) collective-permute-start(bf16[136,2048]{1,0:T(8,128)(2,1)S(1)} %get-tuple-element.132), channel_id=1, source_target_pairs={{0,16},{4,20},{8,24},{12,28},{16,0},{20,4},{24,8},{28,12},{1,17},{... | collective-permute-start | bytes 1671176 | tf_op jit(solution)/shard_map/ppermute | solution.py:21
  242.1 25.3 %collective-permute-start.24 = (bf16[136,2048]{1,0:T(8,128)(2,1)S(1)}, bf16[136,2048]{1,0:T(8,128)(2,1)S(1)}, u32[]{:S(2)}, u32[]{:S(2)}) collective-permute-start(bf16[136,2048]{1,0:T(8,128)(2,1)S(1)} %collective-permute-done.22), channel_id=1, source_target_pairs={{0,16},{4,20},{8,24},{12,28},{16,0},{20,4},{24,8},{28,12},{1,17},{... | collective-permute-start | bytes 1671176 | tf_op jit(solution)/shard_map/ppermute | solution.py:21
  242.4 25.1 %collective-permute-start.26 = (bf16[136,2048]{1,0:T(8,128)(2,1)S(1)}, bf16[136,2048]{1,0:T(8,128)(2,1)S(1)}, u32[]{:S(2)}, u32[]{:S(2)}) collective-permute-start(bf16[136,2048]{1,0:T(8,128)(2,1)S(1)} %get-tuple-element.133), channel_id=1, source_target_pairs={{0,8},{4,12},{8,0},{12,4},{16,24},{20,28},{24,16},{28,20},{1,9},{5... | collective-permute-start | bytes 1671176 | tf_op jit(solution)/shard_map/ppermute | solution.py:21
  244.7 23.2 %collective-permute-start.27 = (bf16[136,2048]{1,0:T(8,128)(2,1)S(1)}, bf16[136,2048]{1,0:T(8,128)(2,1)S(1)}, u32[]{:S(2)}, u32[]{:S(2)}) collective-permute-start(bf16[136,2048]{1,0:T(8,128)(2,1)S(1)} %collective-permute-done.25), channel_id=1, source_target_pairs={{0,8},{4,12},{8,0},{12,4},{16,24},{20,28},{24,16},{28,20},{1,9},{5... | collective-permute-start | bytes 1671176 | tf_op jit(solution)/shard_map/ppermute | solution.py:21
  298.7 20.6 %collective-permute-start.29 = (bf16[1088,2048]{1,0:T(8,128)(2,1)}, bf16[1088,2048]{1,0:T(8,128)(2,1)}, u32[]{:S(2)}, u32[]{:S(2)}) collective-permute-start(bf16[1088,2048]{1,0:T(8,128)(2,1)} %get-tuple-element.147), channel_id=1, source_target_pairs={{0,4},{4,0},{8,12},{12,8},{16,20},{20,16},{24,28},{28,24},{1,5},{5... | collective-permute-start | bytes 13369352 | tf_op jit(solution)/shard_map/ppermute | solution.py:21
  322.6 26.9 %collective-permute-start.31 = (bf16[2,136,2048]{2,1,0:T(8,128)(2,1)S(1)}, bf16[2,136,2048]{2,1,0:T(8,128)(2,1)S(1)}, u32[]{:S(2)}, u32[]{:S(2)}) collective-permute-start(bf16[2,136,2048]{2,1,0:T(8,128)(2,1)S(1)} %bitcast.184), channel_id=1, source_target_pairs={{0,8},{4,12},{8,0},{12,4},{16,24},{20,28},{24,16},{28,20},{1,9},{5... | collective-permute-start | bytes 3342344 | tf_op jit(solution)/shard_map/ppermute | solution.py:21
  324.4 26.6 %collective-permute-start.30 = (bf16[2,136,2048]{2,1,0:T(8,128)(2,1)S(1)}, bf16[2,136,2048]{2,1,0:T(8,128)(2,1)S(1)}, u32[]{:S(2)}, u32[]{:S(2)}) collective-permute-start(bf16[2,136,2048]{2,1,0:T(8,128)(2,1)S(1)} %bitcast.183), channel_id=1, source_target_pairs={{0,16},{4,20},{8,24},{12,28},{16,0},{20,4},{24,8},{28,12},{1,17},{... | collective-permute-start | bytes 3342344 | tf_op jit(solution)/shard_map/ppermute | solution.py:21
  354.6 14.1 %collective-permute-start.32 = (bf16[1,136,2048]{2,1,0:T(8,128)(2,1)}, bf16[1,136,2048]{2,1,0:T(8,128)(2,1)S(1)}, u32[]{:S(2)}, u32[]{:S(2)}) collective-permute-start(bf16[1,136,2048]{2,1,0:T(8,128)(2,1)} %get-tuple-element.149), channel_id=1, source_target_pairs={{0,8},{4,12},{8,0},{12,4},{16,24},{20,28},{24,16},{28,20},{1,9},{5... | collective-permute-start | bytes 1671176 | tf_op jit(solution)/shard_map/ppermute | solution.py:21
  355.3 14.0 %collective-permute-start.33 = (bf16[1,136,2048]{2,1,0:T(8,128)(2,1)}, bf16[1,136,2048]{2,1,0:T(8,128)(2,1)S(1)}, u32[]{:S(2)}, u32[]{:S(2)}) collective-permute-start(bf16[1,136,2048]{2,1,0:T(8,128)(2,1)} %get-tuple-element.150), channel_id=1, source_target_pairs={{0,16},{4,20},{8,24},{12,28},{16,0},{20,4},{24,8},{28,12},{1,17},{... | collective-permute-start | bytes 1671176 | tf_op jit(solution)/shard_map/ppermute | solution.py:21
  374.2 55.9 %all-to-all-start.2 = ((bf16[8,704,256]{2,1,0:T(8,128)(2,1)}), bf16[8,704,256]{2,1,0:T(8,128)(2,1)}, u32[]{:S(2)}, u32[]{:S(2)}) async-start(bf16[8,704,256]{2,1,0:T(8,128)(2,1)} %get-tuple-element.152), calls=%async_computation.2 | async-start | bytes 5767168 | tf_op jit(solution)/shard_map/all_to_all | solution.py:968
  381.4 23.5 %collective-permute-start.35 = (bf16[272,512]{1,0:T(8,128)(2,1)S(1)}, bf16[272,512]{1,0:T(8,128)(2,1)S(1)}, u32[]{:S(2)}, u32[]{:S(2)}) collective-permute-start(bf16[272,512]{1,0:T(8,128)(2,1)S(1)} %copy-done.37), channel_id=1, source_target_pairs={{0,2},{1,3},{2,0},{3,1},{4,6},{5,7},{6,4},{7,5},{8,10},{9,11},{10,... | collective-permute-start | bytes 835592 | tf_op jit(solution)/shard_map/ppermute | solution.py:21
  381.4 23.5 %collective-permute-start.34 = (bf16[272,512]{1,0:T(8,128)(2,1)S(1)}, bf16[272,512]{1,0:T(8,128)(2,1)S(1)}, u32[]{:S(2)}, u32[]{:S(2)}) collective-permute-start(bf16[272,512]{1,0:T(8,128)(2,1)S(1)} %get-tuple-element.154), channel_id=1, source_target_pairs={{0,1},{1,0},{2,3},{3,2},{4,5},{5,4},{6,7},{7,6},{8,9},{9,8},{10,11... | collective-permute-start | bytes 835592 | tf_op jit(solution)/shard_map/ppermute | solution.py:21
  405.0 38.4 %collective-permute-start.37 = (bf16[272,512]{1,0:T(8,128)(2,1)S(1)}, bf16[272,512]{1,0:T(8,128)(2,1)}, u32[]{:S(2)}, u32[]{:S(2)}) collective-permute-start(bf16[272,512]{1,0:T(8,128)(2,1)S(1)} %add_convert_fusion.9.refs_0_), channel_id=1, source_target_pairs={{0,1},{1,0},{2,3},{3,2},{4,5},{5,4},{6,7},{7,6},{8,9},{9,8},{10,11... | collective-permute-start | bytes 835592 | tf_op jit(solution)/shard_map/ppermute | solution.py:21
  405.1 38.3 %collective-permute-start.38 = (bf16[272,512]{1,0:T(8,128)(2,1)S(1)}, bf16[272,512]{1,0:T(8,128)(2,1)}, u32[]{:S(2)}, u32[]{:S(2)}) collective-permute-start(bf16[272,512]{1,0:T(8,128)(2,1)S(1)} %add_convert_fusion.9.refs_0_), channel_id=1, source_target_pairs={{0,2},{1,3},{2,0},{3,1},{4,6},{5,7},{6,4},{7,5},{8,10},{9,11},{10,... | collective-permute-start | bytes 835592 | tf_op jit(solution)/shard_map/ppermute | solution.py:21
  406.9 36.6 %collective-permute-start.39 = (bf16[272,512]{1,0:T(8,128)(2,1)S(1)}, bf16[272,512]{1,0:T(8,128)(2,1)}, u32[]{:S(2)}, u32[]{:S(2)}) collective-permute-start(bf16[272,512]{1,0:T(8,128)(2,1)S(1)} %add_convert_fusion.9.refs_0_), channel_id=1, source_target_pairs={{0,3},{1,2},{2,1},{3,0},{4,7},{5,6},{6,5},{7,4},{8,11},{9,10},{10,... | collective-permute-start | bytes 835592 | tf_op jit(solution)/shard_map/ppermute | solution.py:21
  430.2 51.7 %all-to-all-start.3 = ((bf16[8,256,512]{2,1,0:T(8,128)(2,1)}), bf16[8,256,512]{2,1,0:T(8,128)(2,1)}, u32[]{:S(2)}, u32[]{:S(2)}) async-start(bf16[8,256,512]{2,1,0:T(8,128)(2,1)} %bitcast.150), calls=%async_computation.3 | async-start | bytes 4194304 | tf_op jit(solution)/shard_map/all_to_all | solution.py:970
  434.7 132.2 %reduce-scatter.5.cloned.1.call-start = ((), (), s32[]{:S(2)}) async-start(), calls=%async_computation.8 | async-start | bytes 3538944 | tf_op jit(solution)/shard_map/reduce_scatter | solution.py:1007
  462.2 16.0 %collective-permute-start.41 = (bf16[2,136,512]{2,1,0:T(8,128)(2,1)}, bf16[2,136,512]{2,1,0:T(8,128)(2,1)}, u32[]{:S(2)}, u32[]{:S(2)}) collective-permute-start(bf16[2,136,512]{2,1,0:T(8,128)(2,1)} %bitcast.37), channel_id=1, source_target_pairs={{0,16},{4,20},{8,24},{12,28},{16,0},{20,4},{24,8},{28,12},{1,17},{... | collective-permute-start | bytes 835592 | tf_op jit(solution)/shard_map/ppermute | solution.py:21
  465.8 14.2 %collective-permute-start.43 = (bf16[2,136,512]{2,1,0:T(8,128)(2,1)}, bf16[2,136,512]{2,1,0:T(8,128)(2,1)S(1)}, u32[]{:S(2)}, u32[]{:S(2)}) collective-permute-start(bf16[2,136,512]{2,1,0:T(8,128)(2,1)} %bitcast.41), channel_id=1, source_target_pairs={{0,8},{4,12},{8,0},{12,4},{16,24},{20,28},{24,16},{28,20},{1,9},{5... | collective-permute-start | bytes 835592 | tf_op jit(solution)/shard_map/ppermute | solution.py:21
  501.4 35.8 %all-to-all-start.4 = ((bf16[8,256,512]{2,1,0:T(8,128)(2,1)}), bf16[8,256,512]{2,1,0:T(8,128)(2,1)}, u32[]{:S(2)}, u32[]{:S(2)}) async-start(bf16[8,256,512]{2,1,0:T(8,128)(2,1)} %bitcast.177), calls=%async_computation.6 | async-start | bytes 4194304 | tf_op jit(solution)/shard_map/all_to_all | solution.py:1032
  508.4 49.4 %collective-permute-start.47 = (bf16[2,200,1024]{2,1,0:T(8,128)(2,1)}, bf16[2,200,1024]{2,1,0:T(8,128)(2,1)}, u32[]{:S(2)}, u32[]{:S(2)}) collective-permute-start(bf16[2,200,1024]{2,1,0:T(8,128)(2,1)} %add_convert_fusion.3), channel_id=1, source_target_pairs={{0,16},{4,20},{8,24},{12,28},{16,0},{20,4},{24,8},{28,12},{1,17},{... | collective-permute-start | bytes 2457608 | tf_op jit(solution)/shard_map/ppermute | solution.py:21
  512.6 45.2 %collective-permute-start.49 = (bf16[2,200,1024]{2,1,0:T(8,128)(2,1)}, bf16[2,200,1024]{2,1,0:T(8,128)(2,1)}, u32[]{:S(2)}, u32[]{:S(2)}) collective-permute-start(bf16[2,200,1024]{2,1,0:T(8,128)(2,1)} %add_convert_fusion.2), channel_id=1, source_target_pairs={{0,8},{4,12},{8,0},{12,4},{16,24},{20,28},{24,16},{28,20},{1,9},{5... | collective-permute-start | bytes 2457608 | tf_op jit(solution)/shard_map/ppermute | solution.py:21
  514.1 29.1 %collective-permute-start.50 = (bf16[552,512]{1,0:T(8,128)(2,1)}, bf16[552,512]{1,0:T(8,128)(2,1)S(1)}, u32[]{:S(2)}, u32[]{:S(2)}) collective-permute-start(bf16[552,512]{1,0:T(8,128)(2,1)} %get-tuple-element.179), channel_id=1, source_target_pairs={{0,1},{1,0},{2,3},{3,2},{4,5},{5,4},{6,7},{7,6},{8,9},{9,8},{10,11... | collective-permute-start | bytes 1695752 | tf_op jit(solution)/shard_map/ppermute | solution.py:21
  514.1 41.1 %collective-permute-start.51 = (bf16[552,512]{1,0:T(8,128)(2,1)}, bf16[552,512]{1,0:T(8,128)(2,1)S(1)}, u32[]{:S(2)}, u32[]{:S(2)}) collective-permute-start(bf16[552,512]{1,0:T(8,128)(2,1)} %get-tuple-element.180), channel_id=1, source_target_pairs={{0,2},{1,3},{2,0},{3,1},{4,6},{5,7},{6,4},{7,5},{8,10},{9,11},{10,... | collective-permute-start | bytes 1695752 | tf_op jit(solution)/shard_map/ppermute | solution.py:21
  516.0 39.1 %collective-permute-start.52 = (bf16[552,512]{1,0:T(8,128)(2,1)}, bf16[552,512]{1,0:T(8,128)(2,1)S(1)}, u32[]{:S(2)}, u32[]{:S(2)}) collective-permute-start(bf16[552,512]{1,0:T(8,128)(2,1)} %get-tuple-element.181), channel_id=1, source_target_pairs={{0,3},{1,2},{2,1},{3,0},{4,7},{5,6},{6,5},{7,4},{8,11},{9,10},{10,... | collective-permute-start | bytes 1695752 | tf_op jit(solution)/shard_map/ppermute | solution.py:21
  560.1 12.3 %collective-permute-start.54 = (bf16[1,200,1024]{2,1,0:T(8,128)(2,1)}, bf16[1,200,1024]{2,1,0:T(8,128)(2,1)}, u32[]{:S(2)}, u32[]{:S(2)}) collective-permute-start(bf16[1,200,1024]{2,1,0:T(8,128)(2,1)} %add_convert_fusion.4), channel_id=1, source_target_pairs={{0,16},{4,20},{8,24},{12,28},{16,0},{20,4},{24,8},{28,12},{1,17},{... | collective-permute-start | bytes 1228808 | tf_op jit(solution)/shard_map/ppermute | solution.py:21
  (87 other events, 1057.0 us)
Sparse Core Ops, SparseCore 0:
  10.5 69.4 all-gather.4
  88.6 38.2 all-gather.6
  369.5 107.4 reduce-scatter.2
  480.2 69.5 reduce-scatter.4

commit v7 on v6

--- a/solution.py
+++ b/solution.py
@@ -383,7 +383,7 @@
             jax.ShapeDtypeStruct((total, 2 * f), BF),
             jax.ShapeDtypeStruct((total, dp), BF),
         ),
-        compiler_params=pltpu.CompilerParams(vmem_limit_bytes=58 * MIB),
+        compiler_params=pltpu.CompilerParams(vmem_limit_bytes=36 * MIB),
         cost_estimate=pl.CostEstimate(
             flops=10 * total * dp * f,
             bytes_accessed=8 * total * dp + 6 * f * dp,

time: 616 us -> 625 us (1.015)
  local copies, waits for them, and re-layouts: 65.4 us -> 80.3 us
    unnamed x165 -> x183, local copies, waits for them, and re-layouts: 28.2 us -> 44.1 us
  transfers between devices with their start and end apart: 67 -> 67, of which waited for: 37 -> 37; matrix products, arithmetic and copies ran while one was open for 13% -> 13% of each run, Pallas kernels for 16% -> 15%
where the time goes in v7:
time: 625 us; the launch traced here: 615 us
  waiting for transfers between devices  248 us (40%)
  Pallas kernels  117 us (19%)
  starting transfers between devices  105 us (17%)
  local copies, waits for them, and re-layouts  80.3 us (13%)
  other arithmetic  48.4 us (8%)
  between operations  15.3 us (2%)
    ppermute x58, waiting for transfers between devices, swap(): return lax.ppermute(value, axis, [(i, i ^ mask) for i in range(count)])  192 us
    ppermute x58, starting transfers between devices, swap(): return lax.ppermute(value, axis, [(i, i ^ mask) for i in range(count)])  73.1 us
    unnamed x183, local copies, waits for them, and re-layouts  44.1 us
    pallas_call x11, Pallas kernels, whole_call(): pl.pallas_call(kernel, out_shape=outs, in_specs=specs, out_specs=tuple((p...  39.6 us
    pallas_call x2, Pallas kernels, feed(): pl.pallas_call(lambda *refs: feed_kernel(pair, *refs), grid=(total // ste...  33.2 us
    all_to_all x1, waiting for transfers between devices, shards(): lax.all_to_all(after(gate_up_sent, branch), 'seq', 0, 0).reshape(dp, 2 * fp)  32.8 us
    convert_element_type x10, other arithmetic, scatter_rows(): sent = [total_of([p[keep:] for p in part]).astype(BF) for part in parts]  22.5 us
    pallas_call x1, Pallas kernels, weight_grads(): pl.pallas_call(weights_kernel, grid=(dp // wide,), in_specs=[cols, cols,...  22 us
  transfers between devices with their start and end apart: 67, of which 37 were waited for; matrix products, arithmetic and copies ran while one was open for 13% of the time, Pallas kernels for 15%

profile of v7, /device:TPU:0, one launch (start us, length us, event | category | flops | bytes accessed | tf_op | source)
XLA Modules:
  0.0 614.5 jit_solution(16448334513628202458)
XLA Ops:
  12.0 3.0 collective-permute-start
  16.7 16.7 %collective-permute-done = bf16[136,2048]{1,0:T(8,128)(2,1)S(1)} collective-permute-done((bf16[136,2048]{1,0:T(8,128)(2,1)S(1)}, bf16[136,2048]{1,0:T(8,128)(2,1)S(1)}, u32[]{:S(2)}, u32[]{:S(2)}) %collective-permute-start) | collective-permute-done | bytes 557088 | tf_op jit(solution)/shard_map/ppermute | solution.py:21
  33.4 2.8 collective-permute-done.1
  42.5 2.8 collective-permute-start.5
  46.3 32.8 %collective-permute-done.2 = bf16[272,2048]{1,0:T(8,128)(2,1)} collective-permute-done((bf16[272,2048]{1,0:T(8,128)(2,1)}, bf16[272,2048]{1,0:T(8,128)(2,1)}, u32[]{:S(2)}, u32[]{:S(2)}) %collective-permute-start.2) | collective-permute-done | bytes 1114144 | tf_op jit(solution)/shard_map/ppermute | solution.py:21
  81.5 4.7 shard_map.408
  92.2 3.7 pad_maximum_fusion.1
  98.8 5.7 collective-permute-done.7
  114.8 6.5 %collective-permute-done.13 = bf16[136,512]{1,0:T(8,128)(2,1)S(1)} collective-permute-done((bf16[136,512]{1,0:T(8,128)(2,1)S(1)}, bf16[136,512]{1,0:T(8,128)(2,1)S(1)}, u32[]{:S(2)}, u32[]{:S(2)}) %collective-permute-start.13) | collective-permute-done | bytes 139296 | tf_op jit(solution)/shard_map/ppermute | solution.py:21
  124.8 4.5 all-to-all-start.1
  136.7 3.8 shard_map.409
  144.9 3.7 collective-permute-start.17
  156.4 16.1 %collective-permute-done.16 = bf16[272,512]{1,0:T(8,128)(2,1)S(1)} collective-permute-done((bf16[272,512]{1,0:T(8,128)(2,1)S(1)}, bf16[272,512]{1,0:T(8,128)(2,1)S(1)}, u32[]{:S(2)}, u32[]{:S(2)}) %collective-permute-start.16) | collective-permute-done | bytes 278560 | tf_op jit(solution)/shard_map/ppermute | solution.py:21
  173.4 4.6 all-to-all-start
  185.5 3.1 collective-permute-start.20
  194.4 32.8 %all-to-all-done = bf16[8,256,1024]{2,1,0:T(8,128)(2,1)} async-done(((bf16[8,256,1024]{2,1,0:T(8,128)(2,1)}), bf16[8,256,1024]{2,1,0:T(8,128)(2,1)}, u32[]{:S(2)}, u32[]{:S(2)}) %all-to-all-start) | async-done | bytes 4194336 | tf_op jit(solution)/shard_map/all_to_all | solution.py:888
  231.3 10.8 %collective-permute-done.22 = bf16[136,2048]{1,0:T(8,128)(2,1)S(1)} collective-permute-done((bf16[136,2048]{1,0:T(8,128)(2,1)S(1)}, bf16[136,2048]{1,0:T(8,128)(2,1)S(1)}, u32[]{:S(2)}, u32[]{:S(2)}) %collective-permute-start.22) | collective-permute-done | bytes 557088 | tf_op jit(solution)/shard_map/ppermute | solution.py:21
  246.4 10.3 %collective-permute-done.23 = bf16[136,2048]{1,0:T(8,128)(2,1)S(1)} collective-permute-done((bf16[136,2048]{1,0:T(8,128)(2,1)S(1)}, bf16[136,2048]{1,0:T(8,128)(2,1)S(1)}, u32[]{:S(2)}, u32[]{:S(2)}) %collective-permute-start.23) | collective-permute-done | bytes 557088 | tf_op jit(solution)/shard_map/ppermute | solution.py:21
  256.8 10.7 %collective-permute-done.24 = bf16[136,2048]{1,0:T(8,128)(2,1)S(1)} collective-permute-done((bf16[136,2048]{1,0:T(8,128)(2,1)S(1)}, bf16[136,2048]{1,0:T(8,128)(2,1)S(1)}, u32[]{:S(2)}, u32[]{:S(2)}) %collective-permute-start.24) | collective-permute-done | bytes 557088 | tf_op jit(solution)/shard_map/ppermute | solution.py:21
  270.3 5.3 collective-permute-done.28.refs_0_.xo_ref
  282.5 17.1 %shard_map.413 = (bf16[1088,512]{1,0:T(8,128)(2,1)S(1)}, bf16[1088,1024]{1,0:T(8,128)(2,1)S(1)}, bf16[1088,2048]{1,0:T(8,128)(2,1)}) custom-call(bf16[1088,2048]{1,0:T(8,128)(2,1)S(1)} %copy-done.39, bf16[1088,2048]{1,0:T(8,128)(2,1)} %collective-permute-done.18.refs_1_.co_ref, bf16[2048,1024]{1,0:T(8,128)(2,1)} %bitcast.8.refs_2_, ...), custom_call_target="tpu_custom_call" | custom-call | flops 11408506880 | bytes 24117248 | tf_op jit(solution)/shard_map/pallas_call | solution.py:372
  307.3 16.1 %shard_map.414 = (bf16[1088,512]{1,0:T(8,128)(2,1)S(1)}, bf16[1088,1024]{1,0:T(8,128)(2,1)S(1)}, bf16[1088,2048]{1,0:T(8,128)(2,1)S(1)}) custom-call(bf16[1088,2048]{1,0:T(8,128)(2,1)S(1)} %copy-done.26, bf16[1088,2048]{1,0:T(8,128)(2,1)} %constant_dynamic-update-slice_fusion.10.refs_1_.ce_ref, bf16[2048,1024]{1,0:T(8,128)(2,1)} %bitcast.8.refs_2_, ...), custom_call_target="tpu_custom_call" | custom-call | flops 11408506880 | bytes 24117248 | tf_op jit(solution)/shard_map/pallas_call | solution.py:372
  328.6 3.4 add_convert_fusion
  335.6 22.0 %shard_map.415 = (bf16[2048,512]{1,0:T(8,128)(2,1)S(1)}, bf16[2048,512]{1,0:T(8,128)(2,1)}, bf16[8,704,256]{2,1,0:T(8,128)(2,1)}) custom-call(bf16[1088,2048]{1,0:T(8,128)(2,1)} %copy-done.38, bf16[1088,2048]{1,0:T(8,128)(2,1)} %copy-done.25, bf16[1088,2048]{1,0:T(8,128)(2,1)} %collective-permute-done.18.refs_1_.co_ref, ...), custom_call_target="tpu_custom_call" | custom-call | flops 13690208256 | bytes 17825792 | tf_op jit(solution)/shard_map/pallas_call | solution.py:428
  360.4 3.6 fusion
  366.5 8.7 %shard_map.416 = bf16[8,272,2048]{2,1,0:T(8,128)(2,1)} custom-call(s32[8]{0:T(128)S(1)} %get-tuple-element.258.odd_ref, s32[8]{0:T(128)S(1)} %gather_fusion, s32[8]{0:T(128)S(1)} %gather_fusion.1, s32[8]{0:T(128)S(1)} %fusion.46.la_ref, s32[8]{0:T(128)S(1)} %get-tuple-element.259.lb_ref, bf16[1088,512]{1,0:T(8,128)(2,1)S(1)} %copy-done.49, ...), custom_call_target="tpu_custom_call" | custom-call | flops 4563402752 | bytes 8912896 | tf_op jit(solution)/shard_map/pallas_call | solution.py:484
  375.2 2.8 collective-permute-done.32
  383.6 4.6 all-to-all-start.2
  392.7 7.0 %collective-permute-done.36 = bf16[272,512]{1,0:T(8,128)(2,1)S(1)} collective-permute-done((bf16[272,512]{1,0:T(8,128)(2,1)S(1)}, bf16[272,512]{1,0:T(8,128)(2,1)S(1)}, u32[]{:S(2)}, u32[]{:S(2)}) %collective-permute-start.36) | collective-permute-done | bytes 278560 | tf_op jit(solution)/shard_map/ppermute | solution.py:21
  399.7 14.6 %collective-permute-done.35 = bf16[272,512]{1,0:T(8,128)(2,1)S(1)} collective-permute-done((bf16[272,512]{1,0:T(8,128)(2,1)S(1)}, bf16[272,512]{1,0:T(8,128)(2,1)S(1)}, u32[]{:S(2)}, u32[]{:S(2)}) %collective-permute-start.35) | collective-permute-done | bytes 278560 | tf_op jit(solution)/shard_map/ppermute | solution.py:21
  418.9 20.6 %all-to-all-done.2.d_ref = bf16[8,704,256]{2,1,0:T(8,128)(2,1)} async-done(((bf16[8,704,256]{2,1,0:T(8,128)(2,1)}), bf16[8,704,256]{2,1,0:T(8,128)(2,1)}, u32[]{:S(2)}, u32[]{:S(2)}) %all-to-all-start.2) | async-done | bytes 2883616 | tf_op jit(solution)/shard_map/all_to_all | solution.py:968
  439.6 4.5 all-to-all-start.3
  444.1 8.8 %reduce-scatter.5.cloned.1.call-start = ((), (), s32[]{:S(2)}) async-start(), calls=%async_computation.8 | async-start | bytes 3538944 | tf_op jit(solution)/shard_map/reduce_scatter | solution.py:1007
  452.9 4.7 shard_map.418
  459.2 8.4 %shard_map.419 = (bf16[272,512]{1,0:T(8,128)(2,1)}, bf16[544,512]{1,0:T(8,128)(2,1)}, bf16[544,512]{1,0:T(8,128)(2,1)}, bf16[544,512]{1,0:T(8,128)(2,1)}, bf16[544,512]{1,0:T(8,128)(2,1)}) custom-call(bf16[272,512]{1,0:T(8,128)(2,1)} %copy-done.42, bf16[2176,512]{1,0:T(8,128)(2,1)} %copy-done.35, s32[272,1]{1,0:T(8,128)} %copy-done.24, ...), custom_call_target="tpu_custom_call" | custom-call | flops 3030384640 | bytes 6137408 | tf_op jit(solution)/shard_map/pallas_call | solution.py:127
  476.7 2.7 shard_map.422
  479.5 8.2 %collective-permute-done.41 = bf16[2,136,512]{2,1,0:T(8,128)(2,1)} collective-permute-done((bf16[2,136,512]{2,1,0:T(8,128)(2,1)}, bf16[2,136,512]{2,1,0:T(8,128)(2,1)}, u32[]{:S(2)}, u32[]{:S(2)}) %collective-permute-start.41) | collective-permute-done | bytes 278560 | tf_op jit(solution)/shard_map/ppermute | solution.py:21
  494.2 2.9 collective-permute-done.44
  499.4 10.8 %shard_map.420 = (bf16[4,200,1024]{2,1,0:T(8,128)(2,1)}, bf16[4,200,1024]{2,1,0:T(8,128)(2,1)}, bf16[4,200,1024]{2,1,0:T(8,128)(2,1)}, bf16[4,200,1024]{2,1,0:T(...) custom-call(s32[1]{0:T(128)} %bitcast.5.refs_0_, ...), custom_call_target="tpu_custom_call" | custom-call | flops 2281701376 | bytes 18710536 | tf_op jit(solution)/shard_map/pallas_call | solution.py:127
  510.7 4.5 all-to-all-start.4
  527.8 7.7 %shard_map.423 = (f32[256,4096]{1,0:T(8,128)}, f32[4096,256]{1,0:T(8,128)}, f32[8,192,256]{2,1,0:T(8,128)}) custom-call(s32[1]{0:T(128)} %bitcast.t_ref.refs_1_.token_ref, bf16[8,256,512]{2,1,0:T(8,128)(2,1)} %all-to-all-done.3.g_ref, bf16[8,704,256]{2,1,0:T(8,128)(2,1)} %all-to-all-done.2.d_ref), custom_call_target="tpu_custom_call" | custom-call | bytes 14942208 | tf_op jit(solution)/shard_map/pallas_call | solution.py:702
  546.7 6.0 shard_map.424
  552.7 11.7 %collective-permute-done.51.refs_2_ = bf16[552,512]{1,0:T(8,128)(2,1)S(1)} collective-permute-done((bf16[552,512]{1,0:T(8,128)(2,1)}, bf16[552,512]{1,0:T(8,128)(2,1)S(1)}, u32[]{:S(2)}, u32[]{:S(2)}) %collective-permute-start.51) | collective-permute-done | bytes 565280 | tf_op jit(solution)/shard_map/ppermute | solution.py:21
  564.4 2.9 collective-permute-done.47
  583.6 3.6 collective-permute-done.53
  591.7 3.4 collective-permute-start.57
  595.1 4.4 collective-permute-start.56
  599.5 5.7 collective-permute-done.56
  (391 shorter events, 193.4 us)
Async XLA Ops:
  7.2 73.2 %all-gather.5.cloned.1.call-start = ((), (), s32[]{:S(2)}) async-start(), calls=%async_computation.9 | async-start | bytes 7225344 | tf_op jit(solution)/shard_map/all_gather | solution.py:802
  10.3 131.7 %all-gather.7.cloned.1.call-start = ((), (), s32[]{:S(2)}) async-start(), calls=%async_computation.10 | async-start | bytes 3538944 | tf_op jit(solution)/shard_map/all_gather | solution.py:877
  12.0 21.4 %collective-permute-start = (bf16[136,2048]{1,0:T(8,128)(2,1)S(1)}, bf16[136,2048]{1,0:T(8,128)(2,1)S(1)}, u32[]{:S(2)}, u32[]{:S(2)}) collective-permute-start(bf16[136,2048]{1,0:T(8,128)(2,1)S(1)} %pad_maximum_fusion.7), channel_id=1, source_target_pairs={{0,8},{4,12},{8,0},{12,4},{16,24},{20,28},{24,16},{28,20},{1,9},{5... | collective-permute-start | bytes 1671176 | tf_op jit(solution)/shard_map/ppermute | solution.py:21
  15.1 21.1 %collective-permute-start.1 = (bf16[136,2048]{1,0:T(8,128)(2,1)S(1)}, bf16[136,2048]{1,0:T(8,128)(2,1)S(1)}, u32[]{:S(2)}, u32[]{:S(2)}) collective-permute-start(bf16[136,2048]{1,0:T(8,128)(2,1)S(1)} %pad_maximum_fusion.8), channel_id=1, source_target_pairs={{0,16},{4,20},{8,24},{12,28},{16,0},{20,4},{24,8},{28,12},{1,17},{... | collective-permute-start | bytes 1671176 | tf_op jit(solution)/shard_map/ppermute | solution.py:21
  37.4 41.7 %collective-permute-start.2 = (bf16[272,2048]{1,0:T(8,128)(2,1)}, bf16[272,2048]{1,0:T(8,128)(2,1)}, u32[]{:S(2)}, u32[]{:S(2)}) collective-permute-start(bf16[272,2048]{1,0:T(8,128)(2,1)} %pad_maximum_fusion.2), channel_id=1, source_target_pairs={{0,16},{4,20},{8,24},{12,28},{16,0},{20,4},{24,8},{28,12},{1,17},{... | collective-permute-start | bytes 3342344 | tf_op jit(solution)/shard_map/ppermute | solution.py:21
  41.0 39.4 %collective-permute-start.3 = (bf16[272,2048]{1,0:T(8,128)(2,1)}, bf16[272,2048]{1,0:T(8,128)(2,1)}, u32[]{:S(2)}, u32[]{:S(2)}) collective-permute-start(bf16[272,2048]{1,0:T(8,128)(2,1)} %pad_maximum_fusion.3), channel_id=1, source_target_pairs={{0,8},{4,12},{8,0},{12,4},{16,24},{20,28},{24,16},{28,20},{1,9},{5... | collective-permute-start | bytes 3342344 | tf_op jit(solution)/shard_map/ppermute | solution.py:21
  41.0 40.4 %collective-permute-start.4 = (bf16[272,512]{1,0:T(8,128)(2,1)S(1)}, bf16[272,512]{1,0:T(8,128)(2,1)S(1)}, u32[]{:S(2)}, u32[]{:S(2)}) collective-permute-start(bf16[272,512]{1,0:T(8,128)(2,1)S(1)} %fusion.5.refs_0_.refs_4_), channel_id=1, source_target_pairs={{0,1},{1,0},{2,3},{3,2},{4,5},{5,4},{6,7},{7,6},{8,9},{9,8},{10,11... | collective-permute-start | bytes 835592 | tf_op jit(solution)/shard_map/ppermute | solution.py:21
  42.5 38.9 %collective-permute-start.5 = (bf16[272,512]{1,0:T(8,128)(2,1)S(1)}, bf16[272,512]{1,0:T(8,128)(2,1)S(1)}, u32[]{:S(2)}, u32[]{:S(2)}) collective-permute-start(bf16[272,512]{1,0:T(8,128)(2,1)S(1)} %fusion.5.refs_0_.refs_4_), channel_id=1, source_target_pairs={{0,2},{1,3},{2,0},{3,1},{4,6},{5,7},{6,4},{7,5},{8,10},{9,11},{10,... | collective-permute-start | bytes 835592 | tf_op jit(solution)/shard_map/ppermute | solution.py:21
  45.3 36.2 %collective-permute-start.6 = (bf16[272,512]{1,0:T(8,128)(2,1)S(1)}, bf16[272,512]{1,0:T(8,128)(2,1)S(1)}, u32[]{:S(2)}, u32[]{:S(2)}) collective-permute-start(bf16[272,512]{1,0:T(8,128)(2,1)S(1)} %fusion.5.refs_0_.refs_4_), channel_id=1, source_target_pairs={{0,3},{1,2},{2,1},{3,0},{4,7},{5,6},{6,5},{7,4},{8,11},{9,10},{10,... | collective-permute-start | bytes 835592 | tf_op jit(solution)/shard_map/ppermute | solution.py:21
  97.5 12.5 %collective-permute-start.8 = (bf16[136,512]{1,0:T(8,128)(2,1)S(1)}, bf16[136,512]{1,0:T(8,128)(2,1)S(1)}, u32[]{:S(2)}, u32[]{:S(2)}) collective-permute-start(bf16[136,512]{1,0:T(8,128)(2,1)S(1)} %get-tuple-element.118), channel_id=1, source_target_pairs={{0,16},{4,20},{8,24},{12,28},{16,0},{20,4},{24,8},{28,12},{1,17},{... | collective-permute-start | bytes 417800 | tf_op jit(solution)/shard_map/ppermute | solution.py:21
  124.8 48.6 %all-to-all-start.1 = ((bf16[8,704,256]{2,1,0:T(8,128)(2,1)}), bf16[8,704,256]{2,1,0:T(8,128)(2,1)}, u32[]{:S(2)}, u32[]{:S(2)}) async-start(bf16[8,704,256]{2,1,0:T(8,128)(2,1)} %pad_maximum_fusion.1), calls=%async_computation.1 | async-start | bytes 5767168 | tf_op jit(solution)/shard_map/all_to_all | solution.py:878
  134.1 45.1 %collective-permute-start.18 = (bf16[1088,2048]{1,0:T(8,128)(2,1)}, bf16[1088,2048]{1,0:T(8,128)(2,1)}, u32[]{:S(2)}, u32[]{:S(2)}) collective-permute-start(bf16[1088,2048]{1,0:T(8,128)(2,1)} %constant_dynamic-update-slice_fusion.10.refs_1_.ce_ref), channel_id=1, source_target_pairs={{0,4},{4,0},{8,12},{12,8},{16,20},{20,16},{24,28},{28,24},{1,5},{5... | collective-permute-start | bytes 13369352 | tf_op jit(solution)/shard_map/ppermute | solution.py:21
  144.9 11.5 %collective-permute-start.17 = (bf16[272,512]{1,0:T(8,128)(2,1)S(1)}, bf16[272,512]{1,0:T(8,128)(2,1)S(1)}, u32[]{:S(2)}, u32[]{:S(2)}) collective-permute-start(bf16[272,512]{1,0:T(8,128)(2,1)S(1)} %get-tuple-element.125), channel_id=1, source_target_pairs={{0,3},{1,2},{2,1},{3,0},{4,7},{5,6},{6,5},{7,4},{8,11},{9,10},{10,... | collective-permute-start | bytes 835592 | tf_op jit(solution)/shard_map/ppermute | solution.py:21
  148.6 23.9 %collective-permute-start.16 = (bf16[272,512]{1,0:T(8,128)(2,1)S(1)}, bf16[272,512]{1,0:T(8,128)(2,1)S(1)}, u32[]{:S(2)}, u32[]{:S(2)}) collective-permute-start(bf16[272,512]{1,0:T(8,128)(2,1)S(1)} %get-tuple-element.124), channel_id=1, source_target_pairs={{0,2},{1,3},{2,0},{3,1},{4,6},{5,7},{6,4},{7,5},{8,10},{9,11},{10,... | collective-permute-start | bytes 835592 | tf_op jit(solution)/shard_map/ppermute | solution.py:21
  148.6 23.9 %collective-permute-start.15 = (bf16[272,512]{1,0:T(8,128)(2,1)S(1)}, bf16[272,512]{1,0:T(8,128)(2,1)S(1)}, u32[]{:S(2)}, u32[]{:S(2)}) collective-permute-start(bf16[272,512]{1,0:T(8,128)(2,1)S(1)} %get-tuple-element.123), channel_id=1, source_target_pairs={{0,1},{1,0},{2,3},{3,2},{4,5},{5,4},{6,7},{7,6},{8,9},{9,8},{10,11... | collective-permute-start | bytes 835592 | tf_op jit(solution)/shard_map/ppermute | solution.py:21
  173.4 53.7 %all-to-all-start = ((bf16[8,256,1024]{2,1,0:T(8,128)(2,1)}), bf16[8,256,1024]{2,1,0:T(8,128)(2,1)}, u32[]{:S(2)}, u32[]{:S(2)}) async-start(bf16[8,256,1024]{2,1,0:T(8,128)(2,1)} %pad_maximum_fusion), calls=%async_computation | async-start | bytes 8388608 | tf_op jit(solution)/shard_map/all_to_all | solution.py:888
  178.0 320.0 %reduce-scatter.3.cloned.1.call-start = ((), (), s32[]{:S(2)}) async-start(), calls=%async_computation.7 | async-start | bytes 10027008 | tf_op jit(solution)/shard_map/reduce_scatter | solution.py:967
  185.5 41.6 %collective-permute-start.19 = (bf16[272,512]{1,0:T(8,128)(2,1)S(1)}, bf16[272,512]{1,0:T(8,128)(2,1)S(1)}, u32[]{:S(2)}, u32[]{:S(2)}) collective-permute-start(bf16[272,512]{1,0:T(8,128)(2,1)S(1)} %get-tuple-element.131.refs_0_), channel_id=1, source_target_pairs={{0,1},{1,0},{2,3},{3,2},{4,5},{5,4},{6,7},{7,6},{8,9},{9,8},{10,11... | collective-permute-start | bytes 835592 | tf_op jit(solution)/shard_map/ppermute | solution.py:21
  185.5 41.6 %collective-permute-start.20 = (bf16[272,512]{1,0:T(8,128)(2,1)S(1)}, bf16[272,512]{1,0:T(8,128)(2,1)}, u32[]{:S(2)}, u32[]{:S(2)}) collective-permute-start(bf16[272,512]{1,0:T(8,128)(2,1)S(1)} %get-tuple-element.131.refs_0_), channel_id=1, source_target_pairs={{0,2},{1,3},{2,0},{3,1},{4,6},{5,7},{6,4},{7,5},{8,10},{9,11},{10,... | collective-permute-start | bytes 835592 | tf_op jit(solution)/shard_map/ppermute | solution.py:21
  188.6 38.5 %collective-permute-start.21 = (bf16[272,512]{1,0:T(8,128)(2,1)S(1)}, bf16[272,512]{1,0:T(8,128)(2,1)}, u32[]{:S(2)}, u32[]{:S(2)}) collective-permute-start(bf16[272,512]{1,0:T(8,128)(2,1)S(1)} %get-tuple-element.131.refs_0_), channel_id=1, source_target_pairs={{0,3},{1,2},{2,1},{3,0},{4,7},{5,6},{6,5},{7,4},{8,11},{9,10},{10,... | collective-permute-start | bytes 835592 | tf_op jit(solution)/shard_map/ppermute | solution.py:21
  228.7 13.4 %collective-permute-start.22 = (bf16[136,2048]{1,0:T(8,128)(2,1)S(1)}, bf16[136,2048]{1,0:T(8,128)(2,1)S(1)}, u32[]{:S(2)}, u32[]{:S(2)}) collective-permute-start(bf16[136,2048]{1,0:T(8,128)(2,1)S(1)} %get-tuple-element.132), channel_id=1, source_target_pairs={{0,8},{4,12},{8,0},{12,4},{16,24},{20,28},{24,16},{28,20},{1,9},{5... | collective-permute-start | bytes 1671176 | tf_op jit(solution)/shard_map/ppermute | solution.py:21
  229.3 15.5 %collective-permute-start.25 = (bf16[136,2048]{1,0:T(8,128)(2,1)S(1)}, bf16[136,2048]{1,0:T(8,128)(2,1)S(1)}, u32[]{:S(2)}, u32[]{:S(2)}) collective-permute-start(bf16[136,2048]{1,0:T(8,128)(2,1)S(1)} %get-tuple-element.133), channel_id=1, source_target_pairs={{0,16},{4,20},{8,24},{12,28},{16,0},{20,4},{24,8},{28,12},{1,17},{... | collective-permute-start | bytes 1671176 | tf_op jit(solution)/shard_map/ppermute | solution.py:21
  230.0 26.8 %collective-permute-start.23 = (bf16[136,2048]{1,0:T(8,128)(2,1)S(1)}, bf16[136,2048]{1,0:T(8,128)(2,1)S(1)}, u32[]{:S(2)}, u32[]{:S(2)}) collective-permute-start(bf16[136,2048]{1,0:T(8,128)(2,1)S(1)} %get-tuple-element.132), channel_id=1, source_target_pairs={{0,16},{4,20},{8,24},{12,28},{16,0},{20,4},{24,8},{28,12},{1,17},{... | collective-permute-start | bytes 1671176 | tf_op jit(solution)/shard_map/ppermute | solution.py:21
  242.2 25.3 %collective-permute-start.24 = (bf16[136,2048]{1,0:T(8,128)(2,1)S(1)}, bf16[136,2048]{1,0:T(8,128)(2,1)S(1)}, u32[]{:S(2)}, u32[]{:S(2)}) collective-permute-start(bf16[136,2048]{1,0:T(8,128)(2,1)S(1)} %collective-permute-done.22), channel_id=1, source_target_pairs={{0,16},{4,20},{8,24},{12,28},{16,0},{20,4},{24,8},{28,12},{1,17},{... | collective-permute-start | bytes 1671176 | tf_op jit(solution)/shard_map/ppermute | solution.py:21
  242.5 25.1 %collective-permute-start.26 = (bf16[136,2048]{1,0:T(8,128)(2,1)S(1)}, bf16[136,2048]{1,0:T(8,128)(2,1)S(1)}, u32[]{:S(2)}, u32[]{:S(2)}) collective-permute-start(bf16[136,2048]{1,0:T(8,128)(2,1)S(1)} %get-tuple-element.133), channel_id=1, source_target_pairs={{0,8},{4,12},{8,0},{12,4},{16,24},{20,28},{24,16},{28,20},{1,9},{5... | collective-permute-start | bytes 1671176 | tf_op jit(solution)/shard_map/ppermute | solution.py:21
  244.8 23.2 %collective-permute-start.27 = (bf16[136,2048]{1,0:T(8,128)(2,1)S(1)}, bf16[136,2048]{1,0:T(8,128)(2,1)S(1)}, u32[]{:S(2)}, u32[]{:S(2)}) collective-permute-start(bf16[136,2048]{1,0:T(8,128)(2,1)S(1)} %collective-permute-done.25), channel_id=1, source_target_pairs={{0,8},{4,12},{8,0},{12,4},{16,24},{20,28},{24,16},{28,20},{1,9},{5... | collective-permute-start | bytes 1671176 | tf_op jit(solution)/shard_map/ppermute | solution.py:21
  301.9 26.7 %collective-permute-start.29 = (bf16[1088,2048]{1,0:T(8,128)(2,1)}, bf16[1088,2048]{1,0:T(8,128)(2,1)}, u32[]{:S(2)}, u32[]{:S(2)}) collective-permute-start(bf16[1088,2048]{1,0:T(8,128)(2,1)} %get-tuple-element.147), channel_id=1, source_target_pairs={{0,4},{4,0},{8,12},{12,8},{16,20},{20,16},{24,28},{28,24},{1,5},{5... | collective-permute-start | bytes 13369352 | tf_op jit(solution)/shard_map/ppermute | solution.py:21
  332.0 26.9 %collective-permute-start.31 = (bf16[2,136,2048]{2,1,0:T(8,128)(2,1)S(1)}, bf16[2,136,2048]{2,1,0:T(8,128)(2,1)S(1)}, u32[]{:S(2)}, u32[]{:S(2)}) collective-permute-start(bf16[2,136,2048]{2,1,0:T(8,128)(2,1)S(1)} %bitcast.186), channel_id=1, source_target_pairs={{0,8},{4,12},{8,0},{12,4},{16,24},{20,28},{24,16},{28,20},{1,9},{5... | collective-permute-start | bytes 3342344 | tf_op jit(solution)/shard_map/ppermute | solution.py:21
  333.8 26.6 %collective-permute-start.30 = (bf16[2,136,2048]{2,1,0:T(8,128)(2,1)S(1)}, bf16[2,136,2048]{2,1,0:T(8,128)(2,1)S(1)}, u32[]{:S(2)}, u32[]{:S(2)}) collective-permute-start(bf16[2,136,2048]{2,1,0:T(8,128)(2,1)S(1)} %bitcast.185), channel_id=1, source_target_pairs={{0,16},{4,20},{8,24},{12,28},{16,0},{20,4},{24,8},{28,12},{1,17},{... | collective-permute-start | bytes 3342344 | tf_op jit(solution)/shard_map/ppermute | solution.py:21
  364.0 14.1 %collective-permute-start.32 = (bf16[1,136,2048]{2,1,0:T(8,128)(2,1)}, bf16[1,136,2048]{2,1,0:T(8,128)(2,1)S(1)}, u32[]{:S(2)}, u32[]{:S(2)}) collective-permute-start(bf16[1,136,2048]{2,1,0:T(8,128)(2,1)} %get-tuple-element.149), channel_id=1, source_target_pairs={{0,8},{4,12},{8,0},{12,4},{16,24},{20,28},{24,16},{28,20},{1,9},{5... | collective-permute-start | bytes 1671176 | tf_op jit(solution)/shard_map/ppermute | solution.py:21
  364.7 14.0 %collective-permute-start.33 = (bf16[1,136,2048]{2,1,0:T(8,128)(2,1)}, bf16[1,136,2048]{2,1,0:T(8,128)(2,1)S(1)}, u32[]{:S(2)}, u32[]{:S(2)}) collective-permute-start(bf16[1,136,2048]{2,1,0:T(8,128)(2,1)} %get-tuple-element.150), channel_id=1, source_target_pairs={{0,16},{4,20},{8,24},{12,28},{16,0},{20,4},{24,8},{28,12},{1,17},{... | collective-permute-start | bytes 1671176 | tf_op jit(solution)/shard_map/ppermute | solution.py:21
  383.6 55.9 %all-to-all-start.2 = ((bf16[8,704,256]{2,1,0:T(8,128)(2,1)}), bf16[8,704,256]{2,1,0:T(8,128)(2,1)}, u32[]{:S(2)}, u32[]{:S(2)}) async-start(bf16[8,704,256]{2,1,0:T(8,128)(2,1)} %get-tuple-element.152), calls=%async_computation.2 | async-start | bytes 5767168 | tf_op jit(solution)/shard_map/all_to_all | solution.py:968
  390.9 23.5 %collective-permute-start.35 = (bf16[272,512]{1,0:T(8,128)(2,1)S(1)}, bf16[272,512]{1,0:T(8,128)(2,1)S(1)}, u32[]{:S(2)}, u32[]{:S(2)}) collective-permute-start(bf16[272,512]{1,0:T(8,128)(2,1)S(1)} %copy-done.44), channel_id=1, source_target_pairs={{0,2},{1,3},{2,0},{3,1},{4,6},{5,7},{6,4},{7,5},{8,10},{9,11},{10,... | collective-permute-start | bytes 835592 | tf_op jit(solution)/shard_map/ppermute | solution.py:21
  390.9 23.5 %collective-permute-start.34 = (bf16[272,512]{1,0:T(8,128)(2,1)S(1)}, bf16[272,512]{1,0:T(8,128)(2,1)S(1)}, u32[]{:S(2)}, u32[]{:S(2)}) collective-permute-start(bf16[272,512]{1,0:T(8,128)(2,1)S(1)} %get-tuple-element.154), channel_id=1, source_target_pairs={{0,1},{1,0},{2,3},{3,2},{4,5},{5,4},{6,7},{7,6},{8,9},{9,8},{10,11... | collective-permute-start | bytes 835592 | tf_op jit(solution)/shard_map/ppermute | solution.py:21
  414.5 38.4 %collective-permute-start.37 = (bf16[272,512]{1,0:T(8,128)(2,1)S(1)}, bf16[272,512]{1,0:T(8,128)(2,1)}, u32[]{:S(2)}, u32[]{:S(2)}) collective-permute-start(bf16[272,512]{1,0:T(8,128)(2,1)S(1)} %add_convert_fusion.9.refs_0_), channel_id=1, source_target_pairs={{0,1},{1,0},{2,3},{3,2},{4,5},{5,4},{6,7},{7,6},{8,9},{9,8},{10,11... | collective-permute-start | bytes 835592 | tf_op jit(solution)/shard_map/ppermute | solution.py:21
  414.5 38.3 %collective-permute-start.38 = (bf16[272,512]{1,0:T(8,128)(2,1)S(1)}, bf16[272,512]{1,0:T(8,128)(2,1)}, u32[]{:S(2)}, u32[]{:S(2)}) collective-permute-start(bf16[272,512]{1,0:T(8,128)(2,1)S(1)} %add_convert_fusion.9.refs_0_), channel_id=1, source_target_pairs={{0,2},{1,3},{2,0},{3,1},{4,6},{5,7},{6,4},{7,5},{8,10},{9,11},{10,... | collective-permute-start | bytes 835592 | tf_op jit(solution)/shard_map/ppermute | solution.py:21
  416.3 36.6 %collective-permute-start.39 = (bf16[272,512]{1,0:T(8,128)(2,1)S(1)}, bf16[272,512]{1,0:T(8,128)(2,1)}, u32[]{:S(2)}, u32[]{:S(2)}) collective-permute-start(bf16[272,512]{1,0:T(8,128)(2,1)S(1)} %add_convert_fusion.9.refs_0_), channel_id=1, source_target_pairs={{0,3},{1,2},{2,1},{3,0},{4,7},{5,6},{6,5},{7,4},{8,11},{9,10},{10,... | collective-permute-start | bytes 835592 | tf_op jit(solution)/shard_map/ppermute | solution.py:21
  439.6 51.7 %all-to-all-start.3 = ((bf16[8,256,512]{2,1,0:T(8,128)(2,1)}), bf16[8,256,512]{2,1,0:T(8,128)(2,1)}, u32[]{:S(2)}, u32[]{:S(2)}) async-start(bf16[8,256,512]{2,1,0:T(8,128)(2,1)} %bitcast.150), calls=%async_computation.3 | async-start | bytes 4194304 | tf_op jit(solution)/shard_map/all_to_all | solution.py:970
  444.1 132.3 %reduce-scatter.5.cloned.1.call-start = ((), (), s32[]{:S(2)}) async-start(), calls=%async_computation.8 | async-start | bytes 3538944 | tf_op jit(solution)/shard_map/reduce_scatter | solution.py:1007
  471.7 16.0 %collective-permute-start.41 = (bf16[2,136,512]{2,1,0:T(8,128)(2,1)}, bf16[2,136,512]{2,1,0:T(8,128)(2,1)}, u32[]{:S(2)}, u32[]{:S(2)}) collective-permute-start(bf16[2,136,512]{2,1,0:T(8,128)(2,1)} %bitcast.37), channel_id=1, source_target_pairs={{0,16},{4,20},{8,24},{12,28},{16,0},{20,4},{24,8},{28,12},{1,17},{... | collective-permute-start | bytes 835592 | tf_op jit(solution)/shard_map/ppermute | solution.py:21
  475.2 14.2 %collective-permute-start.43 = (bf16[2,136,512]{2,1,0:T(8,128)(2,1)}, bf16[2,136,512]{2,1,0:T(8,128)(2,1)S(1)}, u32[]{:S(2)}, u32[]{:S(2)}) collective-permute-start(bf16[2,136,512]{2,1,0:T(8,128)(2,1)} %bitcast.41), channel_id=1, source_target_pairs={{0,8},{4,12},{8,0},{12,4},{16,24},{20,28},{24,16},{28,20},{1,9},{5... | collective-permute-start | bytes 835592 | tf_op jit(solution)/shard_map/ppermute | solution.py:21
  510.7 36.0 %all-to-all-start.4 = ((bf16[8,256,512]{2,1,0:T(8,128)(2,1)}), bf16[8,256,512]{2,1,0:T(8,128)(2,1)}, u32[]{:S(2)}, u32[]{:S(2)}) async-start(bf16[8,256,512]{2,1,0:T(8,128)(2,1)} %bitcast.179), calls=%async_computation.6 | async-start | bytes 4194304 | tf_op jit(solution)/shard_map/all_to_all | solution.py:1032
  517.7 49.6 %collective-permute-start.47 = (bf16[2,200,1024]{2,1,0:T(8,128)(2,1)}, bf16[2,200,1024]{2,1,0:T(8,128)(2,1)}, u32[]{:S(2)}, u32[]{:S(2)}) collective-permute-start(bf16[2,200,1024]{2,1,0:T(8,128)(2,1)} %add_convert_fusion.3), channel_id=1, source_target_pairs={{0,16},{4,20},{8,24},{12,28},{16,0},{20,4},{24,8},{28,12},{1,17},{... | collective-permute-start | bytes 2457608 | tf_op jit(solution)/shard_map/ppermute | solution.py:21
  521.9 45.5 %collective-permute-start.49 = (bf16[2,200,1024]{2,1,0:T(8,128)(2,1)}, bf16[2,200,1024]{2,1,0:T(8,128)(2,1)}, u32[]{:S(2)}, u32[]{:S(2)}) collective-permute-start(bf16[2,200,1024]{2,1,0:T(8,128)(2,1)} %add_convert_fusion.2), channel_id=1, source_target_pairs={{0,8},{4,12},{8,0},{12,4},{16,24},{20,28},{24,16},{28,20},{1,9},{5... | collective-permute-start | bytes 2457608 | tf_op jit(solution)/shard_map/ppermute | solution.py:21
  523.4 29.3 %collective-permute-start.50 = (bf16[552,512]{1,0:T(8,128)(2,1)}, bf16[552,512]{1,0:T(8,128)(2,1)S(1)}, u32[]{:S(2)}, u32[]{:S(2)}) collective-permute-start(bf16[552,512]{1,0:T(8,128)(2,1)} %get-tuple-element.179), channel_id=1, source_target_pairs={{0,1},{1,0},{2,3},{3,2},{4,5},{5,4},{6,7},{7,6},{8,9},{9,8},{10,11... | collective-permute-start | bytes 1695752 | tf_op jit(solution)/shard_map/ppermute | solution.py:21
  523.4 41.1 %collective-permute-start.51 = (bf16[552,512]{1,0:T(8,128)(2,1)}, bf16[552,512]{1,0:T(8,128)(2,1)S(1)}, u32[]{:S(2)}, u32[]{:S(2)}) collective-permute-start(bf16[552,512]{1,0:T(8,128)(2,1)} %get-tuple-element.180), channel_id=1, source_target_pairs={{0,2},{1,3},{2,0},{3,1},{4,6},{5,7},{6,4},{7,5},{8,10},{9,11},{10,... | collective-permute-start | bytes 1695752 | tf_op jit(solution)/shard_map/ppermute | solution.py:21
  525.4 39.0 %collective-permute-start.52 = (bf16[552,512]{1,0:T(8,128)(2,1)}, bf16[552,512]{1,0:T(8,128)(2,1)S(1)}, u32[]{:S(2)}, u32[]{:S(2)}) collective-permute-start(bf16[552,512]{1,0:T(8,128)(2,1)} %get-tuple-element.181), channel_id=1, source_target_pairs={{0,3},{1,2},{2,1},{3,0},{4,7},{5,6},{6,5},{7,4},{8,11},{9,10},{10,... | collective-permute-start | bytes 1695752 | tf_op jit(solution)/shard_map/ppermute | solution.py:21
  569.6 12.3 %collective-permute-start.54 = (bf16[1,200,1024]{2,1,0:T(8,128)(2,1)}, bf16[1,200,1024]{2,1,0:T(8,128)(2,1)}, u32[]{:S(2)}, u32[]{:S(2)}) collective-permute-start(bf16[1,200,1024]{2,1,0:T(8,128)(2,1)} %add_convert_fusion.4), channel_id=1, source_target_pairs={{0,16},{4,20},{8,24},{12,28},{16,0},{20,4},{24,8},{28,12},{1,17},{... | collective-permute-start | bytes 1228808 | tf_op jit(solution)/shard_map/ppermute | solution.py:21
  (96 other events, 1076.1 us)
Sparse Core Ops, SparseCore 0:
  10.5 69.4 all-gather.4
  88.6 38.2 all-gather.6
  378.9 107.4 reduce-scatter.2
  489.7 69.5 reduce-scatter.4
